TPU v7x, 32 devices: a whole 2x2x4 slice. The times are simulated.
32 devices in a mesh: frow: 16 (over z, y, core), fcol: 2 (over x).
Axes of the slice: x: 2, y: 2, z: 4, core: 2. Of those that a mesh axis runs over, the one named last changes fastest.
Arguments:
- face_input: bfloat16 [12, 64, 64, 256], P(None, 'frow', 'fcol'), may hold values from -6 to 6
- kernel: bfloat16 [3, 3, 256, 256], replicated, may hold values from -0.125 to 0.125
- convolution_bias: float32 [256], replicated, may hold values from -3 to 3
- upstream: bfloat16 [12, 64, 64, 256], P(None, 'frow', 'fcol'), may hold values from -6 to 6
- adjacency: int32 [12, 4, 3], replicated, may hold values from 0 to 11, as said below
Outputs:
- activation: bfloat16 [12, 64, 64, 256], P(None, 'frow', 'fcol')
- input_gradient: bfloat16 [12, 64, 64, 256], P(None, 'frow', 'fcol')
- kernel_grad: float32 [3, 3, 256, 256], replicated
- bias_grad: float32 [256], replicated
Inputs may be any that keep to these rules, and one draw needn't show every extreme that they name: adjacency[f, s] = (g, t, r): side s of face f (0 top, 1 bottom, 2 left, 3 right) borders side t of face g; t is 0 or 1 exactly when s is; r = 1 when positions along the seam run in opposite directions, else 0; the relation is symmetric, adjacency[g, t] = (f, s, r), and no side borders itself.
All inputs are finite; a program needn't handle non-finite values.
Results may differ from a plain program's by a relative error of at most 0.018.
Values may be sent and summed in bfloat16 or wider, within the bound.
No kernel may reach another device: no remote copies, remote signals or barrier semaphores. Data moves between devices by JAX's collectives and lax.ppermute only.
A program may use at most 128 MiB of HBM per device.

v0:
```python
import math

import jax
import jax.numpy as jnp
from jax import lax
from jax.sharding import PartitionSpec as P

DILATION_STEP = 2


half_root = 0.7071067811865476
density_scale = 0.3989422804014327


def from_partner(value, axis, distance):
    return lax.ppermute(value, axis, [(i, i ^ 1 << distance) for i in range(lax.axis_size(axis))])


def with_halo(block, sides, width):
    for axis, dim in sides:
        count = lax.axis_size(axis)
        forward = [(i, i + 1) for i in range(count - 1)]
        forward.append((count - 1, 0))
        backward = [(target, source) for source, target in forward]
        low = lax.ppermute(
            lax.slice_in_dim(block, block.shape[dim] - width, None, axis=dim), axis, forward
        )
        high = lax.ppermute(lax.slice_in_dim(block, 0, width, axis=dim), axis, backward)
        block = jnp.concatenate([low, block, high], axis=dim)
    return block


def gelu_value(value):
    return 0.5 * value * (1.0 + jax.scipy.special.erf(value * half_root))


def gelu_slope(value):
    return (
        0.5 * (1.0 + jax.scipy.special.erf(value * half_root))
        + value * jnp.exp(-0.5 * value * value) * density_scale
    )


def pick_table(entries, side_near, face_count):
    same_side = (entries[:, 1] == side_near).astype(jnp.int32)
    slot_index = (2 * entries[:, 2] + same_side) * face_count + entries[:, 0]
    return (slot_index[:, None] == jnp.arange(4 * face_count, dtype=jnp.int32)[None, :]).astype(
        jnp.bfloat16
    )


def reflect(row_band, col_band, returning):
    col_bits = lax.axis_size("fcol").bit_length() - 1
    all_bits = (lax.axis_size("frow") * lax.axis_size("fcol")).bit_length() - 1
    for bit_index in range(all_bits):
        moving = row_band if bit_index < col_bits else col_band
        if returning:
            moved = from_partner(moving, ("frow", "fcol"), bit_index)
        else:
            moved = from_partner(moving, ("frow", "fcol"), bit_index)
        if bit_index < col_bits:
            row_band = moved
        else:
            col_band = moved
    return (row_band, col_band)


def fold_border(extended, along, cells, inner_size):
    middle = lax.slice_in_dim(extended, 2 * cells, 2 * cells + inner_size, axis=along)
    before = lax.slice_in_dim(extended, 0, cells, axis=along)
    after_rim = lax.slice_in_dim(
        extended, inner_size + 3 * cells, inner_size + 4 * cells, axis=along
    )
    lead_pads = [(0, 0)] * extended.ndim
    tail_pads = [(0, 0)] * extended.ndim
    lead_pads[along] = (0, inner_size - cells)
    tail_pads[along] = (inner_size - cells, 0)
    return middle + jnp.pad(before, lead_pads) + jnp.pad(after_rim, tail_pads)


def local(face_input, kernel, convolution_bias, upstream, adjacency):
    face_count = face_input.shape[0]
    tile_rows = face_input.shape[1]
    tile_cols = face_input.shape[2]
    dilation_step = DILATION_STEP
    height = tile_rows + 2 * dilation_step
    breadth = tile_cols + 2 * dilation_step
    at_top = lax.axis_index("frow") == 0
    at_bottom = lax.axis_index("frow") == lax.axis_size("frow") - 1
    at_left = lax.axis_index("fcol") == 0
    at_right = lax.axis_index("fcol") == lax.axis_size("fcol") - 1
    column_index = jnp.arange(breadth)
    keep_cols = jnp.logical_not(
        at_left & (column_index < dilation_step)
        | at_right & (column_index >= tile_cols + dilation_step)
    )
    row_index = jnp.arange(height)
    keep_rows = jnp.logical_not(
        at_top & (row_index < dilation_step) | at_bottom & (row_index >= tile_rows + dilation_step)
    )
    padded_input = with_halo(face_input, (("frow", 1), ("fcol", 2)), dilation_step)
    row_wrap = jnp.where(
        at_top, padded_input[:, :dilation_step], padded_input[:, tile_rows + dilation_step :]
    )
    row_own = jnp.where(
        at_top,
        padded_input[:, dilation_step : 2 * dilation_step],
        padded_input[:, tile_rows : tile_rows + dilation_step],
    )
    col_wrap = jnp.where(
        at_left, padded_input[:, :, :dilation_step], padded_input[:, :, tile_cols + dilation_step :]
    )
    col_own = jnp.where(
        at_left,
        padded_input[:, :, dilation_step : 2 * dilation_step],
        padded_input[:, :, tile_cols : tile_cols + dilation_step],
    )
    row_send = jnp.concatenate([row_wrap, row_own], 1)
    col_send = jnp.concatenate([col_wrap, col_own], 2)
    far_rows, far_cols = reflect(row_send, col_send, False)
    row_pick = pick_table(
        jnp.where(at_top, adjacency[:, 0], adjacency[:, 1]), jnp.where(at_top, 0, 1), face_count
    )
    col_pick = pick_table(
        jnp.where(at_left, adjacency[:, 2], adjacency[:, 3]), jnp.where(at_left, 2, 3), face_count
    )
    row_cands = jnp.concatenate(
        [
            row_wrap,
            jnp.flip(row_own, 1),
            jnp.flip(far_rows[:, :dilation_step], 2),
            jnp.flip(far_rows[:, dilation_step:], (1, 2)),
        ],
        0,
    )
    row_halo = jnp.einsum("fk,kdwc->fdwc", row_pick, row_cands, preferred_element_type=jnp.float32)
    row_halo = jnp.where(keep_cols[None, None, :, None], row_halo, 0.0).astype(jnp.bfloat16)
    top_rim = jnp.where(at_top, row_halo, padded_input[:, :dilation_step])
    bottom_rim = jnp.where(at_bottom, row_halo, padded_input[:, tile_rows + dilation_step :])
    padded_input = jnp.concatenate(
        [top_rim, padded_input[:, dilation_step : tile_rows + dilation_step], bottom_rim], 1
    )
    col_cands = jnp.concatenate(
        [
            col_wrap,
            jnp.flip(col_own, 2),
            jnp.flip(far_cols[:, :, :dilation_step], 1),
            jnp.flip(far_cols[:, :, dilation_step:], (1, 2)),
        ],
        0,
    )
    col_halo = jnp.einsum("fk,kadc->fadc", col_pick, col_cands, preferred_element_type=jnp.float32)
    col_halo = jnp.where(keep_rows[None, :, None, None], col_halo, 0.0).astype(jnp.bfloat16)
    left_rim = jnp.where(at_left, col_halo, padded_input[:, :, :dilation_step])
    right_rim = jnp.where(at_right, col_halo, padded_input[:, :, tile_cols + dilation_step :])
    padded_input = jnp.concatenate(
        [left_rim, padded_input[:, :, dilation_step : tile_cols + dilation_step], right_rim], 2
    )
    random_values = ("NHWC", "HWIO", "NHWC")
    preactivation = (
        lax.conv_general_dilated(
            padded_input,
            kernel,
            (1, 1),
            "VALID",
            rhs_dilation=(dilation_step, dilation_step),
            dimension_numbers=random_values,
            preferred_element_type=jnp.float32,
        )
        + convolution_bias
    )
    activation = gelu_value(preactivation).astype(jnp.bfloat16)
    preactivation_gradient = (upstream.astype(jnp.float32) * gelu_slope(preactivation)).astype(
        jnp.bfloat16
    )
    tap_list = []
    for kernel_row_offset in range(3):
        for kernel_column_offset in range(3):
            input_window = padded_input[
                :,
                kernel_row_offset * dilation_step : kernel_row_offset * dilation_step + tile_rows,
                kernel_column_offset * dilation_step : kernel_column_offset * dilation_step
                + tile_cols,
            ]
            tap_list.append(
                lax.dot_general(
                    input_window,
                    preactivation_gradient,
                    (((0, 1, 2), (0, 1, 2)), ((), ())),
                    preferred_element_type=jnp.float32,
                )
            )
    kernel_local = jnp.stack(tap_list, 0).reshape(kernel.shape)
    bias_local = jnp.sum(preactivation_gradient.astype(jnp.float32), axis=(0, 1, 2))
    kernel_total, bias_total = lax.psum((kernel_local, bias_local), ("frow", "fcol"))
    scale = 1.0 / math.sqrt(
        face_count * tile_rows * lax.axis_size("frow") * tile_cols * lax.axis_size("fcol")
    )
    kernel_grad = kernel_total * scale
    bias_grad = bias_total * scale
    rotated_strip = jnp.transpose(jnp.flip(kernel, (0, 1)), (0, 1, 3, 2))
    twice = 2 * dilation_step
    padded_gradient = lax.conv_general_dilated(
        preactivation_gradient,
        rotated_strip,
        (1, 1),
        ((twice, twice), (twice, twice)),
        rhs_dilation=(dilation_step, dilation_step),
        dimension_numbers=random_values,
        preferred_element_type=jnp.float32,
    ).astype(jnp.bfloat16)
    row_seam = jnp.where(
        at_top, padded_gradient[:, :dilation_step], padded_gradient[:, tile_rows + dilation_step :]
    )
    row_seam = jnp.where(keep_cols[None, None, :, None], row_seam, jnp.zeros_like(row_seam))
    row_split = jnp.einsum("fk,fdwc->kdwc", row_pick, row_seam, preferred_element_type=jnp.float32)
    row_split = row_split.reshape((4, face_count) + row_split.shape[1:])
    col_seam = jnp.where(
        at_left,
        padded_gradient[:, :, :dilation_step],
        padded_gradient[:, :, tile_cols + dilation_step :],
    )
    col_seam = jnp.where(keep_rows[None, :, None, None], col_seam, jnp.zeros_like(col_seam))
    col_split = jnp.einsum("fk,fadc->kadc", col_pick, col_seam, preferred_element_type=jnp.float32)
    col_split = col_split.reshape((4, face_count) + col_split.shape[1:])
    row_far_grad = jnp.concatenate(
        [jnp.flip(row_split[2], 2), jnp.flip(row_split[3], (1, 2))], 1
    ).astype(jnp.bfloat16)
    col_far_grad = jnp.concatenate(
        [jnp.flip(col_split[2], 1), jnp.flip(col_split[3], (1, 2))], 2
    ).astype(jnp.bfloat16)
    row_back, col_back = reflect(row_far_grad, col_far_grad, True)
    wrap_rows = row_split[0] + row_back[:, :dilation_step].astype(jnp.float32)
    own_rows = jnp.flip(row_split[1], 1) + row_back[:, dilation_step:].astype(jnp.float32)
    wrap_cols = col_split[0] + col_back[:, :, :dilation_step].astype(jnp.float32)
    own_cols = jnp.flip(col_split[1], 2) + col_back[:, :, dilation_step:].astype(jnp.float32)
    gathered = padded_gradient.astype(jnp.float32)
    middle_rows = gathered[:, dilation_step : tile_rows + dilation_step]
    middle_rows = middle_rows + jnp.pad(
        jnp.where(at_top, own_rows, 0.0), ((0, 0), (0, tile_rows - dilation_step), (0, 0), (0, 0))
    )
    middle_rows = middle_rows + jnp.pad(
        jnp.where(at_bottom, own_rows, 0.0),
        ((0, 0), (tile_rows - dilation_step, 0), (0, 0), (0, 0)),
    )
    top_grad = jnp.where(at_top, wrap_rows, gathered[:, :dilation_step])
    bottom_grad = jnp.where(at_bottom, wrap_rows, gathered[:, tile_rows + dilation_step :])
    gathered = jnp.concatenate([top_grad, middle_rows, bottom_grad], 1)
    middle_cols = gathered[:, :, dilation_step : tile_cols + dilation_step]
    middle_cols = middle_cols + jnp.pad(
        jnp.where(at_left, own_cols, 0.0), ((0, 0), (0, 0), (0, tile_cols - dilation_step), (0, 0))
    )
    middle_cols = middle_cols + jnp.pad(
        jnp.where(at_right, own_cols, 0.0), ((0, 0), (0, 0), (tile_cols - dilation_step, 0), (0, 0))
    )
    left_grad = jnp.where(at_left, wrap_cols, gathered[:, :, :dilation_step])
    right_grad = jnp.where(at_right, wrap_cols, gathered[:, :, tile_cols + dilation_step :])
    gathered = jnp.concatenate([left_grad, middle_cols, right_grad], 2)
    returned = with_halo(
        gathered.astype(jnp.bfloat16), (("frow", 1), ("fcol", 2)), dilation_step
    ).astype(gathered.dtype)
    folded = fold_border(returned, 1, dilation_step, tile_rows)
    folded = fold_border(folded, 2, dilation_step, tile_cols)
    input_gradient = folded.astype(jnp.bfloat16)
    return (activation, input_gradient, kernel_grad, bias_grad)


def solution(mesh):
    return jax.shard_map(
        local,
        mesh=mesh,
        in_specs=(P(None, "frow", "fcol", None), P(), P(), P(None, "frow", "fcol", None), P()),
        out_specs=(P(None, "frow", "fcol", None), P(None, "frow", "fcol", None), P(), P()),
        check_vma=False,
    )
```

profile of v0, /device:TPU:0, one launch (start us, length us, event | category | flops | bytes accessed | tf_op | source)
XLA Modules:
  0.0 288.5 jit_solution(14397074329144345583)
XLA Ops:
  9.5 5.1 %collective-permute-start.1 = (bf16[12,2,32,256]{3,0,2,1:T(8,128)(2,1)S(1)}, bf16[12,2,32,256]{3,0,2,1:T(8,128)(2,1)}, u32[]{:S(2)}, u32[]{:S(2)}) collective-permute-start(bf16[12,2,32,256]{3,0,2,1:T(8,128)(2,1)S(1)} %copy.171), channel_id=1, source_target_pairs={{2,0},{4,2},{6,4},{8,6},{10,8},{12,10},{14,12},{16,14},{18,16},{20... | collective-permute-start | bytes 1179656 | tf_op jit(solution)/shard_map/ppermute | solution.py:28
  14.6 6.8 %collective-permute-done = bf16[12,2,32,256]{3,0,2,1:T(8,128)(2,1)} collective-permute-done((bf16[12,2,32,256]{3,0,2,1:T(8,128)(2,1)S(1)}, bf16[12,2,32,256]{3,0,2,1:T(8,128)(2,1)}, u32[]{:S(2)}, u32[]{:S(2)}) %collective-permute-start) | collective-permute-done | bytes 393248 | tf_op jit(solution)/shard_map/ppermute | solution.py:25
  25.4 2.0 collective-permute-start.3
  27.5 2.9 %collective-permute-done.3 = bf16[12,8,2,256]{3,0,2,1:T(8,128)(2,1)S(1)} collective-permute-done((bf16[12,8,2,256]{3,0,2,1:T(8,128)(2,1)S(1)}, bf16[12,8,2,256]{3,0,2,1:T(8,128)(2,1)S(1)}, u32[]{:S(2)}, u32[]{:S(2)}) %collective-permute-start.3) | collective-permute-done | bytes 98336 | tf_op jit(solution)/shard_map/ppermute | solution.py:28
  30.4 2.7 collective-permute-done.2
  33.1 2.0 collective-permute-start.4
  35.1 1.9 pad_maximum_fusion.1
  43.2 6.7 %collective-permute-done.5 = bf16[12,8,4,256]{3,0,2,1:T(8,128)(2,1)S(1)} collective-permute-done((bf16[12,8,4,256]{3,0,2,1:T(8,128)(2,1)S(1)}, bf16[12,8,4,256]{3,0,2,1:T(8,128)(2,1)S(1)}, u32[]{:S(2)}, u32[]{:S(2)}) %collective-permute-start.5) | collective-permute-done | bytes 196640 | tf_op jit(solution)/shard_map/ppermute | solution.py:16
  51.5 6.3 %collective-permute-done.6 = bf16[12,8,4,256]{3,0,2,1:T(8,128)(2,1)S(1)} collective-permute-done((bf16[12,8,4,256]{3,0,2,1:T(8,128)(2,1)S(1)}, bf16[12,8,4,256]{3,0,2,1:T(8,128)(2,1)S(1)}, u32[]{:S(2)}, u32[]{:S(2)}) %collective-permute-start.6) | collective-permute-done | bytes 196640 | tf_op jit(solution)/shard_map/ppermute | solution.py:16
  57.7 2.8 collective-permute-start.7
  64.4 7.3 %collective-permute-done.7 = bf16[12,8,4,256]{3,0,2,1:T(8,128)(2,1)} collective-permute-done((bf16[12,8,4,256]{3,0,2,1:T(8,128)(2,1)S(1)}, bf16[12,8,4,256]{3,0,2,1:T(8,128)(2,1)}, u32[]{:S(2)}, u32[]{:S(2)}) %collective-permute-start.7) | collective-permute-done | bytes 196640 | tf_op jit(solution)/shard_map/ppermute | solution.py:16
  73.4 3.0 %fusion.111 = (bf16[12,2,36,256]{3,1,2,0:T(2,128)(2,1)S(1)}, bf16[12,2,36,256]{3,1,2,0:T(2,128)(2,1)}) fusion(bf16[12,4,36,256]{3,1,2,0:T(4,128)(2,1)} %collective-permute-done.8), kind=kLoop, calls=%fused_computation.185 | loop fusion | bytes 1769472 | tf_op jit(solution)/shard_map/slice | solution.py:131
  77.3 1.9 rev.54
  83.1 2.7 broadcast_select_fusion.1
  88.5 2.1 pad_maximum_fusion.5
  90.7 2.8 fusion.5
  93.5 2.6 convert_reduce_fusion
  96.1 8.3 %fusion.115 = (f32[12,8,36,256]{3,0,2,1:T(8,128)}, bf16[12,8,36,256]{3,0,2,1:T(8,128)(2,1)S(1)}) fusion(bf16[3,3,256,256]{3,2,1,0:T(8,128)(2,1)S(1)} %copy-done, bf16[12,4,32,256]{3,2,1,0:T(8,128)(2,1)S(1)} %get-tuple-element.21), kind=kOutput, calls=%fused_computation.189 | convolution fusion | flops 1813708800 | bytes 7274496 | tf_op jit(solution)/shard_map/conv_general_dilated | solution.py:203
  104.8 2.6 fusion.60
  111.6 2.0 fusion.108
  119.7 6.2 %collective-permute-done.10 = bf16[12,8,4,256]{3,0,2,1:T(8,128)(2,1)S(1)} collective-permute-done((bf16[12,8,4,256]{3,0,2,1:T(8,128)(2,1)}, bf16[12,8,4,256]{3,0,2,1:T(8,128)(2,1)S(1)}, u32[]{:S(2)}, u32[]{:S(2)}) %collective-permute-start.10) | collective-permute-done | bytes 196640 | tf_op jit(solution)/shard_map/ppermute | solution.py:16
  127.7 5.8 %collective-permute-done.11 = bf16[12,8,4,256]{3,0,2,1:T(8,128)(2,1)S(1)} collective-permute-done((bf16[12,8,4,256]{3,0,2,1:T(8,128)(2,1)S(1)}, bf16[12,8,4,256]{3,0,2,1:T(8,128)(2,1)S(1)}, u32[]{:S(2)}, u32[]{:S(2)}) %collective-permute-start.11) | collective-permute-done | bytes 196640 | tf_op jit(solution)/shard_map/ppermute | solution.py:16
  133.6 2.4 collective-permute-start.12
  137.2 12.1 %collective-permute-done.12 = bf16[12,8,4,256]{3,0,2,1:T(8,128)(2,1)S(1)} collective-permute-done((bf16[12,8,4,256]{3,0,2,1:T(8,128)(2,1)S(1)}, bf16[12,8,4,256]{3,0,2,1:T(8,128)(2,1)S(1)}, u32[]{:S(2)}, u32[]{:S(2)}) %collective-permute-start.12) | collective-permute-done | bytes 196640 | tf_op jit(solution)/shard_map/ppermute | solution.py:16
  149.4 2.2 fusion.110
  151.7 3.5 %slice_select_fusion.3 = (f32[12,2,36,256]{3,0,2,1:T(8,128)S(1)}, f32[12,2,36,256]{3,0,2,1:T(8,128)S(1)}, f32[12,2,36,256]{3,0,2,1:T(8,128)S(1)}) fusion(f32[12,8,36,256]{3,0,2,1:T(8,128)} %get-tuple-element.70, f32[48,2,36,256]{3,0,2,1:T(8,128)} %fusion.60, bf16[12,2,36,256]{3,1,2,0:T(2,128)(2,1)S(1)} %get-tuple-element.57, pred[]{:T(512)S(6)} %eq.57, ...), kind=kLoop, calls=%fused_computation.53 | loop fusion | flops 884736 | bytes 6635522 | tf_op jit(solution)/shard_map/jit(_where)/select_n | solution.py:246
  158.7 4.1 %collective-permute-start.15 = (bf16[12,2,36,256]{3,1,2,0:T(2,128)(2,1)}, bf16[12,2,36,256]{3,1,2,0:T(2,128)(2,1)S(1)}, u32[]{:S(2)}, u32[]{:S(2)}) collective-permute-start(bf16[12,2,36,256]{3,1,2,0:T(2,128)(2,1)} %copy.103), channel_id=1, source_target_pairs={{2,0},{4,2},{6,4},{8,6},{10,8},{12,10},{14,12},{16,14},{18,16},{20... | collective-permute-start | bytes 1327112 | tf_op jit(solution)/shard_map/ppermute | solution.py:28
  164.1 42.6 %psum.15 = f32[256]{0:T(256)S(1)} all-reduce(f32[256]{0:T(256)S(1)} %get-tuple-element.20), channel_id=1, replica_groups=mesh['frow'=16,'fcol'=2] {'frow','fcol'}, use_global_device_ids=true, to_apply=%region_2.3 | all-reduce | flops 256 | bytes 2048 | tf_op jit(solution)/shard_map/psum | solution.py:195
  209.4 2.3 collective-permute-start.16
  211.7 60.8 %all-reduce.8.cloned.1.call-done = f32[3,3,256,256]{3,2,1,0:T(8,128)} async-done(((f32[3,3,256,256]{3,2,1,0:T(8,128)}), f32[3,3,256,256]{3,2,1,0:T(8,128)}) %all-reduce.8.cloned.1.call-update) | async-done | bytes 2359312 | tf_op jit(solution)/shard_map/psum | solution.py:195
  272.5 3.3 %broadcast_multiply_fusion = f32[3,3,256,256]{3,2,1,0:T(8,128)} fusion(f32[3,3,256,256]{3,2,1,0:T(8,128)} %all-reduce.8.cloned.1.call-done), kind=kLoop, calls=%fused_computation.57 | loop fusion | flops 589824 | bytes 4718592 | tf_op jit(solution)/shard_map/mul | solution.py:199
  275.7 2.9 %maximum_convert_fusion = f32[12,12,40,256]{3,0,2,1:T(8,128)S(1)} fusion(bf16[12,12,2,256]{3,0,2,1:T(8,128)(2,1)} %collective-permute-done.17, bf16[12,2,36,256]{3,0,2,1:T(8,128)(2,1)S(1)} %copy.105, bf16[12,8,2,256]{3,0,2,1:T(8,128)(2,1)S(1)} %get-tuple-element.25, bf16[12,8,32,256]{3,0,2,1:T(8,128)(2,1)S(1)} %fusion.1, ...), kind=kLoop, calls=%fused_computation.4 | loop fusion | flops 10321920 | bytes 8847360 | tf_op jit(solution)/shard_map/convert_element_type | solution.py:261
  (142 shorter events, 51.4 us)
Async XLA Ops:
  7.2 83.5 %copy-start = (bf16[3,3,256,256]{3,2,1,0:T(8,128)(2,1)S(1)}, bf16[3,3,256,256]{3,2,1,0:T(8,128)(2,1)}, u32[]{:S(2)}) copy-start(bf16[3,3,256,256]{3,2,1,0:T(8,128)(2,1)} %param.6) | copy-start | bytes 3538948
  7.2 15.3 %copy-start.3 = (bf16[12,4,32,256]{3,2,1,0:T(8,128)(2,1)S(1)}, bf16[12,4,32,256]{3,2,1,0:T(8,128)(2,1)}, u32[]{:S(2)}) copy-start(bf16[12,4,32,256]{3,2,1,0:T(8,128)(2,1)} %param.5) | copy-start | bytes 2359300
  7.2 265.3 %all-reduce.8.cloned.1.call-start = ((), (), s32[]{:S(2)}) async-start(), calls=%async_computation | async-start | bytes 4718592 | tf_op jit(solution)/shard_map/psum | solution.py:195
  8.8 12.6 %collective-permute-start = (bf16[12,2,32,256]{3,0,2,1:T(8,128)(2,1)S(1)}, bf16[12,2,32,256]{3,0,2,1:T(8,128)(2,1)}, u32[]{:S(2)}, u32[]{:S(2)}) collective-permute-start(bf16[12,2,32,256]{3,0,2,1:T(8,128)(2,1)S(1)} %copy.170), channel_id=1, source_target_pairs={{0,2},{2,4},{4,6},{6,8},{8,10},{10,12},{12,14},{14,16},{16,18},{18... | collective-permute-start | bytes 1179656 | tf_op jit(solution)/shard_map/ppermute | solution.py:25
  9.5 17.9 %copy-start.17 = (s32[12,4,3]{0,1,2:T(4,128)S(1)}, s32[12,4,3]{0,1,2:T(4,128)}, u32[]{:S(2)}) copy-start(s32[12,4,3]{0,1,2:T(4,128)} %param.9) | copy-start | bytes 1732
  9.5 13.4 %collective-permute-start.1 = (bf16[12,2,32,256]{3,0,2,1:T(8,128)(2,1)S(1)}, bf16[12,2,32,256]{3,0,2,1:T(8,128)(2,1)}, u32[]{:S(2)}, u32[]{:S(2)}) collective-permute-start(bf16[12,2,32,256]{3,0,2,1:T(8,128)(2,1)S(1)} %copy.171), channel_id=1, source_target_pairs={{2,0},{4,2},{6,4},{8,6},{10,8},{12,10},{14,12},{16,14},{18,16},{20... | collective-permute-start | bytes 1179656 | tf_op jit(solution)/shard_map/ppermute | solution.py:28
  25.4 5.0 %collective-permute-start.3 = (bf16[12,8,2,256]{3,0,2,1:T(8,128)(2,1)S(1)}, bf16[12,8,2,256]{3,0,2,1:T(8,128)(2,1)S(1)}, u32[]{:S(2)}, u32[]{:S(2)}) collective-permute-start(bf16[12,8,2,256]{3,0,2,1:T(8,128)(2,1)S(1)} %get-tuple-element.49), channel_id=1, source_target_pairs={{1,0},{0,1},{3,2},{2,3},{5,4},{4,5},{7,6},{6,7},{9,8},{8,9},{11,10... | collective-permute-start | bytes 294920 | tf_op jit(solution)/shard_map/ppermute | solution.py:28
  27.4 5.7 %collective-permute-start.2 = (bf16[12,8,2,256]{3,0,2,1:T(8,128)(2,1)S(1)}, bf16[12,8,2,256]{3,0,2,1:T(8,128)(2,1)S(1)}, u32[]{:S(2)}, u32[]{:S(2)}) collective-permute-start(bf16[12,8,2,256]{3,0,2,1:T(8,128)(2,1)S(1)} %get-tuple-element.51), channel_id=1, source_target_pairs={{0,1},{1,0},{2,3},{3,2},{4,5},{5,4},{6,7},{7,6},{8,9},{9,8},{10,11... | collective-permute-start | bytes 294920 | tf_op jit(solution)/shard_map/ppermute | solution.py:25
  33.1 8.4 %collective-permute-start.4 = (bf16[12,8,4,256]{3,0,2,1:T(8,128)(2,1)S(1)}, bf16[12,8,4,256]{3,0,2,1:T(8,128)(2,1)S(1)}, u32[]{:S(2)}, u32[]{:S(2)}) collective-permute-start(bf16[12,8,4,256]{3,0,2,1:T(8,128)(2,1)S(1)} %pad_maximum_fusion.12), channel_id=1, source_target_pairs={{0,2},{1,3},{2,0},{3,1},{4,6},{5,7},{6,4},{7,5},{8,10},{9,11},{10,... | collective-permute-start | bytes 589832 | tf_op jit(solution)/shard_map/ppermute | solution.py:16
  37.2 2.9 %copy-start.4 = (bf16[12,2,36,256]{3,0,2,1:T(8,128)(2,1)}, bf16[12,2,36,256]{3,0,2,1:T(8,128)(2,1)S(1)}, u32[]{:S(2)}) copy-start(bf16[12,2,36,256]{3,0,2,1:T(8,128)(2,1)S(1)} %get-tuple-element.38) | copy-start | bytes 1327108
  37.2 4.3 %copy-start.9 = (bf16[12,2,36,256]{3,0,2,1:T(8,128)(2,1)}, bf16[12,2,36,256]{3,0,2,1:T(8,128)(2,1)S(1)}, u32[]{:S(2)}) copy-start(bf16[12,2,36,256]{3,0,2,1:T(8,128)(2,1)S(1)} %get-tuple-element.37) | copy-start | bytes 1327108
  40.1 33.3 %collective-permute-start.8 = (bf16[12,4,36,256]{3,1,2,0:T(4,128)(2,1)}, bf16[12,4,36,256]{3,1,2,0:T(4,128)(2,1)}, u32[]{:S(2)}, u32[]{:S(2)}) collective-permute-start(bf16[12,4,36,256]{3,1,2,0:T(4,128)(2,1)} %copy.94), channel_id=1, source_target_pairs={{0,1},{1,0},{2,3},{3,2},{4,5},{5,4},{6,7},{7,6},{8,9},{9,8},{10,11... | collective-permute-start | bytes 2654216 | tf_op jit(solution)/shard_map/ppermute | solution.py:16
  41.5 8.4 %collective-permute-start.5 = (bf16[12,8,4,256]{3,0,2,1:T(8,128)(2,1)S(1)}, bf16[12,8,4,256]{3,0,2,1:T(8,128)(2,1)S(1)}, u32[]{:S(2)}, u32[]{:S(2)}) collective-permute-start(bf16[12,8,4,256]{3,0,2,1:T(8,128)(2,1)S(1)} %collective-permute-done.4), channel_id=1, source_target_pairs={{0,4},{1,5},{2,6},{3,7},{4,0},{5,1},{6,2},{7,3},{8,12},{9,13},{10,... | collective-permute-start | bytes 589832 | tf_op jit(solution)/shard_map/ppermute | solution.py:16
  43.2 39.9 %copy-start.21 = (pred[36]{0:T(512)(128)(4,1)}, pred[36]{0:T(512)(128)(4,1)S(1)}, u32[]{:S(2)}) copy-start(pred[36]{0:T(512)(128)(4,1)S(1)} %or_not_fusion) | copy-start | bytes 112
  49.9 7.9 %collective-permute-start.6 = (bf16[12,8,4,256]{3,0,2,1:T(8,128)(2,1)S(1)}, bf16[12,8,4,256]{3,0,2,1:T(8,128)(2,1)S(1)}, u32[]{:S(2)}, u32[]{:S(2)}) collective-permute-start(bf16[12,8,4,256]{3,0,2,1:T(8,128)(2,1)S(1)} %collective-permute-done.5), channel_id=1, source_target_pairs={{0,8},{1,9},{2,10},{3,11},{4,12},{5,13},{6,14},{7,15},{8,0},{9,1},... | collective-permute-start | bytes 589832 | tf_op jit(solution)/shard_map/ppermute | solution.py:16
  57.7 14.0 %collective-permute-start.7 = (bf16[12,8,4,256]{3,0,2,1:T(8,128)(2,1)S(1)}, bf16[12,8,4,256]{3,0,2,1:T(8,128)(2,1)}, u32[]{:S(2)}, u32[]{:S(2)}) collective-permute-start(bf16[12,8,4,256]{3,0,2,1:T(8,128)(2,1)S(1)} %collective-permute-done.6), channel_id=1, source_target_pairs={{0,16},{1,17},{2,18},{3,19},{4,20},{5,21},{6,22},{7,23},{8,24},{9,... | collective-permute-start | bytes 589832 | tf_op jit(solution)/shard_map/ppermute | solution.py:16
  90.7 2.8 copy-start.18
  96.1 8.7 %copy-start.22 = (pred[36]{0:T(512)(128)(4,1)S(1)}, pred[36]{0:T(512)(128)(4,1)}, u32[]{:S(2)}) copy-start(pred[36]{0:T(512)(128)(4,1)} %copy-done.21) | copy-start | bytes 112
  104.7 5.2 %copy-start.6 = (f32[48,8,2,256]{3,0,2,1:T(8,128)}, f32[48,8,2,256]{3,0,2,1:T(8,128)S(1)}, u32[]{:S(2)}) copy-start(f32[48,8,2,256]{3,0,2,1:T(8,128)S(1)} %fusion.78) | copy-start | bytes 2359300
  111.5 5.8 %collective-permute-start.9 = (bf16[12,8,4,256]{3,0,2,1:T(8,128)(2,1)S(1)}, bf16[12,8,4,256]{3,0,2,1:T(8,128)(2,1)}, u32[]{:S(2)}, u32[]{:S(2)}) collective-permute-start(bf16[12,8,4,256]{3,0,2,1:T(8,128)(2,1)S(1)} %pad_maximum_fusion.13), channel_id=1, source_target_pairs={{0,2},{1,3},{2,0},{3,1},{4,6},{5,7},{6,4},{7,5},{8,10},{9,11},{10,... | collective-permute-start | bytes 589832 | tf_op jit(solution)/shard_map/ppermute | solution.py:16
  115.4 34.0 %collective-permute-start.13 = (bf16[12,4,36,256]{3,1,2,0:T(4,128)(2,1)}, bf16[12,4,36,256]{3,1,2,0:T(4,128)(2,1)}, u32[]{:S(2)}, u32[]{:S(2)}) collective-permute-start(bf16[12,4,36,256]{3,1,2,0:T(4,128)(2,1)} %copy.99), channel_id=1, source_target_pairs={{0,1},{1,0},{2,3},{3,2},{4,5},{5,4},{6,7},{7,6},{8,9},{9,8},{10,11... | collective-permute-start | bytes 2654216 | tf_op jit(solution)/shard_map/ppermute | solution.py:16
  117.3 8.6 %collective-permute-start.10 = (bf16[12,8,4,256]{3,0,2,1:T(8,128)(2,1)}, bf16[12,8,4,256]{3,0,2,1:T(8,128)(2,1)S(1)}, u32[]{:S(2)}, u32[]{:S(2)}) collective-permute-start(bf16[12,8,4,256]{3,0,2,1:T(8,128)(2,1)} %collective-permute-done.9), channel_id=1, source_target_pairs={{0,4},{1,5},{2,6},{3,7},{4,0},{5,1},{6,2},{7,3},{8,12},{9,13},{10,... | collective-permute-start | bytes 589832 | tf_op jit(solution)/shard_map/ppermute | solution.py:16
  118.4 8.1 %copy-start.10 = (bf16[12,4,32,256]{3,0,2,1:T(8,128)(2,1)S(1)}, bf16[12,4,32,256]{3,0,2,1:T(8,128)(2,1)}, u32[]{:S(2)}) copy-start(bf16[12,4,32,256]{3,0,2,1:T(8,128)(2,1)} %get-tuple-element.54) | copy-start | bytes 2359300
  125.9 7.7 %collective-permute-start.11 = (bf16[12,8,4,256]{3,0,2,1:T(8,128)(2,1)S(1)}, bf16[12,8,4,256]{3,0,2,1:T(8,128)(2,1)S(1)}, u32[]{:S(2)}, u32[]{:S(2)}) collective-permute-start(bf16[12,8,4,256]{3,0,2,1:T(8,128)(2,1)S(1)} %collective-permute-done.10), channel_id=1, source_target_pairs={{0,8},{1,9},{2,10},{3,11},{4,12},{5,13},{6,14},{7,15},{8,0},{9,1},... | collective-permute-start | bytes 589832 | tf_op jit(solution)/shard_map/ppermute | solution.py:16
  126.5 9.4 %copy-start.11 = (bf16[12,4,32,256]{3,0,2,1:T(8,128)(2,1)S(1)}, bf16[12,4,32,256]{3,0,2,1:T(8,128)(2,1)}, u32[]{:S(2)}) copy-start(bf16[12,4,32,256]{3,0,2,1:T(8,128)(2,1)} %get-tuple-element.39) | copy-start | bytes 2359300
  133.6 15.8 %collective-permute-start.12 = (bf16[12,8,4,256]{3,0,2,1:T(8,128)(2,1)S(1)}, bf16[12,8,4,256]{3,0,2,1:T(8,128)(2,1)S(1)}, u32[]{:S(2)}, u32[]{:S(2)}) collective-permute-start(bf16[12,8,4,256]{3,0,2,1:T(8,128)(2,1)S(1)} %collective-permute-done.11), channel_id=1, source_target_pairs={{0,16},{1,17},{2,18},{3,19},{4,20},{5,21},{6,22},{7,23},{8,24},{9,... | collective-permute-start | bytes 589832 | tf_op jit(solution)/shard_map/ppermute | solution.py:16
  151.7 3.9 %slice-start = ((s8[4718592]{0:T(1024)(128)(4,1)}), s8[4194304]{0:T(1024)(128)(4,1)S(1)}, s32[]{:S(2)}) async-start(s8[4718592]{0:T(1024)(128)(4,1)} %bitcast.111), calls=%async_computation.1 | async-start | bytes 8388608
  151.7 4.0 %slice-start.1 = ((s8[4718592]{0:T(1024)(128)(4,1)}), s8[524288]{0:T(1024)(128)(4,1)S(1)}, s32[]{:S(2)}) async-start(s8[4718592]{0:T(1024)(128)(4,1)} %bitcast.111), calls=%async_computation.2 | async-start | bytes 1048576
  158.7 48.6 %collective-permute-start.15 = (bf16[12,2,36,256]{3,1,2,0:T(2,128)(2,1)}, bf16[12,2,36,256]{3,1,2,0:T(2,128)(2,1)S(1)}, u32[]{:S(2)}, u32[]{:S(2)}) collective-permute-start(bf16[12,2,36,256]{3,1,2,0:T(2,128)(2,1)} %copy.103), channel_id=1, source_target_pairs={{2,0},{4,2},{6,4},{8,6},{10,8},{12,10},{14,12},{16,14},{18,16},{20... | collective-permute-start | bytes 1327112 | tf_op jit(solution)/shard_map/ppermute | solution.py:28
  164.1 43.3 %collective-permute-start.14 = (bf16[12,2,36,256]{3,1,2,0:T(2,128)(2,1)}, bf16[12,2,36,256]{3,1,2,0:T(2,128)(2,1)}, u32[]{:S(2)}, u32[]{:S(2)}) collective-permute-start(bf16[12,2,36,256]{3,1,2,0:T(2,128)(2,1)} %copy.102), channel_id=1, source_target_pairs={{0,2},{2,4},{4,6},{6,8},{8,10},{10,12},{12,14},{14,16},{16,18},{18... | collective-permute-start | bytes 1327112 | tf_op jit(solution)/shard_map/ppermute | solution.py:25
  209.4 66.4 %collective-permute-start.16 = (bf16[12,12,2,256]{3,0,2,1:T(8,128)(2,1)}, bf16[12,12,2,256]{3,0,2,1:T(8,128)(2,1)}, u32[]{:S(2)}, u32[]{:S(2)}) collective-permute-start(bf16[12,12,2,256]{3,0,2,1:T(8,128)(2,1)} %get-tuple-element.26), channel_id=1, source_target_pairs={{0,1},{1,0},{2,3},{3,2},{4,5},{5,4},{6,7},{7,6},{8,9},{9,8},{10,11... | collective-permute-start | bytes 442376 | tf_op jit(solution)/shard_map/ppermute | solution.py:25
  211.6 64.1 %collective-permute-start.17 = (bf16[12,12,2,256]{3,0,2,1:T(8,128)(2,1)}, bf16[12,12,2,256]{3,0,2,1:T(8,128)(2,1)}, u32[]{:S(2)}, u32[]{:S(2)}) collective-permute-start(bf16[12,12,2,256]{3,0,2,1:T(8,128)(2,1)} %get-tuple-element.27), channel_id=1, source_target_pairs={{1,0},{0,1},{3,2},{2,3},{5,4},{4,5},{7,6},{6,7},{9,8},{8,9},{11,10... | collective-permute-start | bytes 442376 | tf_op jit(solution)/shard_map/ppermute | solution.py:28
  (12 other events, 17.8 us)
Sparse Core Ops, SparseCore 0:
  137.3 135.0 all-reduce.7
where the time goes:
time: 289 us; the launch traced here: 288 us
  waiting for transfers between devices  118 us (41%)
  blocking collectives  42.6 us (15%)
  local copies, waits for them, and re-layouts  37.7 us (13%)
  starting transfers between devices  28.4 us (10%)
  matrix products  24.5 us (8%)
  other arithmetic  23.1 us (8%)
  between operations  14.6 us (5%)
    psum x1, waiting for transfers between devices, local(): lax.psum((kernel_local, bias_local), ('frow', 'fcol'))  60.8 us
    ppermute x10, waiting for transfers between devices, from_partner(): lax.ppermute(value, axis, [(i, i ^ 1 << distance) for i in range(lax.axis...  44.4 us
    psum x1, blocking collectives, local(): lax.psum((kernel_local, bias_local), ('frow', 'fcol'))  42.6 us
    ppermute x10, starting transfers between devices, from_partner(): lax.ppermute(value, axis, [(i, i ^ 1 << distance) for i in range(lax.axis...  14.2 us
    unnamed x59, local copies, waits for them, and re-layouts  11.3 us
    ppermute x4, starting transfers between devices, with_halo(): lax.ppermute(lax.slice_in_dim(block, 0, width, axis=dim), axis, backward)  11.2 us
    ppermute x4, waiting for transfers between devices, with_halo(): lax.ppermute(lax.slice_in_dim(block, block.shape[dim] - width, None, axis...  9.43 us
    conv_general_dilated x1, matrix products, local(): lax.conv_general_dilated(preactivation_gradient, rotated_strip, (1, 1), (...  8.28 us
  transfers between devices with their start and end apart: 19, of which 10 were waited for; matrix products, arithmetic and copies ran while one was open for 13% of the time, Pallas kernels for 0%

commit v1 on v0

--- a/solution.py
+++ b/solution.py
@@ -10,10 +10,6 @@
 
 half_root = 0.7071067811865476
 density_scale = 0.3989422804014327
-
-
-def from_partner(value, axis, distance):
-    return lax.ppermute(value, axis, [(i, i ^ 1 << distance) for i in range(lax.axis_size(axis))])
 
 
 def with_halo(block, sides, width):
@@ -49,20 +45,99 @@
     )
 
 
-def reflect(row_band, col_band, returning):
+def mirror_pairs(rows, cols, edge_rows, flip_rows, flip_cols):
+    pairs = []
+    for r in range(rows):
+        for c in range(cols):
+            on_edge = r in (0, rows - 1) if edge_rows else c in (0, cols - 1)
+            if on_edge:
+                target_row = rows - 1 - r if flip_rows else r
+                target_col = cols - 1 - c if flip_cols else c
+                pairs.append((r * cols + c, target_row * cols + target_col))
+    return pairs
+
+
+def reflect(row_band, col_band):
+    rows, cols = lax.axis_size("frow"), lax.axis_size("fcol")
+    axes = ("frow", "fcol")
+    row_band = lax.ppermute(row_band, axes, mirror_pairs(rows, cols, True, False, True))
+    col_band = lax.ppermute(col_band, axes, mirror_pairs(rows, cols, False, True, False))
+    return (row_band, col_band)
+
+
+def reduce_stages():
     col_bits = lax.axis_size("fcol").bit_length() - 1
     all_bits = (lax.axis_size("frow") * lax.axis_size("fcol")).bit_length() - 1
-    for bit_index in range(all_bits):
-        moving = row_band if bit_index < col_bits else col_band
-        if returning:
-            moved = from_partner(moving, ("frow", "fcol"), bit_index)
-        else:
-            moved = from_partner(moving, ("frow", "fcol"), bit_index)
-        if bit_index < col_bits:
-            row_band = moved
-        else:
-            col_band = moved
-    return (row_band, col_band)
+    rest = [1 << bit for bit in range(all_bits) if bit != col_bits]
+    stages = [(1 << col_bits,)]
+    while rest:
+        stages.append(tuple(rest[:2]))
+        rest = rest[2:]
+    return stages
+
+
+def stage_offsets(stage):
+    return (0, stage[0]) if len(stage) == 1 else (0, stage[0], stage[1], stage[0] ^ stage[1])
+
+
+def stage_place(index, stage):
+    place = (index // stage[0]) % 2
+    if len(stage) == 2:
+        place = place + 2 * ((index // stage[1]) % 2)
+    return place
+
+
+def fold_sum(terms):
+    while len(terms) > 1:
+        terms = [terms[i] + terms[i + 1] for i in range(0, len(terms), 2)]
+    return terms[0]
+
+
+def reduce_everywhere(matrix, vector):
+    axes = ("frow", "fcol")
+    count = lax.axis_size("frow") * lax.axis_size("fcol")
+    index = lax.axis_index("frow") * lax.axis_size("fcol") + lax.axis_index("fcol")
+    width = matrix.shape[-1]
+    pad = jnp.zeros((7, width), jnp.float32)
+    vector = jnp.concatenate([vector[None], pad], 0)
+    part = matrix.reshape(-1, width)
+    stages = reduce_stages()
+    for stage in stages:
+        offsets = stage_offsets(stage)
+        place = stage_place(index, stage)
+        part = part.reshape(len(offsets), -1, width).astype(jnp.bfloat16)
+        vector = lax.optimization_barrier(vector.astype(jnp.bfloat16))
+        rows = part.shape[1]
+        sums, vectors = [], []
+        for order, offset in enumerate(offsets):
+            piece = lax.dynamic_index_in_dim(part, place ^ order, 0, False)
+            if offset:
+                packed = jnp.concatenate([piece, vector], 0)
+                packed = lax.ppermute(packed, axes, [(i, i ^ offset) for i in range(count)])
+                sums.append(packed[:rows].astype(jnp.float32))
+                vectors.append(packed[rows:].astype(jnp.float32))
+            else:
+                sums.append(piece.astype(jnp.float32))
+                vectors.append(vector.astype(jnp.float32))
+        part = fold_sum(sums)
+        vector = fold_sum(vectors)
+    part = lax.optimization_barrier(part.astype(jnp.bfloat16))[None]
+    for stage in stages[::-1]:
+        offsets = stage_offsets(stage)
+        place = stage_place(index, stage)
+        pieces = [part] + [
+            lax.ppermute(part, axes, [(i, i ^ offset) for i in range(count)])
+            for offset in offsets[1:]
+        ]
+        stacked = jnp.stack(pieces, 0)
+        part = jnp.concatenate(
+            [
+                lax.dynamic_index_in_dim(stacked, place ^ order, 0, False)
+                for order in range(len(offsets))
+            ],
+            0,
+        )
+    return (part.reshape(matrix.shape).astype(jnp.float32), vector[0])
 
 
 def fold_border(extended, along, cells, inner_size):
@@ -117,7 +192,7 @@
     )
     row_send = jnp.concatenate([row_wrap, row_own], 1)
     col_send = jnp.concatenate([col_wrap, col_own], 2)
-    far_rows, far_cols = reflect(row_send, col_send, False)
+    far_rows, far_cols = reflect(row_send, col_send)
     row_pick = pick_table(
         jnp.where(at_top, adjacency[:, 0], adjacency[:, 1]), jnp.where(at_top, 0, 1), face_count
     )
@@ -192,7 +267,7 @@
             )
     kernel_local = jnp.stack(tap_list, 0).reshape(kernel.shape)
     bias_local = jnp.sum(preactivation_gradient.astype(jnp.float32), axis=(0, 1, 2))
-    kernel_total, bias_total = lax.psum((kernel_local, bias_local), ("frow", "fcol"))
+    kernel_total, bias_total = reduce_everywhere(kernel_local, bias_local)
     scale = 1.0 / math.sqrt(
         face_count * tile_rows * lax.axis_size("frow") * tile_cols * lax.axis_size("fcol")
     )
@@ -229,7 +304,7 @@
     col_far_grad = jnp.concatenate(
         [jnp.flip(col_split[2], 1), jnp.flip(col_split[3], (1, 2))], 2
     ).astype(jnp.bfloat16)
-    row_back, col_back = reflect(row_far_grad, col_far_grad, True)
+    row_back, col_back = reflect(row_far_grad, col_far_grad)
     wrap_rows = row_split[0] + row_back[:, :dilation_step].astype(jnp.float32)
     own_rows = jnp.flip(row_split[1], 1) + row_back[:, dilation_step:].astype(jnp.float32)
     wrap_cols = col_split[0] + col_back[:, :, :dilation_step].astype(jnp.float32)

time: 289 us -> 171 us (0.59)
  waiting for transfers between devices: 118 us -> 62.6 us
  blocking collectives: 42.6 us -> 0 us
  between operations: 14.6 us -> 1.65 us
  local copies, waits for them, and re-layouts: 37.7 us -> 30.3 us
  starting transfers between devices: 28.4 us -> 35.1 us
  matrix products: 24.5 us -> 21.2 us
  other arithmetic: 23.1 us -> 19.9 us
    psum x1 -> x0, waiting for transfers between devices: 60.8 us -> none  [local(): lax.psum((kernel_local, bias_local), ('frow', 'fcol'))]
    psum x1 -> x0, blocking collectives: 42.6 us -> none  [local(): lax.psum((kernel_local, bias_local), ('frow', 'fcol'))]
    ppermute x10 -> x18, starting transfers between devices: 14.2 us -> 24.8 us  [the longest x7 8.4 us: reduce_everywhere(): packed = lax.ppermute(packed, axes, [(i, i ^ offset) for i in range(count)])]
    ppermute x4, waiting for transfers between devices: 9.43 us -> 15.1 us  [with_halo(): lax.ppermute(lax.slice_in_dim(block, block.shape[dim] - width, None, axis...]
    convert_element_type x0 -> x6, other arithmetic: none -> 4.1 us  [the longest x1 1.92 us: local(): activation = gelu_value(preactivation).astype(jnp.bfloat16)]
    ppermute x4, starting transfers between devices: 11.2 us -> 8.29 us  [with_halo(): lax.ppermute(lax.slice_in_dim(block, 0, width, axis=dim), axis, backward)]
    unnamed x59 -> x71, local copies, waits for them, and re-layouts: 11.3 us -> 9.34 us
    ppermute x10 -> x18, waiting for transfers between devices: 44.4 us -> 42.8 us  [the longest x7 21.1 us: reduce_everywhere(): lax.ppermute(part, axes, [(i, i ^ offset) for i in range(count)])]
  transfers between devices with their start and end apart: 19 -> 26, of which waited for: 10 -> 11; matrix products, arithmetic and copies ran while one was open for 13% -> 16% of each run, Pallas kernels for 0% -> 0%
where the time goes in v1:
time: 171 us
  waiting for transfers between devices  62.6 us (37%)
  starting transfers between devices  35.1 us (21%)
  local copies, waits for them, and re-layouts  30.3 us (18%)
  matrix products  21.2 us (12%)
  other arithmetic  19.9 us (12%)
    ppermute x7, waiting for transfers between devices, reduce_everywhere(): lax.ppermute(part, axes, [(i, i ^ offset) for i in range(count)])  21.1 us
    ppermute x4, waiting for transfers between devices, with_halo(): lax.ppermute(lax.slice_in_dim(block, block.shape[dim] - width, None, axis...  15.1 us
    ppermute x2, waiting for transfers between devices, reflect(): lax.ppermute(col_band, axes, mirror_pairs(rows, cols, False, True, False))  11.1 us
    ppermute x7, waiting for transfers between devices, reduce_everywhere(): packed = lax.ppermute(packed, axes, [(i, i ^ offset) for i in range(count)])  10.7 us
    unnamed x71, local copies, waits for them, and re-layouts  9.34 us
    ppermute x7, starting transfers between devices, reduce_everywhere(): packed = lax.ppermute(packed, axes, [(i, i ^ offset) for i in range(count)])  8.4 us
    conv_general_dilated x1, matrix products, local(): lax.conv_general_dilated(preactivation_gradient, rotated_strip, (1, 1), (...  8.36 us
    ppermute x7, starting transfers between devices, reduce_everywhere(): lax.ppermute(part, axes, [(i, i ^ offset) for i in range(count)])  8.3 us
  transfers between devices with their start and end apart: 26, of which 11 were waited for; matrix products, arithmetic and copies ran while one was open for 16% of the time, Pallas kernels for 0%

profile of v1, /device:TPU:0, one launch (start us, length us, event | category | flops | bytes accessed | tf_op | source)
XLA Modules:
  0.0 170.8 jit_solution(6214508950867161112)
XLA Ops:
  3.0 5.1 %collective-permute-start.1 = (bf16[12,2,32,256]{3,0,2,1:T(8,128)(2,1)S(1)}, bf16[12,2,32,256]{3,0,2,1:T(8,128)(2,1)S(1)}, u32[]{:S(2)}, u32[]{:S(2)}) collective-permute-start(bf16[12,2,32,256]{3,0,2,1:T(8,128)(2,1)S(1)} %copy.166), channel_id=1, source_target_pairs={{2,0},{4,2},{6,4},{8,6},{10,8},{12,10},{14,12},{16,14},{18,16},{20... | collective-permute-start | bytes 1179656 | tf_op jit(solution)/shard_map/ppermute | solution.py:24
  8.1 6.7 %collective-permute-done = bf16[12,2,32,256]{3,0,2,1:T(8,128)(2,1)} collective-permute-done((bf16[12,2,32,256]{3,0,2,1:T(8,128)(2,1)S(1)}, bf16[12,2,32,256]{3,0,2,1:T(8,128)(2,1)}, u32[]{:S(2)}, u32[]{:S(2)}) %collective-permute-start) | collective-permute-done | bytes 393248 | tf_op jit(solution)/shard_map/ppermute | solution.py:21
  16.5 2.0 %collective-permute-start.3 = (bf16[12,8,2,256]{3,0,2,1:T(8,128)(2,1)S(1)}, bf16[12,8,2,256]{3,0,2,1:T(8,128)(2,1)S(1)}, u32[]{:S(2)}, u32[]{:S(2)}) collective-permute-start(bf16[12,8,2,256]{3,0,2,1:T(8,128)(2,1)S(1)} %get-tuple-element.48), channel_id=1, source_target_pairs={{1,0},{0,1},{3,2},{2,3},{5,4},{4,5},{7,6},{6,7},{9,8},{8,9},{11,10... | collective-permute-start | bytes 294920 | tf_op jit(solution)/shard_map/ppermute | solution.py:24
  19.1 2.4 %collective-permute-done.3 = bf16[12,8,2,256]{3,0,2,1:T(8,128)(2,1)S(1)} collective-permute-done((bf16[12,8,2,256]{3,0,2,1:T(8,128)(2,1)S(1)}, bf16[12,8,2,256]{3,0,2,1:T(8,128)(2,1)S(1)}, u32[]{:S(2)}, u32[]{:S(2)}) %collective-permute-start.3) | collective-permute-done | bytes 98336 | tf_op jit(solution)/shard_map/ppermute | solution.py:24
  21.5 2.8 %collective-permute-done.2 = bf16[12,8,2,256]{3,0,2,1:T(8,128)(2,1)S(1)} collective-permute-done((bf16[12,8,2,256]{3,0,2,1:T(8,128)(2,1)S(1)}, bf16[12,8,2,256]{3,0,2,1:T(8,128)(2,1)S(1)}, u32[]{:S(2)}, u32[]{:S(2)}) %collective-permute-start.2) | collective-permute-done | bytes 98336 | tf_op jit(solution)/shard_map/ppermute | solution.py:21
  26.1 1.6 copy.91
  27.7 3.3 %collective-permute-start.5 = (bf16[12,4,36,256]{3,1,2,0:T(4,128)(2,1)}, bf16[12,4,36,256]{3,1,2,0:T(4,128)(2,1)}, u32[]{:S(2)}, u32[]{:S(2)}) collective-permute-start(bf16[12,4,36,256]{3,1,2,0:T(4,128)(2,1)} %copy.91), channel_id=1, source_target_pairs={{0,1},{1,0},{30,31},{31,30}} | collective-permute-start | bytes 2654216 | tf_op jit(solution)/shard_map/ppermute | solution.py:63
  35.6 7.3 %collective-permute-done.4 = bf16[12,8,4,256]{3,0,2,1:T(8,128)(2,1)} collective-permute-done((bf16[12,8,4,256]{3,0,2,1:T(8,128)(2,1)}, bf16[12,8,4,256]{3,0,2,1:T(8,128)(2,1)}, u32[]{:S(2)}, u32[]{:S(2)}) %collective-permute-start.4) | collective-permute-done | bytes 196640 | tf_op jit(solution)/shard_map/ppermute | solution.py:64
  45.2 3.0 %fusion.145 = (bf16[12,2,36,256]{3,1,2,0:T(2,128)(2,1)S(1)}, bf16[12,2,36,256]{3,1,2,0:T(2,128)(2,1)}) fusion(bf16[12,4,36,256]{3,1,2,0:T(4,128)(2,1)} %collective-permute-done.5), kind=kLoop, calls=%fused_computation.256 | loop fusion | bytes 1769472 | tf_op jit(solution)/shard_map/slice | solution.py:206
  51.1 2.5 %broadcast_select_fusion.1 = (bf16[12,2,36,256]{3,0,2,1:T(8,128)(2,1)S(1)}, bf16[12,2,36,256]{3,0,2,1:T(8,128)(2,1)S(1)}) fusion(pred[]{:T(512)S(6)} %eq.68, bf16[12,8,36,256]{3,0,2,1:T(8,128)(2,1)} %copy-done.2, pred[]{:T(512)S(6)} %eq.69, bf16[12,2,36,256]{3,0,2,1:T(8,128)(2,1)} %rev.55, bf16[12,2,36,256]{3,0,2,1:T(8,128)(2,1)} %rev.54, ...), kind=kOutput, calls=%fused_computation.142 | convolution fusion | flops 29196864 | bytes 3539030 | tf_op jit(solution)/shard_map/fk,kdwc->fdwc/dot_general | solution.py:211
  56.4 2.7 %fusion.5 = f32[12,4,32,256]{3,0,2,1:T(8,128)S(1)} fusion(bf16[3,3,256,256]{3,2,1,0:T(8,128)(2,1)S(1)} %copy-done, bf16[12,8,2,256]{3,0,2,1:T(8,128)(2,1)S(1)} %get-tuple-element.34, bf16[12,8,32,256]{3,0,2,1:T(8,128)(2,1)S(1)} %slice.366, bf16[12,8,2,256]{3,0,2,1:T(8,128)(2,1)S(1)} %get-tuple-element.33), kind=kOutput, calls=%fused_computation.17 | convolution fusion | flops 1813708800 | bytes 4521984 | tf_op jit(solution)/shard_map/conv_general_dilated | solution.py:236
  60.5 8.4 %fusion.149 = (f32[12,8,36,256]{3,0,2,1:T(8,128)}, bf16[12,8,36,256]{3,0,2,1:T(8,128)(2,1)S(1)}) fusion(bf16[3,3,256,256]{3,2,1,0:T(8,128)(2,1)S(1)} %copy-done, bf16[12,4,32,256]{3,2,1,0:T(8,128)(2,1)S(1)} %get-tuple-element.21), kind=kOutput, calls=%fused_computation.260 | convolution fusion | flops 1813708800 | bytes 7274496 | tf_op jit(solution)/shard_map/conv_general_dilated | solution.py:278
  76.3 2.2 %fusion.83 = f32[48,2,36,256]{3,0,2,1:T(8,128)S(1)} fusion(bf16[12,8,36,256]{3,0,2,1:T(8,128)(2,1)} %copy-done.5, pred[36]{0:T(512)(128)(4,1)S(1)} %copy-done.28, pred[]{:T(512)S(6)} %eq.68, s32[12]{0:T(128)S(1)} %fusion.131), kind=kOutput, calls=%fused_computation.133 | convolution fusion | flops 21676608 | bytes 4718677 | tf_op jit(solution)/shard_map/fk,fdwc->kdwc/dot_general | solution.py:291
  78.5 1.8 %copy-done.3 = f32[48,2,36,256]{3,0,2,1:T(8,128)} copy-done((f32[48,2,36,256]{3,0,2,1:T(8,128)}, f32[48,2,36,256]{3,0,2,1:T(8,128)S(1)}, u32[]{:S(2)}) %copy-start.3) | copy-done | bytes 3538968
  81.6 1.9 %rev.77 = bf16[12,2,36,256]{3,0,2,1:T(8,128)(2,1)} reverse(bf16[12,2,36,256]{3,0,2,1:T(8,128)(2,1)} %get-tuple-element.29), dimensions={2} | reverse | bytes 884736 | tf_op jit(solution)/shard_map/jit(_flip)/rev | solution.py:302
  83.5 1.9 %rev.76 = bf16[12,2,36,256]{3,0,2,1:T(8,128)(2,1)} reverse(bf16[12,2,36,256]{3,0,2,1:T(8,128)(2,1)} %get-tuple-element.30), dimensions={1,2} | reverse | bytes 884736 | tf_op jit(solution)/shard_map/jit(_flip)/rev | solution.py:302
  85.4 1.5 pad_maximum_fusion.4
  87.6 2.7 %collective-permute-start.7 = (bf16[12,4,36,256]{3,1,2,0:T(4,128)(2,1)S(1)}, bf16[12,4,36,256]{3,1,2,0:T(4,128)(2,1)S(1)}, u32[]{:S(2)}, u32[]{:S(2)}) collective-permute-start(bf16[12,4,36,256]{3,1,2,0:T(4,128)(2,1)S(1)} %copy.96), channel_id=1, source_target_pairs={{0,1},{1,0},{30,31},{31,30}} | collective-permute-start | bytes 2654216 | tf_op jit(solution)/shard_map/ppermute | solution.py:63
  93.8 2.3 %collective-permute-start.15 = (bf16[296,256]{1,0:T(8,128)(2,1)S(1)}, bf16[296,256]{1,0:T(8,128)(2,1)S(1)}, u32[]{:S(2)}, u32[]{:S(2)}) collective-permute-start(bf16[296,256]{1,0:T(8,128)(2,1)S(1)} %get-tuple-element.94), channel_id=1, source_target_pairs={{0,5},{1,4},{2,7},{3,6},{4,1},{5,0},{6,3},{7,2},{8,13},{9,12},{10,... | collective-permute-start | bytes 454664 | tf_op jit(solution)/shard_map/ppermute | solution.py:116
  96.1 1.9 %multiply_convert_fusion = bf16[12,4,32,256]{3,2,1,0:T(8,128)(2,1)} fusion(f32[256]{0:T(256)S(1)} %copy-done.22, f32[12,4,32,256]{3,0,2,1:T(8,128)S(1)} %fusion.5), kind=kLoop, calls=%fused_computation.48 | loop fusion | flops 2359296 | bytes 2360320 | tf_op jit(solution)/shard_map/convert_element_type | solution.py:247
  98.0 9.4 %collective-permute-done.13 = bf16[296,256]{1,0:T(8,128)(2,1)S(1)} collective-permute-done((bf16[296,256]{1,0:T(8,128)(2,1)S(1)}, bf16[296,256]{1,0:T(8,128)(2,1)S(1)}, u32[]{:S(2)}, u32[]{:S(2)}) %collective-permute-start.13) | collective-permute-done | bytes 151584 | tf_op jit(solution)/shard_map/ppermute | solution.py:116
  107.7 4.3 %collective-permute-start.18 = (bf16[80,256]{1,0:T(8,128)(2,1)S(1)}, bf16[80,256]{1,0:T(8,128)(2,1)S(1)}, u32[]{:S(2)}, u32[]{:S(2)}) collective-permute-start(bf16[80,256]{1,0:T(8,128)(2,1)S(1)} %get-tuple-element.91), channel_id=1, source_target_pairs={{0,24},{1,25},{2,26},{3,27},{4,28},{5,29},{6,30},{7,31},{8,16},{9,... | collective-permute-start | bytes 122888 | tf_op jit(solution)/shard_map/ppermute | solution.py:116
  114.6 3.4 %collective-permute-start.21 = (bf16[1,72,256]{2,1,0:T(8,128)(2,1)S(1)}, bf16[1,72,256]{2,1,0:T(8,128)(2,1)S(1)}, u32[]{:S(2)}, u32[]{:S(2)}) collective-permute-start(bf16[1,72,256]{2,1,0:T(8,128)(2,1)S(1)} %bitcast.240), channel_id=1, source_target_pairs={{0,24},{1,25},{2,26},{3,27},{4,28},{5,29},{6,30},{7,31},{8,16},{9,... | collective-permute-start | bytes 110600 | tf_op jit(solution)/shard_map/ppermute | solution.py:129
  119.0 3.8 %collective-permute-done.6 = bf16[12,8,4,256]{3,0,2,1:T(8,128)(2,1)S(1)} collective-permute-done((bf16[12,8,4,256]{3,0,2,1:T(8,128)(2,1)S(1)}, bf16[12,8,4,256]{3,0,2,1:T(8,128)(2,1)S(1)}, u32[]{:S(2)}, u32[]{:S(2)}) %collective-permute-start.6) | collective-permute-done | bytes 196640 | tf_op jit(solution)/shard_map/ppermute | solution.py:64
  122.9 6.4 %collective-permute-done.20 = bf16[1,72,256]{2,1,0:T(8,128)(2,1)S(1)} collective-permute-done((bf16[1,72,256]{2,1,0:T(8,128)(2,1)S(1)}, bf16[1,72,256]{2,1,0:T(8,128)(2,1)S(1)}, u32[]{:S(2)}, u32[]{:S(2)}) %collective-permute-start.20) | collective-permute-done | bytes 36896 | tf_op jit(solution)/shard_map/ppermute | solution.py:129
  134.5 2.2 %collective-permute-start.23 = (bf16[4,72,256]{2,1,0:T(8,128)(2,1)S(1)}, bf16[4,72,256]{2,1,0:T(8,128)(2,1)S(1)}, u32[]{:S(2)}, u32[]{:S(2)}) collective-permute-start(bf16[4,72,256]{2,1,0:T(8,128)(2,1)S(1)} %get-tuple-element.79), channel_id=1, source_target_pairs={{0,4},{1,5},{2,6},{3,7},{4,0},{5,1},{6,2},{7,3},{8,12},{9,13},{10,... | collective-permute-start | bytes 442376 | tf_op jit(solution)/shard_map/ppermute | solution.py:129
  138.9 14.6 %collective-permute-done.23 = bf16[4,72,256]{2,1,0:T(8,128)(2,1)S(1)} collective-permute-done((bf16[4,72,256]{2,1,0:T(8,128)(2,1)S(1)}, bf16[4,72,256]{2,1,0:T(8,128)(2,1)S(1)}, u32[]{:S(2)}, u32[]{:S(2)}) %collective-permute-start.23) | collective-permute-done | bytes 147488 | tf_op jit(solution)/shard_map/ppermute | solution.py:129
  153.9 1.4 collective-permute-start.10
  156.3 5.6 %collective-permute-done.10 = bf16[12,12,2,256]{3,0,2,1:T(8,128)(2,1)S(1)} collective-permute-done((bf16[12,12,2,256]{3,0,2,1:T(8,128)(2,1)S(1)}, bf16[12,12,2,256]{3,0,2,1:T(8,128)(2,1)S(1)}, u32[]{:S(2)}, u32[]{:S(2)}) %collective-permute-start.10) | collective-permute-done | bytes 147488 | tf_op jit(solution)/shard_map/ppermute | solution.py:21
  161.8 2.3 %collective-permute-done.11 = bf16[12,12,2,256]{3,0,2,1:T(8,128)(2,1)S(1)} collective-permute-done((bf16[12,12,2,256]{3,0,2,1:T(8,128)(2,1)S(1)}, bf16[12,12,2,256]{3,0,2,1:T(8,128)(2,1)S(1)}, u32[]{:S(2)}, u32[]{:S(2)}) %collective-permute-start.11) | collective-permute-done | bytes 147488 | tf_op jit(solution)/shard_map/ppermute | solution.py:24
  164.1 1.6 maximum_convert_fusion
  169.2 1.6 convert_multiply_fusion
  (193 shorter events, 48.5 us)
Async XLA Ops:
  0.6 55.8 %copy-start = (bf16[3,3,256,256]{3,2,1,0:T(8,128)(2,1)S(1)}, bf16[3,3,256,256]{3,2,1,0:T(8,128)(2,1)}, u32[]{:S(2)}) copy-start(bf16[3,3,256,256]{3,2,1,0:T(8,128)(2,1)} %param.6) | copy-start | bytes 3538948
  2.2 12.6 %collective-permute-start = (bf16[12,2,32,256]{3,0,2,1:T(8,128)(2,1)S(1)}, bf16[12,2,32,256]{3,0,2,1:T(8,128)(2,1)}, u32[]{:S(2)}, u32[]{:S(2)}) collective-permute-start(bf16[12,2,32,256]{3,0,2,1:T(8,128)(2,1)S(1)} %copy.165), channel_id=1, source_target_pairs={{0,2},{2,4},{4,6},{6,8},{8,10},{10,12},{12,14},{14,16},{16,18},{18... | collective-permute-start | bytes 1179656 | tf_op jit(solution)/shard_map/ppermute | solution.py:21
  3.0 13.4 %collective-permute-start.1 = (bf16[12,2,32,256]{3,0,2,1:T(8,128)(2,1)S(1)}, bf16[12,2,32,256]{3,0,2,1:T(8,128)(2,1)S(1)}, u32[]{:S(2)}, u32[]{:S(2)}) collective-permute-start(bf16[12,2,32,256]{3,0,2,1:T(8,128)(2,1)S(1)} %copy.166), channel_id=1, source_target_pairs={{2,0},{4,2},{6,4},{8,6},{10,8},{12,10},{14,12},{16,14},{18,16},{20... | collective-permute-start | bytes 1179656 | tf_op jit(solution)/shard_map/ppermute | solution.py:24
  16.5 5.0 %collective-permute-start.3 = (bf16[12,8,2,256]{3,0,2,1:T(8,128)(2,1)S(1)}, bf16[12,8,2,256]{3,0,2,1:T(8,128)(2,1)S(1)}, u32[]{:S(2)}, u32[]{:S(2)}) collective-permute-start(bf16[12,8,2,256]{3,0,2,1:T(8,128)(2,1)S(1)} %get-tuple-element.48), channel_id=1, source_target_pairs={{1,0},{0,1},{3,2},{2,3},{5,4},{4,5},{7,6},{6,7},{9,8},{8,9},{11,10... | collective-permute-start | bytes 294920 | tf_op jit(solution)/shard_map/ppermute | solution.py:24
  18.5 5.8 %collective-permute-start.2 = (bf16[12,8,2,256]{3,0,2,1:T(8,128)(2,1)S(1)}, bf16[12,8,2,256]{3,0,2,1:T(8,128)(2,1)S(1)}, u32[]{:S(2)}, u32[]{:S(2)}) collective-permute-start(bf16[12,8,2,256]{3,0,2,1:T(8,128)(2,1)S(1)} %get-tuple-element.50), channel_id=1, source_target_pairs={{0,1},{1,0},{2,3},{3,2},{4,5},{5,4},{6,7},{7,6},{8,9},{9,8},{10,11... | collective-permute-start | bytes 294920 | tf_op jit(solution)/shard_map/ppermute | solution.py:21
  27.7 17.6 %collective-permute-start.5 = (bf16[12,4,36,256]{3,1,2,0:T(4,128)(2,1)}, bf16[12,4,36,256]{3,1,2,0:T(4,128)(2,1)}, u32[]{:S(2)}, u32[]{:S(2)}) collective-permute-start(bf16[12,4,36,256]{3,1,2,0:T(4,128)(2,1)} %copy.91), channel_id=1, source_target_pairs={{0,1},{1,0},{30,31},{31,30}} | collective-permute-start | bytes 2654216 | tf_op jit(solution)/shard_map/ppermute | solution.py:63
  31.0 23.6 %copy-start.23 = (pred[8]{0:T(512)(128)(4,1)}, pred[8]{0:T(512)(128)(4,1)S(1)}, u32[]{:S(2)}) copy-start(pred[8]{0:T(512)(128)(4,1)S(1)} %or_not_fusion.1) | copy-start | bytes 28
  31.7 11.1 %collective-permute-start.4 = (bf16[12,8,4,256]{3,0,2,1:T(8,128)(2,1)}, bf16[12,8,4,256]{3,0,2,1:T(8,128)(2,1)}, u32[]{:S(2)}, u32[]{:S(2)}) collective-permute-start(bf16[12,8,4,256]{3,0,2,1:T(8,128)(2,1)} %pad_maximum_fusion.18), channel_id=1, source_target_pairs={{0,30},{1,31},{2,28},{3,29},{4,26},{5,27},{6,24},{7,25},{8,22},{9,... | collective-permute-start | bytes 589832 | tf_op jit(solution)/shard_map/ppermute | solution.py:64
  75.4 14.9 %collective-permute-start.12 = (bf16[1160,256]{1,0:T(8,128)(2,1)}, bf16[1160,256]{1,0:T(8,128)(2,1)}, u32[]{:S(2)}, u32[]{:S(2)}) collective-permute-start(bf16[1160,256]{1,0:T(8,128)(2,1)} %pad_maximum_fusion.9), channel_id=1, source_target_pairs={{0,2},{1,3},{2,0},{3,1},{4,6},{5,7},{6,4},{7,5},{8,10},{9,11},{10,... | collective-permute-start | bytes 1781768 | tf_op jit(solution)/shard_map/ppermute | solution.py:116
  87.6 41.8 %collective-permute-start.7 = (bf16[12,4,36,256]{3,1,2,0:T(4,128)(2,1)S(1)}, bf16[12,4,36,256]{3,1,2,0:T(4,128)(2,1)S(1)}, u32[]{:S(2)}, u32[]{:S(2)}) collective-permute-start(bf16[12,4,36,256]{3,1,2,0:T(4,128)(2,1)S(1)} %copy.96), channel_id=1, source_target_pairs={{0,1},{1,0},{30,31},{31,30}} | collective-permute-start | bytes 2654216 | tf_op jit(solution)/shard_map/ppermute | solution.py:63
  91.0 39.0 %slice-start = ((s8[4718592]{0:T(1024)(128)(4,1)}), s8[4194304]{0:T(1024)(128)(4,1)S(1)}, s32[]{:S(2)}) async-start(s8[4718592]{0:T(1024)(128)(4,1)} %bitcast.227), calls=%async_computation | async-start | bytes 8388608
  92.5 14.9 %collective-permute-start.13 = (bf16[296,256]{1,0:T(8,128)(2,1)S(1)}, bf16[296,256]{1,0:T(8,128)(2,1)S(1)}, u32[]{:S(2)}, u32[]{:S(2)}) collective-permute-start(bf16[296,256]{1,0:T(8,128)(2,1)S(1)} %get-tuple-element.92), channel_id=1, source_target_pairs={{0,1},{1,0},{2,3},{3,2},{4,5},{5,4},{6,7},{7,6},{8,9},{9,8},{10,11... | collective-permute-start | bytes 454664 | tf_op jit(solution)/shard_map/ppermute | solution.py:116
  93.8 13.6 %collective-permute-start.14 = (bf16[296,256]{1,0:T(8,128)(2,1)S(1)}, bf16[296,256]{1,0:T(8,128)(2,1)S(1)}, u32[]{:S(2)}, u32[]{:S(2)}) collective-permute-start(bf16[296,256]{1,0:T(8,128)(2,1)S(1)} %get-tuple-element.93), channel_id=1, source_target_pairs={{0,4},{1,5},{2,6},{3,7},{4,0},{5,1},{6,2},{7,3},{8,12},{9,13},{10,... | collective-permute-start | bytes 454664 | tf_op jit(solution)/shard_map/ppermute | solution.py:116
  93.8 18.3 %copy-start.9 = (f32[48,8,2,256]{3,0,2,1:T(8,128)S(1)}, f32[48,8,2,256]{3,0,2,1:T(8,128)}, u32[]{:S(2)}) copy-start(f32[48,8,2,256]{3,0,2,1:T(8,128)} %copy-done.8) | copy-start | bytes 2359300
  93.8 36.2 %slice-start.1 = ((s8[4718592]{0:T(1024)(128)(4,1)}), s8[524288]{0:T(1024)(128)(4,1)S(1)}, s32[]{:S(2)}) async-start(s8[4718592]{0:T(1024)(128)(4,1)} %bitcast.227), calls=%async_computation.1 | async-start | bytes 1048576
  93.8 13.6 %collective-permute-start.15 = (bf16[296,256]{1,0:T(8,128)(2,1)S(1)}, bf16[296,256]{1,0:T(8,128)(2,1)S(1)}, u32[]{:S(2)}, u32[]{:S(2)}) collective-permute-start(bf16[296,256]{1,0:T(8,128)(2,1)S(1)} %get-tuple-element.94), channel_id=1, source_target_pairs={{0,5},{1,4},{2,7},{3,6},{4,1},{5,0},{6,3},{7,2},{8,13},{9,12},{10,... | collective-permute-start | bytes 454664 | tf_op jit(solution)/shard_map/ppermute | solution.py:116
  107.6 5.7 %collective-permute-start.16 = (bf16[80,256]{1,0:T(8,128)(2,1)S(1)}, bf16[80,256]{1,0:T(8,128)(2,1)S(1)}, u32[]{:S(2)}, u32[]{:S(2)}) collective-permute-start(bf16[80,256]{1,0:T(8,128)(2,1)S(1)} %get-tuple-element.89), channel_id=1, source_target_pairs={{0,8},{1,9},{2,10},{3,11},{4,12},{5,13},{6,14},{7,15},{8,0},{9,1},... | collective-permute-start | bytes 122888 | tf_op jit(solution)/shard_map/ppermute | solution.py:116
  107.6 5.6 %collective-permute-start.17 = (bf16[80,256]{1,0:T(8,128)(2,1)S(1)}, bf16[80,256]{1,0:T(8,128)(2,1)S(1)}, u32[]{:S(2)}, u32[]{:S(2)}) collective-permute-start(bf16[80,256]{1,0:T(8,128)(2,1)S(1)} %get-tuple-element.90), channel_id=1, source_target_pairs={{0,16},{1,17},{2,18},{3,19},{4,20},{5,21},{6,22},{7,23},{8,24},{9,... | collective-permute-start | bytes 122888 | tf_op jit(solution)/shard_map/ppermute | solution.py:116
  107.7 6.8 %collective-permute-start.18 = (bf16[80,256]{1,0:T(8,128)(2,1)S(1)}, bf16[80,256]{1,0:T(8,128)(2,1)S(1)}, u32[]{:S(2)}, u32[]{:S(2)}) collective-permute-start(bf16[80,256]{1,0:T(8,128)(2,1)S(1)} %get-tuple-element.91), channel_id=1, source_target_pairs={{0,24},{1,25},{2,26},{3,27},{4,28},{5,29},{6,30},{7,31},{8,16},{9,... | collective-permute-start | bytes 122888 | tf_op jit(solution)/shard_map/ppermute | solution.py:116
  112.1 18.0 %copy-start.4 = (f32[48,2,36,256]{3,0,2,1:T(8,128)S(1)}, f32[48,2,36,256]{3,0,2,1:T(8,128)}, u32[]{:S(2)}) copy-start(f32[48,2,36,256]{3,0,2,1:T(8,128)} %copy-done.3) | copy-start | bytes 10616836
  112.1 10.7 %collective-permute-start.6 = (bf16[12,8,4,256]{3,0,2,1:T(8,128)(2,1)S(1)}, bf16[12,8,4,256]{3,0,2,1:T(8,128)(2,1)S(1)}, u32[]{:S(2)}, u32[]{:S(2)}) collective-permute-start(bf16[12,8,4,256]{3,0,2,1:T(8,128)(2,1)S(1)} %pad_maximum_fusion.19), channel_id=1, source_target_pairs={{0,30},{1,31},{2,28},{3,29},{4,26},{5,27},{6,24},{7,25},{8,22},{9,... | collective-permute-start | bytes 589832 | tf_op jit(solution)/shard_map/ppermute | solution.py:64
  114.6 8.3 %collective-permute-start.21 = (bf16[1,72,256]{2,1,0:T(8,128)(2,1)S(1)}, bf16[1,72,256]{2,1,0:T(8,128)(2,1)S(1)}, u32[]{:S(2)}, u32[]{:S(2)}) collective-permute-start(bf16[1,72,256]{2,1,0:T(8,128)(2,1)S(1)} %bitcast.240), channel_id=1, source_target_pairs={{0,24},{1,25},{2,26},{3,27},{4,28},{5,29},{6,30},{7,31},{8,16},{9,... | collective-permute-start | bytes 110600 | tf_op jit(solution)/shard_map/ppermute | solution.py:129
  118.0 11.3 %collective-permute-start.20 = (bf16[1,72,256]{2,1,0:T(8,128)(2,1)S(1)}, bf16[1,72,256]{2,1,0:T(8,128)(2,1)S(1)}, u32[]{:S(2)}, u32[]{:S(2)}) collective-permute-start(bf16[1,72,256]{2,1,0:T(8,128)(2,1)S(1)} %bitcast.241), channel_id=1, source_target_pairs={{0,16},{1,17},{2,18},{3,19},{4,20},{5,21},{6,22},{7,23},{8,24},{9,... | collective-permute-start | bytes 110600 | tf_op jit(solution)/shard_map/ppermute | solution.py:129
  118.0 11.3 %collective-permute-start.19 = (bf16[1,72,256]{2,1,0:T(8,128)(2,1)S(1)}, bf16[1,72,256]{2,1,0:T(8,128)(2,1)S(1)}, u32[]{:S(2)}, u32[]{:S(2)}) collective-permute-start(bf16[1,72,256]{2,1,0:T(8,128)(2,1)S(1)} %bitcast.242), channel_id=1, source_target_pairs={{0,8},{1,9},{2,10},{3,11},{4,12},{5,13},{6,14},{7,15},{8,0},{9,1},... | collective-permute-start | bytes 110600 | tf_op jit(solution)/shard_map/ppermute | solution.py:129
  133.9 19.7 %collective-permute-start.9 = (bf16[12,2,36,256]{3,1,2,0:T(2,128)(2,1)S(1)}, bf16[12,2,36,256]{3,1,2,0:T(2,128)(2,1)S(1)}, u32[]{:S(2)}, u32[]{:S(2)}) collective-permute-start(bf16[12,2,36,256]{3,1,2,0:T(2,128)(2,1)S(1)} %copy.100), channel_id=1, source_target_pairs={{2,0},{4,2},{6,4},{8,6},{10,8},{12,10},{14,12},{16,14},{18,16},{20... | collective-permute-start | bytes 1327112 | tf_op jit(solution)/shard_map/ppermute | solution.py:24
  134.5 19.2 %collective-permute-start.8 = (bf16[12,2,36,256]{3,1,2,0:T(2,128)(2,1)S(1)}, bf16[12,2,36,256]{3,1,2,0:T(2,128)(2,1)S(1)}, u32[]{:S(2)}, u32[]{:S(2)}) collective-permute-start(bf16[12,2,36,256]{3,1,2,0:T(2,128)(2,1)S(1)} %copy.99), channel_id=1, source_target_pairs={{0,2},{2,4},{4,6},{6,8},{8,10},{10,12},{12,14},{14,16},{16,18},{18... | collective-permute-start | bytes 1327112 | tf_op jit(solution)/shard_map/ppermute | solution.py:21
  134.5 19.0 %collective-permute-start.23 = (bf16[4,72,256]{2,1,0:T(8,128)(2,1)S(1)}, bf16[4,72,256]{2,1,0:T(8,128)(2,1)S(1)}, u32[]{:S(2)}, u32[]{:S(2)}) collective-permute-start(bf16[4,72,256]{2,1,0:T(8,128)(2,1)S(1)} %get-tuple-element.79), channel_id=1, source_target_pairs={{0,4},{1,5},{2,6},{3,7},{4,0},{5,1},{6,2},{7,3},{8,12},{9,13},{10,... | collective-permute-start | bytes 442376 | tf_op jit(solution)/shard_map/ppermute | solution.py:129
  136.8 16.7 %collective-permute-start.22 = (bf16[4,72,256]{2,1,0:T(8,128)(2,1)S(1)}, bf16[4,72,256]{2,1,0:T(8,128)(2,1)S(1)}, u32[]{:S(2)}, u32[]{:S(2)}) collective-permute-start(bf16[4,72,256]{2,1,0:T(8,128)(2,1)S(1)} %get-tuple-element.79), channel_id=1, source_target_pairs={{0,1},{1,0},{2,3},{3,2},{4,5},{5,4},{6,7},{7,6},{8,9},{9,8},{10,11... | collective-permute-start | bytes 442376 | tf_op jit(solution)/shard_map/ppermute | solution.py:129
  137.6 15.9 %collective-permute-start.24 = (bf16[4,72,256]{2,1,0:T(8,128)(2,1)S(1)}, bf16[4,72,256]{2,1,0:T(8,128)(2,1)S(1)}, u32[]{:S(2)}, u32[]{:S(2)}) collective-permute-start(bf16[4,72,256]{2,1,0:T(8,128)(2,1)S(1)} %get-tuple-element.79), channel_id=1, source_target_pairs={{0,5},{1,4},{2,7},{3,6},{4,1},{5,0},{6,3},{7,2},{8,13},{9,12},{10,... | collective-permute-start | bytes 442376 | tf_op jit(solution)/shard_map/ppermute | solution.py:129
  153.9 7.9 %collective-permute-start.10 = (bf16[12,12,2,256]{3,0,2,1:T(8,128)(2,1)S(1)}, bf16[12,12,2,256]{3,0,2,1:T(8,128)(2,1)S(1)}, u32[]{:S(2)}, u32[]{:S(2)}) collective-permute-start(bf16[12,12,2,256]{3,0,2,1:T(8,128)(2,1)S(1)} %get-tuple-element.26), channel_id=1, source_target_pairs={{0,1},{1,0},{2,3},{3,2},{4,5},{5,4},{6,7},{7,6},{8,9},{9,8},{10,11... | collective-permute-start | bytes 442376 | tf_op jit(solution)/shard_map/ppermute | solution.py:21
  155.4 8.8 %collective-permute-start.11 = (bf16[12,12,2,256]{3,0,2,1:T(8,128)(2,1)S(1)}, bf16[12,12,2,256]{3,0,2,1:T(8,128)(2,1)S(1)}, u32[]{:S(2)}, u32[]{:S(2)}) collective-permute-start(bf16[12,12,2,256]{3,0,2,1:T(8,128)(2,1)S(1)} %get-tuple-element.27), channel_id=1, source_target_pairs={{1,0},{0,1},{3,2},{2,3},{5,4},{4,5},{7,6},{6,7},{9,8},{8,9},{11,10... | collective-permute-start | bytes 442376 | tf_op jit(solution)/shard_map/ppermute | solution.py:24
  156.2 12.6 %collective-permute-start.25 = (bf16[16,72,256]{2,1,0:T(8,128)(2,1)S(1)}, bf16[16,72,256]{2,1,0:T(8,128)(2,1)S(1)}, u32[]{:S(2)}, u32[]{:S(2)}) collective-permute-start(bf16[16,72,256]{2,1,0:T(8,128)(2,1)S(1)} %get-tuple-element.65), channel_id=1, source_target_pairs={{0,2},{1,3},{2,0},{3,1},{4,6},{5,7},{6,4},{7,5},{8,10},{9,11},{10,... | collective-permute-start | bytes 1769480 | tf_op jit(solution)/shard_map/ppermute | solution.py:129
  (28 other events, 131.9 us)

commit v2 on v1

--- a/solution.py
+++ b/solution.py
@@ -1,8 +1,12 @@
+import functools
 import math
 
 import jax
 import jax.numpy as jnp
+import numpy as np
 from jax import lax
+from jax.experimental import pallas as pl
+from jax.experimental.pallas import tpu as pltpu
 from jax.sharding import PartitionSpec as P
 
 DILATION_STEP = 2
@@ -10,6 +14,273 @@
 
 half_root = 0.7071067811865476
 density_scale = 0.3989422804014327
+axes = ("frow", "fcol")
+vmem_bytes = 48 * 1024 * 1024
+
+
+def shifted_pairs(row_step, col_step):
+    rows, cols = lax.axis_size("frow"), lax.axis_size("fcol")
+    return [
+        (r * cols + c, (r + row_step) % rows * cols + (c + col_step) % cols)
+        for r in range(rows)
+        for c in range(cols)
+    ]
+
+
+def mirror_pairs(edge_rows, flip_rows, flip_cols):
+    rows, cols = lax.axis_size("frow"), lax.axis_size("fcol")
+    pairs = []
+    for r in range(rows):
+        for c in range(cols):
+            on_edge = r in (0, rows - 1) if edge_rows else c in (0, cols - 1)
+            if on_edge:
+                target_row = rows - 1 - r if flip_rows else r
+                target_col = cols - 1 - c if flip_cols else c
+                pairs.append((r * cols + c, target_row * cols + target_col))
+    return pairs
+
+
+def round_up(value, step):
+    return -(-value // step) * step
+
+
+def col_flips(tile_rows):
+    size = 2 * tile_rows
+    table = np.zeros((4, size, size), np.float32)
+    for kind in range(4):
+        for y in range(tile_rows):
+            for k in range(2):
+                source_y = tile_rows - 1 - y if kind >= 2 else y
+                source_k = 1 - k if kind % 2 else k
+                table[kind, 2 * y + k, 2 * source_y + source_k] = 1
+    return jnp.asarray(table, jnp.bfloat16)
+
+
+def row_flips(width):
+    size = 2 * width + 8
+    table = np.zeros((4, size, size), np.float32)
+    for kind in range(4):
+        for d in range(2):
+            source_d = 1 - d if kind % 2 else d
+            for p in range(width):
+                source_p = width - 1 - p if kind >= 2 else p
+                table[kind, d * width + p, source_d * width + source_p] = 1
+            for e in range(4):
+                source_e = 3 - e if kind >= 2 else e
+                table[kind, 2 * width + 4 * d + e, 2 * width + 4 * source_d + source_e] = 1
+    return jnp.asarray(table, jnp.bfloat16)
+
+
+def tail_picks(tile_rows):
+    table = np.zeros((2, 8, 4 * tile_rows), np.float32)
+    for place, first in enumerate((0, tile_rows - 2)):
+        for d in range(2):
+            for e in range(4):
+                source = 2 * tile_rows * (e // 2) + 2 * (first + d) + e % 2
+                table[place, 4 * d + e, source] = 1
+    return jnp.asarray(table, jnp.bfloat16)
+
+
+def stack_places(tile_rows, width):
+    strip = round_up(2 * width + 8, 16)
+    beside = tile_rows * width
+    above = beside + 4 * tile_rows
+    below = above + strip
+    return (beside, above, below, round_up(below + strip, 128))
+
+
+def stack_row(tile_rows, width, q, w):
+    beside, above, below, _ = stack_places(tile_rows, width)
+    side_cell = w if w < 2 else w - width
+    inner = 2 <= w < width + 2
+    if 2 <= q < tile_rows + 2:
+        y = q - 2
+        if inner:
+            return y * width + w - 2
+        return beside + 2 * tile_rows * (side_cell // 2) + 2 * y + side_cell % 2
+    base, d = (above, q) if q < 2 else (below, q - tile_rows - 2)
+    return base + (d * width + w - 2 if inner else 2 * width + 4 * d + side_cell)
+
+
+def pad_picks(tile_rows, width):
+    breadth = round_up(width + 4, 8)
+    size = stack_places(tile_rows, width)[3]
+    table = np.zeros(((tile_rows + 4) * breadth, size), np.float32)
+    for q in range(tile_rows + 4):
+        for w in range(width + 4):
+            table[q * breadth + w, stack_row(tile_rows, width, q, w)] = 1
+    return jnp.asarray(table, jnp.bfloat16)
+
+
+def pick(table, value):
+    return jnp.dot(table, value, preferred_element_type=jnp.float32).astype(jnp.bfloat16)
+
+
+def seam_of(adjacency, face, side):
+    base = (face * 4 + side) * 3
+    near = (adjacency[base + 1] == side).astype(jnp.int32)
+    return adjacency[base], 2 * adjacency[base + 2] + near
+
+
+def col_kernel(
+    adjacency, field, edges, beside, far_same, far_cross, flips, tails,
+    side_out, top_out, bottom_out, edge_out, seam,
+):
+    face_count, tile_rows, width, channels = field.shape
+    half = 2 * tile_rows
+    row_place, col_place = lax.axis_index("frow"), lax.axis_index("fcol")
+    at_top = row_place == 0
+    at_bottom = row_place == lax.axis_size("frow") - 1
+    at_left = col_place == 0
+    at_right = col_place == lax.axis_size("fcol") - 1
+
+    @pl.loop(0, face_count)
+    def _(face):
+        @pl.when(jnp.logical_or(at_left, at_right))
+        def _():
+            source, kind = seam_of(adjacency, face, jnp.where(at_left, 2, 3))
+
+            @pl.when(kind == 0)
+            def _():
+                both = beside[source]
+                seam[...] = jnp.where(at_left, both[half:], both[:half])
+
+            @pl.when(kind == 1)
+            def _():
+                both = edges[source]
+                seam[...] = pick(flips[1], jnp.where(at_left, both[:half], both[half:]))
+
+            @pl.when(kind == 2)
+            def _():
+                seam[...] = pick(flips[2], far_cross[source])
+
+            @pl.when(kind == 3)
+            def _():
+                seam[...] = pick(flips[3], far_same[source])
+
+        both = beside[face]
+        left = jnp.where(at_left, seam[...], both[half:])
+        right = jnp.where(at_right, seam[...], both[:half])
+        sides = jnp.concatenate([left, right], 0)
+        side_out[face] = sides
+        blank = jnp.zeros_like(left)
+        inner = jnp.concatenate(
+            [jnp.where(at_left, blank, left), jnp.where(at_right, blank, right)], 0
+        )
+        upper = pick(tails[0], jnp.where(at_top, inner, sides))
+        lower = pick(tails[1], jnp.where(at_bottom, inner, sides))
+        for d in range(2):
+            rows = pl.ds(d * width, width)
+            top_out[face, rows] = field[face, d]
+            bottom_out[face, rows] = field[face, tile_rows - 2 + d]
+            edge_out[face, rows] = jnp.where(
+                at_top, field[face, d], field[face, tile_rows - 2 + d]
+            )
+        rows = pl.ds(2 * width, 8)
+        top_out[face, rows] = upper
+        bottom_out[face, rows] = lower
+        edge_out[face, rows] = jnp.where(at_top, upper, lower)
+
+
+def load_stack(adjacency, face, field, sides, up, down, edge, far_same, far_cross, flips, stack):
+    tile_rows, width, channels = field.shape[1:]
+    strip = 2 * width + 8
+    beside, above, below, _ = stack_places(tile_rows, width)
+    row_place = lax.axis_index("frow")
+    stack[pl.ds(0, beside)] = field[face].reshape(beside, channels)
+    stack[pl.ds(beside, 4 * tile_rows)] = sides[face]
+    for side, place, near in ((0, above, up), (1, below, down)):
+        at_edge = row_place == side * (lax.axis_size("frow") - 1)
+        rows = pl.ds(place, strip)
+
+        @pl.when(jnp.logical_not(at_edge))
+        def _():
+            stack[rows] = near[face]
+
+        source, kind = seam_of(adjacency, face, side)
+        for choice, strips in enumerate((near, edge, far_cross, far_same)):
+
+            @pl.when(jnp.logical_and(at_edge, kind == choice))
+            def _():
+                stack[rows] = pick(flips[choice], strips[source])
+
+
+def pad_kernel(
+    adjacency, field, sides, up, down, edge, far_same, far_cross, flips, picks, padded, stack
+):
+    face_count, tile_rows, width, channels = field.shape
+    breadth = picks.shape[0] // (tile_rows + 4)
+    stack[...] = jnp.zeros_like(stack)
+
+    @pl.loop(0, face_count)
+    def _(face):
+        load_stack(
+            adjacency, face, field, sides, up, down, edge, far_same, far_cross, flips, stack
+        )
+        out = pick(picks[...], stack[...])
+        for q in range(tile_rows + 4):
+            padded[face, q] = out[q * breadth : q * breadth + width + 4]
+
+
+def whole(count):
+    return [pl.BlockSpec(memory_space=pltpu.SMEM)] + [
+        pl.BlockSpec(memory_space=pltpu.VMEM) for _ in range(count)
+    ]
+
+
+def gather_strips(field, adjacency):
+    face_count, tile_rows, width, channels = field.shape
+    cols = lax.axis_size("fcol")
+    left = field[:, :, :2].reshape(face_count, 2 * tile_rows, channels)
+    right = field[:, :, width - 2 :].reshape(face_count, 2 * tile_rows, channels)
+    edges = jnp.concatenate([left, right], 1)
+    if cols == 2:
+        beside = lax.ppermute(edges, axes, shifted_pairs(0, 1))
+    else:
+        beside = jnp.concatenate(
+            [
+                lax.ppermute(left, axes, shifted_pairs(0, -1)),
+                lax.ppermute(right, axes, shifted_pairs(0, 1)),
+            ],
+            1,
+        )
+    edge = jnp.where(lax.axis_index("fcol") == 0, left, right)
+    far_same = lax.ppermute(edge, axes, mirror_pairs(False, True, False))
+    far_cross = lax.ppermute(edge, axes, mirror_pairs(False, True, True))
+    strip = jax.ShapeDtypeStruct((face_count, 2 * width + 8, channels), field.dtype)
+    sides, top, bottom, edge_strip = pl.pallas_call(
+        col_kernel,
+        out_shape=(jax.ShapeDtypeStruct(edges.shape, field.dtype), strip, strip, strip),
+        in_specs=whole(7),
+        out_specs=[pl.BlockSpec(memory_space=pltpu.VMEM)] * 4,
+        scratch_shapes=[pltpu.VMEM((2 * tile_rows, channels), field.dtype)],
+        compiler_params=pltpu.CompilerParams(vmem_limit_bytes=vmem_bytes),
+        cost_estimate=pl.CostEstimate(flops=1000, bytes_accessed=3000000, transcendentals=0),
+    )(
+        adjacency, field, edges, beside, far_same, far_cross,
+        col_flips(tile_rows), tail_picks(tile_rows),
+    )
+    up = lax.ppermute(bottom, axes, shifted_pairs(1, 0))
+    down = lax.ppermute(top, axes, shifted_pairs(-1, 0))
+    row_same = lax.ppermute(edge_strip, axes, mirror_pairs(True, False, True))
+    row_cross = lax.ppermute(edge_strip, axes, mirror_pairs(True, True, True))
+    return (field, sides, up, down, edge_strip, row_same, row_cross)
+
+
+def pad_field(field, adjacency):
+    face_count, tile_rows, width, channels = field.shape
+    strips = gather_strips(field, adjacency)
+    padded = (face_count, tile_rows + 4, width + 4, channels)
+    size = stack_places(tile_rows, width)[3]
+    return pl.pallas_call(
+        pad_kernel,
+        out_shape=jax.ShapeDtypeStruct(padded, field.dtype),
+        in_specs=whole(9),
+        out_specs=pl.BlockSpec(memory_space=pltpu.VMEM),
+        scratch_shapes=[pltpu.VMEM((size, channels), field.dtype)],
+        compiler_params=pltpu.CompilerParams(vmem_limit_bytes=vmem_bytes),
+        cost_estimate=pl.CostEstimate(flops=1000, bytes_accessed=5000000, transcendentals=0),
+    )(adjacency, *strips, row_flips(width), pad_picks(tile_rows, width))
 
 
 def with_halo(block, sides, width):
@@ -45,23 +316,9 @@
     )
 
 
-def mirror_pairs(rows, cols, edge_rows, flip_rows, flip_cols):
-    pairs = []
-    for r in range(rows):
-        for c in range(cols):
-            on_edge = r in (0, rows - 1) if edge_rows else c in (0, cols - 1)
-            if on_edge:
-                target_row = rows - 1 - r if flip_rows else r
-                target_col = cols - 1 - c if flip_cols else c
-                pairs.append((r * cols + c, target_row * cols + target_col))
-    return pairs
-
-
 def reflect(row_band, col_band):
-    rows, cols = lax.axis_size("frow"), lax.axis_size("fcol")
-    axes = ("frow", "fcol")
-    row_band = lax.ppermute(row_band, axes, mirror_pairs(rows, cols, True, False, True))
-    col_band = lax.ppermute(col_band, axes, mirror_pairs(rows, cols, False, True, False))
+    row_band = lax.ppermute(row_band, axes, mirror_pairs(True, False, True))
+    col_band = lax.ppermute(col_band, axes, mirror_pairs(False, True, False))
     return (row_band, col_band)
 
 
@@ -94,7 +351,6 @@
 
 
 def reduce_everywhere(matrix, vector):
-    axes = ("frow", "fcol")
     count = lax.axis_size("frow") * lax.axis_size("fcol")
     index = lax.axis_index("frow") * lax.axis_size("fcol") + lax.axis_index("fcol")
     width = matrix.shape[-1]
@@ -173,63 +429,12 @@
     keep_rows = jnp.logical_not(
         at_top & (row_index < dilation_step) | at_bottom & (row_index >= tile_rows + dilation_step)
     )
-    padded_input = with_halo(face_input, (("frow", 1), ("fcol", 2)), dilation_step)
-    row_wrap = jnp.where(
-        at_top, padded_input[:, :dilation_step], padded_input[:, tile_rows + dilation_step :]
-    )
-    row_own = jnp.where(
-        at_top,
-        padded_input[:, dilation_step : 2 * dilation_step],
-        padded_input[:, tile_rows : tile_rows + dilation_step],
-    )
-    col_wrap = jnp.where(
-        at_left, padded_input[:, :, :dilation_step], padded_input[:, :, tile_cols + dilation_step :]
-    )
-    col_own = jnp.where(
-        at_left,
-        padded_input[:, :, dilation_step : 2 * dilation_step],
-        padded_input[:, :, tile_cols : tile_cols + dilation_step],
-    )
-    row_send = jnp.concatenate([row_wrap, row_own], 1)
-    col_send = jnp.concatenate([col_wrap, col_own], 2)
-    far_rows, far_cols = reflect(row_send, col_send)
+    padded_input = pad_field(face_input, adjacency.reshape(-1))
     row_pick = pick_table(
         jnp.where(at_top, adjacency[:, 0], adjacency[:, 1]), jnp.where(at_top, 0, 1), face_count
     )
     col_pick = pick_table(
         jnp.where(at_left, adjacency[:, 2], adjacency[:, 3]), jnp.where(at_left, 2, 3), face_count
-    )
-    row_cands = jnp.concatenate(
-        [
-            row_wrap,
-            jnp.flip(row_own, 1),
-            jnp.flip(far_rows[:, :dilation_step], 2),
-            jnp.flip(far_rows[:, dilation_step:], (1, 2)),
-        ],
-        0,
-    )
-    row_halo = jnp.einsum("fk,kdwc->fdwc", row_pick, row_cands, preferred_element_type=jnp.float32)
-    row_halo = jnp.where(keep_cols[None, None, :, None], row_halo, 0.0).astype(jnp.bfloat16)
-    top_rim = jnp.where(at_top, row_halo, padded_input[:, :dilation_step])
-    bottom_rim = jnp.where(at_bottom, row_halo, padded_input[:, tile_rows + dilation_step :])
-    padded_input = jnp.concatenate(
-        [top_rim, padded_input[:, dilation_step : tile_rows + dilation_step], bottom_rim], 1
-    )
-    col_cands = jnp.concatenate(
-        [
-            col_wrap,
-            jnp.flip(col_own, 2),
-            jnp.flip(far_cols[:, :, :dilation_step], 1),
-            jnp.flip(far_cols[:, :, dilation_step:], (1, 2)),
-        ],
-        0,
-    )
-    col_halo = jnp.einsum("fk,kadc->fadc", col_pick, col_cands, preferred_element_type=jnp.float32)
-    col_halo = jnp.where(keep_rows[None, :, None, None], col_halo, 0.0).astype(jnp.bfloat16)
-    left_rim = jnp.where(at_left, col_halo, padded_input[:, :, :dilation_step])
-    right_rim = jnp.where(at_right, col_halo, padded_input[:, :, tile_cols + dilation_step :])
-    padded_input = jnp.concatenate(
-        [left_rim, padded_input[:, :, dilation_step : tile_cols + dilation_step], right_rim], 2
     )
     random_values = ("NHWC", "HWIO", "NHWC")
     preactivation = (

time: 171 us -> 157 us (0.918)
  local copies, waits for them, and re-layouts: 30.3 us -> 15.4 us
  waiting for transfers between devices: 62.6 us -> 50.8 us
  starting transfers between devices: 35.1 us -> 44.3 us
  Pallas kernels: 0 us -> 9.06 us
  matrix products: 21.2 us -> 17.4 us
  other arithmetic: 19.9 us -> 17.6 us
    ppermute x4 -> x9, starting transfers between devices: 8.12 us -> 24.4 us  [the longest x1 6.44 us: gather_strips(): far_cross = lax.ppermute(edge, axes, mirror_pairs(False, True, True))]
    ppermute x4 -> x2, waiting for transfers between devices: 15.1 us -> 5.48 us  [with_halo(): lax.ppermute(lax.slice_in_dim(block, block.shape[dim] - width, None, axis...]
    pallas_call x0 -> x2, Pallas kernels: none -> 9.06 us  [the longest x1 5.74 us: pad_field(): pl.pallas_call(pad_kernel, out_shape=jax.ShapeDtypeStruct(padded, field.d...]
    ppermute x4 -> x2, starting transfers between devices: 8.29 us -> 2.56 us  [with_halo(): lax.ppermute(lax.slice_in_dim(block, 0, width, axis=dim), axis, backward)]
    rev x6 -> x0, local copies, waits for them, and re-layouts: 4.57 us -> none  [the longest x1 0.87 us: local(): jnp.flip(row_own, 1)]
    unnamed x71 -> x54, local copies, waits for them, and re-layouts: 9.34 us -> 4.84 us
    slice x4 -> x1, local copies, waits for them, and re-layouts: 5.55 us -> 1.26 us  [gather_strips(): right = field[:, :, width - 2:].reshape(face_count, 2 * tile_rows, channels)]
    dot_general x2 -> x0, matrix products: 2.75 us -> none  [the longest x1 2.5 us: local(): jnp.einsum('fk,kdwc->fdwc', row_pick, row_cands, preferred_element_type=j...]
  transfers between devices with their start and end apart: 26 -> 27, of which waited for: 11 -> 9; matrix products, arithmetic and copies ran while one was open for 16% -> 14% of each run, Pallas kernels for 0% -> 0%
where the time goes in v2:
time: 157 us; the launch traced here: 156 us
  waiting for transfers between devices  50.8 us (32%)
  starting transfers between devices  44.3 us (28%)
  other arithmetic  17.6 us (11%)
  matrix products  17.4 us (11%)
  local copies, waits for them, and re-layouts  15.4 us (10%)
  Pallas kernels  9.06 us (6%)
  between operations  1.63 us (1%)
    ppermute x7, waiting for transfers between devices, reduce_everywhere(): lax.ppermute(part, axes, [(i, i ^ offset) for i in range(count)])  20.7 us
    ppermute x7, waiting for transfers between devices, reduce_everywhere(): packed = lax.ppermute(packed, axes, [(i, i ^ offset) for i in range(count)])  9.5 us
    conv_general_dilated x1, matrix products, local(): lax.conv_general_dilated(preactivation_gradient, rotated_strip, (1, 1), (...  8.27 us
    ppermute x7, starting transfers between devices, reduce_everywhere(): lax.ppermute(part, axes, [(i, i ^ offset) for i in range(count)])  8.08 us
    ppermute x7, starting transfers between devices, reduce_everywhere(): packed = lax.ppermute(packed, axes, [(i, i ^ offset) for i in range(count)])  7.99 us
    ppermute x1, starting transfers between devices, gather_strips(): far_cross = lax.ppermute(edge, axes, mirror_pairs(False, True, True))  6.44 us
    ppermute x1, waiting for transfers between devices, gather_strips(): up = lax.ppermute(bottom, axes, shifted_pairs(1, 0))  6.37 us
    pallas_call x1, Pallas kernels, pad_field(): pl.pallas_call(pad_kernel, out_shape=jax.ShapeDtypeStruct(padded, field.d...  5.74 us
  transfers between devices with their start and end apart: 27, of which 9 were waited for; matrix products, arithmetic and copies ran while one was open for 14% of the time, Pallas kernels for 0%

profile of v2, /device:TPU:0, one launch (start us, length us, event | category | flops | bytes accessed | tf_op | source)
XLA Modules:
  0.0 156.1 jit_solution(8441160260626376552)
XLA Ops:
  2.1 6.4 %collective-permute-start.2 = (bf16[12,8,256]{2,1,0:T(8,128)(2,1)S(1)}, bf16[12,8,256]{2,1,0:T(8,128)(2,1)S(1)}, u32[]{:S(2)}, u32[]{:S(2)}) collective-permute-start(bf16[12,8,256]{2,1,0:T(8,128)(2,1)S(1)} %get-tuple-element.71), channel_id=1, source_target_pairs={{0,31},{1,30},{2,29},{3,28},{4,27},{5,26},{6,25},{7,24},{8,23},{9,... | collective-permute-start | bytes 147464 | tf_op jit(solution)/shard_map/ppermute | solution.py:249
  11.2 3.5 %collective-permute-done.1.far_same = bf16[12,8,256]{2,1,0:T(8,128)(2,1)S(1)} collective-permute-done((bf16[12,8,256]{2,1,0:T(8,128)(2,1)S(1)}, bf16[12,8,256]{2,1,0:T(8,128)(2,1)S(1)}, u32[]{:S(2)}, u32[]{:S(2)}) %collective-permute-start.1) | collective-permute-done | bytes 49184 | tf_op jit(solution)/shard_map/ppermute | solution.py:248
  16.1 3.3 %shard_map.120 = (bf16[12,16,256]{2,1,0:T(8,128)(2,1)S(1)}, bf16[12,72,256]{2,1,0:T(8,128)(2,1)S(1)}, bf16[12,72,256]{2,1,0:T(8,128)(2,1)S(1)}, bf16[12,72,256]{2,1,0:T(8,128)(2,1)S(1)}) custom-call(s32[144]{0:T(256)S(1)} %reshape.83.adjacency, bf16[12,4,32,256]{3,2,1,0:T(8,128)(2,1)S(1)} %copy-done.2, bf16[12,16,256]{2,1,0:T(8,128)(2,1)S(1)} %get-tuple-element.72.edges, ...), custom_call_target="tpu_custom_call" | custom-call | flops 1000 | bytes 3000000 | tf_op jit(solution)/shard_map/pallas_call | solution.py:251
  19.4 4.5 %collective-permute-start.6 = (bf16[12,72,256]{2,1,0:T(8,128)(2,1)S(1)}, bf16[12,72,256]{2,1,0:T(8,128)(2,1)S(1)}, u32[]{:S(2)}, u32[]{:S(2)}) collective-permute-start(bf16[12,72,256]{2,1,0:T(8,128)(2,1)S(1)} %get-tuple-element.11.edge), channel_id=1, source_target_pairs={{0,31},{1,30},{30,1},{31,0}} | collective-permute-start | bytes 1327112 | tf_op jit(solution)/shard_map/ppermute | solution.py:266
  23.9 2.7 %collective-permute-start.5 = (bf16[12,72,256]{2,1,0:T(8,128)(2,1)S(1)}, bf16[12,72,256]{2,1,0:T(8,128)(2,1)S(1)}, u32[]{:S(2)}, u32[]{:S(2)}) collective-permute-start(bf16[12,72,256]{2,1,0:T(8,128)(2,1)S(1)} %get-tuple-element.11.edge), channel_id=1, source_target_pairs={{0,1},{1,0},{30,31},{31,30}} | collective-permute-start | bytes 1327112 | tf_op jit(solution)/shard_map/ppermute | solution.py:265
  26.7 4.4 %collective-permute-start.4 = (bf16[12,72,256]{2,1,0:T(8,128)(2,1)S(1)}, bf16[12,72,256]{2,1,0:T(8,128)(2,1)S(1)}, u32[]{:S(2)}, u32[]{:S(2)}) collective-permute-start(bf16[12,72,256]{2,1,0:T(8,128)(2,1)S(1)} %get-tuple-element.10), channel_id=1, source_target_pairs={{0,30},{1,31},{2,0},{3,1},{4,2},{5,3},{6,4},{7,5},{8,6},{9,7},{10,... | collective-permute-start | bytes 1327112 | tf_op jit(solution)/shard_map/ppermute | solution.py:264
  31.1 6.4 %collective-permute-done.3.up = bf16[12,72,256]{2,1,0:T(8,128)(2,1)S(1)} collective-permute-done((bf16[12,72,256]{2,1,0:T(8,128)(2,1)S(1)}, bf16[12,72,256]{2,1,0:T(8,128)(2,1)S(1)}, u32[]{:S(2)}, u32[]{:S(2)}) %collective-permute-start.3) | collective-permute-done | bytes 442400 | tf_op jit(solution)/shard_map/ppermute | solution.py:263
  37.5 5.7 %shard_map.121 = bf16[12,8,36,256]{3,2,1,0:T(8,128)(2,1)S(1)} custom-call(s32[144]{0:T(256)S(1)} %reshape.83.adjacency, bf16[12,4,32,256]{3,2,1,0:T(8,128)(2,1)S(1)} %copy-done.2, bf16[12,16,256]{2,1,0:T(8,128)(2,1)S(1)} %get-tuple-element.8.sides, bf16[12,72,256]{2,1,0:T(8,128)(2,1)S(1)} %collective-permute-done.3.up, ...), custom_call_target="tpu_custom_call" | custom-call | flops 1000 | bytes 5000000 | tf_op jit(solution)/shard_map/pallas_call | solution.py:275
  43.3 3.0 %fusion.5 = f32[12,4,32,256]{3,0,2,1:T(8,128)S(1)} fusion(bf16[3,3,256,256]{3,2,1,0:T(8,128)(2,1)S(1)} %copy-done, bf16[12,8,36,256]{3,2,1,0:T(8,128)(2,1)S(1)} %shard_map.121), kind=kOutput, calls=%fused_computation.11 | convolution fusion | flops 1811939328 | bytes 4521984 | tf_op jit(solution)/shard_map/conv_general_dilated | solution.py:441
  46.4 1.4 fusion.104
  48.2 8.3 %fusion.110 = (f32[12,8,36,256]{3,0,2,1:T(8,128)}, bf16[12,8,36,256]{3,0,2,1:T(8,128)(2,1)S(1)}) fusion(bf16[3,3,256,256]{3,2,1,0:T(8,128)(2,1)S(1)} %copy-done, bf16[12,4,32,256]{3,2,1,0:T(8,128)(2,1)S(1)} %get-tuple-element.29), kind=kOutput, calls=%fused_computation.202 | convolution fusion | flops 1813708800 | bytes 7274496 | tf_op jit(solution)/shard_map/conv_general_dilated | solution.py:483
  63.5 2.0 %fusion.61 = f32[48,2,36,256]{3,0,2,1:T(8,128)S(1)} fusion(bf16[12,8,36,256]{3,0,2,1:T(8,128)(2,1)} %copy-done.9, pred[36]{0:T(512)(128)(4,1)S(1)} %or_not_fusion, pred[]{:T(512)S(6)} %eq.75, s32[12]{0:T(128)S(1)} %fusion.98), kind=kOutput, calls=%fused_computation.99 | convolution fusion | flops 21676608 | bytes 4718677 | tf_op jit(solution)/shard_map/fk,fdwc->kdwc/dot_general | solution.py:496
  66.6 1.9 %rev.47 = bf16[12,2,36,256]{3,0,2,1:T(8,128)(2,1)} reverse(bf16[12,2,36,256]{3,0,2,1:T(8,128)(2,1)} %get-tuple-element.37), dimensions={2} | reverse | bytes 884736 | tf_op jit(solution)/shard_map/jit(_flip)/rev | solution.py:507
  68.6 1.9 %rev.46 = bf16[12,2,36,256]{3,0,2,1:T(8,128)(2,1)} reverse(bf16[12,2,36,256]{3,0,2,1:T(8,128)(2,1)} %get-tuple-element.38), dimensions={1,2} | reverse | bytes 884736 | tf_op jit(solution)/shard_map/jit(_flip)/rev | solution.py:507
  70.5 1.4 pad_maximum_fusion.1
  72.6 2.8 %collective-permute-start.8 = (bf16[12,4,36,256]{3,1,2,0:T(4,128)(2,1)S(1)}, bf16[12,4,36,256]{3,1,2,0:T(4,128)(2,1)S(1)}, u32[]{:S(2)}, u32[]{:S(2)}) collective-permute-start(bf16[12,4,36,256]{3,1,2,0:T(4,128)(2,1)S(1)} %copy.65), channel_id=1, source_target_pairs={{0,1},{1,0},{30,31},{31,30}} | collective-permute-start | bytes 2654216 | tf_op jit(solution)/shard_map/ppermute | solution.py:320
  76.3 1.4 fusion.16
  78.9 2.4 %collective-permute-start.16 = (bf16[296,256]{1,0:T(8,128)(2,1)S(1)}, bf16[296,256]{1,0:T(8,128)(2,1)S(1)}, u32[]{:S(2)}, u32[]{:S(2)}) collective-permute-start(bf16[296,256]{1,0:T(8,128)(2,1)S(1)} %get-tuple-element.80), channel_id=1, source_target_pairs={{0,5},{1,4},{2,7},{3,6},{4,1},{5,0},{6,3},{7,2},{8,13},{9,12},{10,... | collective-permute-start | bytes 454664 | tf_op jit(solution)/shard_map/ppermute | solution.py:372
  81.3 2.0 %multiply_convert_fusion = bf16[12,4,32,256]{3,2,1,0:T(8,128)(2,1)} fusion(f32[256]{0:T(256)S(1)} %copy-done.20, f32[12,4,32,256]{3,0,2,1:T(8,128)S(1)} %copy-done.8), kind=kLoop, calls=%fused_computation.26 | loop fusion | flops 2359296 | bytes 2360320 | tf_op jit(solution)/shard_map/convert_element_type | solution.py:452
  83.3 9.1 %collective-permute-done.14 = bf16[296,256]{1,0:T(8,128)(2,1)S(1)} collective-permute-done((bf16[296,256]{1,0:T(8,128)(2,1)S(1)}, bf16[296,256]{1,0:T(8,128)(2,1)S(1)}, u32[]{:S(2)}, u32[]{:S(2)}) %collective-permute-start.14) | collective-permute-done | bytes 151584 | tf_op jit(solution)/shard_map/ppermute | solution.py:372
  92.7 4.3 %collective-permute-start.19 = (bf16[80,256]{1,0:T(8,128)(2,1)S(1)}, bf16[80,256]{1,0:T(8,128)(2,1)S(1)}, u32[]{:S(2)}, u32[]{:S(2)}) collective-permute-start(bf16[80,256]{1,0:T(8,128)(2,1)S(1)} %get-tuple-element.77), channel_id=1, source_target_pairs={{0,24},{1,25},{2,26},{3,27},{4,28},{5,29},{6,30},{7,31},{8,16},{9,... | collective-permute-start | bytes 122888 | tf_op jit(solution)/shard_map/ppermute | solution.py:372
  97.1 2.8 %collective-permute-start.7 = (bf16[12,8,4,256]{3,0,2,1:T(8,128)(2,1)S(1)}, bf16[12,8,4,256]{3,0,2,1:T(8,128)(2,1)S(1)}, u32[]{:S(2)}, u32[]{:S(2)}) collective-permute-start(bf16[12,8,4,256]{3,0,2,1:T(8,128)(2,1)S(1)} %pad_maximum_fusion.11), channel_id=1, source_target_pairs={{0,30},{1,31},{2,28},{3,29},{4,26},{5,27},{6,24},{7,25},{8,22},{9,... | collective-permute-start | bytes 589832 | tf_op jit(solution)/shard_map/ppermute | solution.py:321
  100.3 3.1 %collective-permute-start.22 = (bf16[1,72,256]{2,1,0:T(8,128)(2,1)S(1)}, bf16[1,72,256]{2,1,0:T(8,128)(2,1)S(1)}, u32[]{:S(2)}, u32[]{:S(2)}) collective-permute-start(bf16[1,72,256]{2,1,0:T(8,128)(2,1)S(1)} %bitcast.229), channel_id=1, source_target_pairs={{0,24},{1,25},{2,26},{3,27},{4,28},{5,29},{6,30},{7,31},{8,16},{9,... | collective-permute-start | bytes 110600 | tf_op jit(solution)/shard_map/ppermute | solution.py:385
  104.8 3.1 %collective-permute-done.7 = bf16[12,8,4,256]{3,0,2,1:T(8,128)(2,1)S(1)} collective-permute-done((bf16[12,8,4,256]{3,0,2,1:T(8,128)(2,1)S(1)}, bf16[12,8,4,256]{3,0,2,1:T(8,128)(2,1)S(1)}, u32[]{:S(2)}, u32[]{:S(2)}) %collective-permute-start.7) | collective-permute-done | bytes 196640 | tf_op jit(solution)/shard_map/ppermute | solution.py:321
  107.9 7.2 %collective-permute-done.21 = bf16[1,72,256]{2,1,0:T(8,128)(2,1)S(1)} collective-permute-done((bf16[1,72,256]{2,1,0:T(8,128)(2,1)S(1)}, bf16[1,72,256]{2,1,0:T(8,128)(2,1)S(1)}, u32[]{:S(2)}, u32[]{:S(2)}) %collective-permute-start.21) | collective-permute-done | bytes 36896 | tf_op jit(solution)/shard_map/ppermute | solution.py:385
  119.7 1.7 %collective-permute-start.10 = (bf16[12,2,36,256]{3,1,2,0:T(2,128)(2,1)S(1)}, bf16[12,2,36,256]{3,1,2,0:T(2,128)(2,1)S(1)}, u32[]{:S(2)}, u32[]{:S(2)}) collective-permute-start(bf16[12,2,36,256]{3,1,2,0:T(2,128)(2,1)S(1)} %copy.69), channel_id=1, source_target_pairs={{2,0},{4,2},{6,4},{8,6},{10,8},{12,10},{14,12},{16,14},{18,16},{20... | collective-permute-start | bytes 1327112 | tf_op jit(solution)/shard_map/ppermute | solution.py:295
  123.1 2.0 %collective-permute-start.25 = (bf16[4,72,256]{2,1,0:T(8,128)(2,1)S(1)}, bf16[4,72,256]{2,1,0:T(8,128)(2,1)S(1)}, u32[]{:S(2)}, u32[]{:S(2)}) collective-permute-start(bf16[4,72,256]{2,1,0:T(8,128)(2,1)S(1)} %get-tuple-element.63), channel_id=1, source_target_pairs={{0,5},{1,4},{2,7},{3,6},{4,1},{5,0},{6,3},{7,2},{8,13},{9,12},{10,... | collective-permute-start | bytes 442376 | tf_op jit(solution)/shard_map/ppermute | solution.py:385
  125.6 13.5 %collective-permute-done.24 = bf16[4,72,256]{2,1,0:T(8,128)(2,1)S(1)} collective-permute-done((bf16[4,72,256]{2,1,0:T(8,128)(2,1)S(1)}, bf16[4,72,256]{2,1,0:T(8,128)(2,1)S(1)}, u32[]{:S(2)}, u32[]{:S(2)}) %collective-permute-start.24) | collective-permute-done | bytes 147488 | tf_op jit(solution)/shard_map/ppermute | solution.py:385
  141.9 5.5 %collective-permute-done.11 = bf16[12,12,2,256]{3,0,2,1:T(8,128)(2,1)S(1)} collective-permute-done((bf16[12,12,2,256]{3,0,2,1:T(8,128)(2,1)S(1)}, bf16[12,12,2,256]{3,0,2,1:T(8,128)(2,1)S(1)}, u32[]{:S(2)}, u32[]{:S(2)}) %collective-permute-start.11) | collective-permute-done | bytes 147488 | tf_op jit(solution)/shard_map/ppermute | solution.py:292
  147.3 2.1 %collective-permute-done.12 = bf16[12,12,2,256]{3,0,2,1:T(8,128)(2,1)S(1)} collective-permute-done((bf16[12,12,2,256]{3,0,2,1:T(8,128)(2,1)S(1)}, bf16[12,12,2,256]{3,0,2,1:T(8,128)(2,1)S(1)}, u32[]{:S(2)}, u32[]{:S(2)}) %collective-permute-start.12) | collective-permute-done | bytes 147488 | tf_op jit(solution)/shard_map/ppermute | solution.py:295
  149.4 1.6 %maximum_convert_fusion = f32[12,12,40,256]{3,0,2,1:T(8,128)S(1)} fusion(bf16[12,12,2,256]{3,0,2,1:T(8,128)(2,1)S(1)} %collective-permute-done.12, bf16[12,2,36,256]{3,0,2,1:T(8,128)(2,1)S(1)} %copy.71, bf16[12,8,2,256]{3,0,2,1:T(8,128)(2,1)S(1)} %get-tuple-element.33, bf16[12,8,32,256]{3,0,2,1:T(8,128)(2,1)S(1)} %fusion.1, ...), kind=kLoop, calls=%fused_computation.4 | loop fusion | flops 10321920 | bytes 8847360 | tf_op jit(solution)/shard_map/convert_element_type | solution.py:541
  154.5 1.6 %convert_multiply_fusion = f32[32,72,256]{2,1,0:T(8,128)} fusion(bf16[16,72,256]{2,1,0:T(8,128)(2,1)S(1)} %get-tuple-element.44, bf16[16,72,256]{2,1,0:T(8,128)(2,1)S(1)} %get-tuple-element.43), kind=kLoop, calls=%fused_computation.13 | loop fusion | flops 1769472 | bytes 3538944 | tf_op jit(solution)/shard_map/mul | solution.py:479
  (161 shorter events, 31.4 us)
Async XLA Ops:
  0.6 42.6 %copy-start = (bf16[3,3,256,256]{3,2,1,0:T(8,128)(2,1)S(1)}, bf16[3,3,256,256]{3,2,1,0:T(8,128)(2,1)}, u32[]{:S(2)}) copy-start(bf16[3,3,256,256]{3,2,1,0:T(8,128)(2,1)} %param.10) | copy-start | bytes 3538948
  0.6 36.8 %copy-start.3 = (bf16[320,384]{1,0:T(8,128)(2,1)S(1)}, bf16[320,384]{1,0:T(8,128)(2,1)}, u32[]{:S(2)}) copy-start(bf16[320,384]{1,0:T(8,128)(2,1)} %constant.208.clone.picks) | copy-start | bytes 737284
  0.7 36.8 %copy-start.4 = (bf16[4,72,72]{2,1,0:T(8,128)(2,1)S(1)}, bf16[4,72,72]{2,1,0:T(8,128)(2,1)}, u32[]{:S(2)}) copy-start(bf16[4,72,72]{2,1,0:T(8,128)(2,1)} %constant.207.clone.flips) | copy-start | bytes 124420
  2.1 9.1 %collective-permute-start.2 = (bf16[12,8,256]{2,1,0:T(8,128)(2,1)S(1)}, bf16[12,8,256]{2,1,0:T(8,128)(2,1)S(1)}, u32[]{:S(2)}, u32[]{:S(2)}) collective-permute-start(bf16[12,8,256]{2,1,0:T(8,128)(2,1)S(1)} %get-tuple-element.71), channel_id=1, source_target_pairs={{0,31},{1,30},{2,29},{3,28},{4,27},{5,26},{6,25},{7,24},{8,23},{9,... | collective-permute-start | bytes 147464 | tf_op jit(solution)/shard_map/ppermute | solution.py:249
  8.5 6.2 %collective-permute-start.1 = (bf16[12,8,256]{2,1,0:T(8,128)(2,1)S(1)}, bf16[12,8,256]{2,1,0:T(8,128)(2,1)S(1)}, u32[]{:S(2)}, u32[]{:S(2)}) collective-permute-start(bf16[12,8,256]{2,1,0:T(8,128)(2,1)S(1)} %get-tuple-element.71), channel_id=1, source_target_pairs={{0,30},{1,31},{2,28},{3,29},{4,26},{5,27},{6,24},{7,25},{8,22},{9,... | collective-permute-start | bytes 147464 | tf_op jit(solution)/shard_map/ppermute | solution.py:248
  8.9 5.8 %collective-permute-start = (bf16[12,16,256]{2,1,0:T(8,128)(2,1)S(1)}, bf16[12,16,256]{2,1,0:T(8,128)(2,1)S(1)}, u32[]{:S(2)}, u32[]{:S(2)}) collective-permute-start(bf16[12,16,256]{2,1,0:T(8,128)(2,1)S(1)} %get-tuple-element.72.edges), channel_id=1, source_target_pairs={{0,1},{1,0},{2,3},{3,2},{4,5},{5,4},{6,7},{7,6},{8,9},{9,8},{10,11... | collective-permute-start | bytes 294920 | tf_op jit(solution)/shard_map/ppermute | solution.py:238
  19.4 18.1 %collective-permute-start.6 = (bf16[12,72,256]{2,1,0:T(8,128)(2,1)S(1)}, bf16[12,72,256]{2,1,0:T(8,128)(2,1)S(1)}, u32[]{:S(2)}, u32[]{:S(2)}) collective-permute-start(bf16[12,72,256]{2,1,0:T(8,128)(2,1)S(1)} %get-tuple-element.11.edge), channel_id=1, source_target_pairs={{0,31},{1,30},{30,1},{31,0}} | collective-permute-start | bytes 1327112 | tf_op jit(solution)/shard_map/ppermute | solution.py:266
  23.9 13.6 %collective-permute-start.5 = (bf16[12,72,256]{2,1,0:T(8,128)(2,1)S(1)}, bf16[12,72,256]{2,1,0:T(8,128)(2,1)S(1)}, u32[]{:S(2)}, u32[]{:S(2)}) collective-permute-start(bf16[12,72,256]{2,1,0:T(8,128)(2,1)S(1)} %get-tuple-element.11.edge), channel_id=1, source_target_pairs={{0,1},{1,0},{30,31},{31,30}} | collective-permute-start | bytes 1327112 | tf_op jit(solution)/shard_map/ppermute | solution.py:265
  26.6 10.9 %collective-permute-start.3 = (bf16[12,72,256]{2,1,0:T(8,128)(2,1)S(1)}, bf16[12,72,256]{2,1,0:T(8,128)(2,1)S(1)}, u32[]{:S(2)}, u32[]{:S(2)}) collective-permute-start(bf16[12,72,256]{2,1,0:T(8,128)(2,1)S(1)} %get-tuple-element.9), channel_id=1, source_target_pairs={{0,2},{1,3},{2,4},{3,5},{4,6},{5,7},{6,8},{7,9},{8,10},{9,11},{10,... | collective-permute-start | bytes 1327112 | tf_op jit(solution)/shard_map/ppermute | solution.py:263
  26.7 10.8 %collective-permute-start.4 = (bf16[12,72,256]{2,1,0:T(8,128)(2,1)S(1)}, bf16[12,72,256]{2,1,0:T(8,128)(2,1)S(1)}, u32[]{:S(2)}, u32[]{:S(2)}) collective-permute-start(bf16[12,72,256]{2,1,0:T(8,128)(2,1)S(1)} %get-tuple-element.10), channel_id=1, source_target_pairs={{0,30},{1,31},{2,0},{3,1},{4,2},{5,3},{6,4},{7,5},{8,6},{9,7},{10,... | collective-permute-start | bytes 1327112 | tf_op jit(solution)/shard_map/ppermute | solution.py:264
  60.8 14.6 %collective-permute-start.13 = (bf16[1160,256]{1,0:T(8,128)(2,1)}, bf16[1160,256]{1,0:T(8,128)(2,1)}, u32[]{:S(2)}, u32[]{:S(2)}) collective-permute-start(bf16[1160,256]{1,0:T(8,128)(2,1)} %pad_maximum_fusion.2), channel_id=1, source_target_pairs={{0,2},{1,3},{2,0},{3,1},{4,6},{5,7},{6,4},{7,5},{8,10},{9,11},{10,... | collective-permute-start | bytes 1781768 | tf_op jit(solution)/shard_map/ppermute | solution.py:372
  72.6 42.6 %collective-permute-start.8 = (bf16[12,4,36,256]{3,1,2,0:T(4,128)(2,1)S(1)}, bf16[12,4,36,256]{3,1,2,0:T(4,128)(2,1)S(1)}, u32[]{:S(2)}, u32[]{:S(2)}) collective-permute-start(bf16[12,4,36,256]{3,1,2,0:T(4,128)(2,1)S(1)} %copy.65), channel_id=1, source_target_pairs={{0,1},{1,0},{30,31},{31,30}} | collective-permute-start | bytes 2654216 | tf_op jit(solution)/shard_map/ppermute | solution.py:320
  76.3 39.6 %slice-start = ((s8[4718592]{0:T(1024)(128)(4,1)}), s8[4194304]{0:T(1024)(128)(4,1)S(1)}, s32[]{:S(2)}) async-start(s8[4718592]{0:T(1024)(128)(4,1)} %bitcast.216), calls=%async_computation | async-start | bytes 8388608
  77.7 14.7 %collective-permute-start.14 = (bf16[296,256]{1,0:T(8,128)(2,1)S(1)}, bf16[296,256]{1,0:T(8,128)(2,1)S(1)}, u32[]{:S(2)}, u32[]{:S(2)}) collective-permute-start(bf16[296,256]{1,0:T(8,128)(2,1)S(1)} %get-tuple-element.78), channel_id=1, source_target_pairs={{0,1},{1,0},{2,3},{3,2},{4,5},{5,4},{6,7},{7,6},{8,9},{9,8},{10,11... | collective-permute-start | bytes 454664 | tf_op jit(solution)/shard_map/ppermute | solution.py:372
  78.9 13.5 %collective-permute-start.15 = (bf16[296,256]{1,0:T(8,128)(2,1)S(1)}, bf16[296,256]{1,0:T(8,128)(2,1)S(1)}, u32[]{:S(2)}, u32[]{:S(2)}) collective-permute-start(bf16[296,256]{1,0:T(8,128)(2,1)S(1)} %get-tuple-element.79), channel_id=1, source_target_pairs={{0,4},{1,5},{2,6},{3,7},{4,0},{5,1},{6,2},{7,3},{8,12},{9,13},{10,... | collective-permute-start | bytes 454664 | tf_op jit(solution)/shard_map/ppermute | solution.py:372
  78.9 37.0 %slice-start.1 = ((s8[4718592]{0:T(1024)(128)(4,1)}), s8[524288]{0:T(1024)(128)(4,1)S(1)}, s32[]{:S(2)}) async-start(s8[4718592]{0:T(1024)(128)(4,1)} %bitcast.216), calls=%async_computation.1 | async-start | bytes 1048576
  78.9 13.5 %collective-permute-start.16 = (bf16[296,256]{1,0:T(8,128)(2,1)S(1)}, bf16[296,256]{1,0:T(8,128)(2,1)S(1)}, u32[]{:S(2)}, u32[]{:S(2)}) collective-permute-start(bf16[296,256]{1,0:T(8,128)(2,1)S(1)} %get-tuple-element.80), channel_id=1, source_target_pairs={{0,5},{1,4},{2,7},{3,6},{4,1},{5,0},{6,3},{7,2},{8,13},{9,12},{10,... | collective-permute-start | bytes 454664 | tf_op jit(solution)/shard_map/ppermute | solution.py:372
  92.6 7.4 %collective-permute-start.17 = (bf16[80,256]{1,0:T(8,128)(2,1)S(1)}, bf16[80,256]{1,0:T(8,128)(2,1)S(1)}, u32[]{:S(2)}, u32[]{:S(2)}) collective-permute-start(bf16[80,256]{1,0:T(8,128)(2,1)S(1)} %get-tuple-element.75), channel_id=1, source_target_pairs={{0,8},{1,9},{2,10},{3,11},{4,12},{5,13},{6,14},{7,15},{8,0},{9,1},... | collective-permute-start | bytes 122888 | tf_op jit(solution)/shard_map/ppermute | solution.py:372
  92.6 7.3 %collective-permute-start.18 = (bf16[80,256]{1,0:T(8,128)(2,1)S(1)}, bf16[80,256]{1,0:T(8,128)(2,1)S(1)}, u32[]{:S(2)}, u32[]{:S(2)}) collective-permute-start(bf16[80,256]{1,0:T(8,128)(2,1)S(1)} %get-tuple-element.76), channel_id=1, source_target_pairs={{0,16},{1,17},{2,18},{3,19},{4,20},{5,21},{6,22},{7,23},{8,24},{9,... | collective-permute-start | bytes 122888 | tf_op jit(solution)/shard_map/ppermute | solution.py:372
  92.7 7.6 %collective-permute-start.19 = (bf16[80,256]{1,0:T(8,128)(2,1)S(1)}, bf16[80,256]{1,0:T(8,128)(2,1)S(1)}, u32[]{:S(2)}, u32[]{:S(2)}) collective-permute-start(bf16[80,256]{1,0:T(8,128)(2,1)S(1)} %get-tuple-element.77), channel_id=1, source_target_pairs={{0,24},{1,25},{2,26},{3,27},{4,28},{5,29},{6,30},{7,31},{8,16},{9,... | collective-permute-start | bytes 122888 | tf_op jit(solution)/shard_map/ppermute | solution.py:372
  97.1 10.7 %collective-permute-start.7 = (bf16[12,8,4,256]{3,0,2,1:T(8,128)(2,1)S(1)}, bf16[12,8,4,256]{3,0,2,1:T(8,128)(2,1)S(1)}, u32[]{:S(2)}, u32[]{:S(2)}) collective-permute-start(bf16[12,8,4,256]{3,0,2,1:T(8,128)(2,1)S(1)} %pad_maximum_fusion.11), channel_id=1, source_target_pairs={{0,30},{1,31},{2,28},{3,29},{4,26},{5,27},{6,24},{7,25},{8,22},{9,... | collective-permute-start | bytes 589832 | tf_op jit(solution)/shard_map/ppermute | solution.py:321
  100.3 7.6 %collective-permute-start.22 = (bf16[1,72,256]{2,1,0:T(8,128)(2,1)S(1)}, bf16[1,72,256]{2,1,0:T(8,128)(2,1)S(1)}, u32[]{:S(2)}, u32[]{:S(2)}) collective-permute-start(bf16[1,72,256]{2,1,0:T(8,128)(2,1)S(1)} %bitcast.229), channel_id=1, source_target_pairs={{0,24},{1,25},{2,26},{3,27},{4,28},{5,29},{6,30},{7,31},{8,16},{9,... | collective-permute-start | bytes 110600 | tf_op jit(solution)/shard_map/ppermute | solution.py:385
  103.5 11.7 %collective-permute-start.21 = (bf16[1,72,256]{2,1,0:T(8,128)(2,1)S(1)}, bf16[1,72,256]{2,1,0:T(8,128)(2,1)S(1)}, u32[]{:S(2)}, u32[]{:S(2)}) collective-permute-start(bf16[1,72,256]{2,1,0:T(8,128)(2,1)S(1)} %bitcast.230), channel_id=1, source_target_pairs={{0,16},{1,17},{2,18},{3,19},{4,20},{5,21},{6,22},{7,23},{8,24},{9,... | collective-permute-start | bytes 110600 | tf_op jit(solution)/shard_map/ppermute | solution.py:385
  103.5 11.7 %collective-permute-start.20 = (bf16[1,72,256]{2,1,0:T(8,128)(2,1)S(1)}, bf16[1,72,256]{2,1,0:T(8,128)(2,1)S(1)}, u32[]{:S(2)}, u32[]{:S(2)}) collective-permute-start(bf16[1,72,256]{2,1,0:T(8,128)(2,1)S(1)} %bitcast.231), channel_id=1, source_target_pairs={{0,8},{1,9},{2,10},{3,11},{4,12},{5,13},{6,14},{7,15},{8,0},{9,1},... | collective-permute-start | bytes 110600 | tf_op jit(solution)/shard_map/ppermute | solution.py:385
  119.7 19.5 %collective-permute-start.10 = (bf16[12,2,36,256]{3,1,2,0:T(2,128)(2,1)S(1)}, bf16[12,2,36,256]{3,1,2,0:T(2,128)(2,1)S(1)}, u32[]{:S(2)}, u32[]{:S(2)}) collective-permute-start(bf16[12,2,36,256]{3,1,2,0:T(2,128)(2,1)S(1)} %copy.69), channel_id=1, source_target_pairs={{2,0},{4,2},{6,4},{8,6},{10,8},{12,10},{14,12},{16,14},{18,16},{20... | collective-permute-start | bytes 1327112 | tf_op jit(solution)/shard_map/ppermute | solution.py:295
  121.5 17.9 %collective-permute-start.9 = (bf16[12,2,36,256]{3,1,2,0:T(2,128)(2,1)S(1)}, bf16[12,2,36,256]{3,1,2,0:T(2,128)(2,1)S(1)}, u32[]{:S(2)}, u32[]{:S(2)}) collective-permute-start(bf16[12,2,36,256]{3,1,2,0:T(2,128)(2,1)S(1)} %copy.68), channel_id=1, source_target_pairs={{0,2},{2,4},{4,6},{6,8},{8,10},{10,12},{12,14},{14,16},{16,18},{18... | collective-permute-start | bytes 1327112 | tf_op jit(solution)/shard_map/ppermute | solution.py:292
  121.5 17.6 %collective-permute-start.24 = (bf16[4,72,256]{2,1,0:T(8,128)(2,1)S(1)}, bf16[4,72,256]{2,1,0:T(8,128)(2,1)S(1)}, u32[]{:S(2)}, u32[]{:S(2)}) collective-permute-start(bf16[4,72,256]{2,1,0:T(8,128)(2,1)S(1)} %get-tuple-element.63), channel_id=1, source_target_pairs={{0,4},{1,5},{2,6},{3,7},{4,0},{5,1},{6,2},{7,3},{8,12},{9,13},{10,... | collective-permute-start | bytes 442376 | tf_op jit(solution)/shard_map/ppermute | solution.py:385
  122.1 17.1 %collective-permute-start.23 = (bf16[4,72,256]{2,1,0:T(8,128)(2,1)S(1)}, bf16[4,72,256]{2,1,0:T(8,128)(2,1)S(1)}, u32[]{:S(2)}, u32[]{:S(2)}) collective-permute-start(bf16[4,72,256]{2,1,0:T(8,128)(2,1)S(1)} %get-tuple-element.63), channel_id=1, source_target_pairs={{0,1},{1,0},{2,3},{3,2},{4,5},{5,4},{6,7},{7,6},{8,9},{9,8},{10,11... | collective-permute-start | bytes 442376 | tf_op jit(solution)/shard_map/ppermute | solution.py:385
  123.1 16.1 %collective-permute-start.25 = (bf16[4,72,256]{2,1,0:T(8,128)(2,1)S(1)}, bf16[4,72,256]{2,1,0:T(8,128)(2,1)S(1)}, u32[]{:S(2)}, u32[]{:S(2)}) collective-permute-start(bf16[4,72,256]{2,1,0:T(8,128)(2,1)S(1)} %get-tuple-element.63), channel_id=1, source_target_pairs={{0,5},{1,4},{2,7},{3,6},{4,1},{5,0},{6,3},{7,2},{8,13},{9,12},{10,... | collective-permute-start | bytes 442376 | tf_op jit(solution)/shard_map/ppermute | solution.py:385
  139.5 7.8 %collective-permute-start.11 = (bf16[12,12,2,256]{3,0,2,1:T(8,128)(2,1)S(1)}, bf16[12,12,2,256]{3,0,2,1:T(8,128)(2,1)S(1)}, u32[]{:S(2)}, u32[]{:S(2)}) collective-permute-start(bf16[12,12,2,256]{3,0,2,1:T(8,128)(2,1)S(1)} %get-tuple-element.34), channel_id=1, source_target_pairs={{0,1},{1,0},{2,3},{3,2},{4,5},{5,4},{6,7},{7,6},{8,9},{9,8},{10,11... | collective-permute-start | bytes 442376 | tf_op jit(solution)/shard_map/ppermute | solution.py:292
  140.8 8.7 %collective-permute-start.12 = (bf16[12,12,2,256]{3,0,2,1:T(8,128)(2,1)S(1)}, bf16[12,12,2,256]{3,0,2,1:T(8,128)(2,1)S(1)}, u32[]{:S(2)}, u32[]{:S(2)}) collective-permute-start(bf16[12,12,2,256]{3,0,2,1:T(8,128)(2,1)S(1)} %get-tuple-element.35), channel_id=1, source_target_pairs={{1,0},{0,1},{3,2},{2,3},{5,4},{4,5},{7,6},{6,7},{9,8},{8,9},{11,10... | collective-permute-start | bytes 442376 | tf_op jit(solution)/shard_map/ppermute | solution.py:295
  141.8 12.3 %collective-permute-start.26 = (bf16[16,72,256]{2,1,0:T(8,128)(2,1)S(1)}, bf16[16,72,256]{2,1,0:T(8,128)(2,1)S(1)}, u32[]{:S(2)}, u32[]{:S(2)}) collective-permute-start(bf16[16,72,256]{2,1,0:T(8,128)(2,1)S(1)} %get-tuple-element.51), channel_id=1, source_target_pairs={{0,2},{1,3},{2,0},{3,1},{4,6},{5,7},{6,4},{7,5},{8,10},{9,11},{10,... | collective-permute-start | bytes 1769480 | tf_op jit(solution)/shard_map/ppermute | solution.py:385
  (23 other events, 159.2 us)

commit v3 on v2

--- a/solution.py
+++ b/solution.py
@@ -283,18 +283,160 @@
     )(adjacency, *strips, row_flips(width), pad_picks(tile_rows, width))
 
 
-def with_halo(block, sides, width):
-    for axis, dim in sides:
-        count = lax.axis_size(axis)
-        forward = [(i, i + 1) for i in range(count - 1)]
-        forward.append((count - 1, 0))
-        backward = [(target, source) for source, target in forward]
-        low = lax.ppermute(
-            lax.slice_in_dim(block, block.shape[dim] - width, None, axis=dim), axis, forward
-        )
-        high = lax.ppermute(lax.slice_in_dim(block, 0, width, axis=dim), axis, backward)
-        block = jnp.concatenate([low, block, high], axis=dim)
-    return block
+def seam_row_picks(width):
+    size = round_up(2 * width + 8, 16)
+    table = np.zeros((3, 2 * width, size), np.float32)
+    for shift in range(3):
+        for d in range(2):
+            for x in range(width):
+                w = x + 2 * shift
+                if 2 <= w < width + 2:
+                    source = d * width + w - 2
+                else:
+                    source = 2 * width + 4 * d + (w if w < 2 else w - width)
+                table[shift, d * width + x, source] = 1
+    return jnp.asarray(table, jnp.bfloat16)
+
+
+def seam_col_picks(tile_rows, width):
+    size = stack_places(tile_rows, width)[3]
+    table = np.zeros((2, 3 * 2 * tile_rows, size), np.float32)
+    for right in range(2):
+        for shift in range(3):
+            for y in range(tile_rows):
+                for k in range(2):
+                    w = width + 2 + k if right else k
+                    table[
+                        right,
+                        (shift * tile_rows + y) * 2 + k,
+                        stack_row(tile_rows, width, y + 2 * shift, w),
+                    ] = 1
+    return jnp.asarray(table, jnp.bfloat16)
+
+
+def tap_dot(value, tap):
+    return lax.dot_general(value, tap, (((1,), (1,)), ((), ())), preferred_element_type=jnp.float32)
+
+
+def return_kernel(
+    adjacency, field, sides, up, down, edge, far_same, far_cross, flips, picks, row_picks,
+    col_picks, kernel, padded, extra, stack, kept_picks, col_terms, col_sum,
+):
+    face_count, tile_rows, width, channels = field.shape
+    breadth = picks.shape[0] // (tile_rows + 4)
+    half = 2 * tile_rows
+    slot = round_up(half, 16)
+    _, above, below, _ = stack_places(tile_rows, width)
+    strip = row_picks.shape[2]
+    row_place, col_place = lax.axis_index("frow"), lax.axis_index("fcol")
+    at_top = row_place == 0
+    at_bottom = row_place == lax.axis_size("frow") - 1
+    at_left = col_place == 0
+    at_right = col_place == lax.axis_size("fcol") - 1
+    on_col_edge = jnp.logical_or(at_left, at_right)
+    stack[...] = jnp.zeros_like(stack)
+    extra[...] = jnp.zeros_like(extra)
+    col_terms[...] = jnp.zeros_like(col_terms)
+    cell = lax.broadcasted_iota(jnp.int32, (breadth, picks.shape[1]), 0)
+    for q in range(tile_rows + 4):
+        rows = pl.ds(q * breadth, breadth)
+        dropped = jnp.logical_or(
+            jnp.logical_and(at_left, cell < 2), jnp.logical_and(at_right, cell >= width + 2)
+        )
+        if q < 2:
+            dropped = jnp.logical_or(dropped, at_top)
+        if q >= tile_rows + 2:
+            dropped = jnp.logical_or(dropped, at_bottom)
+        kept = jnp.where(dropped, 0.0, picks[rows].astype(jnp.float32))
+        kept_picks[rows] = kept.astype(jnp.bfloat16)
+
+    @pl.loop(0, face_count)
+    def _(face):
+        load_stack(
+            adjacency, face, field, sides, up, down, edge, far_same, far_cross, flips, stack
+        )
+        out = pick(kept_picks[...], stack[...])
+        for q in range(tile_rows + 4):
+            padded[face, q] = out[q * breadth : q * breadth + width + 4]
+        for side, place, at_edge in ((0, above, at_top), (1, below, at_bottom)):
+
+            @pl.when(at_edge)
+            def _():
+                base = (face * 4 + side) * 3
+                row_tap = 2 * adjacency[base + 1]
+                turned = adjacency[base + 2]
+                total = jnp.zeros((2 * width, channels), jnp.float32)
+                for shift in range(3):
+                    value = pick(row_picks[shift], stack[pl.ds(place, strip)])
+                    col_tap = jnp.where(turned == 1, shift, 2 - shift)
+                    total += tap_dot(value, kernel[row_tap, col_tap])
+                for d in range(2):
+                    extra[face, side * (tile_rows - 2) + d] = total[d * width : (d + 1) * width]
+
+        @pl.when(on_col_edge)
+        def _():
+            base = (face * 4 + jnp.where(at_left, 2, 3)) * 3
+            variant = 2 * adjacency[base + 2] + adjacency[base + 1] - 2
+            value = jnp.dot(
+                col_picks[jnp.where(at_left, 0, 1)],
+                stack[...],
+                preferred_element_type=jnp.float32,
+            )
+            for shift in range(3):
+                rows = pl.ds(pl.multiple_of(face * slot, 16), half)
+                part = value[shift * half : (shift + 1) * half]
+                col_terms[variant, shift, rows] = part.astype(jnp.bfloat16)
+
+    @pl.when(on_col_edge)
+    def _():
+        total = jnp.zeros(col_sum.shape, jnp.float32)
+        for variant in range(4):
+            for shift in range(3):
+                row_tap = shift if variant >= 2 else 2 - shift
+                total += tap_dot(col_terms[variant, shift], kernel[row_tap, 2 * (variant % 2)])
+        col_sum[...] = total
+
+        @pl.loop(0, face_count)
+        def _(face):
+            value = col_sum[pl.ds(pl.multiple_of(face * slot, 16), half)]
+            for first, at_edge in ((0, at_left), (width - 2, at_right)):
+
+                @pl.when(at_edge)
+                def _():
+                    for y in range(tile_rows):
+                        cells = pl.ds(first, 2)
+                        extra[face, y, cells] = (
+                            extra[face, y, cells] + value[2 * y : 2 * y + 2]
+                        )
+
+
+def return_field(field, adjacency, kernel):
+    face_count, tile_rows, width, channels = field.shape
+    strips = gather_strips(field, adjacency)
+    padded = (face_count, tile_rows + 4, width + 4, channels)
+    size = stack_places(tile_rows, width)[3]
+    picks = pad_picks(tile_rows, width)
+    cells = face_count * round_up(2 * tile_rows, 16)
+    return pl.pallas_call(
+        return_kernel,
+        out_shape=(
+            jax.ShapeDtypeStruct(padded, field.dtype),
+            jax.ShapeDtypeStruct(field.shape, jnp.float32),
+        ),
+        in_specs=whole(12),
+        out_specs=[pl.BlockSpec(memory_space=pltpu.VMEM)] * 2,
+        scratch_shapes=[
+            pltpu.VMEM((size, channels), field.dtype),
+            pltpu.VMEM(picks.shape, field.dtype),
+            pltpu.VMEM((4, 3, cells, channels), field.dtype),
+            pltpu.VMEM((cells, channels), jnp.float32),
+        ],
+        compiler_params=pltpu.CompilerParams(vmem_limit_bytes=vmem_bytes),
+        cost_estimate=pl.CostEstimate(flops=1000, bytes_accessed=8000000, transcendentals=0),
+    )(
+        adjacency, *strips, row_flips(width), picks, seam_row_picks(width),
+        seam_col_picks(tile_rows, width), kernel,
+    )
 
 
 def gelu_value(value):
@@ -306,20 +448,6 @@
         0.5 * (1.0 + jax.scipy.special.erf(value * half_root))
         + value * jnp.exp(-0.5 * value * value) * density_scale
     )
-
-
-def pick_table(entries, side_near, face_count):
-    same_side = (entries[:, 1] == side_near).astype(jnp.int32)
-    slot_index = (2 * entries[:, 2] + same_side) * face_count + entries[:, 0]
-    return (slot_index[:, None] == jnp.arange(4 * face_count, dtype=jnp.int32)[None, :]).astype(
-        jnp.bfloat16
-    )
-
-
-def reflect(row_band, col_band):
-    row_band = lax.ppermute(row_band, axes, mirror_pairs(True, False, True))
-    col_band = lax.ppermute(col_band, axes, mirror_pairs(False, True, False))
-    return (row_band, col_band)
 
 
 def reduce_stages():
@@ -396,152 +524,60 @@
     return (part.reshape(matrix.shape).astype(jnp.float32), vector[0])
 
 
-def fold_border(extended, along, cells, inner_size):
-    middle = lax.slice_in_dim(extended, 2 * cells, 2 * cells + inner_size, axis=along)
-    before = lax.slice_in_dim(extended, 0, cells, axis=along)
-    after_rim = lax.slice_in_dim(
-        extended, inner_size + 3 * cells, inner_size + 4 * cells, axis=along
-    )
-    lead_pads = [(0, 0)] * extended.ndim
-    tail_pads = [(0, 0)] * extended.ndim
-    lead_pads[along] = (0, inner_size - cells)
-    tail_pads[along] = (inner_size - cells, 0)
-    return middle + jnp.pad(before, lead_pads) + jnp.pad(after_rim, tail_pads)
-
-
 def local(face_input, kernel, convolution_bias, upstream, adjacency):
-    face_count = face_input.shape[0]
-    tile_rows = face_input.shape[1]
-    tile_cols = face_input.shape[2]
-    dilation_step = DILATION_STEP
-    height = tile_rows + 2 * dilation_step
-    breadth = tile_cols + 2 * dilation_step
-    at_top = lax.axis_index("frow") == 0
-    at_bottom = lax.axis_index("frow") == lax.axis_size("frow") - 1
-    at_left = lax.axis_index("fcol") == 0
-    at_right = lax.axis_index("fcol") == lax.axis_size("fcol") - 1
-    column_index = jnp.arange(breadth)
-    keep_cols = jnp.logical_not(
-        at_left & (column_index < dilation_step)
-        | at_right & (column_index >= tile_cols + dilation_step)
-    )
-    row_index = jnp.arange(height)
-    keep_rows = jnp.logical_not(
-        at_top & (row_index < dilation_step) | at_bottom & (row_index >= tile_rows + dilation_step)
-    )
-    padded_input = pad_field(face_input, adjacency.reshape(-1))
-    row_pick = pick_table(
-        jnp.where(at_top, adjacency[:, 0], adjacency[:, 1]), jnp.where(at_top, 0, 1), face_count
-    )
-    col_pick = pick_table(
-        jnp.where(at_left, adjacency[:, 2], adjacency[:, 3]), jnp.where(at_left, 2, 3), face_count
-    )
-    random_values = ("NHWC", "HWIO", "NHWC")
+    face_count, tile_rows, tile_cols, channels = face_input.shape
+    table = adjacency.reshape(-1)
+    padded_input = pad_field(face_input, table)
+    layout = ("NHWC", "HWIO", "NHWC")
     preactivation = (
         lax.conv_general_dilated(
             padded_input,
             kernel,
             (1, 1),
             "VALID",
-            rhs_dilation=(dilation_step, dilation_step),
-            dimension_numbers=random_values,
+            rhs_dilation=(DILATION_STEP, DILATION_STEP),
+            dimension_numbers=layout,
             preferred_element_type=jnp.float32,
         )
         + convolution_bias
     )
     activation = gelu_value(preactivation).astype(jnp.bfloat16)
-    preactivation_gradient = (upstream.astype(jnp.float32) * gelu_slope(preactivation)).astype(
-        jnp.bfloat16
-    )
+    pre_grad = (upstream.astype(jnp.float32) * gelu_slope(preactivation)).astype(jnp.bfloat16)
     tap_list = []
-    for kernel_row_offset in range(3):
-        for kernel_column_offset in range(3):
-            input_window = padded_input[
-                :,
-                kernel_row_offset * dilation_step : kernel_row_offset * dilation_step + tile_rows,
-                kernel_column_offset * dilation_step : kernel_column_offset * dilation_step
-                + tile_cols,
-            ]
+    for a in range(3):
+        for b in range(3):
+            row, col = a * DILATION_STEP, b * DILATION_STEP
+            window = padded_input[:, row : row + tile_rows, col : col + tile_cols]
             tap_list.append(
                 lax.dot_general(
-                    input_window,
-                    preactivation_gradient,
+                    window,
+                    pre_grad,
                     (((0, 1, 2), (0, 1, 2)), ((), ())),
                     preferred_element_type=jnp.float32,
                 )
             )
     kernel_local = jnp.stack(tap_list, 0).reshape(kernel.shape)
-    bias_local = jnp.sum(preactivation_gradient.astype(jnp.float32), axis=(0, 1, 2))
+    bias_local = jnp.sum(pre_grad.astype(jnp.float32), axis=(0, 1, 2))
     kernel_total, bias_total = reduce_everywhere(kernel_local, bias_local)
     scale = 1.0 / math.sqrt(
         face_count * tile_rows * lax.axis_size("frow") * tile_cols * lax.axis_size("fcol")
     )
     kernel_grad = kernel_total * scale
     bias_grad = bias_total * scale
-    rotated_strip = jnp.transpose(jnp.flip(kernel, (0, 1)), (0, 1, 3, 2))
-    twice = 2 * dilation_step
-    padded_gradient = lax.conv_general_dilated(
-        preactivation_gradient,
-        rotated_strip,
-        (1, 1),
-        ((twice, twice), (twice, twice)),
-        rhs_dilation=(dilation_step, dilation_step),
-        dimension_numbers=random_values,
-        preferred_element_type=jnp.float32,
+    padded_grad, extra = return_field(pre_grad, table, kernel)
+    rotated = jnp.transpose(jnp.flip(kernel, (0, 1)), (0, 1, 3, 2))
+    input_gradient = (
+        lax.conv_general_dilated(
+            padded_grad,
+            rotated,
+            (1, 1),
+            "VALID",
+            rhs_dilation=(DILATION_STEP, DILATION_STEP),
+            dimension_numbers=layout,
+            preferred_element_type=jnp.float32,
+        )
+        + extra
     ).astype(jnp.bfloat16)
-    row_seam = jnp.where(
-        at_top, padded_gradient[:, :dilation_step], padded_gradient[:, tile_rows + dilation_step :]
-    )
-    row_seam = jnp.where(keep_cols[None, None, :, None], row_seam, jnp.zeros_like(row_seam))
-    row_split = jnp.einsum("fk,fdwc->kdwc", row_pick, row_seam, preferred_element_type=jnp.float32)
-    row_split = row_split.reshape((4, face_count) + row_split.shape[1:])
-    col_seam = jnp.where(
-        at_left,
-        padded_gradient[:, :, :dilation_step],
-        padded_gradient[:, :, tile_cols + dilation_step :],
-    )
-    col_seam = jnp.where(keep_rows[None, :, None, None], col_seam, jnp.zeros_like(col_seam))
-    col_split = jnp.einsum("fk,fadc->kadc", col_pick, col_seam, preferred_element_type=jnp.float32)
-    col_split = col_split.reshape((4, face_count) + col_split.shape[1:])
-    row_far_grad = jnp.concatenate(
-        [jnp.flip(row_split[2], 2), jnp.flip(row_split[3], (1, 2))], 1
-    ).astype(jnp.bfloat16)
-    col_far_grad = jnp.concatenate(
-        [jnp.flip(col_split[2], 1), jnp.flip(col_split[3], (1, 2))], 2
-    ).astype(jnp.bfloat16)
-    row_back, col_back = reflect(row_far_grad, col_far_grad)
-    wrap_rows = row_split[0] + row_back[:, :dilation_step].astype(jnp.float32)
-    own_rows = jnp.flip(row_split[1], 1) + row_back[:, dilation_step:].astype(jnp.float32)
-    wrap_cols = col_split[0] + col_back[:, :, :dilation_step].astype(jnp.float32)
-    own_cols = jnp.flip(col_split[1], 2) + col_back[:, :, dilation_step:].astype(jnp.float32)
-    gathered = padded_gradient.astype(jnp.float32)
-    middle_rows = gathered[:, dilation_step : tile_rows + dilation_step]
-    middle_rows = middle_rows + jnp.pad(
-        jnp.where(at_top, own_rows, 0.0), ((0, 0), (0, tile_rows - dilation_step), (0, 0), (0, 0))
-    )
-    middle_rows = middle_rows + jnp.pad(
-        jnp.where(at_bottom, own_rows, 0.0),
-        ((0, 0), (tile_rows - dilation_step, 0), (0, 0), (0, 0)),
-    )
-    top_grad = jnp.where(at_top, wrap_rows, gathered[:, :dilation_step])
-    bottom_grad = jnp.where(at_bottom, wrap_rows, gathered[:, tile_rows + dilation_step :])
-    gathered = jnp.concatenate([top_grad, middle_rows, bottom_grad], 1)
-    middle_cols = gathered[:, :, dilation_step : tile_cols + dilation_step]
-    middle_cols = middle_cols + jnp.pad(
-        jnp.where(at_left, own_cols, 0.0), ((0, 0), (0, 0), (0, tile_cols - dilation_step), (0, 0))
-    )
-    middle_cols = middle_cols + jnp.pad(
-        jnp.where(at_right, own_cols, 0.0), ((0, 0), (0, 0), (tile_cols - dilation_step, 0), (0, 0))
-    )
-    left_grad = jnp.where(at_left, wrap_cols, gathered[:, :, :dilation_step])
-    right_grad = jnp.where(at_right, wrap_cols, gathered[:, :, tile_cols + dilation_step :])
-    gathered = jnp.concatenate([left_grad, middle_cols, right_grad], 2)
-    returned = with_halo(
-        gathered.astype(jnp.bfloat16), (("frow", 1), ("fcol", 2)), dilation_step
-    ).astype(gathered.dtype)
-    folded = fold_border(returned, 1, dilation_step, tile_rows)
-    folded = fold_border(folded, 2, dilation_step, tile_cols)
-    input_gradient = folded.astype(jnp.bfloat16)
     return (activation, input_gradient, kernel_grad, bias_grad)
 
 

time: 157 us -> 135 us (0.86)
  waiting for transfers between devices: 50.8 us -> 23.2 us
  Pallas kernels: 9.06 us -> 27.8 us
  matrix products: 17.4 us -> 9.8 us
  other arithmetic: 17.6 us -> 10.9 us
  starting transfers between devices: 44.3 us -> 47.9 us
  local copies, waits for them, and re-layouts: 15.4 us -> 12.9 us
    ppermute x7, waiting for transfers between devices: 20.7 us -> 3.57 us  [reduce_everywhere(): lax.ppermute(part, axes, [(i, i ^ offset) for i in range(count)])]
    pallas_call x0 -> x1, Pallas kernels: none -> 15.2 us  [return_field(): pl.pallas_call(return_kernel, out_shape=(jax.ShapeDtypeStruct(padded, fie...]
    ppermute x6 -> x0, waiting for transfers between devices: 10.6 us -> none  [the longest x2 5.48 us: with_halo(): lax.ppermute(lax.slice_in_dim(block, block.shape[dim] - width, None, axis...]
    ppermute x1 -> x2, waiting for transfers between devices: 0.01 us -> 10 us  [gather_strips(): row_cross = lax.ppermute(edge_strip, axes, mirror_pairs(True, True, True))]
    ppermute x6 -> x0, starting transfers between devices: 9.46 us -> none  [the longest x1 2.84 us: reflect(): col_band = lax.ppermute(col_band, axes, mirror_pairs(False, True, False))]
    ppermute x7, waiting for transfers between devices: 9.5 us -> 3.6 us  [reduce_everywhere(): packed = lax.ppermute(packed, axes, [(i, i ^ offset) for i in range(count)])]
    unnamed x54 -> x53, local copies, waits for them, and re-layouts: 4.84 us -> 10.7 us
    ppermute x1 -> x2, waiting for transfers between devices: 6.37 us -> 0.94 us  [gather_strips(): up = lax.ppermute(bottom, axes, shifted_pairs(1, 0))]
  transfers between devices with their start and end apart: 27 -> 28, of which waited for: 9 -> 8; matrix products, arithmetic and copies ran while one was open for 14% -> 7% of each run, Pallas kernels for 0% -> 14%
where the time goes in v3:
time: 135 us; the launch traced here: 134 us
  starting transfers between devices  47.9 us (35%)
  Pallas kernels  27.8 us (21%)
  waiting for transfers between devices  23.2 us (17%)
  local copies, waits for them, and re-layouts  12.9 us (10%)
  other arithmetic  10.9 us (8%)
  matrix products  9.8 us (7%)
    pallas_call x1, Pallas kernels, return_field(): pl.pallas_call(return_kernel, out_shape=(jax.ShapeDtypeStruct(padded, fie...  15.2 us
    unnamed x53, local copies, waits for them, and re-layouts  10.7 us
    ppermute x2, waiting for transfers between devices, gather_strips(): row_cross = lax.ppermute(edge_strip, axes, mirror_pairs(True, True, True))  10 us
    ppermute x7, starting transfers between devices, reduce_everywhere(): lax.ppermute(part, axes, [(i, i ^ offset) for i in range(count)])  8.06 us
    ppermute x7, starting transfers between devices, reduce_everywhere(): packed = lax.ppermute(packed, axes, [(i, i ^ offset) for i in range(count)])  8 us
    ppermute x2, starting transfers between devices, gather_strips(): down = lax.ppermute(top, axes, shifted_pairs(-1, 0))  7.93 us
    pallas_call x2, Pallas kernels, gather_strips(): pl.pallas_call(col_kernel, out_shape=(jax.ShapeDtypeStruct(edges.shape, f...  6.83 us
    ppermute x2, starting transfers between devices, gather_strips(): far_cross = lax.ppermute(edge, axes, mirror_pairs(False, True, True))  6 us
  transfers between devices with their start and end apart: 28, of which 8 were waited for; matrix products, arithmetic and copies ran while one was open for 7% of the time, Pallas kernels for 14%

profile of v3, /device:TPU:0, one launch (start us, length us, event | category | flops | bytes accessed | tf_op | source)
XLA Modules:
  0.0 133.7 jit_solution(5386974091522245051)
XLA Ops:
  1.9 3.0 %collective-permute-start = (bf16[12,16,256]{2,1,0:T(8,128)(2,1)S(1)}, bf16[12,16,256]{2,1,0:T(8,128)(2,1)S(1)}, u32[]{:S(2)}, u32[]{:S(2)}) collective-permute-start(bf16[12,16,256]{2,1,0:T(8,128)(2,1)S(1)} %get-tuple-element.53.edges), channel_id=1, source_target_pairs={{0,1},{1,0},{2,3},{3,2},{4,5},{5,4},{6,7},{7,6},{8,9},{9,8},{10,11... | collective-permute-start | bytes 294920 | tf_op jit(solution)/shard_map/ppermute | solution.py:238
  4.9 3.7 %collective-permute-start.2 = (bf16[12,8,256]{2,1,0:T(8,128)(2,1)S(1)}, bf16[12,8,256]{2,1,0:T(8,128)(2,1)S(1)}, u32[]{:S(2)}, u32[]{:S(2)}) collective-permute-start(bf16[12,8,256]{2,1,0:T(8,128)(2,1)S(1)} %get-tuple-element.52), channel_id=1, source_target_pairs={{0,31},{1,30},{2,29},{3,28},{4,27},{5,26},{6,25},{7,24},{8,23},{9,... | collective-permute-start | bytes 147464 | tf_op jit(solution)/shard_map/ppermute | solution.py:249
  9.8 2.6 %collective-permute-done.2.far_cross = bf16[12,8,256]{2,1,0:T(8,128)(2,1)S(1)} collective-permute-done((bf16[12,8,256]{2,1,0:T(8,128)(2,1)S(1)}, bf16[12,8,256]{2,1,0:T(8,128)(2,1)S(1)}, u32[]{:S(2)}, u32[]{:S(2)}) %collective-permute-start.2) | collective-permute-done | bytes 49184 | tf_op jit(solution)/shard_map/ppermute | solution.py:249
  12.4 2.4 %collective-permute-done.1.far_same = bf16[12,8,256]{2,1,0:T(8,128)(2,1)S(1)} collective-permute-done((bf16[12,8,256]{2,1,0:T(8,128)(2,1)S(1)}, bf16[12,8,256]{2,1,0:T(8,128)(2,1)S(1)}, u32[]{:S(2)}, u32[]{:S(2)}) %collective-permute-start.1) | collective-permute-done | bytes 49184 | tf_op jit(solution)/shard_map/ppermute | solution.py:248
  17.3 3.9 %shard_map.174 = (bf16[12,16,256]{2,1,0:T(8,128)(2,1)S(1)}, bf16[12,72,256]{2,1,0:T(8,128)(2,1)}, bf16[12,72,256]{2,1,0:T(8,128)(2,1)}, bf16[12,72,256]{2,1,0:T(8,128)(2,1)S(1)}) custom-call(s32[144]{0:T(256)S(1)} %reshape.41.adjacency, bf16[12,4,32,256]{3,2,1,0:T(8,128)(2,1)S(1)} %copy-done, bf16[12,16,256]{2,1,0:T(8,128)(2,1)S(1)} %get-tuple-element.53.edges, ...), custom_call_target="tpu_custom_call" | custom-call | flops 1000 | bytes 3000000 | tf_op jit(solution)/shard_map/pallas_call | solution.py:251
  22.8 3.5 %collective-permute-start.4 = (bf16[12,72,256]{2,1,0:T(8,128)(2,1)}, bf16[12,72,256]{2,1,0:T(8,128)(2,1)S(1)}, u32[]{:S(2)}, u32[]{:S(2)}) collective-permute-start(bf16[12,72,256]{2,1,0:T(8,128)(2,1)} %get-tuple-element.16), channel_id=1, source_target_pairs={{0,30},{1,31},{2,0},{3,1},{4,2},{5,3},{6,4},{7,5},{8,6},{9,7},{10,... | collective-permute-start | bytes 1327112 | tf_op jit(solution)/shard_map/ppermute | solution.py:264
  26.3 2.8 %collective-permute-start.6 = (bf16[12,72,256]{2,1,0:T(8,128)(2,1)S(1)}, bf16[12,72,256]{2,1,0:T(8,128)(2,1)S(1)}, u32[]{:S(2)}, u32[]{:S(2)}) collective-permute-start(bf16[12,72,256]{2,1,0:T(8,128)(2,1)S(1)} %get-tuple-element.17.edge), channel_id=1, source_target_pairs={{0,31},{1,30},{30,1},{31,0}} | collective-permute-start | bytes 1327112 | tf_op jit(solution)/shard_map/ppermute | solution.py:266
  29.1 2.5 %collective-permute-start.5 = (bf16[12,72,256]{2,1,0:T(8,128)(2,1)S(1)}, bf16[12,72,256]{2,1,0:T(8,128)(2,1)S(1)}, u32[]{:S(2)}, u32[]{:S(2)}) collective-permute-start(bf16[12,72,256]{2,1,0:T(8,128)(2,1)S(1)} %get-tuple-element.17.edge), channel_id=1, source_target_pairs={{0,1},{1,0},{30,31},{31,30}} | collective-permute-start | bytes 1327112 | tf_op jit(solution)/shard_map/ppermute | solution.py:265
  32.6 7.0 %collective-permute-done.6.far_cross = bf16[12,72,256]{2,1,0:T(8,128)(2,1)S(1)} collective-permute-done((bf16[12,72,256]{2,1,0:T(8,128)(2,1)S(1)}, bf16[12,72,256]{2,1,0:T(8,128)(2,1)S(1)}, u32[]{:S(2)}, u32[]{:S(2)}) %collective-permute-start.6) | collective-permute-done | bytes 442400 | tf_op jit(solution)/shard_map/ppermute | solution.py:266
  44.9 5.7 %shard_map.175 = bf16[12,8,36,256]{3,2,1,0:T(8,128)(2,1)S(1)} custom-call(s32[144]{0:T(256)S(1)} %reshape.41.adjacency, bf16[12,4,32,256]{3,2,1,0:T(8,128)(2,1)S(1)} %copy-done.1, bf16[12,16,256]{2,1,0:T(8,128)(2,1)S(1)} %copy-done.11, bf16[12,72,256]{2,1,0:T(8,128)(2,1)S(1)} %collective-permute-done.3.up, ...), custom_call_target="tpu_custom_call" | custom-call | flops 1000 | bytes 5000000 | tf_op jit(solution)/shard_map/pallas_call | solution.py:275
  50.7 3.0 %fusion.2 = f32[12,4,32,256]{3,0,2,1:T(8,128)S(1)} fusion(bf16[3,3,256,256]{3,2,1,0:T(8,128)(2,1)S(1)} %copy-done.2, bf16[12,8,36,256]{3,2,1,0:T(8,128)(2,1)S(1)} %shard_map.175), kind=kOutput, calls=%fused_computation.3 | convolution fusion | flops 1811939328 | bytes 4521984 | tf_op jit(solution)/shard_map/conv_general_dilated | solution.py:533
  60.6 1.6 %collective-permute-done.14 = bf16[1160,256]{1,0:T(8,128)(2,1)} collective-permute-done((bf16[1160,256]{1,0:T(8,128)(2,1)}, bf16[1160,256]{1,0:T(8,128)(2,1)}, u32[]{:S(2)}, u32[]{:S(2)}) %collective-permute-start.14) | collective-permute-done | bytes 593952 | tf_op jit(solution)/shard_map/ppermute | solution.py:500
  64.2 1.6 %collective-permute-start.15 = (bf16[296,256]{1,0:T(8,128)(2,1)S(1)}, bf16[296,256]{1,0:T(8,128)(2,1)S(1)}, u32[]{:S(2)}, u32[]{:S(2)}) collective-permute-start(bf16[296,256]{1,0:T(8,128)(2,1)S(1)} %get-tuple-element.57), channel_id=1, source_target_pairs={{0,1},{1,0},{2,3},{3,2},{4,5},{5,4},{6,7},{7,6},{8,9},{9,8},{10,11... | collective-permute-start | bytes 454664 | tf_op jit(solution)/shard_map/ppermute | solution.py:500
  65.8 2.0 %collective-permute-start.17 = (bf16[296,256]{1,0:T(8,128)(2,1)S(1)}, bf16[296,256]{1,0:T(8,128)(2,1)S(1)}, u32[]{:S(2)}, u32[]{:S(2)}) collective-permute-start(bf16[296,256]{1,0:T(8,128)(2,1)S(1)} %get-tuple-element.59), channel_id=1, source_target_pairs={{0,5},{1,4},{2,7},{3,6},{4,1},{5,0},{6,3},{7,2},{8,13},{9,12},{10,... | collective-permute-start | bytes 454664 | tf_op jit(solution)/shard_map/ppermute | solution.py:500
  67.8 2.3 %collective-permute-start.9 = (bf16[12,8,256]{2,1,0:T(8,128)(2,1)S(1)}, bf16[12,8,256]{2,1,0:T(8,128)(2,1)S(1)}, u32[]{:S(2)}, u32[]{:S(2)}) collective-permute-start(bf16[12,8,256]{2,1,0:T(8,128)(2,1)S(1)} %get-tuple-element.50), channel_id=1, source_target_pairs={{0,31},{1,30},{2,29},{3,28},{4,27},{5,26},{6,25},{7,24},{8,23},{9,... | collective-permute-start | bytes 147464 | tf_op jit(solution)/shard_map/ppermute | solution.py:249
  70.1 3.1 %collective-permute-start.8 = (bf16[12,8,256]{2,1,0:T(8,128)(2,1)S(1)}, bf16[12,8,256]{2,1,0:T(8,128)(2,1)S(1)}, u32[]{:S(2)}, u32[]{:S(2)}) collective-permute-start(bf16[12,8,256]{2,1,0:T(8,128)(2,1)S(1)} %get-tuple-element.50), channel_id=1, source_target_pairs={{0,30},{1,31},{2,28},{3,29},{4,26},{5,27},{6,24},{7,25},{8,22},{9,... | collective-permute-start | bytes 147464 | tf_op jit(solution)/shard_map/ppermute | solution.py:248
  73.8 2.0 %collective-permute-done.16 = bf16[296,256]{1,0:T(8,128)(2,1)S(1)} collective-permute-done((bf16[296,256]{1,0:T(8,128)(2,1)S(1)}, bf16[296,256]{1,0:T(8,128)(2,1)S(1)}, u32[]{:S(2)}, u32[]{:S(2)}) %collective-permute-start.16) | collective-permute-done | bytes 151584 | tf_op jit(solution)/shard_map/ppermute | solution.py:500
  76.0 3.3 %collective-permute-start.19 = (bf16[80,256]{1,0:T(8,128)(2,1)S(1)}, bf16[80,256]{1,0:T(8,128)(2,1)S(1)}, u32[]{:S(2)}, u32[]{:S(2)}) collective-permute-start(bf16[80,256]{1,0:T(8,128)(2,1)S(1)} %get-tuple-element.55), channel_id=1, source_target_pairs={{0,16},{1,17},{2,18},{3,19},{4,20},{5,21},{6,22},{7,23},{8,24},{9,... | collective-permute-start | bytes 122888 | tf_op jit(solution)/shard_map/ppermute | solution.py:500
  80.4 3.0 %shard_map.176 = (bf16[12,16,256]{2,1,0:T(8,128)(2,1)S(1)}, bf16[12,72,256]{2,1,0:T(8,128)(2,1)S(1)}, bf16[12,72,256]{2,1,0:T(8,128)(2,1)S(1)}, bf16[12,72,256]{2,1,0:T(8,128)(2,1)S(1)}) custom-call(s32[144]{0:T(256)S(1)} %reshape.41.adjacency, bf16[12,4,32,256]{3,2,1,0:T(8,128)(2,1)S(1)} %get-tuple-element.25.field, ...), custom_call_target="tpu_custom_call" | custom-call | flops 1000 | bytes 3000000 | tf_op jit(solution)/shard_map/pallas_call | solution.py:251
  83.4 4.4 %collective-permute-start.11 = (bf16[12,72,256]{2,1,0:T(8,128)(2,1)S(1)}, bf16[12,72,256]{2,1,0:T(8,128)(2,1)S(1)}, u32[]{:S(2)}, u32[]{:S(2)}) collective-permute-start(bf16[12,72,256]{2,1,0:T(8,128)(2,1)S(1)} %get-tuple-element.20), channel_id=1, source_target_pairs={{0,30},{1,31},{2,0},{3,1},{4,2},{5,3},{6,4},{7,5},{8,6},{9,7},{10,... | collective-permute-start | bytes 1327112 | tf_op jit(solution)/shard_map/ppermute | solution.py:264
  88.9 3.4 %collective-permute-start.21 = (bf16[1,72,256]{2,1,0:T(8,128)(2,1)S(1)}, bf16[1,72,256]{2,1,0:T(8,128)(2,1)S(1)}, u32[]{:S(2)}, u32[]{:S(2)}) collective-permute-start(bf16[1,72,256]{2,1,0:T(8,128)(2,1)S(1)} %bitcast.211), channel_id=1, source_target_pairs={{0,8},{1,9},{2,10},{3,11},{4,12},{5,13},{6,14},{7,15},{8,0},{9,1},... | collective-permute-start | bytes 110600 | tf_op jit(solution)/shard_map/ppermute | solution.py:513
  92.3 3.6 %collective-permute-done.23 = bf16[1,72,256]{2,1,0:T(8,128)(2,1)S(1)} collective-permute-done((bf16[1,72,256]{2,1,0:T(8,128)(2,1)S(1)}, bf16[1,72,256]{2,1,0:T(8,128)(2,1)S(1)}, u32[]{:S(2)}, u32[]{:S(2)}) %collective-permute-start.23) | collective-permute-done | bytes 36896 | tf_op jit(solution)/shard_map/ppermute | solution.py:513
  95.9 1.9 %collective-permute-start.13 = (bf16[12,72,256]{2,1,0:T(8,128)(2,1)S(1)}, bf16[12,72,256]{2,1,0:T(8,128)(2,1)S(1)}, u32[]{:S(2)}, u32[]{:S(2)}) collective-permute-start(bf16[12,72,256]{2,1,0:T(8,128)(2,1)S(1)} %get-tuple-element.21.edge), channel_id=1, source_target_pairs={{0,31},{1,30},{30,1},{31,0}} | collective-permute-start | bytes 1327112 | tf_op jit(solution)/shard_map/ppermute | solution.py:266
  97.8 2.8 %collective-permute-start.12 = (bf16[12,72,256]{2,1,0:T(8,128)(2,1)S(1)}, bf16[12,72,256]{2,1,0:T(8,128)(2,1)S(1)}, u32[]{:S(2)}, u32[]{:S(2)}) collective-permute-start(bf16[12,72,256]{2,1,0:T(8,128)(2,1)S(1)} %get-tuple-element.21.edge), channel_id=1, source_target_pairs={{0,1},{1,0},{30,31},{31,30}} | collective-permute-start | bytes 1327112 | tf_op jit(solution)/shard_map/ppermute | solution.py:265
  100.8 1.4 %collective-permute-start.24 = (bf16[4,72,256]{2,1,0:T(8,128)(2,1)S(1)}, bf16[4,72,256]{2,1,0:T(8,128)(2,1)S(1)}, u32[]{:S(2)}, u32[]{:S(2)}) collective-permute-start(bf16[4,72,256]{2,1,0:T(8,128)(2,1)S(1)} %get-tuple-element.42), channel_id=1, source_target_pairs={{0,1},{1,0},{2,3},{3,2},{4,5},{5,4},{6,7},{7,6},{8,9},{9,8},{10,11... | collective-permute-start | bytes 442376 | tf_op jit(solution)/shard_map/ppermute | solution.py:513
  102.2 2.0 %collective-permute-start.26 = (bf16[4,72,256]{2,1,0:T(8,128)(2,1)S(1)}, bf16[4,72,256]{2,1,0:T(8,128)(2,1)S(1)}, u32[]{:S(2)}, u32[]{:S(2)}) collective-permute-start(bf16[4,72,256]{2,1,0:T(8,128)(2,1)S(1)} %get-tuple-element.42), channel_id=1, source_target_pairs={{0,5},{1,4},{2,7},{3,6},{4,1},{5,0},{6,3},{7,2},{8,13},{9,12},{10,... | collective-permute-start | bytes 442376 | tf_op jit(solution)/shard_map/ppermute | solution.py:513
  104.3 2.0 %multiply_convert_fusion = bf16[12,4,32,256]{3,2,1,0:T(8,128)(2,1)} fusion(f32[256]{0:T(256)S(1)} %copy-done.23, f32[12,4,32,256]{3,0,2,1:T(8,128)S(1)} %copy-done.19), kind=kLoop, calls=%fused_computation.15 | loop fusion | flops 2359296 | bytes 2360320 | tf_op jit(solution)/shard_map/convert_element_type | solution.py:544
  106.3 3.0 %collective-permute-done.13.far_cross = bf16[12,72,256]{2,1,0:T(8,128)(2,1)S(1)} collective-permute-done((bf16[12,72,256]{2,1,0:T(8,128)(2,1)S(1)}, bf16[12,72,256]{2,1,0:T(8,128)(2,1)S(1)}, u32[]{:S(2)}, u32[]{:S(2)}) %collective-permute-start.13) | collective-permute-done | bytes 442400 | tf_op jit(solution)/shard_map/ppermute | solution.py:266
  109.3 15.2 %shard_map.177 = (bf16[12,8,36,256]{3,2,1,0:T(8,128)(2,1)}, f32[12,4,32,256]{3,2,1,0:T(8,128)}) custom-call(s32[144]{0:T(256)S(1)} %reshape.41.adjacency, bf16[12,4,32,256]{3,2,1,0:T(8,128)(2,1)S(1)} %get-tuple-element.25.field, bf16[12,16,256]{2,1,0:T(8,128)(2,1)S(1)} %get-tuple-element.18.sides, bf16[12,72,256]{2,1,0:T(8,128)(2,1)S(1)} %collective-permute-done.10.up, ...), custom_call_target="tpu_custom_call" | custom-call | flops 1000 | bytes 8000000 | tf_op jit(solution)/shard_map/pallas_call | solution.py:420
  126.2 3.1 %fusion = f32[12,4,32,256]{3,0,2,1:T(8,128)S(1)} fusion(bf16[3,3,256,256]{3,2,1,0:T(8,128)(2,1)S(1)} %copy-done.2, bf16[12,8,36,256]{3,2,1,0:T(8,128)(2,1)S(1)} %copy-done.24), kind=kOutput, calls=%fused_computation.1 | convolution fusion | flops 1811939328 | bytes 4521984 | tf_op jit(solution)/shard_map/conv_general_dilated | solution.py:570
  129.3 1.8 %fusion.10 = bf16[12,4,32,256]{3,2,1,0:T(8,128)(2,1)} fusion(f32[12,4,32,256]{3,2,1,0:T(8,128)S(1)} %copy-done.20, f32[12,4,32,256]{3,0,2,1:T(8,128)S(1)} %fusion), kind=kLoop, calls=%fused_computation.13 | loop fusion | flops 786432 | bytes 3932160 | tf_op jit(solution)/shard_map/convert_element_type | solution.py:580
  132.0 1.6 %convert_multiply_fusion = f32[32,72,256]{2,1,0:T(8,128)} fusion(bf16[16,72,256]{2,1,0:T(8,128)(2,1)S(1)} %get-tuple-element.27, bf16[16,72,256]{2,1,0:T(8,128)(2,1)S(1)} %get-tuple-element.26), kind=kLoop, calls=%fused_computation.5 | loop fusion | flops 1769472 | bytes 3538944 | tf_op jit(solution)/shard_map/mul | solution.py:565
  (129 shorter events, 27.3 us)
Async XLA Ops:
  0.6 40.5 %copy-start.3 = (bf16[320,384]{1,0:T(8,128)(2,1)S(1)}, bf16[320,384]{1,0:T(8,128)(2,1)}, u32[]{:S(2)}) copy-start(bf16[320,384]{1,0:T(8,128)(2,1)} %constant.195.clone.picks) | copy-start | bytes 737284
  1.9 12.9 %collective-permute-start = (bf16[12,16,256]{2,1,0:T(8,128)(2,1)S(1)}, bf16[12,16,256]{2,1,0:T(8,128)(2,1)S(1)}, u32[]{:S(2)}, u32[]{:S(2)}) collective-permute-start(bf16[12,16,256]{2,1,0:T(8,128)(2,1)S(1)} %get-tuple-element.53.edges), channel_id=1, source_target_pairs={{0,1},{1,0},{2,3},{3,2},{4,5},{5,4},{6,7},{7,6},{8,9},{9,8},{10,11... | collective-permute-start | bytes 294920 | tf_op jit(solution)/shard_map/ppermute | solution.py:238
  4.9 7.5 %collective-permute-start.2 = (bf16[12,8,256]{2,1,0:T(8,128)(2,1)S(1)}, bf16[12,8,256]{2,1,0:T(8,128)(2,1)S(1)}, u32[]{:S(2)}, u32[]{:S(2)}) collective-permute-start(bf16[12,8,256]{2,1,0:T(8,128)(2,1)S(1)} %get-tuple-element.52), channel_id=1, source_target_pairs={{0,31},{1,30},{2,29},{3,28},{4,27},{5,26},{6,25},{7,24},{8,23},{9,... | collective-permute-start | bytes 147464 | tf_op jit(solution)/shard_map/ppermute | solution.py:249
  8.6 6.2 %collective-permute-start.1 = (bf16[12,8,256]{2,1,0:T(8,128)(2,1)S(1)}, bf16[12,8,256]{2,1,0:T(8,128)(2,1)S(1)}, u32[]{:S(2)}, u32[]{:S(2)}) collective-permute-start(bf16[12,8,256]{2,1,0:T(8,128)(2,1)S(1)} %get-tuple-element.52), channel_id=1, source_target_pairs={{0,30},{1,31},{2,28},{3,29},{4,26},{5,27},{6,24},{7,25},{8,22},{9,... | collective-permute-start | bytes 147464 | tf_op jit(solution)/shard_map/ppermute | solution.py:248
  17.3 23.8 %copy-start.1 = (bf16[12,4,32,256]{3,2,1,0:T(8,128)(2,1)S(1)}, bf16[12,4,32,256]{3,2,1,0:T(8,128)(2,1)}, u32[]{:S(2)}) copy-start(bf16[12,4,32,256]{3,2,1,0:T(8,128)(2,1)} %field.3) | copy-start | bytes 2359300
  21.8 10.7 %collective-permute-start.3 = (bf16[12,72,256]{2,1,0:T(8,128)(2,1)}, bf16[12,72,256]{2,1,0:T(8,128)(2,1)S(1)}, u32[]{:S(2)}, u32[]{:S(2)}) collective-permute-start(bf16[12,72,256]{2,1,0:T(8,128)(2,1)} %get-tuple-element.15), channel_id=1, source_target_pairs={{0,2},{1,3},{2,4},{3,5},{4,6},{5,7},{6,8},{7,9},{8,10},{9,11},{10,... | collective-permute-start | bytes 1327112 | tf_op jit(solution)/shard_map/ppermute | solution.py:263
  22.8 9.8 %collective-permute-start.4 = (bf16[12,72,256]{2,1,0:T(8,128)(2,1)}, bf16[12,72,256]{2,1,0:T(8,128)(2,1)S(1)}, u32[]{:S(2)}, u32[]{:S(2)}) collective-permute-start(bf16[12,72,256]{2,1,0:T(8,128)(2,1)} %get-tuple-element.16), channel_id=1, source_target_pairs={{0,30},{1,31},{2,0},{3,1},{4,2},{5,3},{6,4},{7,5},{8,6},{9,7},{10,... | collective-permute-start | bytes 1327112 | tf_op jit(solution)/shard_map/ppermute | solution.py:264
  26.3 13.3 %collective-permute-start.6 = (bf16[12,72,256]{2,1,0:T(8,128)(2,1)S(1)}, bf16[12,72,256]{2,1,0:T(8,128)(2,1)S(1)}, u32[]{:S(2)}, u32[]{:S(2)}) collective-permute-start(bf16[12,72,256]{2,1,0:T(8,128)(2,1)S(1)} %get-tuple-element.17.edge), channel_id=1, source_target_pairs={{0,31},{1,30},{30,1},{31,0}} | collective-permute-start | bytes 1327112 | tf_op jit(solution)/shard_map/ppermute | solution.py:266
  29.1 11.2 %collective-permute-start.5 = (bf16[12,72,256]{2,1,0:T(8,128)(2,1)S(1)}, bf16[12,72,256]{2,1,0:T(8,128)(2,1)S(1)}, u32[]{:S(2)}, u32[]{:S(2)}) collective-permute-start(bf16[12,72,256]{2,1,0:T(8,128)(2,1)S(1)} %get-tuple-element.17.edge), channel_id=1, source_target_pairs={{0,1},{1,0},{30,31},{31,30}} | collective-permute-start | bytes 1327112 | tf_op jit(solution)/shard_map/ppermute | solution.py:265
  59.8 2.4 %collective-permute-start.14 = (bf16[1160,256]{1,0:T(8,128)(2,1)}, bf16[1160,256]{1,0:T(8,128)(2,1)}, u32[]{:S(2)}, u32[]{:S(2)}) collective-permute-start(bf16[1160,256]{1,0:T(8,128)(2,1)} %pad_maximum_fusion), channel_id=1, source_target_pairs={{0,2},{1,3},{2,0},{3,1},{4,6},{5,7},{6,4},{7,5},{8,10},{9,11},{10,... | collective-permute-start | bytes 1781768 | tf_op jit(solution)/shard_map/ppermute | solution.py:500
  64.1 16.3 %copy-start.15 = (bf16[4,8,8]{2,1,0:T(8,128)(2,1)S(1)}, bf16[4,8,8]{2,1,0:T(8,128)(2,1)}, u32[]{:S(2)}) copy-start(bf16[4,8,8]{2,1,0:T(8,128)(2,1)} %constant.192.clone.flips) | copy-start | bytes 1540
  64.2 9.0 %collective-permute-start.15 = (bf16[296,256]{1,0:T(8,128)(2,1)S(1)}, bf16[296,256]{1,0:T(8,128)(2,1)S(1)}, u32[]{:S(2)}, u32[]{:S(2)}) collective-permute-start(bf16[296,256]{1,0:T(8,128)(2,1)S(1)} %get-tuple-element.57), channel_id=1, source_target_pairs={{0,1},{1,0},{2,3},{3,2},{4,5},{5,4},{6,7},{7,6},{8,9},{9,8},{10,11... | collective-permute-start | bytes 454664 | tf_op jit(solution)/shard_map/ppermute | solution.py:500
  65.8 10.0 %collective-permute-start.16 = (bf16[296,256]{1,0:T(8,128)(2,1)S(1)}, bf16[296,256]{1,0:T(8,128)(2,1)S(1)}, u32[]{:S(2)}, u32[]{:S(2)}) collective-permute-start(bf16[296,256]{1,0:T(8,128)(2,1)S(1)} %get-tuple-element.58), channel_id=1, source_target_pairs={{0,4},{1,5},{2,6},{3,7},{4,0},{5,1},{6,2},{7,3},{8,12},{9,13},{10,... | collective-permute-start | bytes 454664 | tf_op jit(solution)/shard_map/ppermute | solution.py:500
  65.8 10.0 %collective-permute-start.17 = (bf16[296,256]{1,0:T(8,128)(2,1)S(1)}, bf16[296,256]{1,0:T(8,128)(2,1)S(1)}, u32[]{:S(2)}, u32[]{:S(2)}) collective-permute-start(bf16[296,256]{1,0:T(8,128)(2,1)S(1)} %get-tuple-element.59), channel_id=1, source_target_pairs={{0,5},{1,4},{2,7},{3,6},{4,1},{5,0},{6,3},{7,2},{8,13},{9,12},{10,... | collective-permute-start | bytes 454664 | tf_op jit(solution)/shard_map/ppermute | solution.py:500
  67.8 11.5 %collective-permute-start.9 = (bf16[12,8,256]{2,1,0:T(8,128)(2,1)S(1)}, bf16[12,8,256]{2,1,0:T(8,128)(2,1)S(1)}, u32[]{:S(2)}, u32[]{:S(2)}) collective-permute-start(bf16[12,8,256]{2,1,0:T(8,128)(2,1)S(1)} %get-tuple-element.50), channel_id=1, source_target_pairs={{0,31},{1,30},{2,29},{3,28},{4,27},{5,26},{6,25},{7,24},{8,23},{9,... | collective-permute-start | bytes 147464 | tf_op jit(solution)/shard_map/ppermute | solution.py:249
  70.1 10.3 %collective-permute-start.8 = (bf16[12,8,256]{2,1,0:T(8,128)(2,1)S(1)}, bf16[12,8,256]{2,1,0:T(8,128)(2,1)S(1)}, u32[]{:S(2)}, u32[]{:S(2)}) collective-permute-start(bf16[12,8,256]{2,1,0:T(8,128)(2,1)S(1)} %get-tuple-element.50), channel_id=1, source_target_pairs={{0,30},{1,31},{2,28},{3,29},{4,26},{5,27},{6,24},{7,25},{8,22},{9,... | collective-permute-start | bytes 147464 | tf_op jit(solution)/shard_map/ppermute | solution.py:248
  73.2 7.2 %collective-permute-start.7 = (bf16[12,16,256]{2,1,0:T(8,128)(2,1)S(1)}, bf16[12,16,256]{2,1,0:T(8,128)(2,1)S(1)}, u32[]{:S(2)}, u32[]{:S(2)}) collective-permute-start(bf16[12,16,256]{2,1,0:T(8,128)(2,1)S(1)} %get-tuple-element.51.edges), channel_id=1, source_target_pairs={{0,1},{1,0},{2,3},{3,2},{4,5},{5,4},{6,7},{7,6},{8,9},{9,8},{10,11... | collective-permute-start | bytes 294920 | tf_op jit(solution)/shard_map/ppermute | solution.py:238
  75.9 11.9 %collective-permute-start.18 = (bf16[80,256]{1,0:T(8,128)(2,1)S(1)}, bf16[80,256]{1,0:T(8,128)(2,1)S(1)}, u32[]{:S(2)}, u32[]{:S(2)}) collective-permute-start(bf16[80,256]{1,0:T(8,128)(2,1)S(1)} %get-tuple-element.54), channel_id=1, source_target_pairs={{0,8},{1,9},{2,10},{3,11},{4,12},{5,13},{6,14},{7,15},{8,0},{9,1},... | collective-permute-start | bytes 122888 | tf_op jit(solution)/shard_map/ppermute | solution.py:500
  76.0 11.8 %collective-permute-start.19 = (bf16[80,256]{1,0:T(8,128)(2,1)S(1)}, bf16[80,256]{1,0:T(8,128)(2,1)S(1)}, u32[]{:S(2)}, u32[]{:S(2)}) collective-permute-start(bf16[80,256]{1,0:T(8,128)(2,1)S(1)} %get-tuple-element.55), channel_id=1, source_target_pairs={{0,16},{1,17},{2,18},{3,19},{4,20},{5,21},{6,22},{7,23},{8,24},{9,... | collective-permute-start | bytes 122888 | tf_op jit(solution)/shard_map/ppermute | solution.py:500
  79.3 8.5 %collective-permute-start.20 = (bf16[80,256]{1,0:T(8,128)(2,1)S(1)}, bf16[80,256]{1,0:T(8,128)(2,1)S(1)}, u32[]{:S(2)}, u32[]{:S(2)}) collective-permute-start(bf16[80,256]{1,0:T(8,128)(2,1)S(1)} %get-tuple-element.56), channel_id=1, source_target_pairs={{0,24},{1,25},{2,26},{3,27},{4,28},{5,29},{6,30},{7,31},{8,16},{9,... | collective-permute-start | bytes 122888 | tf_op jit(solution)/shard_map/ppermute | solution.py:500
  80.4 23.9 %copy-start.19 = (f32[12,4,32,256]{3,0,2,1:T(8,128)S(1)}, f32[12,4,32,256]{3,0,2,1:T(8,128)}, u32[]{:S(2)}) copy-start(f32[12,4,32,256]{3,0,2,1:T(8,128)} %copy-done.18) | copy-start | bytes 4718596
  83.4 17.4 %collective-permute-start.10 = (bf16[12,72,256]{2,1,0:T(8,128)(2,1)S(1)}, bf16[12,72,256]{2,1,0:T(8,128)(2,1)S(1)}, u32[]{:S(2)}, u32[]{:S(2)}) collective-permute-start(bf16[12,72,256]{2,1,0:T(8,128)(2,1)S(1)} %get-tuple-element.19), channel_id=1, source_target_pairs={{0,2},{1,3},{2,4},{3,5},{4,6},{5,7},{6,8},{7,9},{8,10},{9,11},{10,... | collective-permute-start | bytes 1327112 | tf_op jit(solution)/shard_map/ppermute | solution.py:263
  83.4 18.9 %collective-permute-start.11 = (bf16[12,72,256]{2,1,0:T(8,128)(2,1)S(1)}, bf16[12,72,256]{2,1,0:T(8,128)(2,1)S(1)}, u32[]{:S(2)}, u32[]{:S(2)}) collective-permute-start(bf16[12,72,256]{2,1,0:T(8,128)(2,1)S(1)} %get-tuple-element.20), channel_id=1, source_target_pairs={{0,30},{1,31},{2,0},{3,1},{4,2},{5,3},{6,4},{7,5},{8,6},{9,7},{10,... | collective-permute-start | bytes 1327112 | tf_op jit(solution)/shard_map/ppermute | solution.py:264
  87.9 8.0 %collective-permute-start.23 = (bf16[1,72,256]{2,1,0:T(8,128)(2,1)S(1)}, bf16[1,72,256]{2,1,0:T(8,128)(2,1)S(1)}, u32[]{:S(2)}, u32[]{:S(2)}) collective-permute-start(bf16[1,72,256]{2,1,0:T(8,128)(2,1)S(1)} %bitcast.209), channel_id=1, source_target_pairs={{0,24},{1,25},{2,26},{3,27},{4,28},{5,29},{6,30},{7,31},{8,16},{9,... | collective-permute-start | bytes 110600 | tf_op jit(solution)/shard_map/ppermute | solution.py:513
  88.9 8.9 %collective-permute-start.22 = (bf16[1,72,256]{2,1,0:T(8,128)(2,1)S(1)}, bf16[1,72,256]{2,1,0:T(8,128)(2,1)S(1)}, u32[]{:S(2)}, u32[]{:S(2)}) collective-permute-start(bf16[1,72,256]{2,1,0:T(8,128)(2,1)S(1)} %bitcast.210), channel_id=1, source_target_pairs={{0,16},{1,17},{2,18},{3,19},{4,20},{5,21},{6,22},{7,23},{8,24},{9,... | collective-permute-start | bytes 110600 | tf_op jit(solution)/shard_map/ppermute | solution.py:513
  88.9 11.6 %collective-permute-start.21 = (bf16[1,72,256]{2,1,0:T(8,128)(2,1)S(1)}, bf16[1,72,256]{2,1,0:T(8,128)(2,1)S(1)}, u32[]{:S(2)}, u32[]{:S(2)}) collective-permute-start(bf16[1,72,256]{2,1,0:T(8,128)(2,1)S(1)} %bitcast.211), channel_id=1, source_target_pairs={{0,8},{1,9},{2,10},{3,11},{4,12},{5,13},{6,14},{7,15},{8,0},{9,1},... | collective-permute-start | bytes 110600 | tf_op jit(solution)/shard_map/ppermute | solution.py:513
  95.9 13.4 %collective-permute-start.13 = (bf16[12,72,256]{2,1,0:T(8,128)(2,1)S(1)}, bf16[12,72,256]{2,1,0:T(8,128)(2,1)S(1)}, u32[]{:S(2)}, u32[]{:S(2)}) collective-permute-start(bf16[12,72,256]{2,1,0:T(8,128)(2,1)S(1)} %get-tuple-element.21.edge), channel_id=1, source_target_pairs={{0,31},{1,30},{30,1},{31,0}} | collective-permute-start | bytes 1327112 | tf_op jit(solution)/shard_map/ppermute | solution.py:266
  97.8 11.5 %collective-permute-start.12 = (bf16[12,72,256]{2,1,0:T(8,128)(2,1)S(1)}, bf16[12,72,256]{2,1,0:T(8,128)(2,1)S(1)}, u32[]{:S(2)}, u32[]{:S(2)}) collective-permute-start(bf16[12,72,256]{2,1,0:T(8,128)(2,1)S(1)} %get-tuple-element.21.edge), channel_id=1, source_target_pairs={{0,1},{1,0},{30,31},{31,30}} | collective-permute-start | bytes 1327112 | tf_op jit(solution)/shard_map/ppermute | solution.py:265
  100.7 23.8 %collective-permute-start.25 = (bf16[4,72,256]{2,1,0:T(8,128)(2,1)S(1)}, bf16[4,72,256]{2,1,0:T(8,128)(2,1)S(1)}, u32[]{:S(2)}, u32[]{:S(2)}) collective-permute-start(bf16[4,72,256]{2,1,0:T(8,128)(2,1)S(1)} %get-tuple-element.42), channel_id=1, source_target_pairs={{0,4},{1,5},{2,6},{3,7},{4,0},{5,1},{6,2},{7,3},{8,12},{9,13},{10,... | collective-permute-start | bytes 442376 | tf_op jit(solution)/shard_map/ppermute | solution.py:513
  100.8 23.7 %collective-permute-start.24 = (bf16[4,72,256]{2,1,0:T(8,128)(2,1)S(1)}, bf16[4,72,256]{2,1,0:T(8,128)(2,1)S(1)}, u32[]{:S(2)}, u32[]{:S(2)}) collective-permute-start(bf16[4,72,256]{2,1,0:T(8,128)(2,1)S(1)} %get-tuple-element.42), channel_id=1, source_target_pairs={{0,1},{1,0},{2,3},{3,2},{4,5},{5,4},{6,7},{7,6},{8,9},{9,8},{10,11... | collective-permute-start | bytes 442376 | tf_op jit(solution)/shard_map/ppermute | solution.py:513
  102.2 22.3 %collective-permute-start.26 = (bf16[4,72,256]{2,1,0:T(8,128)(2,1)S(1)}, bf16[4,72,256]{2,1,0:T(8,128)(2,1)S(1)}, u32[]{:S(2)}, u32[]{:S(2)}) collective-permute-start(bf16[4,72,256]{2,1,0:T(8,128)(2,1)S(1)} %get-tuple-element.42), channel_id=1, source_target_pairs={{0,5},{1,4},{2,7},{3,6},{4,1},{5,0},{6,3},{7,2},{8,13},{9,12},{10,... | collective-permute-start | bytes 442376 | tf_op jit(solution)/shard_map/ppermute | solution.py:513
  124.8 6.8 %collective-permute-start.27 = (bf16[16,72,256]{2,1,0:T(8,128)(2,1)S(1)}, bf16[16,72,256]{2,1,0:T(8,128)(2,1)S(1)}, u32[]{:S(2)}, u32[]{:S(2)}) collective-permute-start(bf16[16,72,256]{2,1,0:T(8,128)(2,1)S(1)} %get-tuple-element.32), channel_id=1, source_target_pairs={{0,2},{1,3},{2,0},{3,1},{4,6},{5,7},{6,4},{7,5},{8,10},{9,11},{10,... | collective-permute-start | bytes 1769480 | tf_op jit(solution)/shard_map/ppermute | solution.py:513
  (21 other events, 73.4 us)

commit v4 on v3

--- a/solution.py
+++ b/solution.py
@@ -15,7 +15,7 @@
 half_root = 0.7071067811865476
 density_scale = 0.3989422804014327
 axes = ("frow", "fcol")
-vmem_bytes = 48 * 1024 * 1024
+vmem_bytes = 12 * 1024 * 1024
 
 
 def shifted_pairs(row_step, col_step):
@@ -134,33 +134,34 @@
     at_left = col_place == 0
     at_right = col_place == lax.axis_size("fcol") - 1
 
-    @pl.loop(0, face_count)
-    def _(face):
-        @pl.when(jnp.logical_or(at_left, at_right))
-        def _():
+    @pl.when(jnp.logical_or(at_left, at_right))
+    def _():
+        @pl.loop(0, face_count)
+        def _(face):
             source, kind = seam_of(adjacency, face, jnp.where(at_left, 2, 3))
 
             @pl.when(kind == 0)
             def _():
                 both = beside[source]
-                seam[...] = jnp.where(at_left, both[half:], both[:half])
+                seam[face] = jnp.where(at_left, both[half:], both[:half])
 
             @pl.when(kind == 1)
             def _():
                 both = edges[source]
-                seam[...] = pick(flips[1], jnp.where(at_left, both[:half], both[half:]))
+                seam[face] = pick(flips[1], jnp.where(at_left, both[:half], both[half:]))
 
             @pl.when(kind == 2)
             def _():
-                seam[...] = pick(flips[2], far_cross[source])
+                seam[face] = pick(flips[2], far_cross[source])
 
             @pl.when(kind == 3)
             def _():
-                seam[...] = pick(flips[3], far_same[source])
-
+                seam[face] = pick(flips[3], far_same[source])
+
+    for face in range(face_count):
         both = beside[face]
-        left = jnp.where(at_left, seam[...], both[half:])
-        right = jnp.where(at_right, seam[...], both[:half])
+        left = jnp.where(at_left, seam[face], both[half:])
+        right = jnp.where(at_right, seam[face], both[:half])
         sides = jnp.concatenate([left, right], 0)
         side_out[face] = sides
         blank = jnp.zeros_like(left)
@@ -171,11 +172,10 @@
         lower = pick(tails[1], jnp.where(at_bottom, inner, sides))
         for d in range(2):
             rows = pl.ds(d * width, width)
-            top_out[face, rows] = field[face, d]
-            bottom_out[face, rows] = field[face, tile_rows - 2 + d]
-            edge_out[face, rows] = jnp.where(
-                at_top, field[face, d], field[face, tile_rows - 2 + d]
-            )
+            first, last = field[face, d], field[face, tile_rows - 2 + d]
+            top_out[face, rows] = first
+            bottom_out[face, rows] = last
+            edge_out[face, rows] = jnp.where(at_top, first, last)
         rows = pl.ds(2 * width, 8)
         top_out[face, rows] = upper
         bottom_out[face, rows] = lower
@@ -187,29 +187,37 @@
     strip = 2 * width + 8
     beside, above, below, _ = stack_places(tile_rows, width)
     row_place = lax.axis_index("frow")
-    stack[pl.ds(0, beside)] = field[face].reshape(beside, channels)
-    stack[pl.ds(beside, 4 * tile_rows)] = sides[face]
+    stack[face, pl.ds(0, beside)] = field[face].reshape(beside, channels)
+    stack[face, pl.ds(beside, 4 * tile_rows)] = sides[face]
     for side, place, near in ((0, above, up), (1, below, down)):
         at_edge = row_place == side * (lax.axis_size("frow") - 1)
         rows = pl.ds(place, strip)
 
         @pl.when(jnp.logical_not(at_edge))
         def _():
-            stack[rows] = near[face]
+            stack[face, rows] = near[face]
 
         source, kind = seam_of(adjacency, face, side)
         for choice, strips in enumerate((near, edge, far_cross, far_same)):
 
             @pl.when(jnp.logical_and(at_edge, kind == choice))
             def _():
-                stack[rows] = pick(flips[choice], strips[source])
+                stack[face, rows] = pick(flips[choice], strips[source])
+
+
+def write_padded(picks, stack, padded):
+    face_count, rows, breadth, channels = padded.shape
+    step = picks.shape[0] // rows
+    for face in range(face_count):
+        out = pick(picks[...], stack[face])
+        for q in range(rows):
+            padded[face, q] = out[q * step : q * step + breadth]
 
 
 def pad_kernel(
     adjacency, field, sides, up, down, edge, far_same, far_cross, flips, picks, padded, stack
 ):
     face_count, tile_rows, width, channels = field.shape
-    breadth = picks.shape[0] // (tile_rows + 4)
     stack[...] = jnp.zeros_like(stack)
 
     @pl.loop(0, face_count)
@@ -217,9 +225,8 @@
         load_stack(
             adjacency, face, field, sides, up, down, edge, far_same, far_cross, flips, stack
         )
-        out = pick(picks[...], stack[...])
-        for q in range(tile_rows + 4):
-            padded[face, q] = out[q * breadth : q * breadth + width + 4]
+
+    write_padded(picks, stack, padded)
 
 
 def whole(count):
@@ -253,7 +260,7 @@
         out_shape=(jax.ShapeDtypeStruct(edges.shape, field.dtype), strip, strip, strip),
         in_specs=whole(7),
         out_specs=[pl.BlockSpec(memory_space=pltpu.VMEM)] * 4,
-        scratch_shapes=[pltpu.VMEM((2 * tile_rows, channels), field.dtype)],
+        scratch_shapes=[pltpu.VMEM((face_count, 2 * tile_rows, channels), field.dtype)],
         compiler_params=pltpu.CompilerParams(vmem_limit_bytes=vmem_bytes),
         cost_estimate=pl.CostEstimate(flops=1000, bytes_accessed=3000000, transcendentals=0),
     )(
@@ -277,7 +284,7 @@
         out_shape=jax.ShapeDtypeStruct(padded, field.dtype),
         in_specs=whole(9),
         out_specs=pl.BlockSpec(memory_space=pltpu.VMEM),
-        scratch_shapes=[pltpu.VMEM((size, channels), field.dtype)],
+        scratch_shapes=[pltpu.VMEM((face_count, size, channels), field.dtype)],
         compiler_params=pltpu.CompilerParams(vmem_limit_bytes=vmem_bytes),
         cost_estimate=pl.CostEstimate(flops=1000, bytes_accessed=5000000, transcendentals=0),
     )(adjacency, *strips, row_flips(width), pad_picks(tile_rows, width))
@@ -314,29 +321,26 @@
     return jnp.asarray(table, jnp.bfloat16)
 
 
-def tap_dot(value, tap):
-    return lax.dot_general(value, tap, (((1,), (1,)), ((), ())), preferred_element_type=jnp.float32)
-
-
 def return_kernel(
     adjacency, field, sides, up, down, edge, far_same, far_cross, flips, picks, row_picks,
-    col_picks, kernel, padded, extra, stack, kept_picks, col_terms, col_sum,
+    col_picks, rotated, padded, extra, stack, kept_picks, row_terms, col_terms, col_sum,
 ):
     face_count, tile_rows, width, channels = field.shape
     breadth = picks.shape[0] // (tile_rows + 4)
     half = 2 * tile_rows
     slot = round_up(half, 16)
+    row_slot = 2 * width
     _, above, below, _ = stack_places(tile_rows, width)
-    strip = row_picks.shape[2]
+    strip = row_picks.shape[1]
     row_place, col_place = lax.axis_index("frow"), lax.axis_index("fcol")
     at_top = row_place == 0
     at_bottom = row_place == lax.axis_size("frow") - 1
     at_left = col_place == 0
     at_right = col_place == lax.axis_size("fcol") - 1
+    on_row_edge = jnp.logical_or(at_top, at_bottom)
     on_col_edge = jnp.logical_or(at_left, at_right)
     stack[...] = jnp.zeros_like(stack)
     extra[...] = jnp.zeros_like(extra)
-    col_terms[...] = jnp.zeros_like(col_terms)
     cell = lax.broadcasted_iota(jnp.int32, (breadth, picks.shape[1]), 0)
     for q in range(tile_rows + 4):
         rows = pl.ds(q * breadth, breadth)
@@ -355,62 +359,84 @@
         load_stack(
             adjacency, face, field, sides, up, down, edge, far_same, far_cross, flips, stack
         )
-        out = pick(kept_picks[...], stack[...])
-        for q in range(tile_rows + 4):
-            padded[face, q] = out[q * breadth : q * breadth + width + 4]
-        for side, place, at_edge in ((0, above, at_top), (1, below, at_bottom)):
-
-            @pl.when(at_edge)
-            def _():
-                base = (face * 4 + side) * 3
-                row_tap = 2 * adjacency[base + 1]
-                turned = adjacency[base + 2]
-                total = jnp.zeros((2 * width, channels), jnp.float32)
-                for shift in range(3):
-                    value = pick(row_picks[shift], stack[pl.ds(place, strip)])
-                    col_tap = jnp.where(turned == 1, shift, 2 - shift)
-                    total += tap_dot(value, kernel[row_tap, col_tap])
-                for d in range(2):
-                    extra[face, side * (tile_rows - 2) + d] = total[d * width : (d + 1) * width]
-
-        @pl.when(on_col_edge)
-        def _():
-            base = (face * 4 + jnp.where(at_left, 2, 3)) * 3
-            variant = 2 * adjacency[base + 2] + adjacency[base + 1] - 2
-            value = jnp.dot(
-                col_picks[jnp.where(at_left, 0, 1)],
-                stack[...],
-                preferred_element_type=jnp.float32,
-            )
-            for shift in range(3):
-                rows = pl.ds(pl.multiple_of(face * slot, 16), half)
-                part = value[shift * half : (shift + 1) * half]
-                col_terms[variant, shift, rows] = part.astype(jnp.bfloat16)
+
+    write_padded(kept_picks, stack, padded)
 
     @pl.when(on_col_edge)
     def _():
-        total = jnp.zeros(col_sum.shape, jnp.float32)
-        for variant in range(4):
-            for shift in range(3):
-                row_tap = shift if variant >= 2 else 2 - shift
-                total += tap_dot(col_terms[variant, shift], kernel[row_tap, 2 * (variant % 2)])
-        col_sum[...] = total
+        col_terms[...] = jnp.zeros_like(col_terms)
+        table = col_picks[jnp.where(at_left, 0, 1)]
 
         @pl.loop(0, face_count)
         def _(face):
-            value = col_sum[pl.ds(pl.multiple_of(face * slot, 16), half)]
-            for first, at_edge in ((0, at_left), (width - 2, at_right)):
-
-                @pl.when(at_edge)
-                def _():
-                    for y in range(tile_rows):
-                        cells = pl.ds(first, 2)
-                        extra[face, y, cells] = (
-                            extra[face, y, cells] + value[2 * y : 2 * y + 2]
-                        )
-
-
-def return_field(field, adjacency, kernel):
+            base = (face * 4 + jnp.where(at_left, 2, 3)) * 3
+            turned = adjacency[base + 2]
+            value = jnp.dot(table, stack[face], preferred_element_type=jnp.float32)
+            rows = pl.ds(pl.multiple_of(face * slot, 16), half)
+            for shift in range(3):
+                part = value[shift * half : (shift + 1) * half].astype(jnp.bfloat16)
+                tap = jnp.where(turned == 1, 2 - shift, shift)
+                col_terms[adjacency[base + 1] - 2, tap, rows] = part
+
+        total = jnp.zeros(col_sum.shape, jnp.float32)
+        for side in range(2):
+            for tap in range(3):
+                total += jnp.dot(
+                    col_terms[side, tap],
+                    rotated[tap, 2 - 2 * side],
+                    preferred_element_type=jnp.float32,
+                )
+        col_sum[...] = total
+
+    @pl.when(on_row_edge)
+    def _():
+        row_terms[...] = jnp.zeros_like(row_terms)
+
+        @pl.loop(0, face_count)
+        def _(face):
+            base = (face * 4 + jnp.where(at_top, 0, 1)) * 3
+            turned = adjacency[base + 2]
+            place = pl.multiple_of(jnp.where(at_top, above, below), 16)
+            value = pick(row_picks[...], stack[face, pl.ds(place, strip)])
+            rows = pl.ds(pl.multiple_of(face * row_slot, 16), row_slot)
+            for shift in range(3):
+                part = value[shift * row_slot : (shift + 1) * row_slot]
+                tap = jnp.where(turned == 1, 2 - shift, shift)
+                row_terms[adjacency[base + 1], tap, rows] = part
+
+        first = jnp.where(at_top, 0, tile_rows - 2)
+
+        group = math.gcd(face_count, 4)
+
+        @pl.loop(0, face_count // group)
+        def _(part):
+            size = group * row_slot
+            rows = pl.ds(pl.multiple_of(part * size, 16), size)
+            total = jnp.zeros((size, channels), jnp.float32)
+            for side in range(2):
+                for tap in range(3):
+                    total += jnp.dot(
+                        row_terms[side, tap, rows],
+                        rotated[2 - 2 * side, tap],
+                        preferred_element_type=jnp.float32,
+                    )
+            for face in range(group):
+                for d in range(2):
+                    start = face * row_slot + d * width
+                    extra[part * group + face, first + d] = total[start : start + width]
+
+    for edge_col, at_edge in ((0, at_left), (width - 2, at_right)):
+
+        @pl.when(at_edge)
+        def _():
+            cells = pl.ds(edge_col, 2)
+            for face in range(face_count):
+                value = col_sum[pl.ds(face * slot, half)]
+                for y in range(tile_rows):
+                    extra[face, y, cells] = extra[face, y, cells] + value[2 * y : 2 * y + 2]
+
+
+def return_field(field, adjacency, rotated):
     face_count, tile_rows, width, channels = field.shape
     strips = gather_strips(field, adjacency)
     padded = (face_count, tile_rows + 4, width + 4, channels)
@@ -426,16 +452,18 @@
         in_specs=whole(12),
         out_specs=[pl.BlockSpec(memory_space=pltpu.VMEM)] * 2,
         scratch_shapes=[
-            pltpu.VMEM((size, channels), field.dtype),
+            pltpu.VMEM((face_count, size, channels), field.dtype),
             pltpu.VMEM(picks.shape, field.dtype),
-            pltpu.VMEM((4, 3, cells, channels), field.dtype),
+            pltpu.VMEM((2, 3, face_count * 2 * width, channels), field.dtype),
+            pltpu.VMEM((2, 3, cells, channels), field.dtype),
             pltpu.VMEM((cells, channels), jnp.float32),
         ],
         compiler_params=pltpu.CompilerParams(vmem_limit_bytes=vmem_bytes),
         cost_estimate=pl.CostEstimate(flops=1000, bytes_accessed=8000000, transcendentals=0),
     )(
-        adjacency, *strips, row_flips(width), picks, seam_row_picks(width),
-        seam_col_picks(tile_rows, width), kernel,
+        adjacency, *strips, row_flips(width), picks,
+        seam_row_picks(width).reshape(6 * width, -1),
+        seam_col_picks(tile_rows, width), rotated,
     )
 
 
@@ -466,9 +494,9 @@
 
 
 def stage_place(index, stage):
-    place = (index // stage[0]) % 2
+    place = (index >> (stage[0].bit_length() - 1)) & 1
     if len(stage) == 2:
-        place = place + 2 * ((index // stage[1]) % 2)
+        place = place + 2 * ((index >> (stage[1].bit_length() - 1)) & 1)
     return place
 
 
@@ -494,7 +522,7 @@
         rows = part.shape[1]
         sums, vectors = [], []
         for order, offset in enumerate(offsets):
-            piece = lax.dynamic_index_in_dim(part, place ^ order, 0, False)
+            piece = lax.dynamic_slice_in_dim(part, place ^ order, 1, 0)[0]
             if offset:
                 packed = jnp.concatenate([piece, vector], 0)
                 packed = lax.ppermute(packed, axes, [(i, i ^ offset) for i in range(count)])
@@ -564,8 +592,8 @@
     )
     kernel_grad = kernel_total * scale
     bias_grad = bias_total * scale
-    padded_grad, extra = return_field(pre_grad, table, kernel)
     rotated = jnp.transpose(jnp.flip(kernel, (0, 1)), (0, 1, 3, 2))
+    padded_grad, extra = return_field(pre_grad, table, rotated)
     input_gradient = (
         lax.conv_general_dilated(
             padded_grad,

time: 135 us -> 124 us (0.919)
  Pallas kernels: 27.8 us -> 18.7 us
  local copies, waits for them, and re-layouts: 12.9 us -> 7.7 us
  waiting for transfers between devices: 23.2 us -> 27.8 us
  other arithmetic: 10.9 us -> 9.17 us
    ppermute x2, waiting for transfers between devices: 0.01 us -> 5.98 us  [gather_strips(): row_same = lax.ppermute(edge_strip, axes, mirror_pairs(True, False, True))]
    pallas_call x1, Pallas kernels: 15.2 us -> 9.79 us  [return_field(): pl.pallas_call(return_kernel, out_shape=(jax.ShapeDtypeStruct(padded, fie...]
    unnamed x53 -> x40, local copies, waits for them, and re-layouts: 10.7 us -> 5.96 us
    pallas_call x2, Pallas kernels: 6.83 us -> 4.59 us  [gather_strips(): pl.pallas_call(col_kernel, out_shape=(jax.ShapeDtypeStruct(edges.shape, f...]
    ppermute x2, waiting for transfers between devices: 10 us -> 8.08 us  [gather_strips(): row_cross = lax.ppermute(edge_strip, axes, mirror_pairs(True, True, True))]
    ppermute x7, waiting for transfers between devices: 3.57 us -> 1.72 us  [reduce_everywhere(): lax.ppermute(part, axes, [(i, i ^ offset) for i in range(count)])]
    ppermute x2, waiting for transfers between devices: 2.59 us -> 4.32 us  [gather_strips(): far_cross = lax.ppermute(edge, axes, mirror_pairs(False, True, True))]
    pallas_call x1, Pallas kernels: 5.75 us -> 4.31 us  [pad_field(): pl.pallas_call(pad_kernel, out_shape=jax.ShapeDtypeStruct(padded, field.d...]
  transfers between devices with their start and end apart: 28 -> 28, of which waited for: 8 -> 10; matrix products, arithmetic and copies ran while one was open for 7% -> 8% of each run, Pallas kernels for 14% -> 10%
where the time goes in v4:
time: 124 us; the launch traced here: 123 us
  starting transfers between devices  48.4 us (39%)
  waiting for transfers between devices  27.8 us (22%)
  Pallas kernels  18.7 us (15%)
  matrix products  9.88 us (8%)
  other arithmetic  9.17 us (7%)
  local copies, waits for them, and re-layouts  7.7 us (6%)
  between operations  1.27 us (1%)
    pallas_call x1, Pallas kernels, return_field(): pl.pallas_call(return_kernel, out_shape=(jax.ShapeDtypeStruct(padded, fie...  9.79 us
    ppermute x2, waiting for transfers between devices, gather_strips(): row_cross = lax.ppermute(edge_strip, axes, mirror_pairs(True, True, True))  8.08 us
    ppermute x7, starting transfers between devices, reduce_everywhere(): lax.ppermute(part, axes, [(i, i ^ offset) for i in range(count)])  8.05 us
    ppermute x7, starting transfers between devices, reduce_everywhere(): packed = lax.ppermute(packed, axes, [(i, i ^ offset) for i in range(count)])  7.98 us
    ppermute x2, starting transfers between devices, gather_strips(): down = lax.ppermute(top, axes, shifted_pairs(-1, 0))  7.92 us
    ppermute x2, waiting for transfers between devices, gather_strips(): row_same = lax.ppermute(edge_strip, axes, mirror_pairs(True, False, True))  5.98 us
    unnamed x40, local copies, waits for them, and re-layouts  5.96 us
    ppermute x2, starting transfers between devices, gather_strips(): far_cross = lax.ppermute(edge, axes, mirror_pairs(False, True, True))  5.64 us
  transfers between devices with their start and end apart: 28, of which 10 were waited for; matrix products, arithmetic and copies ran while one was open for 8% of the time, Pallas kernels for 10%

profile of v4, /device:TPU:0, one launch (start us, length us, event | category | flops | bytes accessed | tf_op | source)
XLA Modules:
  0.0 123.0 jit_solution(2786701049162164102)
XLA Ops:
  1.9 3.0 %collective-permute-start = (bf16[12,16,256]{2,1,0:T(8,128)(2,1)S(1)}, bf16[12,16,256]{2,1,0:T(8,128)(2,1)S(1)}, u32[]{:S(2)}, u32[]{:S(2)}) collective-permute-start(bf16[12,16,256]{2,1,0:T(8,128)(2,1)S(1)} %get-tuple-element.53.edges), channel_id=1, source_target_pairs={{0,1},{1,0},{2,3},{3,2},{4,5},{5,4},{6,7},{7,6},{8,9},{9,8},{10,11... | collective-permute-start | bytes 294920 | tf_op jit(solution)/shard_map/ppermute | solution.py:245
  4.9 3.7 %collective-permute-start.1 = (bf16[12,8,256]{2,1,0:T(8,128)(2,1)S(1)}, bf16[12,8,256]{2,1,0:T(8,128)(2,1)S(1)}, u32[]{:S(2)}, u32[]{:S(2)}) collective-permute-start(bf16[12,8,256]{2,1,0:T(8,128)(2,1)S(1)} %get-tuple-element.52), channel_id=1, source_target_pairs={{0,30},{1,31},{2,28},{3,29},{4,26},{5,27},{6,24},{7,25},{8,22},{9,... | collective-permute-start | bytes 147464 | tf_op jit(solution)/shard_map/ppermute | solution.py:255
  9.8 1.6 %collective-permute-done.1.far_same = bf16[12,8,256]{2,1,0:T(8,128)(2,1)S(1)} collective-permute-done((bf16[12,8,256]{2,1,0:T(8,128)(2,1)S(1)}, bf16[12,8,256]{2,1,0:T(8,128)(2,1)S(1)}, u32[]{:S(2)}, u32[]{:S(2)}) %collective-permute-start.1) | collective-permute-done | bytes 49184 | tf_op jit(solution)/shard_map/ppermute | solution.py:255
  11.4 4.3 %collective-permute-done.2.far_cross = bf16[12,8,256]{2,1,0:T(8,128)(2,1)S(1)} collective-permute-done((bf16[12,8,256]{2,1,0:T(8,128)(2,1)S(1)}, bf16[12,8,256]{2,1,0:T(8,128)(2,1)S(1)}, u32[]{:S(2)}, u32[]{:S(2)}) %collective-permute-start.2) | collective-permute-done | bytes 49184 | tf_op jit(solution)/shard_map/ppermute | solution.py:256
  18.3 2.7 %shard_map.174 = (bf16[12,16,256]{2,1,0:T(8,128)(2,1)S(1)}, bf16[12,72,256]{2,1,0:T(8,128)(2,1)}, bf16[12,72,256]{2,1,0:T(8,128)(2,1)}, bf16[12,72,256]{2,1,0:T(8,128)(2,1)S(1)}) custom-call(s32[144]{0:T(256)S(1)} %reshape.44.adjacency, bf16[12,4,32,256]{3,2,1,0:T(8,128)(2,1)S(1)} %copy-done, bf16[12,16,256]{2,1,0:T(8,128)(2,1)S(1)} %get-tuple-element.53.edges, ...), custom_call_target="tpu_custom_call" | custom-call | flops 1000 | bytes 3000000 | tf_op jit(solution)/shard_map/pallas_call | solution.py:258
  21.9 3.5 %collective-permute-start.4 = (bf16[12,72,256]{2,1,0:T(8,128)(2,1)}, bf16[12,72,256]{2,1,0:T(8,128)(2,1)S(1)}, u32[]{:S(2)}, u32[]{:S(2)}) collective-permute-start(bf16[12,72,256]{2,1,0:T(8,128)(2,1)} %get-tuple-element.16), channel_id=1, source_target_pairs={{0,30},{1,31},{2,0},{3,1},{4,2},{5,3},{6,4},{7,5},{8,6},{9,7},{10,... | collective-permute-start | bytes 1327112 | tf_op jit(solution)/shard_map/ppermute | solution.py:271
  25.4 2.4 %collective-permute-start.5 = (bf16[12,72,256]{2,1,0:T(8,128)(2,1)S(1)}, bf16[12,72,256]{2,1,0:T(8,128)(2,1)S(1)}, u32[]{:S(2)}, u32[]{:S(2)}) collective-permute-start(bf16[12,72,256]{2,1,0:T(8,128)(2,1)S(1)} %get-tuple-element.17.edge), channel_id=1, source_target_pairs={{0,1},{1,0},{30,31},{31,30}} | collective-permute-start | bytes 1327112 | tf_op jit(solution)/shard_map/ppermute | solution.py:272
  27.8 2.6 %collective-permute-start.6 = (bf16[12,72,256]{2,1,0:T(8,128)(2,1)S(1)}, bf16[12,72,256]{2,1,0:T(8,128)(2,1)S(1)}, u32[]{:S(2)}, u32[]{:S(2)}) collective-permute-start(bf16[12,72,256]{2,1,0:T(8,128)(2,1)S(1)} %get-tuple-element.17.edge), channel_id=1, source_target_pairs={{0,31},{1,30},{30,1},{31,0}} | collective-permute-start | bytes 1327112 | tf_op jit(solution)/shard_map/ppermute | solution.py:273
  31.7 3.9 %collective-permute-done.5.far_same = bf16[12,72,256]{2,1,0:T(8,128)(2,1)S(1)} collective-permute-done((bf16[12,72,256]{2,1,0:T(8,128)(2,1)S(1)}, bf16[12,72,256]{2,1,0:T(8,128)(2,1)S(1)}, u32[]{:S(2)}, u32[]{:S(2)}) %collective-permute-start.5) | collective-permute-done | bytes 442400 | tf_op jit(solution)/shard_map/ppermute | solution.py:272
  35.6 5.4 %collective-permute-done.6.far_cross = bf16[12,72,256]{2,1,0:T(8,128)(2,1)S(1)} collective-permute-done((bf16[12,72,256]{2,1,0:T(8,128)(2,1)S(1)}, bf16[12,72,256]{2,1,0:T(8,128)(2,1)S(1)}, u32[]{:S(2)}, u32[]{:S(2)}) %collective-permute-start.6) | collective-permute-done | bytes 442400 | tf_op jit(solution)/shard_map/ppermute | solution.py:273
  41.0 4.3 %shard_map.175 = bf16[12,8,36,256]{3,2,1,0:T(8,128)(2,1)S(1)} custom-call(s32[144]{0:T(256)S(1)} %reshape.44.adjacency, bf16[12,4,32,256]{3,2,1,0:T(8,128)(2,1)S(1)} %copy-done.1, bf16[12,16,256]{2,1,0:T(8,128)(2,1)S(1)} %get-tuple-element.14.sides, bf16[12,72,256]{2,1,0:T(8,128)(2,1)S(1)} %collective-permute-done.3.up, ...), custom_call_target="tpu_custom_call" | custom-call | flops 1000 | bytes 5000000 | tf_op jit(solution)/shard_map/pallas_call | solution.py:282
  45.4 3.0 %fusion.2 = f32[12,4,32,256]{3,0,2,1:T(8,128)S(1)} fusion(bf16[3,3,256,256]{3,2,1,0:T(8,128)(2,1)S(1)} %copy-done.13, bf16[12,8,36,256]{3,2,1,0:T(8,128)(2,1)S(1)} %shard_map.175), kind=kOutput, calls=%fused_computation.3 | convolution fusion | flops 1811939328 | bytes 4521984 | tf_op jit(solution)/shard_map/conv_general_dilated | solution.py:561
  54.8 2.1 %collective-permute-done.14 = bf16[1160,256]{1,0:T(8,128)(2,1)S(1)} collective-permute-done((bf16[1160,256]{1,0:T(8,128)(2,1)}, bf16[1160,256]{1,0:T(8,128)(2,1)S(1)}, u32[]{:S(2)}, u32[]{:S(2)}) %collective-permute-start.14) | collective-permute-done | bytes 593952 | tf_op jit(solution)/shard_map/ppermute | solution.py:528
  57.2 3.0 %collective-permute-start.16 = (bf16[296,256]{1,0:T(8,128)(2,1)S(1)}, bf16[296,256]{1,0:T(8,128)(2,1)S(1)}, u32[]{:S(2)}, u32[]{:S(2)}) collective-permute-start(bf16[296,256]{1,0:T(8,128)(2,1)S(1)} %get-tuple-element.58), channel_id=1, source_target_pairs={{0,4},{1,5},{2,6},{3,7},{4,0},{5,1},{6,2},{7,3},{8,12},{9,13},{10,... | collective-permute-start | bytes 454664 | tf_op jit(solution)/shard_map/ppermute | solution.py:528
  60.8 5.4 %collective-permute-start.9 = (bf16[12,8,256]{2,1,0:T(8,128)(2,1)S(1)}, bf16[12,8,256]{2,1,0:T(8,128)(2,1)S(1)}, u32[]{:S(2)}, u32[]{:S(2)}) collective-permute-start(bf16[12,8,256]{2,1,0:T(8,128)(2,1)S(1)} %get-tuple-element.50), channel_id=1, source_target_pairs={{0,31},{1,30},{2,29},{3,28},{4,27},{5,26},{6,25},{7,24},{8,23},{9,... | collective-permute-start | bytes 147464 | tf_op jit(solution)/shard_map/ppermute | solution.py:256
  66.7 2.7 %collective-permute-done.16 = bf16[296,256]{1,0:T(8,128)(2,1)S(1)} collective-permute-done((bf16[296,256]{1,0:T(8,128)(2,1)S(1)}, bf16[296,256]{1,0:T(8,128)(2,1)S(1)}, u32[]{:S(2)}, u32[]{:S(2)}) %collective-permute-start.16) | collective-permute-done | bytes 151584 | tf_op jit(solution)/shard_map/ppermute | solution.py:528
  69.8 4.3 %collective-permute-start.18 = (bf16[80,256]{1,0:T(8,128)(2,1)S(1)}, bf16[80,256]{1,0:T(8,128)(2,1)S(1)}, u32[]{:S(2)}, u32[]{:S(2)}) collective-permute-start(bf16[80,256]{1,0:T(8,128)(2,1)S(1)} %get-tuple-element.54), channel_id=1, source_target_pairs={{0,8},{1,9},{2,10},{3,11},{4,12},{5,13},{6,14},{7,15},{8,0},{9,1},... | collective-permute-start | bytes 122888 | tf_op jit(solution)/shard_map/ppermute | solution.py:528
  74.1 1.5 %copy.27 = bf16[3,3,256,256]{2,3,1,0:T(8,128)(2,1)} copy(bf16[3,3,256,256]{3,2,1,0:T(8,128)(2,1)S(1)} %copy-done.14) | data formatting | bytes 2359296 | tf_op args[1]
  75.6 1.9 %shard_map.176 = (bf16[12,16,256]{2,1,0:T(8,128)(2,1)S(1)}, bf16[12,72,256]{2,1,0:T(8,128)(2,1)S(1)}, bf16[12,72,256]{2,1,0:T(8,128)(2,1)S(1)}, bf16[12,72,256]{2,1,0:T(8,128)(2,1)S(1)}) custom-call(s32[144]{0:T(256)S(1)} %reshape.44.adjacency, bf16[12,4,32,256]{3,2,1,0:T(8,128)(2,1)S(1)} %get-tuple-element.25.field, ...), custom_call_target="tpu_custom_call" | custom-call | flops 1000 | bytes 3000000 | tf_op jit(solution)/shard_map/pallas_call | solution.py:258
  77.6 4.4 %collective-permute-start.11 = (bf16[12,72,256]{2,1,0:T(8,128)(2,1)S(1)}, bf16[12,72,256]{2,1,0:T(8,128)(2,1)S(1)}, u32[]{:S(2)}, u32[]{:S(2)}) collective-permute-start(bf16[12,72,256]{2,1,0:T(8,128)(2,1)S(1)} %get-tuple-element.20), channel_id=1, source_target_pairs={{0,30},{1,31},{2,0},{3,1},{4,2},{5,3},{6,4},{7,5},{8,6},{9,7},{10,... | collective-permute-start | bytes 1327112 | tf_op jit(solution)/shard_map/ppermute | solution.py:271
  82.3 4.3 %collective-permute-start.21 = (bf16[1,72,256]{2,1,0:T(8,128)(2,1)S(1)}, bf16[1,72,256]{2,1,0:T(8,128)(2,1)S(1)}, u32[]{:S(2)}, u32[]{:S(2)}) collective-permute-start(bf16[1,72,256]{2,1,0:T(8,128)(2,1)S(1)} %bitcast.213), channel_id=1, source_target_pairs={{0,8},{1,9},{2,10},{3,11},{4,12},{5,13},{6,14},{7,15},{8,0},{9,1},... | collective-permute-start | bytes 110600 | tf_op jit(solution)/shard_map/ppermute | solution.py:541
  86.7 1.7 %collective-permute-done.23 = bf16[1,72,256]{2,1,0:T(8,128)(2,1)S(1)} collective-permute-done((bf16[1,72,256]{2,1,0:T(8,128)(2,1)S(1)}, bf16[1,72,256]{2,1,0:T(8,128)(2,1)S(1)}, u32[]{:S(2)}, u32[]{:S(2)}) %collective-permute-start.23) | collective-permute-done | bytes 36896 | tf_op jit(solution)/shard_map/ppermute | solution.py:541
  88.4 2.5 %collective-permute-start.12 = (bf16[12,72,256]{2,1,0:T(8,128)(2,1)S(1)}, bf16[12,72,256]{2,1,0:T(8,128)(2,1)S(1)}, u32[]{:S(2)}, u32[]{:S(2)}) collective-permute-start(bf16[12,72,256]{2,1,0:T(8,128)(2,1)S(1)} %get-tuple-element.21.edge), channel_id=1, source_target_pairs={{0,1},{1,0},{30,31},{31,30}} | collective-permute-start | bytes 1327112 | tf_op jit(solution)/shard_map/ppermute | solution.py:272
  90.9 3.0 %collective-permute-start.13 = (bf16[12,72,256]{2,1,0:T(8,128)(2,1)S(1)}, bf16[12,72,256]{2,1,0:T(8,128)(2,1)S(1)}, u32[]{:S(2)}, u32[]{:S(2)}) collective-permute-start(bf16[12,72,256]{2,1,0:T(8,128)(2,1)S(1)} %get-tuple-element.21.edge), channel_id=1, source_target_pairs={{0,31},{1,30},{30,1},{31,0}} | collective-permute-start | bytes 1327112 | tf_op jit(solution)/shard_map/ppermute | solution.py:273
  94.2 2.1 %collective-permute-start.25 = (bf16[4,72,256]{2,1,0:T(8,128)(2,1)S(1)}, bf16[4,72,256]{2,1,0:T(8,128)(2,1)S(1)}, u32[]{:S(2)}, u32[]{:S(2)}) collective-permute-start(bf16[4,72,256]{2,1,0:T(8,128)(2,1)S(1)} %get-tuple-element.42), channel_id=1, source_target_pairs={{0,4},{1,5},{2,6},{3,7},{4,0},{5,1},{6,2},{7,3},{8,12},{9,13},{10,... | collective-permute-start | bytes 442376 | tf_op jit(solution)/shard_map/ppermute | solution.py:541
  97.6 2.0 %multiply_convert_fusion = bf16[12,4,32,256]{3,2,1,0:T(8,128)(2,1)} fusion(f32[256]{0:T(256)S(1)} %copy-done.17, f32[12,4,32,256]{3,0,2,1:T(8,128)S(1)} %copy-done.11), kind=kLoop, calls=%fused_computation.15 | loop fusion | flops 2359296 | bytes 2360320 | tf_op jit(solution)/shard_map/convert_element_type | solution.py:572
  99.6 2.1 %collective-permute-done.12.far_same = bf16[12,72,256]{2,1,0:T(8,128)(2,1)S(1)} collective-permute-done((bf16[12,72,256]{2,1,0:T(8,128)(2,1)S(1)}, bf16[12,72,256]{2,1,0:T(8,128)(2,1)S(1)}, u32[]{:S(2)}, u32[]{:S(2)}) %collective-permute-start.12) | collective-permute-done | bytes 442400 | tf_op jit(solution)/shard_map/ppermute | solution.py:272
  101.7 2.6 %collective-permute-done.13.far_cross = bf16[12,72,256]{2,1,0:T(8,128)(2,1)S(1)} collective-permute-done((bf16[12,72,256]{2,1,0:T(8,128)(2,1)S(1)}, bf16[12,72,256]{2,1,0:T(8,128)(2,1)S(1)}, u32[]{:S(2)}, u32[]{:S(2)}) %collective-permute-start.13) | collective-permute-done | bytes 442400 | tf_op jit(solution)/shard_map/ppermute | solution.py:273
  104.4 9.8 %shard_map.177 = (bf16[12,8,36,256]{3,2,1,0:T(8,128)(2,1)S(1)}, f32[12,4,32,256]{3,2,1,0:T(8,128)S(1)}) custom-call(s32[144]{0:T(256)S(1)} %reshape.44.adjacency, bf16[12,4,32,256]{3,2,1,0:T(8,128)(2,1)S(1)} %get-tuple-element.25.field, bf16[12,16,256]{2,1,0:T(8,128)(2,1)S(1)} %get-tuple-element.18.sides, ...), custom_call_target="tpu_custom_call" | custom-call | flops 1000 | bytes 8000000 | tf_op jit(solution)/shard_map/pallas_call | solution.py:446
  115.6 3.0 %fusion = f32[12,4,32,256]{3,0,2,1:T(8,128)S(1)} fusion(bf16[3,3,256,256]{3,2,1,0:T(8,128)(2,1)S(1)} %copy-done.15, bf16[12,8,36,256]{3,2,1,0:T(8,128)(2,1)S(1)} %get-tuple-element.22), kind=kOutput, calls=%fused_computation.1 | convolution fusion | flops 1811939328 | bytes 4521984 | tf_op jit(solution)/shard_map/conv_general_dilated | solution.py:598
  118.6 1.8 %fusion.10 = bf16[12,4,32,256]{3,2,1,0:T(8,128)(2,1)} fusion(f32[12,4,32,256]{3,2,1,0:T(8,128)S(1)} %get-tuple-element.23, f32[12,4,32,256]{3,0,2,1:T(8,128)S(1)} %fusion), kind=kLoop, calls=%fused_computation.13 | loop fusion | flops 786432 | bytes 3932160 | tf_op jit(solution)/shard_map/convert_element_type | solution.py:608
  121.4 1.6 %convert_multiply_fusion = f32[32,72,256]{2,1,0:T(8,128)} fusion(bf16[16,72,256]{2,1,0:T(8,128)(2,1)S(1)} %get-tuple-element.27, bf16[16,72,256]{2,1,0:T(8,128)(2,1)S(1)} %get-tuple-element.26), kind=kLoop, calls=%fused_computation.5 | loop fusion | flops 1769472 | bytes 3538944 | tf_op jit(solution)/shard_map/mul | solution.py:593
  (117 shorter events, 19.3 us)
Async XLA Ops:
  0.6 40.4 %copy-start.3 = (bf16[4,72,72]{2,1,0:T(8,128)(2,1)S(1)}, bf16[4,72,72]{2,1,0:T(8,128)(2,1)}, u32[]{:S(2)}) copy-start(bf16[4,72,72]{2,1,0:T(8,128)(2,1)} %constant.76.clone.flips) | copy-start | bytes 124420
  0.6 40.4 %copy-start.2 = (bf16[320,384]{1,0:T(8,128)(2,1)S(1)}, bf16[320,384]{1,0:T(8,128)(2,1)}, u32[]{:S(2)}) copy-start(bf16[320,384]{1,0:T(8,128)(2,1)} %constant.77.clone.picks) | copy-start | bytes 737284
  1.9 13.8 %collective-permute-start = (bf16[12,16,256]{2,1,0:T(8,128)(2,1)S(1)}, bf16[12,16,256]{2,1,0:T(8,128)(2,1)S(1)}, u32[]{:S(2)}, u32[]{:S(2)}) collective-permute-start(bf16[12,16,256]{2,1,0:T(8,128)(2,1)S(1)} %get-tuple-element.53.edges), channel_id=1, source_target_pairs={{0,1},{1,0},{2,3},{3,2},{4,5},{5,4},{6,7},{7,6},{8,9},{9,8},{10,11... | collective-permute-start | bytes 294920 | tf_op jit(solution)/shard_map/ppermute | solution.py:245
  4.9 6.5 %collective-permute-start.1 = (bf16[12,8,256]{2,1,0:T(8,128)(2,1)S(1)}, bf16[12,8,256]{2,1,0:T(8,128)(2,1)S(1)}, u32[]{:S(2)}, u32[]{:S(2)}) collective-permute-start(bf16[12,8,256]{2,1,0:T(8,128)(2,1)S(1)} %get-tuple-element.52), channel_id=1, source_target_pairs={{0,30},{1,31},{2,28},{3,29},{4,26},{5,27},{6,24},{7,25},{8,22},{9,... | collective-permute-start | bytes 147464 | tf_op jit(solution)/shard_map/ppermute | solution.py:255
  8.6 7.1 %collective-permute-start.2 = (bf16[12,8,256]{2,1,0:T(8,128)(2,1)S(1)}, bf16[12,8,256]{2,1,0:T(8,128)(2,1)S(1)}, u32[]{:S(2)}, u32[]{:S(2)}) collective-permute-start(bf16[12,8,256]{2,1,0:T(8,128)(2,1)S(1)} %get-tuple-element.52), channel_id=1, source_target_pairs={{0,31},{1,30},{2,29},{3,28},{4,27},{5,26},{6,25},{7,24},{8,23},{9,... | collective-permute-start | bytes 147464 | tf_op jit(solution)/shard_map/ppermute | solution.py:256
  18.3 22.8 %copy-start.1 = (bf16[12,4,32,256]{3,2,1,0:T(8,128)(2,1)S(1)}, bf16[12,4,32,256]{3,2,1,0:T(8,128)(2,1)}, u32[]{:S(2)}) copy-start(bf16[12,4,32,256]{3,2,1,0:T(8,128)(2,1)} %field.3) | copy-start | bytes 2359300
  21.0 10.7 %collective-permute-start.3 = (bf16[12,72,256]{2,1,0:T(8,128)(2,1)}, bf16[12,72,256]{2,1,0:T(8,128)(2,1)S(1)}, u32[]{:S(2)}, u32[]{:S(2)}) collective-permute-start(bf16[12,72,256]{2,1,0:T(8,128)(2,1)} %get-tuple-element.15), channel_id=1, source_target_pairs={{0,2},{1,3},{2,4},{3,5},{4,6},{5,7},{6,8},{7,9},{8,10},{9,11},{10,... | collective-permute-start | bytes 1327112 | tf_op jit(solution)/shard_map/ppermute | solution.py:270
  21.9 9.8 %collective-permute-start.4 = (bf16[12,72,256]{2,1,0:T(8,128)(2,1)}, bf16[12,72,256]{2,1,0:T(8,128)(2,1)S(1)}, u32[]{:S(2)}, u32[]{:S(2)}) collective-permute-start(bf16[12,72,256]{2,1,0:T(8,128)(2,1)} %get-tuple-element.16), channel_id=1, source_target_pairs={{0,30},{1,31},{2,0},{3,1},{4,2},{5,3},{6,4},{7,5},{8,6},{9,7},{10,... | collective-permute-start | bytes 1327112 | tf_op jit(solution)/shard_map/ppermute | solution.py:271
  25.4 10.2 %collective-permute-start.5 = (bf16[12,72,256]{2,1,0:T(8,128)(2,1)S(1)}, bf16[12,72,256]{2,1,0:T(8,128)(2,1)S(1)}, u32[]{:S(2)}, u32[]{:S(2)}) collective-permute-start(bf16[12,72,256]{2,1,0:T(8,128)(2,1)S(1)} %get-tuple-element.17.edge), channel_id=1, source_target_pairs={{0,1},{1,0},{30,31},{31,30}} | collective-permute-start | bytes 1327112 | tf_op jit(solution)/shard_map/ppermute | solution.py:272
  27.8 13.2 %collective-permute-start.6 = (bf16[12,72,256]{2,1,0:T(8,128)(2,1)S(1)}, bf16[12,72,256]{2,1,0:T(8,128)(2,1)S(1)}, u32[]{:S(2)}, u32[]{:S(2)}) collective-permute-start(bf16[12,72,256]{2,1,0:T(8,128)(2,1)S(1)} %get-tuple-element.17.edge), channel_id=1, source_target_pairs={{0,31},{1,30},{30,1},{31,0}} | collective-permute-start | bytes 1327112 | tf_op jit(solution)/shard_map/ppermute | solution.py:273
  54.7 2.2 %collective-permute-start.14 = (bf16[1160,256]{1,0:T(8,128)(2,1)}, bf16[1160,256]{1,0:T(8,128)(2,1)S(1)}, u32[]{:S(2)}, u32[]{:S(2)}) collective-permute-start(bf16[1160,256]{1,0:T(8,128)(2,1)} %pad_maximum_fusion), channel_id=1, source_target_pairs={{0,2},{1,3},{2,0},{3,1},{4,6},{5,7},{6,4},{7,5},{8,10},{9,11},{10,... | collective-permute-start | bytes 1781768 | tf_op jit(solution)/shard_map/ppermute | solution.py:528
  57.0 17.0 %copy-start.14 = (bf16[3,3,256,256]{3,2,1,0:T(8,128)(2,1)S(1)}, bf16[3,3,256,256]{3,2,1,0:T(8,128)(2,1)}, u32[]{:S(2)}) copy-start(bf16[3,3,256,256]{3,2,1,0:T(8,128)(2,1)} %param.16) | copy-start | bytes 3538948
  57.2 9.1 %collective-permute-start.17 = (bf16[296,256]{1,0:T(8,128)(2,1)S(1)}, bf16[296,256]{1,0:T(8,128)(2,1)S(1)}, u32[]{:S(2)}, u32[]{:S(2)}) collective-permute-start(bf16[296,256]{1,0:T(8,128)(2,1)S(1)} %get-tuple-element.59), channel_id=1, source_target_pairs={{0,5},{1,4},{2,7},{3,6},{4,1},{5,0},{6,3},{7,2},{8,13},{9,12},{10,... | collective-permute-start | bytes 454664 | tf_op jit(solution)/shard_map/ppermute | solution.py:528
  57.2 12.2 %collective-permute-start.16 = (bf16[296,256]{1,0:T(8,128)(2,1)S(1)}, bf16[296,256]{1,0:T(8,128)(2,1)S(1)}, u32[]{:S(2)}, u32[]{:S(2)}) collective-permute-start(bf16[296,256]{1,0:T(8,128)(2,1)S(1)} %get-tuple-element.58), channel_id=1, source_target_pairs={{0,4},{1,5},{2,6},{3,7},{4,0},{5,1},{6,2},{7,3},{8,12},{9,13},{10,... | collective-permute-start | bytes 454664 | tf_op jit(solution)/shard_map/ppermute | solution.py:528
  60.2 9.2 %collective-permute-start.15 = (bf16[296,256]{1,0:T(8,128)(2,1)S(1)}, bf16[296,256]{1,0:T(8,128)(2,1)S(1)}, u32[]{:S(2)}, u32[]{:S(2)}) collective-permute-start(bf16[296,256]{1,0:T(8,128)(2,1)S(1)} %get-tuple-element.57), channel_id=1, source_target_pairs={{0,1},{1,0},{2,3},{3,2},{4,5},{5,4},{6,7},{7,6},{8,9},{9,8},{10,11... | collective-permute-start | bytes 454664 | tf_op jit(solution)/shard_map/ppermute | solution.py:528
  60.7 9.1 %collective-permute-start.8 = (bf16[12,8,256]{2,1,0:T(8,128)(2,1)S(1)}, bf16[12,8,256]{2,1,0:T(8,128)(2,1)S(1)}, u32[]{:S(2)}, u32[]{:S(2)}) collective-permute-start(bf16[12,8,256]{2,1,0:T(8,128)(2,1)S(1)} %get-tuple-element.50), channel_id=1, source_target_pairs={{0,30},{1,31},{2,28},{3,29},{4,26},{5,27},{6,24},{7,25},{8,22},{9,... | collective-permute-start | bytes 147464 | tf_op jit(solution)/shard_map/ppermute | solution.py:255
  60.8 14.8 %collective-permute-start.9 = (bf16[12,8,256]{2,1,0:T(8,128)(2,1)S(1)}, bf16[12,8,256]{2,1,0:T(8,128)(2,1)S(1)}, u32[]{:S(2)}, u32[]{:S(2)}) collective-permute-start(bf16[12,8,256]{2,1,0:T(8,128)(2,1)S(1)} %get-tuple-element.50), channel_id=1, source_target_pairs={{0,31},{1,30},{2,29},{3,28},{4,27},{5,26},{6,25},{7,24},{8,23},{9,... | collective-permute-start | bytes 147464 | tf_op jit(solution)/shard_map/ppermute | solution.py:256
  66.2 9.4 %collective-permute-start.7 = (bf16[12,16,256]{2,1,0:T(8,128)(2,1)S(1)}, bf16[12,16,256]{2,1,0:T(8,128)(2,1)S(1)}, u32[]{:S(2)}, u32[]{:S(2)}) collective-permute-start(bf16[12,16,256]{2,1,0:T(8,128)(2,1)S(1)} %get-tuple-element.51.edges), channel_id=1, source_target_pairs={{0,1},{1,0},{2,3},{3,2},{4,5},{5,4},{6,7},{7,6},{8,9},{9,8},{10,11... | collective-permute-start | bytes 294920 | tf_op jit(solution)/shard_map/ppermute | solution.py:245
  69.6 12.4 %collective-permute-start.20 = (bf16[80,256]{1,0:T(8,128)(2,1)S(1)}, bf16[80,256]{1,0:T(8,128)(2,1)S(1)}, u32[]{:S(2)}, u32[]{:S(2)}) collective-permute-start(bf16[80,256]{1,0:T(8,128)(2,1)S(1)} %get-tuple-element.56), channel_id=1, source_target_pairs={{0,24},{1,25},{2,26},{3,27},{4,28},{5,29},{6,30},{7,31},{8,16},{9,... | collective-permute-start | bytes 122888 | tf_op jit(solution)/shard_map/ppermute | solution.py:528
  69.7 12.4 %collective-permute-start.19 = (bf16[80,256]{1,0:T(8,128)(2,1)S(1)}, bf16[80,256]{1,0:T(8,128)(2,1)S(1)}, u32[]{:S(2)}, u32[]{:S(2)}) collective-permute-start(bf16[80,256]{1,0:T(8,128)(2,1)S(1)} %get-tuple-element.55), channel_id=1, source_target_pairs={{0,16},{1,17},{2,18},{3,19},{4,20},{5,21},{6,22},{7,23},{8,24},{9,... | collective-permute-start | bytes 122888 | tf_op jit(solution)/shard_map/ppermute | solution.py:528
  69.8 12.3 %collective-permute-start.18 = (bf16[80,256]{1,0:T(8,128)(2,1)S(1)}, bf16[80,256]{1,0:T(8,128)(2,1)S(1)}, u32[]{:S(2)}, u32[]{:S(2)}) collective-permute-start(bf16[80,256]{1,0:T(8,128)(2,1)S(1)} %get-tuple-element.54), channel_id=1, source_target_pairs={{0,8},{1,9},{2,10},{3,11},{4,12},{5,13},{6,14},{7,15},{8,0},{9,1},... | collective-permute-start | bytes 122888 | tf_op jit(solution)/shard_map/ppermute | solution.py:528
  77.6 16.6 %collective-permute-start.10 = (bf16[12,72,256]{2,1,0:T(8,128)(2,1)S(1)}, bf16[12,72,256]{2,1,0:T(8,128)(2,1)S(1)}, u32[]{:S(2)}, u32[]{:S(2)}) collective-permute-start(bf16[12,72,256]{2,1,0:T(8,128)(2,1)S(1)} %get-tuple-element.19), channel_id=1, source_target_pairs={{0,2},{1,3},{2,4},{3,5},{4,6},{5,7},{6,8},{7,9},{8,10},{9,11},{10,... | collective-permute-start | bytes 1327112 | tf_op jit(solution)/shard_map/ppermute | solution.py:270
  77.6 18.6 %collective-permute-start.11 = (bf16[12,72,256]{2,1,0:T(8,128)(2,1)S(1)}, bf16[12,72,256]{2,1,0:T(8,128)(2,1)S(1)}, u32[]{:S(2)}, u32[]{:S(2)}) collective-permute-start(bf16[12,72,256]{2,1,0:T(8,128)(2,1)S(1)} %get-tuple-element.20), channel_id=1, source_target_pairs={{0,30},{1,31},{2,0},{3,1},{4,2},{5,3},{6,4},{7,5},{8,6},{9,7},{10,... | collective-permute-start | bytes 1327112 | tf_op jit(solution)/shard_map/ppermute | solution.py:271
  82.1 6.2 %collective-permute-start.23 = (bf16[1,72,256]{2,1,0:T(8,128)(2,1)S(1)}, bf16[1,72,256]{2,1,0:T(8,128)(2,1)S(1)}, u32[]{:S(2)}, u32[]{:S(2)}) collective-permute-start(bf16[1,72,256]{2,1,0:T(8,128)(2,1)S(1)} %bitcast.211), channel_id=1, source_target_pairs={{0,24},{1,25},{2,26},{3,27},{4,28},{5,29},{6,30},{7,31},{8,16},{9,... | collective-permute-start | bytes 110600 | tf_op jit(solution)/shard_map/ppermute | solution.py:541
  82.2 8.7 %collective-permute-start.22 = (bf16[1,72,256]{2,1,0:T(8,128)(2,1)S(1)}, bf16[1,72,256]{2,1,0:T(8,128)(2,1)S(1)}, u32[]{:S(2)}, u32[]{:S(2)}) collective-permute-start(bf16[1,72,256]{2,1,0:T(8,128)(2,1)S(1)} %bitcast.212), channel_id=1, source_target_pairs={{0,16},{1,17},{2,18},{3,19},{4,20},{5,21},{6,22},{7,23},{8,24},{9,... | collective-permute-start | bytes 110600 | tf_op jit(solution)/shard_map/ppermute | solution.py:541
  82.3 11.7 %collective-permute-start.21 = (bf16[1,72,256]{2,1,0:T(8,128)(2,1)S(1)}, bf16[1,72,256]{2,1,0:T(8,128)(2,1)S(1)}, u32[]{:S(2)}, u32[]{:S(2)}) collective-permute-start(bf16[1,72,256]{2,1,0:T(8,128)(2,1)S(1)} %bitcast.213), channel_id=1, source_target_pairs={{0,8},{1,9},{2,10},{3,11},{4,12},{5,13},{6,14},{7,15},{8,0},{9,1},... | collective-permute-start | bytes 110600 | tf_op jit(solution)/shard_map/ppermute | solution.py:541
  88.4 13.3 %collective-permute-start.12 = (bf16[12,72,256]{2,1,0:T(8,128)(2,1)S(1)}, bf16[12,72,256]{2,1,0:T(8,128)(2,1)S(1)}, u32[]{:S(2)}, u32[]{:S(2)}) collective-permute-start(bf16[12,72,256]{2,1,0:T(8,128)(2,1)S(1)} %get-tuple-element.21.edge), channel_id=1, source_target_pairs={{0,1},{1,0},{30,31},{31,30}} | collective-permute-start | bytes 1327112 | tf_op jit(solution)/shard_map/ppermute | solution.py:272
  90.9 13.4 %collective-permute-start.13 = (bf16[12,72,256]{2,1,0:T(8,128)(2,1)S(1)}, bf16[12,72,256]{2,1,0:T(8,128)(2,1)S(1)}, u32[]{:S(2)}, u32[]{:S(2)}) collective-permute-start(bf16[12,72,256]{2,1,0:T(8,128)(2,1)S(1)} %get-tuple-element.21.edge), channel_id=1, source_target_pairs={{0,31},{1,30},{30,1},{31,0}} | collective-permute-start | bytes 1327112 | tf_op jit(solution)/shard_map/ppermute | solution.py:273
  94.1 20.1 %collective-permute-start.26 = (bf16[4,72,256]{2,1,0:T(8,128)(2,1)S(1)}, bf16[4,72,256]{2,1,0:T(8,128)(2,1)S(1)}, u32[]{:S(2)}, u32[]{:S(2)}) collective-permute-start(bf16[4,72,256]{2,1,0:T(8,128)(2,1)S(1)} %get-tuple-element.42), channel_id=1, source_target_pairs={{0,5},{1,4},{2,7},{3,6},{4,1},{5,0},{6,3},{7,2},{8,13},{9,12},{10,... | collective-permute-start | bytes 442376 | tf_op jit(solution)/shard_map/ppermute | solution.py:541
  94.2 20.0 %collective-permute-start.25 = (bf16[4,72,256]{2,1,0:T(8,128)(2,1)S(1)}, bf16[4,72,256]{2,1,0:T(8,128)(2,1)S(1)}, u32[]{:S(2)}, u32[]{:S(2)}) collective-permute-start(bf16[4,72,256]{2,1,0:T(8,128)(2,1)S(1)} %get-tuple-element.42), channel_id=1, source_target_pairs={{0,4},{1,5},{2,6},{3,7},{4,0},{5,1},{6,2},{7,3},{8,12},{9,13},{10,... | collective-permute-start | bytes 442376 | tf_op jit(solution)/shard_map/ppermute | solution.py:541
  96.3 17.9 %collective-permute-start.24 = (bf16[4,72,256]{2,1,0:T(8,128)(2,1)S(1)}, bf16[4,72,256]{2,1,0:T(8,128)(2,1)S(1)}, u32[]{:S(2)}, u32[]{:S(2)}) collective-permute-start(bf16[4,72,256]{2,1,0:T(8,128)(2,1)S(1)} %get-tuple-element.42), channel_id=1, source_target_pairs={{0,1},{1,0},{2,3},{3,2},{4,5},{5,4},{6,7},{7,6},{8,9},{9,8},{10,11... | collective-permute-start | bytes 442376 | tf_op jit(solution)/shard_map/ppermute | solution.py:541
  114.5 6.5 %collective-permute-start.27 = (bf16[16,72,256]{2,1,0:T(8,128)(2,1)S(1)}, bf16[16,72,256]{2,1,0:T(8,128)(2,1)S(1)}, u32[]{:S(2)}, u32[]{:S(2)}) collective-permute-start(bf16[16,72,256]{2,1,0:T(8,128)(2,1)S(1)} %get-tuple-element.32), channel_id=1, source_target_pairs={{0,2},{1,3},{2,0},{3,1},{4,6},{5,7},{6,4},{7,5},{8,10},{9,11},{10,... | collective-permute-start | bytes 1769480 | tf_op jit(solution)/shard_map/ppermute | solution.py:541
  (14 other events, 75.0 us)

commit v5 on v4

--- a/solution.py
+++ b/solution.py
@@ -42,18 +42,6 @@
 
 def round_up(value, step):
     return -(-value // step) * step
-
-
-def col_flips(tile_rows):
-    size = 2 * tile_rows
-    table = np.zeros((4, size, size), np.float32)
-    for kind in range(4):
-        for y in range(tile_rows):
-            for k in range(2):
-                source_y = tile_rows - 1 - y if kind >= 2 else y
-                source_k = 1 - k if kind % 2 else k
-                table[kind, 2 * y + k, 2 * source_y + source_k] = 1
-    return jnp.asarray(table, jnp.bfloat16)
 
 
 def row_flips(width):
@@ -71,13 +59,12 @@
     return jnp.asarray(table, jnp.bfloat16)
 
 
-def tail_picks(tile_rows):
-    table = np.zeros((2, 8, 4 * tile_rows), np.float32)
-    for place, first in enumerate((0, tile_rows - 2)):
-        for d in range(2):
-            for e in range(4):
-                source = 2 * tile_rows * (e // 2) + 2 * (first + d) + e % 2
-                table[place, 4 * d + e, source] = 1
+def corner_picks(width):
+    table = np.zeros((2, 8, 2 * width), np.float32)
+    for d in range(2):
+        for k in range(2):
+            table[0, 4 * d + 2 + k, d * width + k] = 1
+            table[1, 4 * d + k, d * width + width - 2 + k] = 1
     return jnp.asarray(table, jnp.bfloat16)
 
 
@@ -122,11 +109,30 @@
     return adjacency[base], 2 * adjacency[base + 2] + near
 
 
-def col_kernel(
-    adjacency, field, edges, beside, far_same, far_cross, flips, tails,
-    side_out, top_out, bottom_out, edge_out, seam,
+def one_hot(source, size):
+    columns = lax.broadcasted_iota(jnp.int32, (source.shape[0], size), 1)
+    return jnp.where(source == columns, 1.0, 0.0).astype(jnp.bfloat16)
+
+
+def col_flip(kind, tile_rows):
+    size = 2 * tile_rows
+    row = lax.broadcasted_iota(jnp.int32, (size, size), 0)
+    if kind >= 2:
+        row = 2 * (tile_rows - 1 - (row >> 1)) + (row & 1)
+    return one_hot(row ^ 1 if kind % 2 else row, size)
+
+
+def tail_pick(first, tile_rows):
+    row = lax.broadcasted_iota(jnp.int32, (8, 4 * tile_rows), 0)
+    place = 2 * tile_rows * ((row >> 1) & 1) + 2 * (first + (row >> 2)) + (row & 1)
+    return one_hot(place, 4 * tile_rows)
+
+
+def side_kernel(
+    adjacency, edges, beside, far_same, far_cross, side_out, upper_out, lower_out, seam
 ):
-    face_count, tile_rows, width, channels = field.shape
+    face_count, both_sides, channels = edges.shape
+    tile_rows = both_sides // 4
     half = 2 * tile_rows
     row_place, col_place = lax.axis_index("frow"), lax.axis_index("fcol")
     at_top = row_place == 0
@@ -148,16 +154,19 @@
             @pl.when(kind == 1)
             def _():
                 both = edges[source]
-                seam[face] = pick(flips[1], jnp.where(at_left, both[:half], both[half:]))
+                own = jnp.where(at_left, both[:half], both[half:])
+                seam[face] = pick(col_flip(1, tile_rows), own)
 
             @pl.when(kind == 2)
             def _():
-                seam[face] = pick(flips[2], far_cross[source])
+                seam[face] = pick(col_flip(2, tile_rows), far_cross[source])
 
             @pl.when(kind == 3)
             def _():
-                seam[face] = pick(flips[3], far_same[source])
-
+                seam[face] = pick(col_flip(3, tile_rows), far_same[source])
+
+    upper_pick = tail_pick(0, tile_rows)
+    lower_pick = tail_pick(tile_rows - 2, tile_rows)
     for face in range(face_count):
         both = beside[face]
         left = jnp.where(at_left, seam[face], both[half:])
@@ -168,41 +177,51 @@
         inner = jnp.concatenate(
             [jnp.where(at_left, blank, left), jnp.where(at_right, blank, right)], 0
         )
-        upper = pick(tails[0], jnp.where(at_top, inner, sides))
-        lower = pick(tails[1], jnp.where(at_bottom, inner, sides))
-        for d in range(2):
-            rows = pl.ds(d * width, width)
-            first, last = field[face, d], field[face, tile_rows - 2 + d]
-            top_out[face, rows] = first
-            bottom_out[face, rows] = last
-            edge_out[face, rows] = jnp.where(at_top, first, last)
-        rows = pl.ds(2 * width, 8)
-        top_out[face, rows] = upper
-        bottom_out[face, rows] = lower
-        edge_out[face, rows] = jnp.where(at_top, upper, lower)
-
-
-def load_stack(adjacency, face, field, sides, up, down, edge, far_same, far_cross, flips, stack):
+        upper_out[face] = pick(upper_pick, jnp.where(at_top, inner, sides))
+        lower_out[face] = pick(lower_pick, jnp.where(at_bottom, inner, sides))
+
+
+def load_stack(adjacency, face, strips, flips, corners, stack):
+    field, sides, tails, up, down, up_tail, down_tail, edge, far_same, far_cross = strips[:10]
     tile_rows, width, channels = field.shape[1:]
     strip = 2 * width + 8
     beside, above, below, _ = stack_places(tile_rows, width)
-    row_place = lax.axis_index("frow")
+    row_place, col_place = lax.axis_index("frow"), lax.axis_index("fcol")
     stack[face, pl.ds(0, beside)] = field[face].reshape(beside, channels)
     stack[face, pl.ds(beside, 4 * tile_rows)] = sides[face]
-    for side, place, near in ((0, above, up), (1, below, down)):
+    for side, place, near, near_tail in (
+        (0, above, up, up_tail), (1, below, down, down_tail),
+    ):
         at_edge = row_place == side * (lax.axis_size("frow") - 1)
         rows = pl.ds(place, strip)
 
         @pl.when(jnp.logical_not(at_edge))
         def _():
-            stack[face, rows] = near[face]
+            stack[face, pl.ds(place, 2 * width)] = near[face]
+            stack[face, pl.ds(place + 2 * width, 8)] = near_tail[face]
 
         source, kind = seam_of(adjacency, face, side)
-        for choice, strips in enumerate((near, edge, far_cross, far_same)):
+        for choice, main in enumerate((near, edge, far_cross, far_same)):
 
             @pl.when(jnp.logical_and(at_edge, kind == choice))
             def _():
-                stack[face, rows] = pick(flips[choice], strips[source])
+                if choice == 0:
+                    tail = near_tail[source]
+                elif choice == 1:
+                    tail = tails[side][source]
+                elif len(strips) > 10:
+                    tail = strips[13 - choice][source]
+                else:
+                    other = near if choice == 2 else edge
+                    tail = pick(corners[1 - col_place], other[source])
+                stack[face, rows] = pick(
+                    flips[choice], jnp.concatenate([main[source], tail], 0)
+                )
+
+
+def unpack_strips(refs, count):
+    strips = list(refs[:count])
+    return (strips[0], strips[1], (strips[2], strips[3]), *strips[4:])
 
 
 def write_padded(picks, stack, padded):
@@ -214,17 +233,15 @@
             padded[face, q] = out[q * step : q * step + breadth]
 
 
-def pad_kernel(
-    adjacency, field, sides, up, down, edge, far_same, far_cross, flips, picks, padded, stack
-):
-    face_count, tile_rows, width, channels = field.shape
+def pad_kernel(count, adjacency, *refs):
+    strips = unpack_strips(refs, count)
+    flips, corners, picks, padded, stack = refs[count:]
+    face_count = strips[0].shape[0]
     stack[...] = jnp.zeros_like(stack)
 
     @pl.loop(0, face_count)
     def _(face):
-        load_stack(
-            adjacency, face, field, sides, up, down, edge, far_same, far_cross, flips, stack
-        )
+        load_stack(adjacency, face, strips, flips, corners, stack)
 
     write_padded(picks, stack, padded)
 
@@ -238,6 +255,14 @@
 def gather_strips(field, adjacency):
     face_count, tile_rows, width, channels = field.shape
     cols = lax.axis_size("fcol")
+    at_top = lax.axis_index("frow") == 0
+    top = field[:, :2].reshape(face_count, 2 * width, channels)
+    bottom = field[:, tile_rows - 2 :].reshape(face_count, 2 * width, channels)
+    edge_strip = jnp.where(at_top, top, bottom)
+    row_same = lax.ppermute(edge_strip, axes, mirror_pairs(True, False, True))
+    row_cross = lax.ppermute(edge_strip, axes, mirror_pairs(True, True, True))
+    up = lax.ppermute(bottom, axes, shifted_pairs(1, 0))
+    down = lax.ppermute(top, axes, shifted_pairs(-1, 0))
     left = field[:, :, :2].reshape(face_count, 2 * tile_rows, channels)
     right = field[:, :, width - 2 :].reshape(face_count, 2 * tile_rows, channels)
     edges = jnp.concatenate([left, right], 1)
@@ -254,24 +279,26 @@
     edge = jnp.where(lax.axis_index("fcol") == 0, left, right)
     far_same = lax.ppermute(edge, axes, mirror_pairs(False, True, False))
     far_cross = lax.ppermute(edge, axes, mirror_pairs(False, True, True))
-    strip = jax.ShapeDtypeStruct((face_count, 2 * width + 8, channels), field.dtype)
-    sides, top, bottom, edge_strip = pl.pallas_call(
-        col_kernel,
-        out_shape=(jax.ShapeDtypeStruct(edges.shape, field.dtype), strip, strip, strip),
-        in_specs=whole(7),
-        out_specs=[pl.BlockSpec(memory_space=pltpu.VMEM)] * 4,
+    tail = jax.ShapeDtypeStruct((face_count, 8, channels), field.dtype)
+    sides, upper, lower = pl.pallas_call(
+        side_kernel,
+        out_shape=(jax.ShapeDtypeStruct(edges.shape, field.dtype), tail, tail),
+        in_specs=whole(4),
+        out_specs=[pl.BlockSpec(memory_space=pltpu.VMEM)] * 3,
         scratch_shapes=[pltpu.VMEM((face_count, 2 * tile_rows, channels), field.dtype)],
         compiler_params=pltpu.CompilerParams(vmem_limit_bytes=vmem_bytes),
         cost_estimate=pl.CostEstimate(flops=1000, bytes_accessed=3000000, transcendentals=0),
-    )(
-        adjacency, field, edges, beside, far_same, far_cross,
-        col_flips(tile_rows), tail_picks(tile_rows),
-    )
-    up = lax.ppermute(bottom, axes, shifted_pairs(1, 0))
-    down = lax.ppermute(top, axes, shifted_pairs(-1, 0))
-    row_same = lax.ppermute(edge_strip, axes, mirror_pairs(True, False, True))
-    row_cross = lax.ppermute(edge_strip, axes, mirror_pairs(True, True, True))
-    return (field, sides, up, down, edge_strip, row_same, row_cross)
+    )(adjacency, edges, beside, far_same, far_cross)
+    up_tail = lax.ppermute(lower, axes, shifted_pairs(1, 0))
+    down_tail = lax.ppermute(upper, axes, shifted_pairs(-1, 0))
+    strips = [
+        field, sides, upper, lower, up, down, up_tail, down_tail, edge_strip, row_same, row_cross,
+    ]
+    if cols > 2:
+        own_tail = jnp.where(at_top, upper, lower)
+        strips.append(lax.ppermute(own_tail, axes, mirror_pairs(True, False, True)))
+        strips.append(lax.ppermute(own_tail, axes, mirror_pairs(True, True, True)))
+    return strips
 
 
 def pad_field(field, adjacency):
@@ -280,14 +307,14 @@
     padded = (face_count, tile_rows + 4, width + 4, channels)
     size = stack_places(tile_rows, width)[3]
     return pl.pallas_call(
-        pad_kernel,
+        functools.partial(pad_kernel, len(strips)),
         out_shape=jax.ShapeDtypeStruct(padded, field.dtype),
-        in_specs=whole(9),
+        in_specs=whole(len(strips) + 3),
         out_specs=pl.BlockSpec(memory_space=pltpu.VMEM),
         scratch_shapes=[pltpu.VMEM((face_count, size, channels), field.dtype)],
         compiler_params=pltpu.CompilerParams(vmem_limit_bytes=vmem_bytes),
         cost_estimate=pl.CostEstimate(flops=1000, bytes_accessed=5000000, transcendentals=0),
-    )(adjacency, *strips, row_flips(width), pad_picks(tile_rows, width))
+    )(adjacency, *strips, row_flips(width), corner_picks(width), pad_picks(tile_rows, width))
 
 
 def seam_row_picks(width):
@@ -321,10 +348,11 @@
     return jnp.asarray(table, jnp.bfloat16)
 
 
-def return_kernel(
-    adjacency, field, sides, up, down, edge, far_same, far_cross, flips, picks, row_picks,
-    col_picks, rotated, padded, extra, stack, kept_picks, row_terms, col_terms, col_sum,
-):
+def return_kernel(count, adjacency, *refs):
+    strips = unpack_strips(refs, count)
+    flips, corners, picks, row_picks, col_picks, rotated, padded, extra = refs[count : count + 8]
+    stack, kept_picks, row_terms, col_terms, col_sum = refs[count + 8 :]
+    field = strips[0]
     face_count, tile_rows, width, channels = field.shape
     breadth = picks.shape[0] // (tile_rows + 4)
     half = 2 * tile_rows
@@ -356,9 +384,7 @@
 
     @pl.loop(0, face_count)
     def _(face):
-        load_stack(
-            adjacency, face, field, sides, up, down, edge, far_same, far_cross, flips, stack
-        )
+        load_stack(adjacency, face, strips, flips, corners, stack)
 
     write_padded(kept_picks, stack, padded)
 
@@ -444,12 +470,12 @@
     picks = pad_picks(tile_rows, width)
     cells = face_count * round_up(2 * tile_rows, 16)
     return pl.pallas_call(
-        return_kernel,
+        functools.partial(return_kernel, len(strips)),
         out_shape=(
             jax.ShapeDtypeStruct(padded, field.dtype),
             jax.ShapeDtypeStruct(field.shape, jnp.float32),
         ),
-        in_specs=whole(12),
+        in_specs=whole(len(strips) + 6),
         out_specs=[pl.BlockSpec(memory_space=pltpu.VMEM)] * 2,
         scratch_shapes=[
             pltpu.VMEM((face_count, size, channels), field.dtype),
@@ -461,7 +487,7 @@
         compiler_params=pltpu.CompilerParams(vmem_limit_bytes=vmem_bytes),
         cost_estimate=pl.CostEstimate(flops=1000, bytes_accessed=8000000, transcendentals=0),
     )(
-        adjacency, *strips, row_flips(width), picks,
+        adjacency, *strips, row_flips(width), corner_picks(width), picks,
         seam_row_picks(width).reshape(6 * width, -1),
         seam_col_picks(tile_rows, width), rotated,
     )

time: 124 us -> 144 us (1.16)
  waiting for transfers between devices: 27.8 us -> 40.9 us
  starting transfers between devices: 48.4 us -> 53.1 us
  other arithmetic: 9.17 us -> 12.3 us
    ppermute x0 -> x4, waiting for transfers between devices: none -> 20.7 us  [the longest x2 17.3 us: gather_strips(): up_tail = lax.ppermute(lower, axes, shifted_pairs(1, 0))]
    ppermute x2, waiting for transfers between devices: 8.08 us -> 0.01 us  [gather_strips(): row_cross = lax.ppermute(edge_strip, axes, mirror_pairs(True, True, True))]
    ppermute x2, waiting for transfers between devices: 5.98 us -> 0.01 us  [gather_strips(): row_same = lax.ppermute(edge_strip, axes, mirror_pairs(True, False, True))]
    ppermute x2, waiting for transfers between devices: 1.63 us -> 7.59 us  [gather_strips(): far_same = lax.ppermute(edge, axes, mirror_pairs(False, True, False))]
    ppermute x2, waiting for transfers between devices: 0.01 us -> 3.6 us  [gather_strips(): beside = lax.ppermute(edges, axes, shifted_pairs(0, 1))]
    ppermute x2, starting transfers between devices: 4.94 us -> 7.9 us  [gather_strips(): row_same = lax.ppermute(edge_strip, axes, mirror_pairs(True, False, True))]
    slice x0 -> x2, local copies, waits for them, and re-layouts: none -> 2.22 us  [gather_strips(): top = field[:, :2].reshape(face_count, 2 * width, channels)]
    ppermute x2, waiting for transfers between devices: 4.32 us -> 2.13 us  [gather_strips(): far_cross = lax.ppermute(edge, axes, mirror_pairs(False, True, True))]
  transfers between devices with their start and end apart: 28 -> 32, of which waited for: 10 -> 12; matrix products, arithmetic and copies ran while one was open for 8% -> 6% of each run, Pallas kernels for 10% -> 10%
where the time goes in v5:
time: 144 us
  starting transfers between devices  53.1 us (37%)
  waiting for transfers between devices  40.9 us (28%)
  Pallas kernels  18.8 us (13%)
  other arithmetic  12.3 us (9%)
  matrix products  9.87 us (7%)
  local copies, waits for them, and re-layouts  7.23 us (5%)
    ppermute x2, waiting for transfers between devices, gather_strips(): up_tail = lax.ppermute(lower, axes, shifted_pairs(1, 0))  17.3 us
    pallas_call x1, Pallas kernels, return_field(): pl.pallas_call(functools.partial(return_kernel, len(strips)), out_shape=(...  10 us
    ppermute x2, starting transfers between devices, gather_strips(): down = lax.ppermute(top, axes, shifted_pairs(-1, 0))  8.87 us
    ppermute x7, starting transfers between devices, reduce_everywhere(): packed = lax.ppermute(packed, axes, [(i, i ^ offset) for i in range(count)])  8.8 us
    ppermute x7, starting transfers between devices, reduce_everywhere(): lax.ppermute(part, axes, [(i, i ^ offset) for i in range(count)])  8.01 us
    ppermute x2, starting transfers between devices, gather_strips(): row_same = lax.ppermute(edge_strip, axes, mirror_pairs(True, False, True))  7.9 us
    ppermute x2, waiting for transfers between devices, gather_strips(): far_same = lax.ppermute(edge, axes, mirror_pairs(False, True, False))  7.59 us
    ppermute x2, starting transfers between devices, gather_strips(): row_cross = lax.ppermute(edge_strip, axes, mirror_pairs(True, True, True))  7.52 us
  transfers between devices with their start and end apart: 32, of which 12 were waited for; matrix products, arithmetic and copies ran while one was open for 6% of the time, Pallas kernels for 10%

profile of v5, /device:TPU:0, one launch (start us, length us, event | category | flops | bytes accessed | tf_op | source)
XLA Modules:
  0.0 143.6 jit_solution(17431161330827967664)
XLA Ops:
  0.7 2.2 %fusion.66 = (bf16[12,2,32,256]{3,2,1,0:T(8,128)(2,1)}, bf16[12,2,32,256]{3,2,1,0:T(8,128)(2,1)}) fusion(bf16[12,4,32,256]{3,2,1,0:T(8,128)(2,1)} %refs_0_.1), kind=kLoop, calls=%fused_computation.128 | loop fusion | bytes 1572864 | tf_op jit(solution)/shard_map/slice | solution.py:259
  4.0 4.8 %collective-permute-start.7 = (bf16[12,64,256]{2,1,0:T(8,128)(2,1)S(1)}, bf16[12,64,256]{2,1,0:T(8,128)(2,1)S(1)}, u32[]{:S(2)}, u32[]{:S(2)}) collective-permute-start(bf16[12,64,256]{2,1,0:T(8,128)(2,1)S(1)} %broadcast_select_fusion.1.refs_8_), channel_id=1, source_target_pairs={{0,1},{1,0},{30,31},{31,30}} | collective-permute-start | bytes 1179656 | tf_op jit(solution)/shard_map/ppermute | solution.py:262
  8.9 5.6 %collective-permute-start.8 = (bf16[12,64,256]{2,1,0:T(8,128)(2,1)S(1)}, bf16[12,64,256]{2,1,0:T(8,128)(2,1)S(1)}, u32[]{:S(2)}, u32[]{:S(2)}) collective-permute-start(bf16[12,64,256]{2,1,0:T(8,128)(2,1)S(1)} %broadcast_select_fusion.1.refs_8_), channel_id=1, source_target_pairs={{0,31},{1,30},{30,1},{31,0}} | collective-permute-start | bytes 1179656 | tf_op jit(solution)/shard_map/ppermute | solution.py:263
  14.5 4.4 %collective-permute-start.4 = (bf16[12,64,256]{2,1,0:T(8,128)(2,1)}, bf16[12,64,256]{2,1,0:T(8,128)(2,1)S(1)}, u32[]{:S(2)}, u32[]{:S(2)}) collective-permute-start(bf16[12,64,256]{2,1,0:T(8,128)(2,1)} %bitcast.1), channel_id=1, source_target_pairs={{0,30},{1,31},{2,0},{3,1},{4,2},{5,3},{6,4},{7,5},{8,6},{9,7},{10,... | collective-permute-start | bytes 1179656 | tf_op jit(solution)/shard_map/ppermute | solution.py:265
  19.2 7.6 %collective-permute-done.1.far_same = bf16[12,8,256]{2,1,0:T(8,128)(2,1)S(1)} collective-permute-done((bf16[12,8,256]{2,1,0:T(8,128)(2,1)S(1)}, bf16[12,8,256]{2,1,0:T(8,128)(2,1)S(1)}, u32[]{:S(2)}, u32[]{:S(2)}) %collective-permute-start.1) | collective-permute-done | bytes 49184 | tf_op jit(solution)/shard_map/ppermute | solution.py:280
  26.8 5.0 %collective-permute-start.2 = (bf16[12,8,256]{2,1,0:T(8,128)(2,1)S(1)}, bf16[12,8,256]{2,1,0:T(8,128)(2,1)S(1)}, u32[]{:S(2)}, u32[]{:S(2)}) collective-permute-start(bf16[12,8,256]{2,1,0:T(8,128)(2,1)S(1)} %get-tuple-element.52), channel_id=1, source_target_pairs={{0,31},{1,30},{2,29},{3,28},{4,27},{5,26},{6,25},{7,24},{8,23},{9,... | collective-permute-start | bytes 147464 | tf_op jit(solution)/shard_map/ppermute | solution.py:281
  31.8 2.1 %collective-permute-done.2.far_cross = bf16[12,8,256]{2,1,0:T(8,128)(2,1)S(1)} collective-permute-done((bf16[12,8,256]{2,1,0:T(8,128)(2,1)S(1)}, bf16[12,8,256]{2,1,0:T(8,128)(2,1)S(1)}, u32[]{:S(2)}, u32[]{:S(2)}) %collective-permute-start.2) | collective-permute-done | bytes 49184 | tf_op jit(solution)/shard_map/ppermute | solution.py:281
  35.6 3.6 %collective-permute-done.beside = bf16[12,16,256]{2,1,0:T(8,128)(2,1)S(1)} collective-permute-done((bf16[12,16,256]{2,1,0:T(8,128)(2,1)S(1)}, bf16[12,16,256]{2,1,0:T(8,128)(2,1)S(1)}, u32[]{:S(2)}, u32[]{:S(2)}) %collective-permute-start) | collective-permute-done | bytes 98336 | tf_op jit(solution)/shard_map/ppermute | solution.py:270
  40.0 2.1 %shard_map.156 = (bf16[12,16,256]{2,1,0:T(8,128)(2,1)S(1)}, bf16[12,8,256]{2,1,0:T(8,128)(2,1)S(1)}, bf16[12,8,256]{2,1,0:T(8,128)(2,1)S(1)}) custom-call(s32[144]{0:T(256)S(1)} %reshape.56.adjacency, bf16[12,16,256]{2,1,0:T(8,128)(2,1)S(1)} %get-tuple-element.53.edges, bf16[12,16,256]{2,1,0:T(8,128)(2,1)S(1)} %collective-permute-done.beside, ...), custom_call_target="tpu_custom_call" | custom-call | flops 1000 | bytes 3000000 | tf_op jit(solution)/shard_map/pallas_call | solution.py:283
  42.2 6.2 %collective-permute-done.5.refs_6_ = bf16[12,8,256]{2,1,0:T(8,128)(2,1)S(1)} collective-permute-done((bf16[12,8,256]{2,1,0:T(8,128)(2,1)S(1)}, bf16[12,8,256]{2,1,0:T(8,128)(2,1)S(1)}, u32[]{:S(2)}, u32[]{:S(2)}) %collective-permute-start.5) | collective-permute-done | bytes 49184 | tf_op jit(solution)/shard_map/ppermute | solution.py:292
  48.4 1.8 %collective-permute-done.6.refs_7_ = bf16[12,8,256]{2,1,0:T(8,128)(2,1)S(1)} collective-permute-done((bf16[12,8,256]{2,1,0:T(8,128)(2,1)S(1)}, bf16[12,8,256]{2,1,0:T(8,128)(2,1)S(1)}, u32[]{:S(2)}, u32[]{:S(2)}) %collective-permute-start.6) | collective-permute-done | bytes 49184 | tf_op jit(solution)/shard_map/ppermute | solution.py:293
  50.2 4.5 %shard_map.157 = bf16[12,8,36,256]{3,2,1,0:T(8,128)(2,1)S(1)} custom-call(s32[144]{0:T(256)S(1)} %reshape.56.adjacency, bf16[12,4,32,256]{3,2,1,0:T(8,128)(2,1)S(1)} %copy-done, bf16[12,16,256]{2,1,0:T(8,128)(2,1)S(1)} %get-tuple-element.12.refs_1_, bf16[12,8,256]{2,1,0:T(8,128)(2,1)S(1)} %get-tuple-element.13.refs_2_, ...), custom_call_target="tpu_custom_call" | custom-call | flops 1000 | bytes 5000000 | tf_op jit(solution)/shard_map/pallas_call | solution.py:309
  54.8 3.0 %fusion.2 = f32[12,4,32,256]{3,0,2,1:T(8,128)S(1)} fusion(bf16[3,3,256,256]{3,2,1,0:T(8,128)(2,1)S(1)} %copy-done.10, bf16[12,8,36,256]{3,2,1,0:T(8,128)(2,1)S(1)} %shard_map.157), kind=kOutput, calls=%fused_computation.3 | convolution fusion | flops 1811939328 | bytes 4521984 | tf_op jit(solution)/shard_map/conv_general_dilated | solution.py:587
  68.9 2.2 %collective-permute-start.20 = (bf16[296,256]{1,0:T(8,128)(2,1)S(1)}, bf16[296,256]{1,0:T(8,128)(2,1)S(1)}, u32[]{:S(2)}, u32[]{:S(2)}) collective-permute-start(bf16[296,256]{1,0:T(8,128)(2,1)S(1)} %get-tuple-element.58), channel_id=1, source_target_pairs={{0,4},{1,5},{2,6},{3,7},{4,0},{5,1},{6,2},{7,3},{8,12},{9,13},{10,... | collective-permute-start | bytes 454664 | tf_op jit(solution)/shard_map/ppermute | solution.py:554
  72.4 3.6 %collective-permute-start.10 = (bf16[12,8,256]{2,1,0:T(8,128)(2,1)S(1)}, bf16[12,8,256]{2,1,0:T(8,128)(2,1)S(1)}, u32[]{:S(2)}, u32[]{:S(2)}) collective-permute-start(bf16[12,8,256]{2,1,0:T(8,128)(2,1)S(1)} %get-tuple-element.50), channel_id=1, source_target_pairs={{0,30},{1,31},{2,28},{3,29},{4,26},{5,27},{6,24},{7,25},{8,22},{9,... | collective-permute-start | bytes 147464 | tf_op jit(solution)/shard_map/ppermute | solution.py:280
  77.2 2.3 %collective-permute-done.20 = bf16[296,256]{1,0:T(8,128)(2,1)S(1)} collective-permute-done((bf16[296,256]{1,0:T(8,128)(2,1)S(1)}, bf16[296,256]{1,0:T(8,128)(2,1)S(1)}, u32[]{:S(2)}, u32[]{:S(2)}) %collective-permute-start.20) | collective-permute-done | bytes 151584 | tf_op jit(solution)/shard_map/ppermute | solution.py:554
  79.6 4.6 %collective-permute-start.24 = (bf16[80,256]{1,0:T(8,128)(2,1)S(1)}, bf16[80,256]{1,0:T(8,128)(2,1)S(1)}, u32[]{:S(2)}, u32[]{:S(2)}) collective-permute-start(bf16[80,256]{1,0:T(8,128)(2,1)S(1)} %get-tuple-element.56), channel_id=1, source_target_pairs={{0,24},{1,25},{2,26},{3,27},{4,28},{5,29},{6,30},{7,31},{8,16},{9,... | collective-permute-start | bytes 122888 | tf_op jit(solution)/shard_map/ppermute | solution.py:554
  84.9 1.5 %collective-permute-done.24 = bf16[80,256]{1,0:T(8,128)(2,1)S(1)} collective-permute-done((bf16[80,256]{1,0:T(8,128)(2,1)S(1)}, bf16[80,256]{1,0:T(8,128)(2,1)S(1)}, u32[]{:S(2)}, u32[]{:S(2)}) %collective-permute-start.24) | collective-permute-done | bytes 40992 | tf_op jit(solution)/shard_map/ppermute | solution.py:554
  87.6 1.5 %collective-permute-done.23 = bf16[80,256]{1,0:T(8,128)(2,1)S(1)} collective-permute-done((bf16[80,256]{1,0:T(8,128)(2,1)S(1)}, bf16[80,256]{1,0:T(8,128)(2,1)S(1)}, u32[]{:S(2)}, u32[]{:S(2)}) %collective-permute-start.23) | collective-permute-done | bytes 40992 | tf_op jit(solution)/shard_map/ppermute | solution.py:554
  89.1 4.4 %collective-permute-start.13 = (bf16[12,64,256]{2,1,0:T(8,128)(2,1)S(1)}, bf16[12,64,256]{2,1,0:T(8,128)(2,1)S(1)}, u32[]{:S(2)}, u32[]{:S(2)}) collective-permute-start(bf16[12,64,256]{2,1,0:T(8,128)(2,1)S(1)} %bitcast.211), channel_id=1, source_target_pairs={{0,30},{1,31},{2,0},{3,1},{4,2},{5,3},{6,4},{7,5},{8,6},{9,7},{10,... | collective-permute-start | bytes 1179656 | tf_op jit(solution)/shard_map/ppermute | solution.py:265
  94.4 3.7 %collective-permute-start.25 = (bf16[1,72,256]{2,1,0:T(8,128)(2,1)S(1)}, bf16[1,72,256]{2,1,0:T(8,128)(2,1)S(1)}, u32[]{:S(2)}, u32[]{:S(2)}) collective-permute-start(bf16[1,72,256]{2,1,0:T(8,128)(2,1)S(1)} %bitcast.223), channel_id=1, source_target_pairs={{0,8},{1,9},{2,10},{3,11},{4,12},{5,13},{6,14},{7,15},{8,0},{9,1},... | collective-permute-start | bytes 110600 | tf_op jit(solution)/shard_map/ppermute | solution.py:567
  98.1 2.1 %shard_map.158 = (bf16[12,16,256]{2,1,0:T(8,128)(2,1)S(1)}, bf16[12,8,256]{2,1,0:T(8,128)(2,1)S(1)}, bf16[12,8,256]{2,1,0:T(8,128)(2,1)S(1)}) custom-call(s32[144]{0:T(256)S(1)} %reshape.56.adjacency, bf16[12,16,256]{2,1,0:T(8,128)(2,1)S(1)} %get-tuple-element.51.edges, bf16[12,16,256]{2,1,0:T(8,128)(2,1)S(1)} %collective-permute-done.9.beside, ...), custom_call_target="tpu_custom_call" | custom-call | flops 1000 | bytes 3000000 | tf_op jit(solution)/shard_map/pallas_call | solution.py:283
  101.2 3.1 %collective-permute-start.16 = (bf16[12,64,256]{2,1,0:T(8,128)(2,1)S(1)}, bf16[12,64,256]{2,1,0:T(8,128)(2,1)S(1)}, u32[]{:S(2)}, u32[]{:S(2)}) collective-permute-start(bf16[12,64,256]{2,1,0:T(8,128)(2,1)S(1)} %broadcast_select_fusion.refs_8_), channel_id=1, source_target_pairs={{0,1},{1,0},{30,31},{31,30}} | collective-permute-start | bytes 1179656 | tf_op jit(solution)/shard_map/ppermute | solution.py:262
  104.3 1.9 %collective-permute-start.17 = (bf16[12,64,256]{2,1,0:T(8,128)(2,1)S(1)}, bf16[12,64,256]{2,1,0:T(8,128)(2,1)S(1)}, u32[]{:S(2)}, u32[]{:S(2)}) collective-permute-start(bf16[12,64,256]{2,1,0:T(8,128)(2,1)S(1)} %broadcast_select_fusion.refs_8_), channel_id=1, source_target_pairs={{0,31},{1,30},{30,1},{31,0}} | collective-permute-start | bytes 1179656 | tf_op jit(solution)/shard_map/ppermute | solution.py:263
  106.4 11.1 %collective-permute-done.14.refs_6_ = bf16[12,8,256]{2,1,0:T(8,128)(2,1)S(1)} collective-permute-done((bf16[12,8,256]{2,1,0:T(8,128)(2,1)S(1)}, bf16[12,8,256]{2,1,0:T(8,128)(2,1)S(1)}, u32[]{:S(2)}, u32[]{:S(2)}) %collective-permute-start.14) | collective-permute-done | bytes 49184 | tf_op jit(solution)/shard_map/ppermute | solution.py:292
  117.5 1.7 %collective-permute-done.15.refs_7_ = bf16[12,8,256]{2,1,0:T(8,128)(2,1)S(1)} collective-permute-done((bf16[12,8,256]{2,1,0:T(8,128)(2,1)S(1)}, bf16[12,8,256]{2,1,0:T(8,128)(2,1)S(1)}, u32[]{:S(2)}, u32[]{:S(2)}) %collective-permute-start.15) | collective-permute-done | bytes 49184 | tf_op jit(solution)/shard_map/ppermute | solution.py:293
  119.2 2.4 %collective-permute-start.29 = (bf16[4,72,256]{2,1,0:T(8,128)(2,1)S(1)}, bf16[4,72,256]{2,1,0:T(8,128)(2,1)S(1)}, u32[]{:S(2)}, u32[]{:S(2)}) collective-permute-start(bf16[4,72,256]{2,1,0:T(8,128)(2,1)S(1)} %get-tuple-element.42), channel_id=1, source_target_pairs={{0,4},{1,5},{2,6},{3,7},{4,0},{5,1},{6,2},{7,3},{8,12},{9,13},{10,... | collective-permute-start | bytes 442376 | tf_op jit(solution)/shard_map/ppermute | solution.py:567
  122.7 2.0 %multiply_convert_fusion = bf16[12,4,32,256]{3,2,1,0:T(8,128)(2,1)} fusion(f32[256]{0:T(256)S(1)} %copy-done.16, f32[12,4,32,256]{3,0,2,1:T(8,128)S(1)} %copy-done.9), kind=kLoop, calls=%fused_computation.15 | loop fusion | flops 2359296 | bytes 2360320 | tf_op jit(solution)/shard_map/convert_element_type | solution.py:598
  124.7 10.0 %shard_map.159 = (bf16[12,8,36,256]{3,2,1,0:T(8,128)(2,1)S(1)}, f32[12,4,32,256]{3,2,1,0:T(8,128)S(1)}) custom-call(s32[144]{0:T(256)S(1)} %reshape.56.adjacency, bf16[12,4,32,256]{3,2,1,0:T(8,128)(2,1)S(1)} %get-tuple-element.21.refs_0_, bf16[12,16,256]{2,1,0:T(8,128)(2,1)S(1)} %get-tuple-element.15.refs_1_, ...), custom_call_target="tpu_custom_call" | custom-call | flops 1000 | bytes 8000000 | tf_op jit(solution)/shard_map/pallas_call | solution.py:472
  136.1 3.1 %fusion = f32[12,4,32,256]{3,0,2,1:T(8,128)S(1)} fusion(bf16[3,3,256,256]{3,2,1,0:T(8,128)(2,1)S(1)} %copy-done.12, bf16[12,8,36,256]{3,2,1,0:T(8,128)(2,1)S(1)} %get-tuple-element.18), kind=kOutput, calls=%fused_computation.1 | convolution fusion | flops 1811939328 | bytes 4521984 | tf_op jit(solution)/shard_map/conv_general_dilated | solution.py:624
  139.2 1.8 %fusion.10 = bf16[12,4,32,256]{3,2,1,0:T(8,128)(2,1)} fusion(f32[12,4,32,256]{3,2,1,0:T(8,128)S(1)} %get-tuple-element.19, f32[12,4,32,256]{3,0,2,1:T(8,128)S(1)} %fusion), kind=kLoop, calls=%fused_computation.13 | loop fusion | flops 786432 | bytes 3932160 | tf_op jit(solution)/shard_map/convert_element_type | solution.py:634
  142.0 1.6 %convert_multiply_fusion = f32[32,72,256]{2,1,0:T(8,128)} fusion(bf16[16,72,256]{2,1,0:T(8,128)(2,1)S(1)} %get-tuple-element.23, bf16[16,72,256]{2,1,0:T(8,128)(2,1)S(1)} %get-tuple-element.22), kind=kLoop, calls=%fused_computation.5 | loop fusion | flops 1769472 | bytes 3538944 | tf_op jit(solution)/shard_map/mul | solution.py:619
  (127 shorter events, 24.8 us)
Async XLA Ops:
  4.0 46.1 %collective-permute-start.7 = (bf16[12,64,256]{2,1,0:T(8,128)(2,1)S(1)}, bf16[12,64,256]{2,1,0:T(8,128)(2,1)S(1)}, u32[]{:S(2)}, u32[]{:S(2)}) collective-permute-start(bf16[12,64,256]{2,1,0:T(8,128)(2,1)S(1)} %broadcast_select_fusion.1.refs_8_), channel_id=1, source_target_pairs={{0,1},{1,0},{30,31},{31,30}} | collective-permute-start | bytes 1179656 | tf_op jit(solution)/shard_map/ppermute | solution.py:262
  8.9 41.3 %collective-permute-start.8 = (bf16[12,64,256]{2,1,0:T(8,128)(2,1)S(1)}, bf16[12,64,256]{2,1,0:T(8,128)(2,1)S(1)}, u32[]{:S(2)}, u32[]{:S(2)}) collective-permute-start(bf16[12,64,256]{2,1,0:T(8,128)(2,1)S(1)} %broadcast_select_fusion.1.refs_8_), channel_id=1, source_target_pairs={{0,31},{1,30},{30,1},{31,0}} | collective-permute-start | bytes 1179656 | tf_op jit(solution)/shard_map/ppermute | solution.py:263
  14.5 35.7 %collective-permute-start.3 = (bf16[12,64,256]{2,1,0:T(8,128)(2,1)}, bf16[12,64,256]{2,1,0:T(8,128)(2,1)S(1)}, u32[]{:S(2)}, u32[]{:S(2)}) collective-permute-start(bf16[12,64,256]{2,1,0:T(8,128)(2,1)} %bitcast), channel_id=1, source_target_pairs={{0,2},{1,3},{2,4},{3,5},{4,6},{5,7},{6,8},{7,9},{8,10},{9,11},{10,... | collective-permute-start | bytes 1179656 | tf_op jit(solution)/shard_map/ppermute | solution.py:264
  14.5 35.6 %collective-permute-start.4 = (bf16[12,64,256]{2,1,0:T(8,128)(2,1)}, bf16[12,64,256]{2,1,0:T(8,128)(2,1)S(1)}, u32[]{:S(2)}, u32[]{:S(2)}) collective-permute-start(bf16[12,64,256]{2,1,0:T(8,128)(2,1)} %bitcast.1), channel_id=1, source_target_pairs={{0,30},{1,31},{2,0},{3,1},{4,2},{5,3},{6,4},{7,5},{8,6},{9,7},{10,... | collective-permute-start | bytes 1179656 | tf_op jit(solution)/shard_map/ppermute | solution.py:265
  19.2 7.7 %collective-permute-start.1 = (bf16[12,8,256]{2,1,0:T(8,128)(2,1)S(1)}, bf16[12,8,256]{2,1,0:T(8,128)(2,1)S(1)}, u32[]{:S(2)}, u32[]{:S(2)}) collective-permute-start(bf16[12,8,256]{2,1,0:T(8,128)(2,1)S(1)} %get-tuple-element.52), channel_id=1, source_target_pairs={{0,30},{1,31},{2,28},{3,29},{4,26},{5,27},{6,24},{7,25},{8,22},{9,... | collective-permute-start | bytes 147464 | tf_op jit(solution)/shard_map/ppermute | solution.py:280
  26.8 7.1 %collective-permute-start.2 = (bf16[12,8,256]{2,1,0:T(8,128)(2,1)S(1)}, bf16[12,8,256]{2,1,0:T(8,128)(2,1)S(1)}, u32[]{:S(2)}, u32[]{:S(2)}) collective-permute-start(bf16[12,8,256]{2,1,0:T(8,128)(2,1)S(1)} %get-tuple-element.52), channel_id=1, source_target_pairs={{0,31},{1,30},{2,29},{3,28},{4,27},{5,26},{6,25},{7,24},{8,23},{9,... | collective-permute-start | bytes 147464 | tf_op jit(solution)/shard_map/ppermute | solution.py:281
  34.5 4.6 %collective-permute-start = (bf16[12,16,256]{2,1,0:T(8,128)(2,1)S(1)}, bf16[12,16,256]{2,1,0:T(8,128)(2,1)S(1)}, u32[]{:S(2)}, u32[]{:S(2)}) collective-permute-start(bf16[12,16,256]{2,1,0:T(8,128)(2,1)S(1)} %get-tuple-element.53.edges), channel_id=1, source_target_pairs={{0,1},{1,0},{2,3},{3,2},{4,5},{5,4},{6,7},{7,6},{8,9},{9,8},{10,11... | collective-permute-start | bytes 294920 | tf_op jit(solution)/shard_map/ppermute | solution.py:270
  42.1 6.3 %collective-permute-start.5 = (bf16[12,8,256]{2,1,0:T(8,128)(2,1)S(1)}, bf16[12,8,256]{2,1,0:T(8,128)(2,1)S(1)}, u32[]{:S(2)}, u32[]{:S(2)}) collective-permute-start(bf16[12,8,256]{2,1,0:T(8,128)(2,1)S(1)} %get-tuple-element.14.refs_3_), channel_id=1, source_target_pairs={{0,2},{1,3},{2,4},{3,5},{4,6},{5,7},{6,8},{7,9},{8,10},{9,11},{10,... | collective-permute-start | bytes 147464 | tf_op jit(solution)/shard_map/ppermute | solution.py:292
  48.4 1.8 %collective-permute-start.6 = (bf16[12,8,256]{2,1,0:T(8,128)(2,1)S(1)}, bf16[12,8,256]{2,1,0:T(8,128)(2,1)S(1)}, u32[]{:S(2)}, u32[]{:S(2)}) collective-permute-start(bf16[12,8,256]{2,1,0:T(8,128)(2,1)S(1)} %get-tuple-element.13.refs_2_), channel_id=1, source_target_pairs={{0,30},{1,31},{2,0},{3,1},{4,2},{5,3},{6,4},{7,5},{8,6},{9,7},{10,... | collective-permute-start | bytes 147464 | tf_op jit(solution)/shard_map/ppermute | solution.py:293
  64.3 2.4 %collective-permute-start.18 = (bf16[1160,256]{1,0:T(8,128)(2,1)}, bf16[1160,256]{1,0:T(8,128)(2,1)}, u32[]{:S(2)}, u32[]{:S(2)}) collective-permute-start(bf16[1160,256]{1,0:T(8,128)(2,1)} %pad_maximum_fusion), channel_id=1, source_target_pairs={{0,2},{1,3},{2,0},{3,1},{4,6},{5,7},{6,4},{7,5},{8,10},{9,11},{10,... | collective-permute-start | bytes 1781768 | tf_op jit(solution)/shard_map/ppermute | solution.py:554
  68.8 8.3 %collective-permute-start.21 = (bf16[296,256]{1,0:T(8,128)(2,1)S(1)}, bf16[296,256]{1,0:T(8,128)(2,1)S(1)}, u32[]{:S(2)}, u32[]{:S(2)}) collective-permute-start(bf16[296,256]{1,0:T(8,128)(2,1)S(1)} %get-tuple-element.59), channel_id=1, source_target_pairs={{0,5},{1,4},{2,7},{3,6},{4,1},{5,0},{6,3},{7,2},{8,13},{9,12},{10,... | collective-permute-start | bytes 454664 | tf_op jit(solution)/shard_map/ppermute | solution.py:554
  68.9 10.5 %collective-permute-start.20 = (bf16[296,256]{1,0:T(8,128)(2,1)S(1)}, bf16[296,256]{1,0:T(8,128)(2,1)S(1)}, u32[]{:S(2)}, u32[]{:S(2)}) collective-permute-start(bf16[296,256]{1,0:T(8,128)(2,1)S(1)} %get-tuple-element.58), channel_id=1, source_target_pairs={{0,4},{1,5},{2,6},{3,7},{4,0},{5,1},{6,2},{7,3},{8,12},{9,13},{10,... | collective-permute-start | bytes 454664 | tf_op jit(solution)/shard_map/ppermute | solution.py:554
  71.2 8.3 %collective-permute-start.19 = (bf16[296,256]{1,0:T(8,128)(2,1)S(1)}, bf16[296,256]{1,0:T(8,128)(2,1)S(1)}, u32[]{:S(2)}, u32[]{:S(2)}) collective-permute-start(bf16[296,256]{1,0:T(8,128)(2,1)S(1)} %get-tuple-element.57), channel_id=1, source_target_pairs={{0,1},{1,0},{2,3},{3,2},{4,5},{5,4},{6,7},{7,6},{8,9},{9,8},{10,11... | collective-permute-start | bytes 454664 | tf_op jit(solution)/shard_map/ppermute | solution.py:554
  72.4 21.1 %collective-permute-start.10 = (bf16[12,8,256]{2,1,0:T(8,128)(2,1)S(1)}, bf16[12,8,256]{2,1,0:T(8,128)(2,1)S(1)}, u32[]{:S(2)}, u32[]{:S(2)}) collective-permute-start(bf16[12,8,256]{2,1,0:T(8,128)(2,1)S(1)} %get-tuple-element.50), channel_id=1, source_target_pairs={{0,30},{1,31},{2,28},{3,29},{4,26},{5,27},{6,24},{7,25},{8,22},{9,... | collective-permute-start | bytes 147464 | tf_op jit(solution)/shard_map/ppermute | solution.py:280
  76.1 18.3 %collective-permute-start.11 = (bf16[12,8,256]{2,1,0:T(8,128)(2,1)S(1)}, bf16[12,8,256]{2,1,0:T(8,128)(2,1)S(1)}, u32[]{:S(2)}, u32[]{:S(2)}) collective-permute-start(bf16[12,8,256]{2,1,0:T(8,128)(2,1)S(1)} %get-tuple-element.50), channel_id=1, source_target_pairs={{0,31},{1,30},{2,29},{3,28},{4,27},{5,26},{6,25},{7,24},{8,23},{9,... | collective-permute-start | bytes 147464 | tf_op jit(solution)/shard_map/ppermute | solution.py:281
  79.6 6.8 %collective-permute-start.24 = (bf16[80,256]{1,0:T(8,128)(2,1)S(1)}, bf16[80,256]{1,0:T(8,128)(2,1)S(1)}, u32[]{:S(2)}, u32[]{:S(2)}) collective-permute-start(bf16[80,256]{1,0:T(8,128)(2,1)S(1)} %get-tuple-element.56), channel_id=1, source_target_pairs={{0,24},{1,25},{2,26},{3,27},{4,28},{5,29},{6,30},{7,31},{8,16},{9,... | collective-permute-start | bytes 122888 | tf_op jit(solution)/shard_map/ppermute | solution.py:554
  84.2 4.9 %collective-permute-start.23 = (bf16[80,256]{1,0:T(8,128)(2,1)S(1)}, bf16[80,256]{1,0:T(8,128)(2,1)S(1)}, u32[]{:S(2)}, u32[]{:S(2)}) collective-permute-start(bf16[80,256]{1,0:T(8,128)(2,1)S(1)} %get-tuple-element.55), channel_id=1, source_target_pairs={{0,16},{1,17},{2,18},{3,19},{4,20},{5,21},{6,22},{7,23},{8,24},{9,... | collective-permute-start | bytes 122888 | tf_op jit(solution)/shard_map/ppermute | solution.py:554
  84.2 4.9 %collective-permute-start.22 = (bf16[80,256]{1,0:T(8,128)(2,1)S(1)}, bf16[80,256]{1,0:T(8,128)(2,1)S(1)}, u32[]{:S(2)}, u32[]{:S(2)}) collective-permute-start(bf16[80,256]{1,0:T(8,128)(2,1)S(1)} %get-tuple-element.54), channel_id=1, source_target_pairs={{0,8},{1,9},{2,10},{3,11},{4,12},{5,13},{6,14},{7,15},{8,0},{9,1},... | collective-permute-start | bytes 122888 | tf_op jit(solution)/shard_map/ppermute | solution.py:554
  86.4 8.0 %collective-permute-start.9 = (bf16[12,16,256]{2,1,0:T(8,128)(2,1)S(1)}, bf16[12,16,256]{2,1,0:T(8,128)(2,1)S(1)}, u32[]{:S(2)}, u32[]{:S(2)}) collective-permute-start(bf16[12,16,256]{2,1,0:T(8,128)(2,1)S(1)} %get-tuple-element.51.edges), channel_id=1, source_target_pairs={{0,1},{1,0},{2,3},{3,2},{4,5},{5,4},{6,7},{7,6},{8,9},{9,8},{10,11... | collective-permute-start | bytes 294920 | tf_op jit(solution)/shard_map/ppermute | solution.py:270
  89.1 30.1 %collective-permute-start.12 = (bf16[12,64,256]{2,1,0:T(8,128)(2,1)S(1)}, bf16[12,64,256]{2,1,0:T(8,128)(2,1)S(1)}, u32[]{:S(2)}, u32[]{:S(2)}) collective-permute-start(bf16[12,64,256]{2,1,0:T(8,128)(2,1)S(1)} %bitcast.212), channel_id=1, source_target_pairs={{0,2},{1,3},{2,4},{3,5},{4,6},{5,7},{6,8},{7,9},{8,10},{9,11},{10,... | collective-permute-start | bytes 1179656 | tf_op jit(solution)/shard_map/ppermute | solution.py:264
  89.1 32.5 %collective-permute-start.13 = (bf16[12,64,256]{2,1,0:T(8,128)(2,1)S(1)}, bf16[12,64,256]{2,1,0:T(8,128)(2,1)S(1)}, u32[]{:S(2)}, u32[]{:S(2)}) collective-permute-start(bf16[12,64,256]{2,1,0:T(8,128)(2,1)S(1)} %bitcast.211), channel_id=1, source_target_pairs={{0,30},{1,31},{2,0},{3,1},{4,2},{5,3},{6,4},{7,5},{8,6},{9,7},{10,... | collective-permute-start | bytes 1179656 | tf_op jit(solution)/shard_map/ppermute | solution.py:265
  93.6 7.7 %collective-permute-start.27 = (bf16[1,72,256]{2,1,0:T(8,128)(2,1)S(1)}, bf16[1,72,256]{2,1,0:T(8,128)(2,1)S(1)}, u32[]{:S(2)}, u32[]{:S(2)}) collective-permute-start(bf16[1,72,256]{2,1,0:T(8,128)(2,1)S(1)} %bitcast.221), channel_id=1, source_target_pairs={{0,24},{1,25},{2,26},{3,27},{4,28},{5,29},{6,30},{7,31},{8,16},{9,... | collective-permute-start | bytes 110600 | tf_op jit(solution)/shard_map/ppermute | solution.py:567
  94.4 9.9 %collective-permute-start.26 = (bf16[1,72,256]{2,1,0:T(8,128)(2,1)S(1)}, bf16[1,72,256]{2,1,0:T(8,128)(2,1)S(1)}, u32[]{:S(2)}, u32[]{:S(2)}) collective-permute-start(bf16[1,72,256]{2,1,0:T(8,128)(2,1)S(1)} %bitcast.222), channel_id=1, source_target_pairs={{0,16},{1,17},{2,18},{3,19},{4,20},{5,21},{6,22},{7,23},{8,24},{9,... | collective-permute-start | bytes 110600 | tf_op jit(solution)/shard_map/ppermute | solution.py:567
  94.4 11.9 %collective-permute-start.25 = (bf16[1,72,256]{2,1,0:T(8,128)(2,1)S(1)}, bf16[1,72,256]{2,1,0:T(8,128)(2,1)S(1)}, u32[]{:S(2)}, u32[]{:S(2)}) collective-permute-start(bf16[1,72,256]{2,1,0:T(8,128)(2,1)S(1)} %bitcast.223), channel_id=1, source_target_pairs={{0,8},{1,9},{2,10},{3,11},{4,12},{5,13},{6,14},{7,15},{8,0},{9,1},... | collective-permute-start | bytes 110600 | tf_op jit(solution)/shard_map/ppermute | solution.py:567
  101.2 23.5 %collective-permute-start.16 = (bf16[12,64,256]{2,1,0:T(8,128)(2,1)S(1)}, bf16[12,64,256]{2,1,0:T(8,128)(2,1)S(1)}, u32[]{:S(2)}, u32[]{:S(2)}) collective-permute-start(bf16[12,64,256]{2,1,0:T(8,128)(2,1)S(1)} %broadcast_select_fusion.refs_8_), channel_id=1, source_target_pairs={{0,1},{1,0},{30,31},{31,30}} | collective-permute-start | bytes 1179656 | tf_op jit(solution)/shard_map/ppermute | solution.py:262
  104.3 20.4 %collective-permute-start.17 = (bf16[12,64,256]{2,1,0:T(8,128)(2,1)S(1)}, bf16[12,64,256]{2,1,0:T(8,128)(2,1)S(1)}, u32[]{:S(2)}, u32[]{:S(2)}) collective-permute-start(bf16[12,64,256]{2,1,0:T(8,128)(2,1)S(1)} %broadcast_select_fusion.refs_8_), channel_id=1, source_target_pairs={{0,31},{1,30},{30,1},{31,0}} | collective-permute-start | bytes 1179656 | tf_op jit(solution)/shard_map/ppermute | solution.py:263
  106.2 11.2 %collective-permute-start.14 = (bf16[12,8,256]{2,1,0:T(8,128)(2,1)S(1)}, bf16[12,8,256]{2,1,0:T(8,128)(2,1)S(1)}, u32[]{:S(2)}, u32[]{:S(2)}) collective-permute-start(bf16[12,8,256]{2,1,0:T(8,128)(2,1)S(1)} %get-tuple-element.17.refs_3_), channel_id=1, source_target_pairs={{0,2},{1,3},{2,4},{3,5},{4,6},{5,7},{6,8},{7,9},{8,10},{9,11},{10,... | collective-permute-start | bytes 147464 | tf_op jit(solution)/shard_map/ppermute | solution.py:292
  117.5 1.8 %collective-permute-start.15 = (bf16[12,8,256]{2,1,0:T(8,128)(2,1)S(1)}, bf16[12,8,256]{2,1,0:T(8,128)(2,1)S(1)}, u32[]{:S(2)}, u32[]{:S(2)}) collective-permute-start(bf16[12,8,256]{2,1,0:T(8,128)(2,1)S(1)} %get-tuple-element.16.refs_2_), channel_id=1, source_target_pairs={{0,30},{1,31},{2,0},{3,1},{4,2},{5,3},{6,4},{7,5},{8,6},{9,7},{10,... | collective-permute-start | bytes 147464 | tf_op jit(solution)/shard_map/ppermute | solution.py:293
  119.2 15.5 %collective-permute-start.30 = (bf16[4,72,256]{2,1,0:T(8,128)(2,1)S(1)}, bf16[4,72,256]{2,1,0:T(8,128)(2,1)S(1)}, u32[]{:S(2)}, u32[]{:S(2)}) collective-permute-start(bf16[4,72,256]{2,1,0:T(8,128)(2,1)S(1)} %get-tuple-element.42), channel_id=1, source_target_pairs={{0,5},{1,4},{2,7},{3,6},{4,1},{5,0},{6,3},{7,2},{8,13},{9,12},{10,... | collective-permute-start | bytes 442376 | tf_op jit(solution)/shard_map/ppermute | solution.py:567
  119.2 15.5 %collective-permute-start.29 = (bf16[4,72,256]{2,1,0:T(8,128)(2,1)S(1)}, bf16[4,72,256]{2,1,0:T(8,128)(2,1)S(1)}, u32[]{:S(2)}, u32[]{:S(2)}) collective-permute-start(bf16[4,72,256]{2,1,0:T(8,128)(2,1)S(1)} %get-tuple-element.42), channel_id=1, source_target_pairs={{0,4},{1,5},{2,6},{3,7},{4,0},{5,1},{6,2},{7,3},{8,12},{9,13},{10,... | collective-permute-start | bytes 442376 | tf_op jit(solution)/shard_map/ppermute | solution.py:567
  121.6 13.1 %collective-permute-start.28 = (bf16[4,72,256]{2,1,0:T(8,128)(2,1)S(1)}, bf16[4,72,256]{2,1,0:T(8,128)(2,1)S(1)}, u32[]{:S(2)}, u32[]{:S(2)}) collective-permute-start(bf16[4,72,256]{2,1,0:T(8,128)(2,1)S(1)} %get-tuple-element.42), channel_id=1, source_target_pairs={{0,1},{1,0},{2,3},{3,2},{4,5},{5,4},{6,7},{7,6},{8,9},{9,8},{10,11... | collective-permute-start | bytes 442376 | tf_op jit(solution)/shard_map/ppermute | solution.py:567
  135.0 6.5 %collective-permute-start.31 = (bf16[16,72,256]{2,1,0:T(8,128)(2,1)S(1)}, bf16[16,72,256]{2,1,0:T(8,128)(2,1)S(1)}, u32[]{:S(2)}, u32[]{:S(2)}) collective-permute-start(bf16[16,72,256]{2,1,0:T(8,128)(2,1)S(1)} %get-tuple-element.32), channel_id=1, source_target_pairs={{0,2},{1,3},{2,0},{3,1},{4,6},{5,7},{6,4},{7,5},{8,10},{9,11},{10,... | collective-permute-start | bytes 1769480 | tf_op jit(solution)/shard_map/ppermute | solution.py:567
  (17 other events, 271.7 us)

commit v6 on v5

--- a/solution.py
+++ b/solution.py
@@ -181,47 +181,78 @@
         lower_out[face] = pick(lower_pick, jnp.where(at_bottom, inner, sides))
 
 
-def load_stack(adjacency, face, strips, flips, corners, stack):
-    field, sides, tails, up, down, up_tail, down_tail, edge, far_same, far_cross = strips[:10]
+def col_kernel(
+    adjacency, field, edges, beside, far_same, far_cross, side_out, top_out, bottom_out, edge_out,
+    upper, lower, seam,
+):
+    face_count, tile_rows, width, channels = field.shape
+    at_top = lax.axis_index("frow") == 0
+    side_kernel(adjacency, edges, beside, far_same, far_cross, side_out, upper, lower, seam)
+    for face in range(face_count):
+        for d in range(2):
+            rows = pl.ds(d * width, width)
+            first, last = field[face, d], field[face, tile_rows - 2 + d]
+            top_out[face, rows] = first
+            bottom_out[face, rows] = last
+            edge_out[face, rows] = jnp.where(at_top, first, last)
+        rows = pl.ds(2 * width, 8)
+        top_out[face, rows] = upper[face]
+        bottom_out[face, rows] = lower[face]
+        edge_out[face, rows] = jnp.where(at_top, upper[face], lower[face])
+
+
+def joint_readers(up, down, edge, far_same, far_cross):
+    def reader(ref):
+        return lambda source: ref[source]
+
+    return [[reader(ref) for ref in (near, edge, far_cross, far_same)] for near in (up, down)]
+
+
+def split_readers(
+    upper, lower, up, down, up_tail, down_tail, edge, far_same, far_cross, corners,
+    same_tail=None, cross_tail=None,
+):
+    def reader(main, tail):
+        return lambda source: jnp.concatenate([main[source], tail[source]], 0)
+
+    def corner_reader(main, other):
+        def read(source):
+            tail = pick(corners[1 - lax.axis_index("fcol")], other[source])
+            return jnp.concatenate([main[source], tail], 0)
+
+        return read
+
+    readers = []
+    for near, near_tail, own_tail in ((up, up_tail, upper), (down, down_tail, lower)):
+        readers.append([reader(near, near_tail), reader(edge, own_tail)])
+        if same_tail is None:
+            readers[-1] += [corner_reader(far_cross, near), corner_reader(far_same, edge)]
+        else:
+            readers[-1] += [reader(far_cross, cross_tail), reader(far_same, same_tail)]
+    return readers
+
+
+def load_stack(adjacency, face, field, sides, readers, flips, stack):
     tile_rows, width, channels = field.shape[1:]
     strip = 2 * width + 8
     beside, above, below, _ = stack_places(tile_rows, width)
-    row_place, col_place = lax.axis_index("frow"), lax.axis_index("fcol")
+    row_place = lax.axis_index("frow")
     stack[face, pl.ds(0, beside)] = field[face].reshape(beside, channels)
     stack[face, pl.ds(beside, 4 * tile_rows)] = sides[face]
-    for side, place, near, near_tail in (
-        (0, above, up, up_tail), (1, below, down, down_tail),
-    ):
+    for side, place in ((0, above), (1, below)):
         at_edge = row_place == side * (lax.axis_size("frow") - 1)
         rows = pl.ds(place, strip)
 
         @pl.when(jnp.logical_not(at_edge))
         def _():
-            stack[face, pl.ds(place, 2 * width)] = near[face]
-            stack[face, pl.ds(place + 2 * width, 8)] = near_tail[face]
+            stack[face, rows] = readers[side][0](face)
 
         source, kind = seam_of(adjacency, face, side)
-        for choice, main in enumerate((near, edge, far_cross, far_same)):
+        for choice, read in enumerate(readers[side]):
 
             @pl.when(jnp.logical_and(at_edge, kind == choice))
             def _():
-                if choice == 0:
-                    tail = near_tail[source]
-                elif choice == 1:
-                    tail = tails[side][source]
-                elif len(strips) > 10:
-                    tail = strips[13 - choice][source]
-                else:
-                    other = near if choice == 2 else edge
-                    tail = pick(corners[1 - col_place], other[source])
-                stack[face, rows] = pick(
-                    flips[choice], jnp.concatenate([main[source], tail], 0)
-                )
-
-
-def unpack_strips(refs, count):
-    strips = list(refs[:count])
-    return (strips[0], strips[1], (strips[2], strips[3]), *strips[4:])
+                stack[face, rows] = pick(flips[choice], read(source))
 
 
 def write_padded(picks, stack, padded):
@@ -233,15 +264,14 @@
             padded[face, q] = out[q * step : q * step + breadth]
 
 
-def pad_kernel(count, adjacency, *refs):
-    strips = unpack_strips(refs, count)
-    flips, corners, picks, padded, stack = refs[count:]
-    face_count = strips[0].shape[0]
+def pad_kernel(adjacency, flips, picks, field, sides, *refs):
+    padded, stack = refs[-2:]
+    readers = split_readers(*refs[:-2])
     stack[...] = jnp.zeros_like(stack)
 
-    @pl.loop(0, face_count)
+    @pl.loop(0, field.shape[0])
     def _(face):
-        load_stack(adjacency, face, strips, flips, corners, stack)
+        load_stack(adjacency, face, field, sides, readers, flips, stack)
 
     write_padded(picks, stack, padded)
 
@@ -252,21 +282,12 @@
     ]
 
 
-def gather_strips(field, adjacency):
+def exchange_cols(field):
     face_count, tile_rows, width, channels = field.shape
-    cols = lax.axis_size("fcol")
-    at_top = lax.axis_index("frow") == 0
-    top = field[:, :2].reshape(face_count, 2 * width, channels)
-    bottom = field[:, tile_rows - 2 :].reshape(face_count, 2 * width, channels)
-    edge_strip = jnp.where(at_top, top, bottom)
-    row_same = lax.ppermute(edge_strip, axes, mirror_pairs(True, False, True))
-    row_cross = lax.ppermute(edge_strip, axes, mirror_pairs(True, True, True))
-    up = lax.ppermute(bottom, axes, shifted_pairs(1, 0))
-    down = lax.ppermute(top, axes, shifted_pairs(-1, 0))
     left = field[:, :, :2].reshape(face_count, 2 * tile_rows, channels)
     right = field[:, :, width - 2 :].reshape(face_count, 2 * tile_rows, channels)
     edges = jnp.concatenate([left, right], 1)
-    if cols == 2:
+    if lax.axis_size("fcol") == 2:
         beside = lax.ppermute(edges, axes, shifted_pairs(0, 1))
     else:
         beside = jnp.concatenate(
@@ -279,42 +300,93 @@
     edge = jnp.where(lax.axis_index("fcol") == 0, left, right)
     far_same = lax.ppermute(edge, axes, mirror_pairs(False, True, False))
     far_cross = lax.ppermute(edge, axes, mirror_pairs(False, True, True))
-    tail = jax.ShapeDtypeStruct((face_count, 8, channels), field.dtype)
-    sides, upper, lower = pl.pallas_call(
-        side_kernel,
-        out_shape=(jax.ShapeDtypeStruct(edges.shape, field.dtype), tail, tail),
-        in_specs=whole(4),
-        out_specs=[pl.BlockSpec(memory_space=pltpu.VMEM)] * 3,
-        scratch_shapes=[pltpu.VMEM((face_count, 2 * tile_rows, channels), field.dtype)],
+    return (edges, beside, far_same, far_cross)
+
+
+def exchange_rows(top, bottom, edge):
+    up = lax.ppermute(bottom, axes, shifted_pairs(1, 0))
+    down = lax.ppermute(top, axes, shifted_pairs(-1, 0))
+    if edge is None:
+        return (up, down)
+    row_same = lax.ppermute(edge, axes, mirror_pairs(True, False, True))
+    row_cross = lax.ppermute(edge, axes, mirror_pairs(True, True, True))
+    return (up, down, row_same, row_cross)
+
+
+def side_call(body, field, inputs, outputs, scratch):
+    face_count, tile_rows, _, channels = field.shape
+    scratch = [*scratch, (face_count, 2 * tile_rows, channels)]
+    return pl.pallas_call(
+        body,
+        out_shape=[jax.ShapeDtypeStruct(shape, field.dtype) for shape in outputs],
+        in_specs=whole(len(inputs) - 1),
+        out_specs=[pl.BlockSpec(memory_space=pltpu.VMEM) for _ in outputs],
+        scratch_shapes=[pltpu.VMEM(shape, field.dtype) for shape in scratch],
         compiler_params=pltpu.CompilerParams(vmem_limit_bytes=vmem_bytes),
         cost_estimate=pl.CostEstimate(flops=1000, bytes_accessed=3000000, transcendentals=0),
-    )(adjacency, edges, beside, far_same, far_cross)
-    up_tail = lax.ppermute(lower, axes, shifted_pairs(1, 0))
-    down_tail = lax.ppermute(upper, axes, shifted_pairs(-1, 0))
+    )(*inputs)
+
+
+def joint_strips(field, adjacency):
+    face_count, tile_rows, width, channels = field.shape
+    cols = exchange_cols(field)
+    strip = (face_count, 2 * width + 8, channels)
+    tail = (face_count, 8, channels)
+    sides, top, bottom, edge = side_call(
+        col_kernel,
+        field,
+        (adjacency, field, *cols),
+        (cols[0].shape, strip, strip, strip),
+        (tail, tail),
+    )
+    up, down, row_same, row_cross = exchange_rows(top, bottom, edge)
+    return (field, sides, up, down, edge, row_same, row_cross)
+
+
+def split_strips(field, adjacency):
+    face_count, tile_rows, width, channels = field.shape
+    edges, beside, far_same, far_cross = exchange_cols(field)
+    at_top = lax.axis_index("frow") == 0
+    later, beside, far_same, far_cross = lax.optimization_barrier(
+        (field, beside, far_same, far_cross)
+    )
+    top = later[:, :2].reshape(face_count, 2 * width, channels)
+    bottom = later[:, tile_rows - 2 :].reshape(face_count, 2 * width, channels)
+    edge = jnp.where(at_top, top, bottom)
+    up, down, row_same, row_cross = exchange_rows(top, bottom, edge)
+    tail = (face_count, 8, channels)
+    sides, upper, lower = side_call(
+        side_kernel,
+        field,
+        (adjacency, edges, beside, far_same, far_cross),
+        (edges.shape, tail, tail),
+        (),
+    )
+    up_tail, down_tail = exchange_rows(upper, lower, None)
     strips = [
-        field, sides, upper, lower, up, down, up_tail, down_tail, edge_strip, row_same, row_cross,
+        field, sides, upper, lower, up, down, up_tail, down_tail, edge, row_same, row_cross,
+        corner_picks(width),
     ]
-    if cols > 2:
+    if lax.axis_size("fcol") > 2:
         own_tail = jnp.where(at_top, upper, lower)
-        strips.append(lax.ppermute(own_tail, axes, mirror_pairs(True, False, True)))
-        strips.append(lax.ppermute(own_tail, axes, mirror_pairs(True, True, True)))
+        strips += exchange_rows(upper, lower, own_tail)[2:]
     return strips
 
 
 def pad_field(field, adjacency):
     face_count, tile_rows, width, channels = field.shape
-    strips = gather_strips(field, adjacency)
+    strips = split_strips(field, adjacency)
     padded = (face_count, tile_rows + 4, width + 4, channels)
     size = stack_places(tile_rows, width)[3]
     return pl.pallas_call(
-        functools.partial(pad_kernel, len(strips)),
+        pad_kernel,
         out_shape=jax.ShapeDtypeStruct(padded, field.dtype),
-        in_specs=whole(len(strips) + 3),
+        in_specs=whole(len(strips) + 2),
         out_specs=pl.BlockSpec(memory_space=pltpu.VMEM),
         scratch_shapes=[pltpu.VMEM((face_count, size, channels), field.dtype)],
         compiler_params=pltpu.CompilerParams(vmem_limit_bytes=vmem_bytes),
         cost_estimate=pl.CostEstimate(flops=1000, bytes_accessed=5000000, transcendentals=0),
-    )(adjacency, *strips, row_flips(width), corner_picks(width), pad_picks(tile_rows, width))
+    )(adjacency, row_flips(width), pad_picks(tile_rows, width), *strips)
 
 
 def seam_row_picks(width):
@@ -348,11 +420,11 @@
     return jnp.asarray(table, jnp.bfloat16)
 
 
-def return_kernel(count, adjacency, *refs):
-    strips = unpack_strips(refs, count)
-    flips, corners, picks, row_picks, col_picks, rotated, padded, extra = refs[count : count + 8]
-    stack, kept_picks, row_terms, col_terms, col_sum = refs[count + 8 :]
-    field = strips[0]
+def return_kernel(
+    adjacency, flips, picks, row_picks, col_picks, rotated, field, sides, up, down, edge,
+    far_same, far_cross, padded, extra, stack, kept_picks, row_terms, col_terms, col_sum,
+):
+    readers = joint_readers(up, down, edge, far_same, far_cross)
     face_count, tile_rows, width, channels = field.shape
     breadth = picks.shape[0] // (tile_rows + 4)
     half = 2 * tile_rows
@@ -384,7 +456,7 @@
 
     @pl.loop(0, face_count)
     def _(face):
-        load_stack(adjacency, face, strips, flips, corners, stack)
+        load_stack(adjacency, face, field, sides, readers, flips, stack)
 
     write_padded(kept_picks, stack, padded)
 
@@ -464,18 +536,18 @@
 
 def return_field(field, adjacency, rotated):
     face_count, tile_rows, width, channels = field.shape
-    strips = gather_strips(field, adjacency)
+    strips = joint_strips(field, adjacency)
     padded = (face_count, tile_rows + 4, width + 4, channels)
     size = stack_places(tile_rows, width)[3]
     picks = pad_picks(tile_rows, width)
     cells = face_count * round_up(2 * tile_rows, 16)
     return pl.pallas_call(
-        functools.partial(return_kernel, len(strips)),
+        return_kernel,
         out_shape=(
             jax.ShapeDtypeStruct(padded, field.dtype),
             jax.ShapeDtypeStruct(field.shape, jnp.float32),
         ),
-        in_specs=whole(len(strips) + 6),
+        in_specs=whole(len(strips) + 5),
         out_specs=[pl.BlockSpec(memory_space=pltpu.VMEM)] * 2,
         scratch_shapes=[
             pltpu.VMEM((face_count, size, channels), field.dtype),
@@ -487,9 +559,9 @@
         compiler_params=pltpu.CompilerParams(vmem_limit_bytes=vmem_bytes),
         cost_estimate=pl.CostEstimate(flops=1000, bytes_accessed=8000000, transcendentals=0),
     )(
-        adjacency, *strips, row_flips(width), corner_picks(width), picks,
+        adjacency, row_flips(width), picks,
         seam_row_picks(width).reshape(6 * width, -1),
-        seam_col_picks(tile_rows, width), rotated,
+        seam_col_picks(tile_rows, width), rotated, *strips,
     )
 
 

time: 144 us -> 128 us (0.89)
  waiting for transfers between devices: 40.9 us -> 29.8 us
  starting transfers between devices: 53.1 us -> 48.8 us
    ppermute x18 -> x16, waiting for transfers between devices: 34.1 us -> 22 us  [the longest x3 7.74 us: exchange_rows(): up = lax.ppermute(bottom, axes, shifted_pairs(1, 0))]
    ppermute x18 -> x16, starting transfers between devices: 36.3 us -> 31.9 us  [the longest x3 7.92 us: exchange_rows(): down = lax.ppermute(top, axes, shifted_pairs(-1, 0))]
    ppermute x7, waiting for transfers between devices: 0.99 us -> 4.55 us  [reduce_everywhere(): lax.ppermute(part, axes, [(i, i ^ offset) for i in range(count)])]
    ppermute x7, waiting for transfers between devices: 5.88 us -> 3.23 us  [reduce_everywhere(): packed = lax.ppermute(packed, axes, [(i, i ^ offset) for i in range(count)])]
    slice x4 -> x3, local copies, waits for them, and re-layouts: 2.38 us -> 3.28 us  [the longest x1 2.09 us: split_strips(): top = later[:, :2].reshape(face_count, 2 * width, channels)]
    unnamed x38 -> x34, local copies, waits for them, and re-layouts: 4.34 us -> 3.59 us
  transfers between devices with their start and end apart: 32 -> 30, of which waited for: 12 -> 9; matrix products, arithmetic and copies ran while one was open for 6% -> 8% of each run, Pallas kernels for 10% -> 11%
where the time goes in v6:
time: 128 us; the launch traced here: 127 us
  starting transfers between devices  48.8 us (38%)
  waiting for transfers between devices  29.8 us (23%)
  Pallas kernels  18.6 us (15%)
  other arithmetic  11.2 us (9%)
  matrix products  9.87 us (8%)
  local copies, waits for them, and re-layouts  7.37 us (6%)
  between operations  1.35 us (1%)
    pallas_call x1, Pallas kernels, return_field(): pl.pallas_call(return_kernel, out_shape=(jax.ShapeDtypeStruct(padded, fie...  9.82 us
    ppermute x7, starting transfers between devices, reduce_everywhere(): packed = lax.ppermute(packed, axes, [(i, i ^ offset) for i in range(count)])  8.89 us
    ppermute x7, starting transfers between devices, reduce_everywhere(): lax.ppermute(part, axes, [(i, i ^ offset) for i in range(count)])  8.06 us
    ppermute x3, starting transfers between devices, exchange_rows(): down = lax.ppermute(top, axes, shifted_pairs(-1, 0))  7.92 us
    ppermute x3, waiting for transfers between devices, exchange_rows(): up = lax.ppermute(bottom, axes, shifted_pairs(1, 0))  7.74 us
    ppermute x2, starting transfers between devices, exchange_cols(): far_same = lax.ppermute(edge, axes, mirror_pairs(False, True, False))  7.36 us
    ppermute x2, starting transfers between devices, exchange_rows(): row_same = lax.ppermute(edge, axes, mirror_pairs(True, False, True))  5.31 us
    pallas_call x1, Pallas kernels, pad_field(): pl.pallas_call(pad_kernel, out_shape=jax.ShapeDtypeStruct(padded, field.d...  5.04 us
  transfers between devices with their start and end apart: 30, of which 9 were waited for; matrix products, arithmetic and copies ran while one was open for 8% of the time, Pallas kernels for 11%

profile of v6, /device:TPU:0, one launch (start us, length us, event | category | flops | bytes accessed | tf_op | source)
XLA Modules:
  0.0 127.1 jit_solution(7325788908414480723)
XLA Ops:
  1.9 3.0 %collective-permute-start = (bf16[12,16,256]{2,1,0:T(8,128)(2,1)S(1)}, bf16[12,16,256]{2,1,0:T(8,128)(2,1)S(1)}, u32[]{:S(2)}, u32[]{:S(2)}) collective-permute-start(bf16[12,16,256]{2,1,0:T(8,128)(2,1)S(1)} %get-tuple-element.61.edges), channel_id=1, source_target_pairs={{0,1},{1,0},{2,3},{3,2},{4,5},{5,4},{6,7},{7,6},{8,9},{9,8},{10,11... | collective-permute-start | bytes 294920 | tf_op jit(solution)/shard_map/ppermute | solution.py:291
  4.9 3.7 %collective-permute-start.1 = (bf16[12,8,256]{2,1,0:T(8,128)(2,1)S(1)}, bf16[12,8,256]{2,1,0:T(8,128)(2,1)S(1)}, u32[]{:S(2)}, u32[]{:S(2)}) collective-permute-start(bf16[12,8,256]{2,1,0:T(8,128)(2,1)S(1)} %get-tuple-element.60), channel_id=1, source_target_pairs={{0,30},{1,31},{2,28},{3,29},{4,26},{5,27},{6,24},{7,25},{8,22},{9,... | collective-permute-start | bytes 147464 | tf_op jit(solution)/shard_map/ppermute | solution.py:301
  8.9 2.6 %collective-permute-done.1.far_same = bf16[12,8,256]{2,1,0:T(8,128)(2,1)S(1)} collective-permute-done((bf16[12,8,256]{2,1,0:T(8,128)(2,1)S(1)}, bf16[12,8,256]{2,1,0:T(8,128)(2,1)S(1)}, u32[]{:S(2)}, u32[]{:S(2)}) %collective-permute-start.1) | collective-permute-done | bytes 49184 | tf_op jit(solution)/shard_map/ppermute | solution.py:301
  11.4 4.3 %collective-permute-done.2.far_cross = bf16[12,8,256]{2,1,0:T(8,128)(2,1)S(1)} collective-permute-done((bf16[12,8,256]{2,1,0:T(8,128)(2,1)S(1)}, bf16[12,8,256]{2,1,0:T(8,128)(2,1)S(1)}, u32[]{:S(2)}, u32[]{:S(2)}) %collective-permute-start.2) | collective-permute-done | bytes 49184 | tf_op jit(solution)/shard_map/ppermute | solution.py:302
  15.8 2.1 %fusion.65 = (bf16[12,2,32,256]{3,2,1,0:T(8,128)(2,1)}, bf16[12,2,32,256]{3,2,1,0:T(8,128)(2,1)}) fusion(bf16[12,4,32,256]{3,2,1,0:T(8,128)(2,1)} %field.1), kind=kLoop, calls=%fused_computation.126 | loop fusion | bytes 1572864 | tf_op jit(solution)/shard_map/slice | solution.py:353
  18.8 3.5 %collective-permute-start.4 = (bf16[12,64,256]{2,1,0:T(8,128)(2,1)}, bf16[12,64,256]{2,1,0:T(8,128)(2,1)S(1)}, u32[]{:S(2)}, u32[]{:S(2)}) collective-permute-start(bf16[12,64,256]{2,1,0:T(8,128)(2,1)} %bitcast.1), channel_id=1, source_target_pairs={{0,30},{1,31},{2,0},{3,1},{4,2},{5,3},{6,4},{7,5},{8,6},{9,7},{10,... | collective-permute-start | bytes 1179656 | tf_op jit(solution)/shard_map/ppermute | solution.py:308
  23.4 2.4 %collective-permute-start.7 = (bf16[12,64,256]{2,1,0:T(8,128)(2,1)S(1)}, bf16[12,64,256]{2,1,0:T(8,128)(2,1)S(1)}, u32[]{:S(2)}, u32[]{:S(2)}) collective-permute-start(bf16[12,64,256]{2,1,0:T(8,128)(2,1)S(1)} %broadcast_select_fusion.refs_6_), channel_id=1, source_target_pairs={{0,1},{1,0},{30,31},{31,30}} | collective-permute-start | bytes 1179656 | tf_op jit(solution)/shard_map/ppermute | solution.py:311
  25.9 2.6 %collective-permute-start.8 = (bf16[12,64,256]{2,1,0:T(8,128)(2,1)S(1)}, bf16[12,64,256]{2,1,0:T(8,128)(2,1)S(1)}, u32[]{:S(2)}, u32[]{:S(2)}) collective-permute-start(bf16[12,64,256]{2,1,0:T(8,128)(2,1)S(1)} %broadcast_select_fusion.refs_6_), channel_id=1, source_target_pairs={{0,31},{1,30},{30,1},{31,0}} | collective-permute-start | bytes 1179656 | tf_op jit(solution)/shard_map/ppermute | solution.py:312
  29.5 1.9 %shard_map.147 = (bf16[12,16,256]{2,1,0:T(8,128)(2,1)S(1)}, bf16[12,8,256]{2,1,0:T(8,128)(2,1)S(1)}, bf16[12,8,256]{2,1,0:T(8,128)(2,1)S(1)}) custom-call(s32[144]{0:T(256)S(1)} %reshape.50.adjacency, bf16[12,16,256]{2,1,0:T(8,128)(2,1)S(1)} %get-tuple-element.61.edges, bf16[12,16,256]{2,1,0:T(8,128)(2,1)S(1)} %collective-permute-done.beside, ...), custom_call_target="tpu_custom_call" | custom-call | flops 1000 | bytes 3000000 | tf_op jit(solution)/shard_map/pallas_call | solution.py:319
  31.5 7.7 %collective-permute-done.5.refs_4_ = bf16[12,8,256]{2,1,0:T(8,128)(2,1)S(1)} collective-permute-done((bf16[12,8,256]{2,1,0:T(8,128)(2,1)S(1)}, bf16[12,8,256]{2,1,0:T(8,128)(2,1)S(1)}, u32[]{:S(2)}, u32[]{:S(2)}) %collective-permute-start.5) | collective-permute-done | bytes 49184 | tf_op jit(solution)/shard_map/ppermute | solution.py:307
  39.2 1.8 %collective-permute-done.6.refs_5_ = bf16[12,8,256]{2,1,0:T(8,128)(2,1)S(1)} collective-permute-done((bf16[12,8,256]{2,1,0:T(8,128)(2,1)S(1)}, bf16[12,8,256]{2,1,0:T(8,128)(2,1)S(1)}, u32[]{:S(2)}, u32[]{:S(2)}) %collective-permute-start.6) | collective-permute-done | bytes 49184 | tf_op jit(solution)/shard_map/ppermute | solution.py:308
  41.0 5.0 %shard_map.148 = bf16[12,8,36,256]{3,2,1,0:T(8,128)(2,1)S(1)} custom-call(s32[144]{0:T(256)S(1)} %reshape.50.adjacency, bf16[4,72,72]{2,1,0:T(8,128)(2,1)S(1)} %copy-done.2, bf16[320,384]{1,0:T(8,128)(2,1)S(1)} %copy-done.1, bf16[12,4,32,256]{3,2,1,0:T(8,128)(2,1)S(1)} %copy-done, bf16[12,16,256]{2,1,0:T(8,128)(2,1)S(1)} %get-tuple-element.20.sides, ...), custom_call_target="tpu_custom_call" | custom-call | flops 1000 | bytes 5000000 | tf_op jit(solution)/shard_map/pallas_call | solution.py:381
  46.1 3.0 %fusion.2 = f32[12,4,32,256]{3,0,2,1:T(8,128)S(1)} fusion(bf16[3,3,256,256]{3,2,1,0:T(8,128)(2,1)S(1)} %copy-done.10, bf16[12,8,36,256]{3,2,1,0:T(8,128)(2,1)S(1)} %shard_map.148), kind=kOutput, calls=%fused_computation.3 | convolution fusion | flops 1811939328 | bytes 4521984 | tf_op jit(solution)/shard_map/conv_general_dilated | solution.py:659
  54.9 1.9 %collective-permute-done.16 = bf16[1160,256]{1,0:T(8,128)(2,1)} collective-permute-done((bf16[1160,256]{1,0:T(8,128)(2,1)S(1)}, bf16[1160,256]{1,0:T(8,128)(2,1)}, u32[]{:S(2)}, u32[]{:S(2)}) %collective-permute-start.16) | collective-permute-done | bytes 593952 | tf_op jit(solution)/shard_map/ppermute | solution.py:626
  58.9 2.5 %collective-permute-start.18 = (bf16[296,256]{1,0:T(8,128)(2,1)S(1)}, bf16[296,256]{1,0:T(8,128)(2,1)S(1)}, u32[]{:S(2)}, u32[]{:S(2)}) collective-permute-start(bf16[296,256]{1,0:T(8,128)(2,1)S(1)} %get-tuple-element.66), channel_id=1, source_target_pairs={{0,4},{1,5},{2,6},{3,7},{4,0},{5,1},{6,2},{7,3},{8,12},{9,13},{10,... | collective-permute-start | bytes 454664 | tf_op jit(solution)/shard_map/ppermute | solution.py:626
  62.4 3.6 %collective-permute-start.10 = (bf16[12,8,256]{2,1,0:T(8,128)(2,1)S(1)}, bf16[12,8,256]{2,1,0:T(8,128)(2,1)S(1)}, u32[]{:S(2)}, u32[]{:S(2)}) collective-permute-start(bf16[12,8,256]{2,1,0:T(8,128)(2,1)S(1)} %get-tuple-element.58), channel_id=1, source_target_pairs={{0,30},{1,31},{2,28},{3,29},{4,26},{5,27},{6,24},{7,25},{8,22},{9,... | collective-permute-start | bytes 147464 | tf_op jit(solution)/shard_map/ppermute | solution.py:301
  69.8 4.6 %collective-permute-start.22 = (bf16[80,256]{1,0:T(8,128)(2,1)S(1)}, bf16[80,256]{1,0:T(8,128)(2,1)S(1)}, u32[]{:S(2)}, u32[]{:S(2)}) collective-permute-start(bf16[80,256]{1,0:T(8,128)(2,1)S(1)} %get-tuple-element.64), channel_id=1, source_target_pairs={{0,24},{1,25},{2,26},{3,27},{4,28},{5,29},{6,30},{7,31},{8,16},{9,... | collective-permute-start | bytes 122888 | tf_op jit(solution)/shard_map/ppermute | solution.py:626
  75.0 1.6 %copy.24 = bf16[3,3,256,256]{2,3,1,0:T(8,128)(2,1)S(1)} copy(bf16[3,3,256,256]{3,2,1,0:T(8,128)(2,1)} %param.13) | data formatting | bytes 2359296 | tf_op args[1]
  76.6 1.9 %shard_map.149 = (bf16[12,16,256]{2,1,0:T(8,128)(2,1)S(1)}, bf16[12,72,256]{2,1,0:T(8,128)(2,1)S(1)}, bf16[12,72,256]{2,1,0:T(8,128)(2,1)S(1)}, bf16[12,72,256]{2,1,0:T(8,128)(2,1)S(1)}) custom-call(s32[144]{0:T(256)S(1)} %reshape.50.adjacency, bf16[12,4,32,256]{3,2,1,0:T(8,128)(2,1)S(1)} %get-tuple-element.31.field, ...), custom_call_target="tpu_custom_call" | custom-call | flops 1000 | bytes 3000000 | tf_op jit(solution)/shard_map/pallas_call | solution.py:319
  78.6 4.4 %collective-permute-start.13 = (bf16[12,72,256]{2,1,0:T(8,128)(2,1)S(1)}, bf16[12,72,256]{2,1,0:T(8,128)(2,1)S(1)}, u32[]{:S(2)}, u32[]{:S(2)}) collective-permute-start(bf16[12,72,256]{2,1,0:T(8,128)(2,1)S(1)} %get-tuple-element.26), channel_id=1, source_target_pairs={{0,30},{1,31},{2,0},{3,1},{4,2},{5,3},{6,4},{7,5},{8,6},{9,7},{10,... | collective-permute-start | bytes 1327112 | tf_op jit(solution)/shard_map/ppermute | solution.py:308
  83.1 2.0 %collective-permute-start.25 = (bf16[1,72,256]{2,1,0:T(8,128)(2,1)S(1)}, bf16[1,72,256]{2,1,0:T(8,128)(2,1)S(1)}, u32[]{:S(2)}, u32[]{:S(2)}) collective-permute-start(bf16[1,72,256]{2,1,0:T(8,128)(2,1)S(1)} %bitcast.215), channel_id=1, source_target_pairs={{0,24},{1,25},{2,26},{3,27},{4,28},{5,29},{6,30},{7,31},{8,16},{9,... | collective-permute-start | bytes 110600 | tf_op jit(solution)/shard_map/ppermute | solution.py:639
  85.1 2.4 %collective-permute-start.23 = (bf16[1,72,256]{2,1,0:T(8,128)(2,1)S(1)}, bf16[1,72,256]{2,1,0:T(8,128)(2,1)S(1)}, u32[]{:S(2)}, u32[]{:S(2)}) collective-permute-start(bf16[1,72,256]{2,1,0:T(8,128)(2,1)S(1)} %bitcast.217), channel_id=1, source_target_pairs={{0,8},{1,9},{2,10},{3,11},{4,12},{5,13},{6,14},{7,15},{8,0},{9,1},... | collective-permute-start | bytes 110600 | tf_op jit(solution)/shard_map/ppermute | solution.py:639
  87.6 4.5 %collective-permute-done.25 = bf16[1,72,256]{2,1,0:T(8,128)(2,1)S(1)} collective-permute-done((bf16[1,72,256]{2,1,0:T(8,128)(2,1)S(1)}, bf16[1,72,256]{2,1,0:T(8,128)(2,1)S(1)}, u32[]{:S(2)}, u32[]{:S(2)}) %collective-permute-start.25) | collective-permute-done | bytes 36896 | tf_op jit(solution)/shard_map/ppermute | solution.py:639
  92.2 2.9 %collective-permute-start.14 = (bf16[12,72,256]{2,1,0:T(8,128)(2,1)S(1)}, bf16[12,72,256]{2,1,0:T(8,128)(2,1)S(1)}, u32[]{:S(2)}, u32[]{:S(2)}) collective-permute-start(bf16[12,72,256]{2,1,0:T(8,128)(2,1)S(1)} %get-tuple-element.27.edge), channel_id=1, source_target_pairs={{0,1},{1,0},{30,31},{31,30}} | collective-permute-start | bytes 1327112 | tf_op jit(solution)/shard_map/ppermute | solution.py:311
  95.1 2.1 %collective-permute-start.15 = (bf16[12,72,256]{2,1,0:T(8,128)(2,1)S(1)}, bf16[12,72,256]{2,1,0:T(8,128)(2,1)S(1)}, u32[]{:S(2)}, u32[]{:S(2)}) collective-permute-start(bf16[12,72,256]{2,1,0:T(8,128)(2,1)S(1)} %get-tuple-element.27.edge), channel_id=1, source_target_pairs={{0,31},{1,30},{30,1},{31,0}} | collective-permute-start | bytes 1327112 | tf_op jit(solution)/shard_map/ppermute | solution.py:312
  97.4 2.5 %collective-permute-start.27 = (bf16[4,72,256]{2,1,0:T(8,128)(2,1)S(1)}, bf16[4,72,256]{2,1,0:T(8,128)(2,1)S(1)}, u32[]{:S(2)}, u32[]{:S(2)}) collective-permute-start(bf16[4,72,256]{2,1,0:T(8,128)(2,1)S(1)} %get-tuple-element.50), channel_id=1, source_target_pairs={{0,4},{1,5},{2,6},{3,7},{4,0},{5,1},{6,2},{7,3},{8,12},{9,13},{10,... | collective-permute-start | bytes 442376 | tf_op jit(solution)/shard_map/ppermute | solution.py:639
  100.9 2.0 %multiply_convert_fusion = bf16[12,4,32,256]{3,2,1,0:T(8,128)(2,1)} fusion(f32[256]{0:T(256)S(1)} %copy-done.14, f32[12,4,32,256]{3,0,2,1:T(8,128)S(1)} %copy-done.9), kind=kLoop, calls=%fused_computation.15 | loop fusion | flops 2359296 | bytes 2360320 | tf_op jit(solution)/shard_map/convert_element_type | solution.py:670
  103.8 4.6 %collective-permute-done.15.far_cross = bf16[12,72,256]{2,1,0:T(8,128)(2,1)S(1)} collective-permute-done((bf16[12,72,256]{2,1,0:T(8,128)(2,1)S(1)}, bf16[12,72,256]{2,1,0:T(8,128)(2,1)S(1)}, u32[]{:S(2)}, u32[]{:S(2)}) %collective-permute-start.15) | collective-permute-done | bytes 442400 | tf_op jit(solution)/shard_map/ppermute | solution.py:312
  108.4 9.8 %shard_map.150 = (bf16[12,8,36,256]{3,2,1,0:T(8,128)(2,1)S(1)}, f32[12,4,32,256]{3,2,1,0:T(8,128)S(1)}) custom-call(s32[144]{0:T(256)S(1)} %reshape.50.adjacency, bf16[4,72,72]{2,1,0:T(8,128)(2,1)S(1)} %copy-done.2, bf16[320,384]{1,0:T(8,128)(2,1)S(1)} %copy-done.1, bf16[192,80]{1,0:T(8,128)(2,1)S(1)} %copy-done.3, bf16[2,24,384]{2,1,0:T(8,128)(2,1)S(1)} %copy-done.6, ...), custom_call_target="tpu_custom_call" | custom-call | flops 1000 | bytes 8000000 | tf_op jit(solution)/shard_map/pallas_call | solution.py:544
  119.7 3.0 %fusion = f32[12,4,32,256]{3,0,2,1:T(8,128)S(1)} fusion(bf16[3,3,256,256]{3,2,1,0:T(8,128)(2,1)S(1)} %copy-done.11, bf16[12,8,36,256]{3,2,1,0:T(8,128)(2,1)S(1)} %get-tuple-element.28), kind=kOutput, calls=%fused_computation.1 | convolution fusion | flops 1811939328 | bytes 4521984 | tf_op jit(solution)/shard_map/conv_general_dilated | solution.py:696
  122.7 1.8 %fusion.10 = bf16[12,4,32,256]{3,2,1,0:T(8,128)(2,1)} fusion(f32[12,4,32,256]{3,2,1,0:T(8,128)S(1)} %get-tuple-element.29, f32[12,4,32,256]{3,0,2,1:T(8,128)S(1)} %fusion), kind=kLoop, calls=%fused_computation.13 | loop fusion | flops 786432 | bytes 3932160 | tf_op jit(solution)/shard_map/convert_element_type | solution.py:706
  125.5 1.6 %convert_multiply_fusion = f32[32,72,256]{2,1,0:T(8,128)} fusion(bf16[16,72,256]{2,1,0:T(8,128)(2,1)S(1)} %get-tuple-element.33, bf16[16,72,256]{2,1,0:T(8,128)(2,1)S(1)} %get-tuple-element.32), kind=kLoop, calls=%fused_computation.5 | loop fusion | flops 1769472 | bytes 3538944 | tf_op jit(solution)/shard_map/mul | solution.py:691
  (117 shorter events, 22.2 us)
Async XLA Ops:
  1.9 39.1 %copy-start = (bf16[12,4,32,256]{3,2,1,0:T(8,128)(2,1)S(1)}, bf16[12,4,32,256]{3,2,1,0:T(8,128)(2,1)}, u32[]{:S(2)}) copy-start(bf16[12,4,32,256]{3,2,1,0:T(8,128)(2,1)} %field.1) | copy-start | bytes 2359300
  1.9 39.1 %copy-start.1 = (bf16[320,384]{1,0:T(8,128)(2,1)S(1)}, bf16[320,384]{1,0:T(8,128)(2,1)}, u32[]{:S(2)}) copy-start(bf16[320,384]{1,0:T(8,128)(2,1)} %constant.74.clone.picks) | copy-start | bytes 737284
  1.9 13.8 %collective-permute-start = (bf16[12,16,256]{2,1,0:T(8,128)(2,1)S(1)}, bf16[12,16,256]{2,1,0:T(8,128)(2,1)S(1)}, u32[]{:S(2)}, u32[]{:S(2)}) collective-permute-start(bf16[12,16,256]{2,1,0:T(8,128)(2,1)S(1)} %get-tuple-element.61.edges), channel_id=1, source_target_pairs={{0,1},{1,0},{2,3},{3,2},{4,5},{5,4},{6,7},{7,6},{8,9},{9,8},{10,11... | collective-permute-start | bytes 294920 | tf_op jit(solution)/shard_map/ppermute | solution.py:291
  4.9 6.5 %collective-permute-start.1 = (bf16[12,8,256]{2,1,0:T(8,128)(2,1)S(1)}, bf16[12,8,256]{2,1,0:T(8,128)(2,1)S(1)}, u32[]{:S(2)}, u32[]{:S(2)}) collective-permute-start(bf16[12,8,256]{2,1,0:T(8,128)(2,1)S(1)} %get-tuple-element.60), channel_id=1, source_target_pairs={{0,30},{1,31},{2,28},{3,29},{4,26},{5,27},{6,24},{7,25},{8,22},{9,... | collective-permute-start | bytes 147464 | tf_op jit(solution)/shard_map/ppermute | solution.py:301
  8.6 7.1 %collective-permute-start.2 = (bf16[12,8,256]{2,1,0:T(8,128)(2,1)S(1)}, bf16[12,8,256]{2,1,0:T(8,128)(2,1)S(1)}, u32[]{:S(2)}, u32[]{:S(2)}) collective-permute-start(bf16[12,8,256]{2,1,0:T(8,128)(2,1)S(1)} %get-tuple-element.60), channel_id=1, source_target_pairs={{0,31},{1,30},{2,29},{3,28},{4,27},{5,26},{6,25},{7,24},{8,23},{9,... | collective-permute-start | bytes 147464 | tf_op jit(solution)/shard_map/ppermute | solution.py:302
  17.8 23.1 %collective-permute-start.3 = (bf16[12,64,256]{2,1,0:T(8,128)(2,1)}, bf16[12,64,256]{2,1,0:T(8,128)(2,1)S(1)}, u32[]{:S(2)}, u32[]{:S(2)}) collective-permute-start(bf16[12,64,256]{2,1,0:T(8,128)(2,1)} %bitcast), channel_id=1, source_target_pairs={{0,2},{1,3},{2,4},{3,5},{4,6},{5,7},{6,8},{7,9},{8,10},{9,11},{10,... | collective-permute-start | bytes 1179656 | tf_op jit(solution)/shard_map/ppermute | solution.py:307
  18.8 22.2 %collective-permute-start.4 = (bf16[12,64,256]{2,1,0:T(8,128)(2,1)}, bf16[12,64,256]{2,1,0:T(8,128)(2,1)S(1)}, u32[]{:S(2)}, u32[]{:S(2)}) collective-permute-start(bf16[12,64,256]{2,1,0:T(8,128)(2,1)} %bitcast.1), channel_id=1, source_target_pairs={{0,30},{1,31},{2,0},{3,1},{4,2},{5,3},{6,4},{7,5},{8,6},{9,7},{10,... | collective-permute-start | bytes 1179656 | tf_op jit(solution)/shard_map/ppermute | solution.py:308
  23.4 17.5 %collective-permute-start.7 = (bf16[12,64,256]{2,1,0:T(8,128)(2,1)S(1)}, bf16[12,64,256]{2,1,0:T(8,128)(2,1)S(1)}, u32[]{:S(2)}, u32[]{:S(2)}) collective-permute-start(bf16[12,64,256]{2,1,0:T(8,128)(2,1)S(1)} %broadcast_select_fusion.refs_6_), channel_id=1, source_target_pairs={{0,1},{1,0},{30,31},{31,30}} | collective-permute-start | bytes 1179656 | tf_op jit(solution)/shard_map/ppermute | solution.py:311
  25.9 15.1 %collective-permute-start.8 = (bf16[12,64,256]{2,1,0:T(8,128)(2,1)S(1)}, bf16[12,64,256]{2,1,0:T(8,128)(2,1)S(1)}, u32[]{:S(2)}, u32[]{:S(2)}) collective-permute-start(bf16[12,64,256]{2,1,0:T(8,128)(2,1)S(1)} %broadcast_select_fusion.refs_6_), channel_id=1, source_target_pairs={{0,31},{1,30},{30,1},{31,0}} | collective-permute-start | bytes 1179656 | tf_op jit(solution)/shard_map/ppermute | solution.py:312
  31.4 7.8 %collective-permute-start.5 = (bf16[12,8,256]{2,1,0:T(8,128)(2,1)S(1)}, bf16[12,8,256]{2,1,0:T(8,128)(2,1)S(1)}, u32[]{:S(2)}, u32[]{:S(2)}) collective-permute-start(bf16[12,8,256]{2,1,0:T(8,128)(2,1)S(1)} %get-tuple-element.22.refs_1_), channel_id=1, source_target_pairs={{0,2},{1,3},{2,4},{3,5},{4,6},{5,7},{6,8},{7,9},{8,10},{9,11},{10,... | collective-permute-start | bytes 147464 | tf_op jit(solution)/shard_map/ppermute | solution.py:307
  39.2 1.8 %collective-permute-start.6 = (bf16[12,8,256]{2,1,0:T(8,128)(2,1)S(1)}, bf16[12,8,256]{2,1,0:T(8,128)(2,1)S(1)}, u32[]{:S(2)}, u32[]{:S(2)}) collective-permute-start(bf16[12,8,256]{2,1,0:T(8,128)(2,1)S(1)} %get-tuple-element.21.refs_0_), channel_id=1, source_target_pairs={{0,30},{1,31},{2,0},{3,1},{4,2},{5,3},{6,4},{7,5},{8,6},{9,7},{10,... | collective-permute-start | bytes 147464 | tf_op jit(solution)/shard_map/ppermute | solution.py:308
  54.6 2.2 %collective-permute-start.16 = (bf16[1160,256]{1,0:T(8,128)(2,1)S(1)}, bf16[1160,256]{1,0:T(8,128)(2,1)}, u32[]{:S(2)}, u32[]{:S(2)}) collective-permute-start(bf16[1160,256]{1,0:T(8,128)(2,1)S(1)} %pad_maximum_fusion), channel_id=1, source_target_pairs={{0,2},{1,3},{2,0},{3,1},{4,6},{5,7},{6,4},{7,5},{8,10},{9,11},{10,... | collective-permute-start | bytes 1781768 | tf_op jit(solution)/shard_map/ppermute | solution.py:626
  58.8 8.6 %collective-permute-start.19 = (bf16[296,256]{1,0:T(8,128)(2,1)S(1)}, bf16[296,256]{1,0:T(8,128)(2,1)S(1)}, u32[]{:S(2)}, u32[]{:S(2)}) collective-permute-start(bf16[296,256]{1,0:T(8,128)(2,1)S(1)} %get-tuple-element.67), channel_id=1, source_target_pairs={{0,5},{1,4},{2,7},{3,6},{4,1},{5,0},{6,3},{7,2},{8,13},{9,12},{10,... | collective-permute-start | bytes 454664 | tf_op jit(solution)/shard_map/ppermute | solution.py:626
  58.9 10.8 %collective-permute-start.18 = (bf16[296,256]{1,0:T(8,128)(2,1)S(1)}, bf16[296,256]{1,0:T(8,128)(2,1)S(1)}, u32[]{:S(2)}, u32[]{:S(2)}) collective-permute-start(bf16[296,256]{1,0:T(8,128)(2,1)S(1)} %get-tuple-element.66), channel_id=1, source_target_pairs={{0,4},{1,5},{2,6},{3,7},{4,0},{5,1},{6,2},{7,3},{8,12},{9,13},{10,... | collective-permute-start | bytes 454664 | tf_op jit(solution)/shard_map/ppermute | solution.py:626
  61.4 8.3 %collective-permute-start.17 = (bf16[296,256]{1,0:T(8,128)(2,1)S(1)}, bf16[296,256]{1,0:T(8,128)(2,1)S(1)}, u32[]{:S(2)}, u32[]{:S(2)}) collective-permute-start(bf16[296,256]{1,0:T(8,128)(2,1)S(1)} %get-tuple-element.65), channel_id=1, source_target_pairs={{0,1},{1,0},{2,3},{3,2},{4,5},{5,4},{6,7},{7,6},{8,9},{9,8},{10,11... | collective-permute-start | bytes 454664 | tf_op jit(solution)/shard_map/ppermute | solution.py:626
  62.4 12.1 %collective-permute-start.10 = (bf16[12,8,256]{2,1,0:T(8,128)(2,1)S(1)}, bf16[12,8,256]{2,1,0:T(8,128)(2,1)S(1)}, u32[]{:S(2)}, u32[]{:S(2)}) collective-permute-start(bf16[12,8,256]{2,1,0:T(8,128)(2,1)S(1)} %get-tuple-element.58), channel_id=1, source_target_pairs={{0,30},{1,31},{2,28},{3,29},{4,26},{5,27},{6,24},{7,25},{8,22},{9,... | collective-permute-start | bytes 147464 | tf_op jit(solution)/shard_map/ppermute | solution.py:301
  66.0 10.6 %collective-permute-start.11 = (bf16[12,8,256]{2,1,0:T(8,128)(2,1)S(1)}, bf16[12,8,256]{2,1,0:T(8,128)(2,1)S(1)}, u32[]{:S(2)}, u32[]{:S(2)}) collective-permute-start(bf16[12,8,256]{2,1,0:T(8,128)(2,1)S(1)} %get-tuple-element.58), channel_id=1, source_target_pairs={{0,31},{1,30},{2,29},{3,28},{4,27},{5,26},{6,25},{7,24},{8,23},{9,... | collective-permute-start | bytes 147464 | tf_op jit(solution)/shard_map/ppermute | solution.py:302
  67.4 9.3 %collective-permute-start.9 = (bf16[12,16,256]{2,1,0:T(8,128)(2,1)S(1)}, bf16[12,16,256]{2,1,0:T(8,128)(2,1)S(1)}, u32[]{:S(2)}, u32[]{:S(2)}) collective-permute-start(bf16[12,16,256]{2,1,0:T(8,128)(2,1)S(1)} %get-tuple-element.59.edges), channel_id=1, source_target_pairs={{0,1},{1,0},{2,3},{3,2},{4,5},{5,4},{6,7},{7,6},{8,9},{9,8},{10,11... | collective-permute-start | bytes 294920 | tf_op jit(solution)/shard_map/ppermute | solution.py:291
  69.8 13.3 %collective-permute-start.22 = (bf16[80,256]{1,0:T(8,128)(2,1)S(1)}, bf16[80,256]{1,0:T(8,128)(2,1)S(1)}, u32[]{:S(2)}, u32[]{:S(2)}) collective-permute-start(bf16[80,256]{1,0:T(8,128)(2,1)S(1)} %get-tuple-element.64), channel_id=1, source_target_pairs={{0,24},{1,25},{2,26},{3,27},{4,28},{5,29},{6,30},{7,31},{8,16},{9,... | collective-permute-start | bytes 122888 | tf_op jit(solution)/shard_map/ppermute | solution.py:626
  74.4 8.6 %collective-permute-start.21 = (bf16[80,256]{1,0:T(8,128)(2,1)S(1)}, bf16[80,256]{1,0:T(8,128)(2,1)S(1)}, u32[]{:S(2)}, u32[]{:S(2)}) collective-permute-start(bf16[80,256]{1,0:T(8,128)(2,1)S(1)} %get-tuple-element.63), channel_id=1, source_target_pairs={{0,16},{1,17},{2,18},{3,19},{4,20},{5,21},{6,22},{7,23},{8,24},{9,... | collective-permute-start | bytes 122888 | tf_op jit(solution)/shard_map/ppermute | solution.py:626
  74.4 8.6 %collective-permute-start.20 = (bf16[80,256]{1,0:T(8,128)(2,1)S(1)}, bf16[80,256]{1,0:T(8,128)(2,1)S(1)}, u32[]{:S(2)}, u32[]{:S(2)}) collective-permute-start(bf16[80,256]{1,0:T(8,128)(2,1)S(1)} %get-tuple-element.62), channel_id=1, source_target_pairs={{0,8},{1,9},{2,10},{3,11},{4,12},{5,13},{6,14},{7,15},{8,0},{9,1},... | collective-permute-start | bytes 122888 | tf_op jit(solution)/shard_map/ppermute | solution.py:626
  78.5 18.8 %collective-permute-start.12 = (bf16[12,72,256]{2,1,0:T(8,128)(2,1)S(1)}, bf16[12,72,256]{2,1,0:T(8,128)(2,1)S(1)}, u32[]{:S(2)}, u32[]{:S(2)}) collective-permute-start(bf16[12,72,256]{2,1,0:T(8,128)(2,1)S(1)} %get-tuple-element.25), channel_id=1, source_target_pairs={{0,2},{1,3},{2,4},{3,5},{4,6},{5,7},{6,8},{7,9},{8,10},{9,11},{10,... | collective-permute-start | bytes 1327112 | tf_op jit(solution)/shard_map/ppermute | solution.py:307
  78.6 21.3 %collective-permute-start.13 = (bf16[12,72,256]{2,1,0:T(8,128)(2,1)S(1)}, bf16[12,72,256]{2,1,0:T(8,128)(2,1)S(1)}, u32[]{:S(2)}, u32[]{:S(2)}) collective-permute-start(bf16[12,72,256]{2,1,0:T(8,128)(2,1)S(1)} %get-tuple-element.26), channel_id=1, source_target_pairs={{0,30},{1,31},{2,0},{3,1},{4,2},{5,3},{6,4},{7,5},{8,6},{9,7},{10,... | collective-permute-start | bytes 1327112 | tf_op jit(solution)/shard_map/ppermute | solution.py:308
  83.1 9.1 %collective-permute-start.25 = (bf16[1,72,256]{2,1,0:T(8,128)(2,1)S(1)}, bf16[1,72,256]{2,1,0:T(8,128)(2,1)S(1)}, u32[]{:S(2)}, u32[]{:S(2)}) collective-permute-start(bf16[1,72,256]{2,1,0:T(8,128)(2,1)S(1)} %bitcast.215), channel_id=1, source_target_pairs={{0,24},{1,25},{2,26},{3,27},{4,28},{5,29},{6,30},{7,31},{8,16},{9,... | collective-permute-start | bytes 110600 | tf_op jit(solution)/shard_map/ppermute | solution.py:639
  85.1 9.9 %collective-permute-start.24 = (bf16[1,72,256]{2,1,0:T(8,128)(2,1)S(1)}, bf16[1,72,256]{2,1,0:T(8,128)(2,1)S(1)}, u32[]{:S(2)}, u32[]{:S(2)}) collective-permute-start(bf16[1,72,256]{2,1,0:T(8,128)(2,1)S(1)} %bitcast.216), channel_id=1, source_target_pairs={{0,16},{1,17},{2,18},{3,19},{4,20},{5,21},{6,22},{7,23},{8,24},{9,... | collective-permute-start | bytes 110600 | tf_op jit(solution)/shard_map/ppermute | solution.py:639
  85.1 12.1 %collective-permute-start.23 = (bf16[1,72,256]{2,1,0:T(8,128)(2,1)S(1)}, bf16[1,72,256]{2,1,0:T(8,128)(2,1)S(1)}, u32[]{:S(2)}, u32[]{:S(2)}) collective-permute-start(bf16[1,72,256]{2,1,0:T(8,128)(2,1)S(1)} %bitcast.217), channel_id=1, source_target_pairs={{0,8},{1,9},{2,10},{3,11},{4,12},{5,13},{6,14},{7,15},{8,0},{9,1},... | collective-permute-start | bytes 110600 | tf_op jit(solution)/shard_map/ppermute | solution.py:639
  92.2 11.6 %collective-permute-start.14 = (bf16[12,72,256]{2,1,0:T(8,128)(2,1)S(1)}, bf16[12,72,256]{2,1,0:T(8,128)(2,1)S(1)}, u32[]{:S(2)}, u32[]{:S(2)}) collective-permute-start(bf16[12,72,256]{2,1,0:T(8,128)(2,1)S(1)} %get-tuple-element.27.edge), channel_id=1, source_target_pairs={{0,1},{1,0},{30,31},{31,30}} | collective-permute-start | bytes 1327112 | tf_op jit(solution)/shard_map/ppermute | solution.py:311
  95.1 13.4 %collective-permute-start.15 = (bf16[12,72,256]{2,1,0:T(8,128)(2,1)S(1)}, bf16[12,72,256]{2,1,0:T(8,128)(2,1)S(1)}, u32[]{:S(2)}, u32[]{:S(2)}) collective-permute-start(bf16[12,72,256]{2,1,0:T(8,128)(2,1)S(1)} %get-tuple-element.27.edge), channel_id=1, source_target_pairs={{0,31},{1,30},{30,1},{31,0}} | collective-permute-start | bytes 1327112 | tf_op jit(solution)/shard_map/ppermute | solution.py:312
  97.3 21.0 %collective-permute-start.28 = (bf16[4,72,256]{2,1,0:T(8,128)(2,1)S(1)}, bf16[4,72,256]{2,1,0:T(8,128)(2,1)S(1)}, u32[]{:S(2)}, u32[]{:S(2)}) collective-permute-start(bf16[4,72,256]{2,1,0:T(8,128)(2,1)S(1)} %get-tuple-element.50), channel_id=1, source_target_pairs={{0,5},{1,4},{2,7},{3,6},{4,1},{5,0},{6,3},{7,2},{8,13},{9,12},{10,... | collective-permute-start | bytes 442376 | tf_op jit(solution)/shard_map/ppermute | solution.py:639
  97.4 20.9 %collective-permute-start.27 = (bf16[4,72,256]{2,1,0:T(8,128)(2,1)S(1)}, bf16[4,72,256]{2,1,0:T(8,128)(2,1)S(1)}, u32[]{:S(2)}, u32[]{:S(2)}) collective-permute-start(bf16[4,72,256]{2,1,0:T(8,128)(2,1)S(1)} %get-tuple-element.50), channel_id=1, source_target_pairs={{0,4},{1,5},{2,6},{3,7},{4,0},{5,1},{6,2},{7,3},{8,12},{9,13},{10,... | collective-permute-start | bytes 442376 | tf_op jit(solution)/shard_map/ppermute | solution.py:639
  99.9 18.4 %collective-permute-start.26 = (bf16[4,72,256]{2,1,0:T(8,128)(2,1)S(1)}, bf16[4,72,256]{2,1,0:T(8,128)(2,1)S(1)}, u32[]{:S(2)}, u32[]{:S(2)}) collective-permute-start(bf16[4,72,256]{2,1,0:T(8,128)(2,1)S(1)} %get-tuple-element.50), channel_id=1, source_target_pairs={{0,1},{1,0},{2,3},{3,2},{4,5},{5,4},{6,7},{7,6},{8,9},{9,8},{10,11... | collective-permute-start | bytes 442376 | tf_op jit(solution)/shard_map/ppermute | solution.py:639
  118.6 6.5 %collective-permute-start.29 = (bf16[16,72,256]{2,1,0:T(8,128)(2,1)S(1)}, bf16[16,72,256]{2,1,0:T(8,128)(2,1)S(1)}, u32[]{:S(2)}, u32[]{:S(2)}) collective-permute-start(bf16[16,72,256]{2,1,0:T(8,128)(2,1)S(1)} %get-tuple-element.40), channel_id=1, source_target_pairs={{0,2},{1,3},{2,0},{3,1},{4,6},{5,7},{6,4},{7,5},{8,10},{9,11},{10,... | collective-permute-start | bytes 1769480 | tf_op jit(solution)/shard_map/ppermute | solution.py:639
  (13 other events, 172.6 us)

commit v7 on v6

--- a/solution.py
+++ b/solution.py
@@ -44,7 +44,7 @@
     return -(-value // step) * step
 
 
-def row_flips(width):
+def flip_table(width):
     size = 2 * width + 8
     table = np.zeros((4, size, size), np.float32)
     for kind in range(4):
@@ -56,16 +56,11 @@
             for e in range(4):
                 source_e = 3 - e if kind >= 2 else e
                 table[kind, 2 * width + 4 * d + e, 2 * width + 4 * source_d + source_e] = 1
-    return jnp.asarray(table, jnp.bfloat16)
-
-
-def corner_picks(width):
-    table = np.zeros((2, 8, 2 * width), np.float32)
-    for d in range(2):
-        for k in range(2):
-            table[0, 4 * d + 2 + k, d * width + k] = 1
-            table[1, 4 * d + k, d * width + width - 2 + k] = 1
-    return jnp.asarray(table, jnp.bfloat16)
+    return table
+
+
+def row_flips(width):
+    return jnp.asarray(flip_table(width), jnp.bfloat16)
 
 
 def stack_places(tile_rows, width):
@@ -208,30 +203,6 @@
     return [[reader(ref) for ref in (near, edge, far_cross, far_same)] for near in (up, down)]
 
 
-def split_readers(
-    upper, lower, up, down, up_tail, down_tail, edge, far_same, far_cross, corners,
-    same_tail=None, cross_tail=None,
-):
-    def reader(main, tail):
-        return lambda source: jnp.concatenate([main[source], tail[source]], 0)
-
-    def corner_reader(main, other):
-        def read(source):
-            tail = pick(corners[1 - lax.axis_index("fcol")], other[source])
-            return jnp.concatenate([main[source], tail], 0)
-
-        return read
-
-    readers = []
-    for near, near_tail, own_tail in ((up, up_tail, upper), (down, down_tail, lower)):
-        readers.append([reader(near, near_tail), reader(edge, own_tail)])
-        if same_tail is None:
-            readers[-1] += [corner_reader(far_cross, near), corner_reader(far_same, edge)]
-        else:
-            readers[-1] += [reader(far_cross, cross_tail), reader(far_same, same_tail)]
-    return readers
-
-
 def load_stack(adjacency, face, field, sides, readers, flips, stack):
     tile_rows, width, channels = field.shape[1:]
     strip = 2 * width + 8
@@ -266,7 +237,7 @@
 
 def pad_kernel(adjacency, flips, picks, field, sides, *refs):
     padded, stack = refs[-2:]
-    readers = split_readers(*refs[:-2])
+    readers = joint_readers(*refs[:-2])
     stack[...] = jnp.zeros_like(stack)
 
     @pl.loop(0, field.shape[0])
@@ -306,8 +277,6 @@
 def exchange_rows(top, bottom, edge):
     up = lax.ppermute(bottom, axes, shifted_pairs(1, 0))
     down = lax.ppermute(top, axes, shifted_pairs(-1, 0))
-    if edge is None:
-        return (up, down)
     row_same = lax.ppermute(edge, axes, mirror_pairs(True, False, True))
     row_cross = lax.ppermute(edge, axes, mirror_pairs(True, True, True))
     return (up, down, row_same, row_cross)
@@ -343,39 +312,9 @@
     return (field, sides, up, down, edge, row_same, row_cross)
 
 
-def split_strips(field, adjacency):
-    face_count, tile_rows, width, channels = field.shape
-    edges, beside, far_same, far_cross = exchange_cols(field)
-    at_top = lax.axis_index("frow") == 0
-    later, beside, far_same, far_cross = lax.optimization_barrier(
-        (field, beside, far_same, far_cross)
-    )
-    top = later[:, :2].reshape(face_count, 2 * width, channels)
-    bottom = later[:, tile_rows - 2 :].reshape(face_count, 2 * width, channels)
-    edge = jnp.where(at_top, top, bottom)
-    up, down, row_same, row_cross = exchange_rows(top, bottom, edge)
-    tail = (face_count, 8, channels)
-    sides, upper, lower = side_call(
-        side_kernel,
-        field,
-        (adjacency, edges, beside, far_same, far_cross),
-        (edges.shape, tail, tail),
-        (),
-    )
-    up_tail, down_tail = exchange_rows(upper, lower, None)
-    strips = [
-        field, sides, upper, lower, up, down, up_tail, down_tail, edge, row_same, row_cross,
-        corner_picks(width),
-    ]
-    if lax.axis_size("fcol") > 2:
-        own_tail = jnp.where(at_top, upper, lower)
-        strips += exchange_rows(upper, lower, own_tail)[2:]
-    return strips
-
-
 def pad_field(field, adjacency):
     face_count, tile_rows, width, channels = field.shape
-    strips = split_strips(field, adjacency)
+    strips = joint_strips(field, adjacency)
     padded = (face_count, tile_rows + 4, width + 4, channels)
     size = stack_places(tile_rows, width)[3]
     return pl.pallas_call(
@@ -390,8 +329,8 @@
 
 
 def seam_row_picks(width):
-    size = round_up(2 * width + 8, 16)
-    table = np.zeros((3, 2 * width, size), np.float32)
+    flips = flip_table(width)
+    table = np.zeros((3 * 2 * width, 2 * width + 8), np.float32)
     for shift in range(3):
         for d in range(2):
             for x in range(width):
@@ -400,8 +339,10 @@
                     source = d * width + w - 2
                 else:
                     source = 2 * width + 4 * d + (w if w < 2 else w - width)
-                table[shift, d * width + x, source] = 1
-    return jnp.asarray(table, jnp.bfloat16)
+                table[(shift * 2 + d) * width + x, source] = 1
+    turned = table.reshape(3, 2 * width, -1)[::-1].reshape(table.shape)
+    parts = [(turned if kind >= 2 else table) @ flips[kind] for kind in range(4)]
+    return jnp.asarray(np.stack(parts), jnp.bfloat16)
 
 
 def seam_col_picks(tile_rows, width):
@@ -421,56 +362,50 @@
 
 
 def return_kernel(
-    adjacency, flips, picks, row_picks, col_picks, rotated, field, sides, up, down, edge,
-    far_same, far_cross, padded, extra, stack, kept_picks, row_terms, col_terms, col_sum,
+    adjacency, picks, col_picks, rotated, field, sides, up, down, padded, extra, stack,
+    kept_picks, col_terms, col_sum,
 ):
-    readers = joint_readers(up, down, edge, far_same, far_cross)
     face_count, tile_rows, width, channels = field.shape
     breadth = picks.shape[0] // (tile_rows + 4)
     half = 2 * tile_rows
     slot = round_up(half, 16)
-    row_slot = 2 * width
-    _, above, below, _ = stack_places(tile_rows, width)
-    strip = row_picks.shape[1]
+    beside, above, below, _ = stack_places(tile_rows, width)
     row_place, col_place = lax.axis_index("frow"), lax.axis_index("fcol")
     at_top = row_place == 0
     at_bottom = row_place == lax.axis_size("frow") - 1
     at_left = col_place == 0
     at_right = col_place == lax.axis_size("fcol") - 1
-    on_row_edge = jnp.logical_or(at_top, at_bottom)
-    on_col_edge = jnp.logical_or(at_left, at_right)
     stack[...] = jnp.zeros_like(stack)
     extra[...] = jnp.zeros_like(extra)
     cell = lax.broadcasted_iota(jnp.int32, (breadth, picks.shape[1]), 0)
+    dropped = jnp.logical_or(
+        jnp.logical_and(at_left, cell < 2), jnp.logical_and(at_right, cell >= width + 2)
+    )
     for q in range(tile_rows + 4):
         rows = pl.ds(q * breadth, breadth)
-        dropped = jnp.logical_or(
-            jnp.logical_and(at_left, cell < 2), jnp.logical_and(at_right, cell >= width + 2)
-        )
-        if q < 2:
-            dropped = jnp.logical_or(dropped, at_top)
-        if q >= tile_rows + 2:
-            dropped = jnp.logical_or(dropped, at_bottom)
         kept = jnp.where(dropped, 0.0, picks[rows].astype(jnp.float32))
         kept_picks[rows] = kept.astype(jnp.bfloat16)
-
-    @pl.loop(0, face_count)
-    def _(face):
-        load_stack(adjacency, face, field, sides, readers, flips, stack)
+    for face in range(face_count):
+        stack[face, pl.ds(0, beside)] = field[face].reshape(beside, channels)
+        stack[face, pl.ds(beside, 4 * tile_rows)] = sides[face]
+    for near, place, at_edge in ((up, above, at_top), (down, below, at_bottom)):
+
+        @pl.when(jnp.logical_not(at_edge))
+        def _():
+            for face in range(face_count):
+                stack[face, pl.ds(place, near.shape[1])] = near[face]
 
     write_padded(kept_picks, stack, padded)
 
-    @pl.when(on_col_edge)
+    @pl.when(jnp.logical_or(at_left, at_right))
     def _():
         col_terms[...] = jnp.zeros_like(col_terms)
         table = col_picks[jnp.where(at_left, 0, 1)]
-
-        @pl.loop(0, face_count)
-        def _(face):
+        for face in range(face_count):
             base = (face * 4 + jnp.where(at_left, 2, 3)) * 3
             turned = adjacency[base + 2]
             value = jnp.dot(table, stack[face], preferred_element_type=jnp.float32)
-            rows = pl.ds(pl.multiple_of(face * slot, 16), half)
+            rows = pl.ds(face * slot, half)
             for shift in range(3):
                 part = value[shift * half : (shift + 1) * half].astype(jnp.bfloat16)
                 tap = jnp.where(turned == 1, 2 - shift, shift)
@@ -486,43 +421,6 @@
                 )
         col_sum[...] = total
 
-    @pl.when(on_row_edge)
-    def _():
-        row_terms[...] = jnp.zeros_like(row_terms)
-
-        @pl.loop(0, face_count)
-        def _(face):
-            base = (face * 4 + jnp.where(at_top, 0, 1)) * 3
-            turned = adjacency[base + 2]
-            place = pl.multiple_of(jnp.where(at_top, above, below), 16)
-            value = pick(row_picks[...], stack[face, pl.ds(place, strip)])
-            rows = pl.ds(pl.multiple_of(face * row_slot, 16), row_slot)
-            for shift in range(3):
-                part = value[shift * row_slot : (shift + 1) * row_slot]
-                tap = jnp.where(turned == 1, 2 - shift, shift)
-                row_terms[adjacency[base + 1], tap, rows] = part
-
-        first = jnp.where(at_top, 0, tile_rows - 2)
-
-        group = math.gcd(face_count, 4)
-
-        @pl.loop(0, face_count // group)
-        def _(part):
-            size = group * row_slot
-            rows = pl.ds(pl.multiple_of(part * size, 16), size)
-            total = jnp.zeros((size, channels), jnp.float32)
-            for side in range(2):
-                for tap in range(3):
-                    total += jnp.dot(
-                        row_terms[side, tap, rows],
-                        rotated[2 - 2 * side, tap],
-                        preferred_element_type=jnp.float32,
-                    )
-            for face in range(group):
-                for d in range(2):
-                    start = face * row_slot + d * width
-                    extra[part * group + face, first + d] = total[start : start + width]
-
     for edge_col, at_edge in ((0, at_left), (width - 2, at_right)):
 
         @pl.when(at_edge)
@@ -531,37 +429,92 @@
             for face in range(face_count):
                 value = col_sum[pl.ds(face * slot, half)]
                 for y in range(tile_rows):
-                    extra[face, y, cells] = extra[face, y, cells] + value[2 * y : 2 * y + 2]
+                    extra[face, y, cells] = value[2 * y : 2 * y + 2]
+
+
+def seam_kernel(
+    adjacency, row_picks, rotated, partial, up, down, edge, far_same, far_cross, out, values
+):
+    face_count, tile_rows, width, channels = partial.shape
+    row_place = lax.axis_index("frow")
+    out[...] = partial[...].astype(jnp.bfloat16)
+    readers = joint_readers(up, down, edge, far_same, far_cross)
+    for side in range(2):
+
+        @pl.when(row_place == side * (lax.axis_size("frow") - 1))
+        def _():
+            @pl.loop(0, face_count)
+            def _(face):
+                source, kind = seam_of(adjacency, face, side)
+                for choice, read in enumerate(readers[side]):
+
+                    @pl.when(kind == choice)
+                    def _():
+                        values[face] = pick(row_picks[choice], read(source))
+
+            for face in range(face_count):
+                row_tap = 2 - 2 * adjacency[(face * 4 + side) * 3 + 1]
+                total = jnp.zeros((2 * width, channels), jnp.float32)
+                for tap in range(3):
+                    total += jnp.dot(
+                        values[face, pl.ds(tap * 2 * width, 2 * width)],
+                        rotated[row_tap, tap],
+                        preferred_element_type=jnp.float32,
+                    )
+                for d in range(2):
+                    y = side * (tile_rows - 2) + d
+                    term = total[d * width : (d + 1) * width]
+                    out[face, y] = (partial[face, y] + term).astype(jnp.bfloat16)
 
 
 def return_field(field, adjacency, rotated):
     face_count, tile_rows, width, channels = field.shape
-    strips = joint_strips(field, adjacency)
+    _, sides, up, down, edge, row_same, row_cross = joint_strips(field, adjacency)
     padded = (face_count, tile_rows + 4, width + 4, channels)
     size = stack_places(tile_rows, width)[3]
     picks = pad_picks(tile_rows, width)
     cells = face_count * round_up(2 * tile_rows, 16)
-    return pl.pallas_call(
+    padded_grad, extra = pl.pallas_call(
         return_kernel,
         out_shape=(
             jax.ShapeDtypeStruct(padded, field.dtype),
             jax.ShapeDtypeStruct(field.shape, jnp.float32),
         ),
-        in_specs=whole(len(strips) + 5),
+        in_specs=whole(7),
         out_specs=[pl.BlockSpec(memory_space=pltpu.VMEM)] * 2,
         scratch_shapes=[
             pltpu.VMEM((face_count, size, channels), field.dtype),
             pltpu.VMEM(picks.shape, field.dtype),
-            pltpu.VMEM((2, 3, face_count * 2 * width, channels), field.dtype),
             pltpu.VMEM((2, 3, cells, channels), field.dtype),
             pltpu.VMEM((cells, channels), jnp.float32),
         ],
         compiler_params=pltpu.CompilerParams(vmem_limit_bytes=vmem_bytes),
         cost_estimate=pl.CostEstimate(flops=1000, bytes_accessed=8000000, transcendentals=0),
+    )(adjacency, picks, seam_col_picks(tile_rows, width), rotated, field, sides, up, down)
+    partial = conv(padded_grad, rotated) + extra
+    return pl.pallas_call(
+        seam_kernel,
+        out_shape=jax.ShapeDtypeStruct(field.shape, field.dtype),
+        in_specs=whole(8),
+        out_specs=pl.BlockSpec(memory_space=pltpu.VMEM),
+        scratch_shapes=[pltpu.VMEM((face_count, 6 * width, channels), field.dtype)],
+        compiler_params=pltpu.CompilerParams(vmem_limit_bytes=vmem_bytes),
+        cost_estimate=pl.CostEstimate(flops=1000, bytes_accessed=5000000, transcendentals=0),
     )(
-        adjacency, row_flips(width), picks,
-        seam_row_picks(width).reshape(6 * width, -1),
-        seam_col_picks(tile_rows, width), rotated, *strips,
+        adjacency, seam_row_picks(width), rotated, partial, up, down, edge, row_same,
+        row_cross,
+    )
+
+
+def conv(value, taps):
+    return lax.conv_general_dilated(
+        value,
+        taps,
+        (1, 1),
+        "VALID",
+        rhs_dilation=(DILATION_STEP, DILATION_STEP),
+        dimension_numbers=("NHWC", "HWIO", "NHWC"),
+        preferred_element_type=jnp.float32,
     )
 
 
@@ -654,19 +607,7 @@
     face_count, tile_rows, tile_cols, channels = face_input.shape
     table = adjacency.reshape(-1)
     padded_input = pad_field(face_input, table)
-    layout = ("NHWC", "HWIO", "NHWC")
-    preactivation = (
-        lax.conv_general_dilated(
-            padded_input,
-            kernel,
-            (1, 1),
-            "VALID",
-            rhs_dilation=(DILATION_STEP, DILATION_STEP),
-            dimension_numbers=layout,
-            preferred_element_type=jnp.float32,
-        )
-        + convolution_bias
-    )
+    preactivation = conv(padded_input, kernel) + convolution_bias
     activation = gelu_value(preactivation).astype(jnp.bfloat16)
     pre_grad = (upstream.astype(jnp.float32) * gelu_slope(preactivation)).astype(jnp.bfloat16)
     tap_list = []
@@ -691,19 +632,7 @@
     kernel_grad = kernel_total * scale
     bias_grad = bias_total * scale
     rotated = jnp.transpose(jnp.flip(kernel, (0, 1)), (0, 1, 3, 2))
-    padded_grad, extra = return_field(pre_grad, table, rotated)
-    input_gradient = (
-        lax.conv_general_dilated(
-            padded_grad,
-            rotated,
-            (1, 1),
-            "VALID",
-            rhs_dilation=(DILATION_STEP, DILATION_STEP),
-            dimension_numbers=layout,
-            preferred_element_type=jnp.float32,
-        )
-        + extra
-    ).astype(jnp.bfloat16)
+    input_gradient = return_field(pre_grad, table, rotated)
     return (activation, input_gradient, kernel_grad, bias_grad)
 
 

time: 128 us -> 127 us (level)
  other arithmetic: 11.2 us -> 13.7 us
  Pallas kernels: 18.6 us -> 16.5 us
    pallas_call x1, Pallas kernels: 9.82 us -> 2.86 us  [return_field(): pl.pallas_call(return_kernel, out_shape=(jax.ShapeDtypeStruct(padded, fie...]
    pallas_call x0 -> x1, Pallas kernels: none -> 4.57 us  [return_field(): pl.pallas_call(seam_kernel, out_shape=jax.ShapeDtypeStruct(field.shape, f...]
    ppermute x7, waiting for transfers between devices: 4.55 us -> 0.02 us  [reduce_everywhere(): lax.ppermute(part, axes, [(i, i ^ offset) for i in range(count)])]
    ppermute x3 -> x2, waiting for transfers between devices: 7.74 us -> 3.54 us  [exchange_rows(): up = lax.ppermute(bottom, axes, shifted_pairs(1, 0))]
    ppermute x7, waiting for transfers between devices: 3.23 us -> 7.16 us  [reduce_everywhere(): packed = lax.ppermute(packed, axes, [(i, i ^ offset) for i in range(count)])]
    ppermute x2, waiting for transfers between devices: 4.63 us -> 8.28 us  [exchange_rows(): row_cross = lax.ppermute(edge, axes, mirror_pairs(True, True, True))]
    ppermute x2, starting transfers between devices: 7.36 us -> 3.79 us  [exchange_cols(): far_same = lax.ppermute(edge, axes, mirror_pairs(False, True, False))]
    ppermute x2, starting transfers between devices: 1.6 us -> 4.71 us  [exchange_cols(): far_cross = lax.ppermute(edge, axes, mirror_pairs(False, True, True))]
  transfers between devices with their start and end apart: 30 -> 28, of which waited for: 9 -> 10; matrix products, arithmetic and copies ran while one was open for 8% -> 8% of each run, Pallas kernels for 11% -> 7%
where the time goes in v7:
time: 127 us
  starting transfers between devices  49.3 us (39%)
  waiting for transfers between devices  29 us (23%)
  Pallas kernels  16.5 us (13%)
  other arithmetic  13.7 us (11%)
  matrix products  9.81 us (8%)
  local copies, waits for them, and re-layouts  7.37 us (6%)
    ppermute x7, starting transfers between devices, reduce_everywhere(): lax.ppermute(part, axes, [(i, i ^ offset) for i in range(count)])  9.1 us
    ppermute x2, waiting for transfers between devices, exchange_rows(): row_cross = lax.ppermute(edge, axes, mirror_pairs(True, True, True))  8.28 us
    ppermute x7, starting transfers between devices, reduce_everywhere(): packed = lax.ppermute(packed, axes, [(i, i ^ offset) for i in range(count)])  7.93 us
    ppermute x2, starting transfers between devices, exchange_rows(): down = lax.ppermute(top, axes, shifted_pairs(-1, 0))  7.92 us
    ppermute x7, waiting for transfers between devices, reduce_everywhere(): packed = lax.ppermute(packed, axes, [(i, i ^ offset) for i in range(count)])  7.16 us
    conv_general_dilated x2, matrix products, conv(): lax.conv_general_dilated(value, taps, (1, 1), 'VALID', rhs_dilation=(DILA...  6.01 us
    ppermute x2, starting transfers between devices, exchange_rows(): row_same = lax.ppermute(edge, axes, mirror_pairs(True, False, True))  5.92 us
    pallas_call x2, Pallas kernels, side_call(): pl.pallas_call(body, out_shape=[jax.ShapeDtypeStruct(shape, field.dtype)...  4.79 us
  transfers between devices with their start and end apart: 28, of which 10 were waited for; matrix products, arithmetic and copies ran while one was open for 8% of the time, Pallas kernels for 7%

profile of v7, /device:TPU:0, one launch (start us, length us, event | category | flops | bytes accessed | tf_op | source)
XLA Modules:
  0.0 126.8 jit_solution(15157627828562629106)
XLA Ops:
  1.9 3.0 %collective-permute-start = (bf16[12,16,256]{2,1,0:T(8,128)(2,1)S(1)}, bf16[12,16,256]{2,1,0:T(8,128)(2,1)S(1)}, u32[]{:S(2)}, u32[]{:S(2)}) collective-permute-start(bf16[12,16,256]{2,1,0:T(8,128)(2,1)S(1)} %get-tuple-element.53.edges), channel_id=1, source_target_pairs={{0,1},{1,0},{2,3},{3,2},{4,5},{5,4},{6,7},{7,6},{8,9},{9,8},{10,11... | collective-permute-start | bytes 294920 | tf_op jit(solution)/shard_map/ppermute | solution.py:262
  4.9 3.7 %collective-permute-start.1 = (bf16[12,8,256]{2,1,0:T(8,128)(2,1)S(1)}, bf16[12,8,256]{2,1,0:T(8,128)(2,1)S(1)}, u32[]{:S(2)}, u32[]{:S(2)}) collective-permute-start(bf16[12,8,256]{2,1,0:T(8,128)(2,1)S(1)} %get-tuple-element.52), channel_id=1, source_target_pairs={{0,30},{1,31},{2,28},{3,29},{4,26},{5,27},{6,24},{7,25},{8,22},{9,... | collective-permute-start | bytes 147464 | tf_op jit(solution)/shard_map/ppermute | solution.py:272
  9.8 1.6 %collective-permute-done.1.far_same = bf16[12,8,256]{2,1,0:T(8,128)(2,1)S(1)} collective-permute-done((bf16[12,8,256]{2,1,0:T(8,128)(2,1)S(1)}, bf16[12,8,256]{2,1,0:T(8,128)(2,1)S(1)}, u32[]{:S(2)}, u32[]{:S(2)}) %collective-permute-start.1) | collective-permute-done | bytes 49184 | tf_op jit(solution)/shard_map/ppermute | solution.py:272
  11.4 4.3 %collective-permute-done.2.far_cross = bf16[12,8,256]{2,1,0:T(8,128)(2,1)S(1)} collective-permute-done((bf16[12,8,256]{2,1,0:T(8,128)(2,1)S(1)}, bf16[12,8,256]{2,1,0:T(8,128)(2,1)S(1)}, u32[]{:S(2)}, u32[]{:S(2)}) %collective-permute-start.2) | collective-permute-done | bytes 49184 | tf_op jit(solution)/shard_map/ppermute | solution.py:273
  16.9 2.9 %shard_map.129 = (bf16[12,16,256]{2,1,0:T(8,128)(2,1)S(1)}, bf16[12,72,256]{2,1,0:T(8,128)(2,1)}, bf16[12,72,256]{2,1,0:T(8,128)(2,1)}, bf16[12,72,256]{2,1,0:T(8,128)(2,1)S(1)}) custom-call(s32[144]{0:T(256)S(1)} %reshape.41.adjacency, bf16[12,4,32,256]{3,2,1,0:T(8,128)(2,1)S(1)} %copy-done, bf16[12,16,256]{2,1,0:T(8,128)(2,1)S(1)} %get-tuple-element.53.edges, ...), custom_call_target="tpu_custom_call" | custom-call | flops 1000 | bytes 3000000 | tf_op jit(solution)/shard_map/pallas_call | solution.py:288
  20.7 3.5 %collective-permute-start.4 = (bf16[12,72,256]{2,1,0:T(8,128)(2,1)}, bf16[12,72,256]{2,1,0:T(8,128)(2,1)S(1)}, u32[]{:S(2)}, u32[]{:S(2)}) collective-permute-start(bf16[12,72,256]{2,1,0:T(8,128)(2,1)} %get-tuple-element.16), channel_id=1, source_target_pairs={{0,30},{1,31},{2,0},{3,1},{4,2},{5,3},{6,4},{7,5},{8,6},{9,7},{10,... | collective-permute-start | bytes 1327112 | tf_op jit(solution)/shard_map/ppermute | solution.py:279
  24.2 2.4 %collective-permute-start.5 = (bf16[12,72,256]{2,1,0:T(8,128)(2,1)S(1)}, bf16[12,72,256]{2,1,0:T(8,128)(2,1)S(1)}, u32[]{:S(2)}, u32[]{:S(2)}) collective-permute-start(bf16[12,72,256]{2,1,0:T(8,128)(2,1)S(1)} %get-tuple-element.17.refs_2_), channel_id=1, source_target_pairs={{0,1},{1,0},{30,31},{31,30}} | collective-permute-start | bytes 1327112 | tf_op jit(solution)/shard_map/ppermute | solution.py:280
  26.6 2.6 %collective-permute-start.6 = (bf16[12,72,256]{2,1,0:T(8,128)(2,1)S(1)}, bf16[12,72,256]{2,1,0:T(8,128)(2,1)S(1)}, u32[]{:S(2)}, u32[]{:S(2)}) collective-permute-start(bf16[12,72,256]{2,1,0:T(8,128)(2,1)S(1)} %get-tuple-element.17.refs_2_), channel_id=1, source_target_pairs={{0,31},{1,30},{30,1},{31,0}} | collective-permute-start | bytes 1327112 | tf_op jit(solution)/shard_map/ppermute | solution.py:281
  30.5 3.9 %collective-permute-done.5.refs_3_ = bf16[12,72,256]{2,1,0:T(8,128)(2,1)S(1)} collective-permute-done((bf16[12,72,256]{2,1,0:T(8,128)(2,1)S(1)}, bf16[12,72,256]{2,1,0:T(8,128)(2,1)S(1)}, u32[]{:S(2)}, u32[]{:S(2)}) %collective-permute-start.5) | collective-permute-done | bytes 442400 | tf_op jit(solution)/shard_map/ppermute | solution.py:280
  34.4 5.5 %collective-permute-done.6.refs_4_ = bf16[12,72,256]{2,1,0:T(8,128)(2,1)S(1)} collective-permute-done((bf16[12,72,256]{2,1,0:T(8,128)(2,1)S(1)}, bf16[12,72,256]{2,1,0:T(8,128)(2,1)S(1)}, u32[]{:S(2)}, u32[]{:S(2)}) %collective-permute-start.6) | collective-permute-done | bytes 442400 | tf_op jit(solution)/shard_map/ppermute | solution.py:281
  39.9 4.3 %shard_map.130 = bf16[12,8,36,256]{3,2,1,0:T(8,128)(2,1)S(1)} custom-call(s32[144]{0:T(256)S(1)} %reshape.41.adjacency, bf16[4,72,72]{2,1,0:T(8,128)(2,1)S(1)} %copy-done.4, bf16[320,384]{1,0:T(8,128)(2,1)S(1)} %copy-done.2, bf16[12,4,32,256]{3,2,1,0:T(8,128)(2,1)S(1)} %copy-done.1, bf16[12,16,256]{2,1,0:T(8,128)(2,1)S(1)} %get-tuple-element.14.sides, ...), custom_call_target="tpu_custom_call" | custom-call | flops 1000 | bytes 5000000 | tf_op jit(solution)/shard_map/pallas_call | solution.py:320
  44.2 3.0 %fusion.2 = f32[12,4,32,256]{3,0,2,1:T(8,128)S(1)} fusion(bf16[3,3,256,256]{3,2,1,0:T(8,128)(2,1)S(1)} %copy-done.7, bf16[12,8,36,256]{3,2,1,0:T(8,128)(2,1)S(1)} %shard_map.130), kind=kOutput, calls=%fused_computation.3 | convolution fusion | flops 1811939328 | bytes 4521984 | tf_op jit(solution)/shard_map/conv_general_dilated | solution.py:510
  53.7 2.4 %copy.22 = bf16[3,3,256,256]{2,3,1,0:T(8,128)(2,1)} copy(bf16[3,3,256,256]{3,2,1,0:T(8,128)(2,1)} %param.11) | data formatting | bytes 2359296 | tf_op args[1]
  56.7 2.2 %fusion.10 = bf16[1152,256]{1,0:T(8,128)(2,1)} fusion(bf16[1160,256]{1,0:T(8,128)(2,1)} %collective-permute-done.14, bf16[2,1152,256]{2,1,0:T(8,128)(2,1)} %bitcast.202, s32[]{:T(128)S(6)} %select_n.58), kind=kLoop, calls=%fused_computation.21 | loop fusion | flops 1179648 | bytes 1769476 | tf_op jit(solution)/shard_map/convert_element_type | solution.py:571
  60.8 3.0 %collective-permute-start.16 = (bf16[296,256]{1,0:T(8,128)(2,1)}, bf16[296,256]{1,0:T(8,128)(2,1)}, u32[]{:S(2)}, u32[]{:S(2)}) collective-permute-start(bf16[296,256]{1,0:T(8,128)(2,1)} %get-tuple-element.58), channel_id=1, source_target_pairs={{0,4},{1,5},{2,6},{3,7},{4,0},{5,1},{6,2},{7,3},{8,12},{9,13},{10,... | collective-permute-start | bytes 454664 | tf_op jit(solution)/shard_map/ppermute | solution.py:579
  64.4 4.3 %collective-permute-done.17 = bf16[296,256]{1,0:T(8,128)(2,1)} collective-permute-done((bf16[296,256]{1,0:T(8,128)(2,1)}, bf16[296,256]{1,0:T(8,128)(2,1)}, u32[]{:S(2)}, u32[]{:S(2)}) %collective-permute-start.17) | collective-permute-done | bytes 151584 | tf_op jit(solution)/shard_map/ppermute | solution.py:579
  68.8 2.8 %collective-permute-done.16 = bf16[296,256]{1,0:T(8,128)(2,1)} collective-permute-done((bf16[296,256]{1,0:T(8,128)(2,1)}, bf16[296,256]{1,0:T(8,128)(2,1)}, u32[]{:S(2)}, u32[]{:S(2)}) %collective-permute-start.16) | collective-permute-done | bytes 151584 | tf_op jit(solution)/shard_map/ppermute | solution.py:579
  73.7 4.3 %collective-permute-start.18 = (bf16[80,256]{1,0:T(8,128)(2,1)S(1)}, bf16[80,256]{1,0:T(8,128)(2,1)S(1)}, u32[]{:S(2)}, u32[]{:S(2)}) collective-permute-start(bf16[80,256]{1,0:T(8,128)(2,1)S(1)} %get-tuple-element.54), channel_id=1, source_target_pairs={{0,8},{1,9},{2,10},{3,11},{4,12},{5,13},{6,14},{7,15},{8,0},{9,1},... | collective-permute-start | bytes 122888 | tf_op jit(solution)/shard_map/ppermute | solution.py:579
  78.1 4.5 %collective-permute-start.9 = (bf16[12,8,256]{2,1,0:T(8,128)(2,1)S(1)}, bf16[12,8,256]{2,1,0:T(8,128)(2,1)S(1)}, u32[]{:S(2)}, u32[]{:S(2)}) collective-permute-start(bf16[12,8,256]{2,1,0:T(8,128)(2,1)S(1)} %get-tuple-element.50), channel_id=1, source_target_pairs={{0,31},{1,30},{2,29},{3,28},{4,27},{5,26},{6,25},{7,24},{8,23},{9,... | collective-permute-start | bytes 147464 | tf_op jit(solution)/shard_map/ppermute | solution.py:273
  84.3 4.2 %collective-permute-start.21 = (bf16[1,72,256]{2,1,0:T(8,128)(2,1)S(1)}, bf16[1,72,256]{2,1,0:T(8,128)(2,1)S(1)}, u32[]{:S(2)}, u32[]{:S(2)}) collective-permute-start(bf16[1,72,256]{2,1,0:T(8,128)(2,1)S(1)} %bitcast.211), channel_id=1, source_target_pairs={{0,8},{1,9},{2,10},{3,11},{4,12},{5,13},{6,14},{7,15},{8,0},{9,1},... | collective-permute-start | bytes 110600 | tf_op jit(solution)/shard_map/ppermute | solution.py:592
  88.6 1.9 %shard_map.131 = (bf16[12,16,256]{2,1,0:T(8,128)(2,1)S(1)}, bf16[12,72,256]{2,1,0:T(8,128)(2,1)S(1)}, bf16[12,72,256]{2,1,0:T(8,128)(2,1)S(1)}, bf16[12,72,256]{2,1,0:T(8,128)(2,1)S(1)}) custom-call(s32[144]{0:T(256)S(1)} %reshape.41.adjacency, bf16[12,4,32,256]{3,2,1,0:T(8,128)(2,1)S(1)} %get-tuple-element.25.field, ...), custom_call_target="tpu_custom_call" | custom-call | flops 1000 | bytes 3000000 | tf_op jit(solution)/shard_map/pallas_call | solution.py:288
  90.6 4.4 %collective-permute-start.11 = (bf16[12,72,256]{2,1,0:T(8,128)(2,1)S(1)}, bf16[12,72,256]{2,1,0:T(8,128)(2,1)S(1)}, u32[]{:S(2)}, u32[]{:S(2)}) collective-permute-start(bf16[12,72,256]{2,1,0:T(8,128)(2,1)S(1)} %get-tuple-element.20), channel_id=1, source_target_pairs={{0,30},{1,31},{2,0},{3,1},{4,2},{5,3},{6,4},{7,5},{8,6},{9,7},{10,... | collective-permute-start | bytes 1327112 | tf_op jit(solution)/shard_map/ppermute | solution.py:279
  95.2 2.0 %collective-permute-start.25 = (bf16[4,72,256]{2,1,0:T(8,128)(2,1)S(1)}, bf16[4,72,256]{2,1,0:T(8,128)(2,1)S(1)}, u32[]{:S(2)}, u32[]{:S(2)}) collective-permute-start(bf16[4,72,256]{2,1,0:T(8,128)(2,1)S(1)} %get-tuple-element.42), channel_id=1, source_target_pairs={{0,4},{1,5},{2,6},{3,7},{4,0},{5,1},{6,2},{7,3},{8,12},{9,13},{10,... | collective-permute-start | bytes 442376 | tf_op jit(solution)/shard_map/ppermute | solution.py:592
  98.7 1.9 %multiply_convert_fusion = bf16[12,4,32,256]{3,2,1,0:T(8,128)(2,1)} fusion(f32[256]{0:T(256)S(1)} %copy-done.11, f32[12,4,32,256]{3,0,2,1:T(8,128)S(1)} %fusion.2), kind=kLoop, calls=%fused_computation.14 | loop fusion | flops 2359296 | bytes 2360320 | tf_op jit(solution)/shard_map/convert_element_type | solution.py:611
  100.6 2.3 %collective-permute-done.10.up = bf16[12,72,256]{2,1,0:T(8,128)(2,1)S(1)} collective-permute-done((bf16[12,72,256]{2,1,0:T(8,128)(2,1)S(1)}, bf16[12,72,256]{2,1,0:T(8,128)(2,1)S(1)}, u32[]{:S(2)}, u32[]{:S(2)}) %collective-permute-start.10) | collective-permute-done | bytes 442400 | tf_op jit(solution)/shard_map/ppermute | solution.py:278
  102.9 3.5 %collective-permute-start.12 = (bf16[12,72,256]{2,1,0:T(8,128)(2,1)S(1)}, bf16[12,72,256]{2,1,0:T(8,128)(2,1)S(1)}, u32[]{:S(2)}, u32[]{:S(2)}) collective-permute-start(bf16[12,72,256]{2,1,0:T(8,128)(2,1)S(1)} %get-tuple-element.23.edge), channel_id=1, source_target_pairs={{0,1},{1,0},{30,31},{31,30}} | collective-permute-start | bytes 1327112 | tf_op jit(solution)/shard_map/ppermute | solution.py:280
  106.4 1.9 %collective-permute-start.13 = (bf16[12,72,256]{2,1,0:T(8,128)(2,1)S(1)}, bf16[12,72,256]{2,1,0:T(8,128)(2,1)S(1)}, u32[]{:S(2)}, u32[]{:S(2)}) collective-permute-start(bf16[12,72,256]{2,1,0:T(8,128)(2,1)S(1)} %get-tuple-element.23.edge), channel_id=1, source_target_pairs={{0,31},{1,30},{30,1},{31,0}} | collective-permute-start | bytes 1327112 | tf_op jit(solution)/shard_map/ppermute | solution.py:281
  108.3 2.9 %shard_map.132 = (bf16[12,8,36,256]{3,2,1,0:T(8,128)(2,1)S(1)}, f32[12,4,32,256]{3,2,1,0:T(8,128)S(1)}) custom-call(s32[144]{0:T(256)S(1)} %reshape.41.adjacency, bf16[320,384]{1,0:T(8,128)(2,1)S(1)} %copy-done.2, bf16[2,24,384]{2,1,0:T(8,128)(2,1)S(1)} %copy-done.5, bf16[3,3,256,256]{3,2,1,0:T(8,128)(2,1)S(1)} %reverse_bitcast_fusion.rotated, ...), custom_call_target="tpu_custom_call" | custom-call | flops 1000 | bytes 8000000 | tf_op jit(solution)/shard_map/pallas_call | solution.py:477
  112.7 3.0 %fusion = f32[12,4,32,256]{3,0,2,1:T(8,128)S(1)} fusion(bf16[3,3,256,256]{3,2,1,0:T(8,128)(2,1)S(1)} %copy-done.8, bf16[12,8,36,256]{3,2,1,0:T(8,128)(2,1)S(1)} %get-tuple-element.21), kind=kOutput, calls=%fused_computation.1 | convolution fusion | flops 1811939328 | bytes 4521984 | tf_op jit(solution)/shard_map/conv_general_dilated | solution.py:510
  116.8 2.8 %collective-permute-done.13.far_cross = bf16[12,72,256]{2,1,0:T(8,128)(2,1)S(1)} collective-permute-done((bf16[12,72,256]{2,1,0:T(8,128)(2,1)S(1)}, bf16[12,72,256]{2,1,0:T(8,128)(2,1)S(1)}, u32[]{:S(2)}, u32[]{:S(2)}) %collective-permute-start.13) | collective-permute-done | bytes 442400 | tf_op jit(solution)/shard_map/ppermute | solution.py:281
  119.6 4.6 %shard_map.133 = bf16[12,4,32,256]{3,2,1,0:T(8,128)(2,1)} custom-call(s32[144]{0:T(256)S(1)} %reshape.41.adjacency, bf16[4,192,72]{2,1,0:T(8,128)(2,1)S(1)} %copy-done.3, bf16[3,3,256,256]{3,2,1,0:T(8,128)(2,1)S(1)} %reverse_bitcast_fusion.rotated, f32[12,4,32,256]{3,2,1,0:T(8,128)S(1)} %copy_add_fusion.partial, ...), custom_call_target="tpu_custom_call" | custom-call | flops 1000 | bytes 5000000 | tf_op jit(solution)/shard_map/pallas_call | solution.py:495
  125.2 1.6 %convert_multiply_fusion = f32[32,72,256]{2,1,0:T(8,128)} fusion(bf16[16,72,256]{2,1,0:T(8,128)(2,1)S(1)} %get-tuple-element.27, bf16[16,72,256]{2,1,0:T(8,128)(2,1)S(1)} %get-tuple-element.26), kind=kLoop, calls=%fused_computation.5 | loop fusion | flops 1769472 | bytes 3538944 | tf_op jit(solution)/shard_map/mul | solution.py:632
  (106 shorter events, 24.5 us)
Async XLA Ops:
  0.6 39.2 %copy-start.4 = (bf16[4,72,72]{2,1,0:T(8,128)(2,1)S(1)}, bf16[4,72,72]{2,1,0:T(8,128)(2,1)}, u32[]{:S(2)}) copy-start(bf16[4,72,72]{2,1,0:T(8,128)(2,1)} %constant.70.clone.flips) | copy-start | bytes 124420
  0.6 39.2 %copy-start.2 = (bf16[320,384]{1,0:T(8,128)(2,1)S(1)}, bf16[320,384]{1,0:T(8,128)(2,1)}, u32[]{:S(2)}) copy-start(bf16[320,384]{1,0:T(8,128)(2,1)} %constant.71.clone.picks) | copy-start | bytes 737284
  1.9 13.8 %collective-permute-start = (bf16[12,16,256]{2,1,0:T(8,128)(2,1)S(1)}, bf16[12,16,256]{2,1,0:T(8,128)(2,1)S(1)}, u32[]{:S(2)}, u32[]{:S(2)}) collective-permute-start(bf16[12,16,256]{2,1,0:T(8,128)(2,1)S(1)} %get-tuple-element.53.edges), channel_id=1, source_target_pairs={{0,1},{1,0},{2,3},{3,2},{4,5},{5,4},{6,7},{7,6},{8,9},{9,8},{10,11... | collective-permute-start | bytes 294920 | tf_op jit(solution)/shard_map/ppermute | solution.py:262
  4.9 6.5 %collective-permute-start.1 = (bf16[12,8,256]{2,1,0:T(8,128)(2,1)S(1)}, bf16[12,8,256]{2,1,0:T(8,128)(2,1)S(1)}, u32[]{:S(2)}, u32[]{:S(2)}) collective-permute-start(bf16[12,8,256]{2,1,0:T(8,128)(2,1)S(1)} %get-tuple-element.52), channel_id=1, source_target_pairs={{0,30},{1,31},{2,28},{3,29},{4,26},{5,27},{6,24},{7,25},{8,22},{9,... | collective-permute-start | bytes 147464 | tf_op jit(solution)/shard_map/ppermute | solution.py:272
  8.6 7.1 %collective-permute-start.2 = (bf16[12,8,256]{2,1,0:T(8,128)(2,1)S(1)}, bf16[12,8,256]{2,1,0:T(8,128)(2,1)S(1)}, u32[]{:S(2)}, u32[]{:S(2)}) collective-permute-start(bf16[12,8,256]{2,1,0:T(8,128)(2,1)S(1)} %get-tuple-element.52), channel_id=1, source_target_pairs={{0,31},{1,30},{2,29},{3,28},{4,27},{5,26},{6,25},{7,24},{8,23},{9,... | collective-permute-start | bytes 147464 | tf_op jit(solution)/shard_map/ppermute | solution.py:273
  16.9 23.0 %copy-start.1 = (bf16[12,4,32,256]{3,2,1,0:T(8,128)(2,1)S(1)}, bf16[12,4,32,256]{3,2,1,0:T(8,128)(2,1)}, u32[]{:S(2)}) copy-start(bf16[12,4,32,256]{3,2,1,0:T(8,128)(2,1)} %field.3) | copy-start | bytes 2359300
  19.7 10.7 %collective-permute-start.3 = (bf16[12,72,256]{2,1,0:T(8,128)(2,1)}, bf16[12,72,256]{2,1,0:T(8,128)(2,1)S(1)}, u32[]{:S(2)}, u32[]{:S(2)}) collective-permute-start(bf16[12,72,256]{2,1,0:T(8,128)(2,1)} %get-tuple-element.15), channel_id=1, source_target_pairs={{0,2},{1,3},{2,4},{3,5},{4,6},{5,7},{6,8},{7,9},{8,10},{9,11},{10,... | collective-permute-start | bytes 1327112 | tf_op jit(solution)/shard_map/ppermute | solution.py:278
  20.7 9.8 %collective-permute-start.4 = (bf16[12,72,256]{2,1,0:T(8,128)(2,1)}, bf16[12,72,256]{2,1,0:T(8,128)(2,1)S(1)}, u32[]{:S(2)}, u32[]{:S(2)}) collective-permute-start(bf16[12,72,256]{2,1,0:T(8,128)(2,1)} %get-tuple-element.16), channel_id=1, source_target_pairs={{0,30},{1,31},{2,0},{3,1},{4,2},{5,3},{6,4},{7,5},{8,6},{9,7},{10,... | collective-permute-start | bytes 1327112 | tf_op jit(solution)/shard_map/ppermute | solution.py:279
  24.2 10.2 %collective-permute-start.5 = (bf16[12,72,256]{2,1,0:T(8,128)(2,1)S(1)}, bf16[12,72,256]{2,1,0:T(8,128)(2,1)S(1)}, u32[]{:S(2)}, u32[]{:S(2)}) collective-permute-start(bf16[12,72,256]{2,1,0:T(8,128)(2,1)S(1)} %get-tuple-element.17.refs_2_), channel_id=1, source_target_pairs={{0,1},{1,0},{30,31},{31,30}} | collective-permute-start | bytes 1327112 | tf_op jit(solution)/shard_map/ppermute | solution.py:280
  26.6 13.2 %collective-permute-start.6 = (bf16[12,72,256]{2,1,0:T(8,128)(2,1)S(1)}, bf16[12,72,256]{2,1,0:T(8,128)(2,1)S(1)}, u32[]{:S(2)}, u32[]{:S(2)}) collective-permute-start(bf16[12,72,256]{2,1,0:T(8,128)(2,1)S(1)} %get-tuple-element.17.refs_2_), channel_id=1, source_target_pairs={{0,31},{1,30},{30,1},{31,0}} | collective-permute-start | bytes 1327112 | tf_op jit(solution)/shard_map/ppermute | solution.py:281
  53.7 2.4 %collective-permute-start.14 = (bf16[1160,256]{1,0:T(8,128)(2,1)}, bf16[1160,256]{1,0:T(8,128)(2,1)}, u32[]{:S(2)}, u32[]{:S(2)}) collective-permute-start(bf16[1160,256]{1,0:T(8,128)(2,1)} %pad_maximum_fusion), channel_id=1, source_target_pairs={{0,2},{1,3},{2,0},{3,1},{4,6},{5,7},{6,4},{7,5},{8,10},{9,11},{10,... | collective-permute-start | bytes 1781768 | tf_op jit(solution)/shard_map/ppermute | solution.py:579
  60.8 8.0 %collective-permute-start.17 = (bf16[296,256]{1,0:T(8,128)(2,1)}, bf16[296,256]{1,0:T(8,128)(2,1)}, u32[]{:S(2)}, u32[]{:S(2)}) collective-permute-start(bf16[296,256]{1,0:T(8,128)(2,1)} %get-tuple-element.59), channel_id=1, source_target_pairs={{0,5},{1,4},{2,7},{3,6},{4,1},{5,0},{6,3},{7,2},{8,13},{9,12},{10,... | collective-permute-start | bytes 454664 | tf_op jit(solution)/shard_map/ppermute | solution.py:579
  60.8 10.8 %collective-permute-start.16 = (bf16[296,256]{1,0:T(8,128)(2,1)}, bf16[296,256]{1,0:T(8,128)(2,1)}, u32[]{:S(2)}, u32[]{:S(2)}) collective-permute-start(bf16[296,256]{1,0:T(8,128)(2,1)} %get-tuple-element.58), channel_id=1, source_target_pairs={{0,4},{1,5},{2,6},{3,7},{4,0},{5,1},{6,2},{7,3},{8,12},{9,13},{10,... | collective-permute-start | bytes 454664 | tf_op jit(solution)/shard_map/ppermute | solution.py:579
  63.7 7.9 %collective-permute-start.15 = (bf16[296,256]{1,0:T(8,128)(2,1)}, bf16[296,256]{1,0:T(8,128)(2,1)}, u32[]{:S(2)}, u32[]{:S(2)}) collective-permute-start(bf16[296,256]{1,0:T(8,128)(2,1)} %get-tuple-element.57), channel_id=1, source_target_pairs={{0,1},{1,0},{2,3},{3,2},{4,5},{5,4},{6,7},{7,6},{8,9},{9,8},{10,11... | collective-permute-start | bytes 454664 | tf_op jit(solution)/shard_map/ppermute | solution.py:579
  64.4 24.1 %copy-start.6 = (bf16[3,3,256,256]{2,3,1,0:T(8,128)(2,1)S(1)}, bf16[3,3,256,256]{2,3,1,0:T(8,128)(2,1)}, u32[]{:S(2)}) copy-start(bf16[3,3,256,256]{2,3,1,0:T(8,128)(2,1)} %copy.22) | copy-start | bytes 3538948
  73.5 9.0 %collective-permute-start.20 = (bf16[80,256]{1,0:T(8,128)(2,1)S(1)}, bf16[80,256]{1,0:T(8,128)(2,1)S(1)}, u32[]{:S(2)}, u32[]{:S(2)}) collective-permute-start(bf16[80,256]{1,0:T(8,128)(2,1)S(1)} %get-tuple-element.56), channel_id=1, source_target_pairs={{0,24},{1,25},{2,26},{3,27},{4,28},{5,29},{6,30},{7,31},{8,16},{9,... | collective-permute-start | bytes 122888 | tf_op jit(solution)/shard_map/ppermute | solution.py:579
  73.6 10.4 %collective-permute-start.19 = (bf16[80,256]{1,0:T(8,128)(2,1)S(1)}, bf16[80,256]{1,0:T(8,128)(2,1)S(1)}, u32[]{:S(2)}, u32[]{:S(2)}) collective-permute-start(bf16[80,256]{1,0:T(8,128)(2,1)S(1)} %get-tuple-element.55), channel_id=1, source_target_pairs={{0,16},{1,17},{2,18},{3,19},{4,20},{5,21},{6,22},{7,23},{8,24},{9,... | collective-permute-start | bytes 122888 | tf_op jit(solution)/shard_map/ppermute | solution.py:579
  73.7 10.3 %collective-permute-start.18 = (bf16[80,256]{1,0:T(8,128)(2,1)S(1)}, bf16[80,256]{1,0:T(8,128)(2,1)S(1)}, u32[]{:S(2)}, u32[]{:S(2)}) collective-permute-start(bf16[80,256]{1,0:T(8,128)(2,1)S(1)} %get-tuple-element.54), channel_id=1, source_target_pairs={{0,8},{1,9},{2,10},{3,11},{4,12},{5,13},{6,14},{7,15},{8,0},{9,1},... | collective-permute-start | bytes 122888 | tf_op jit(solution)/shard_map/ppermute | solution.py:579
  78.0 6.3 %collective-permute-start.8 = (bf16[12,8,256]{2,1,0:T(8,128)(2,1)S(1)}, bf16[12,8,256]{2,1,0:T(8,128)(2,1)S(1)}, u32[]{:S(2)}, u32[]{:S(2)}) collective-permute-start(bf16[12,8,256]{2,1,0:T(8,128)(2,1)S(1)} %get-tuple-element.50), channel_id=1, source_target_pairs={{0,30},{1,31},{2,28},{3,29},{4,26},{5,27},{6,24},{7,25},{8,22},{9,... | collective-permute-start | bytes 147464 | tf_op jit(solution)/shard_map/ppermute | solution.py:272
  78.1 10.5 %collective-permute-start.9 = (bf16[12,8,256]{2,1,0:T(8,128)(2,1)S(1)}, bf16[12,8,256]{2,1,0:T(8,128)(2,1)S(1)}, u32[]{:S(2)}, u32[]{:S(2)}) collective-permute-start(bf16[12,8,256]{2,1,0:T(8,128)(2,1)S(1)} %get-tuple-element.50), channel_id=1, source_target_pairs={{0,31},{1,30},{2,29},{3,28},{4,27},{5,26},{6,25},{7,24},{8,23},{9,... | collective-permute-start | bytes 147464 | tf_op jit(solution)/shard_map/ppermute | solution.py:273
  82.5 6.0 %collective-permute-start.7 = (bf16[12,16,256]{2,1,0:T(8,128)(2,1)S(1)}, bf16[12,16,256]{2,1,0:T(8,128)(2,1)S(1)}, u32[]{:S(2)}, u32[]{:S(2)}) collective-permute-start(bf16[12,16,256]{2,1,0:T(8,128)(2,1)S(1)} %get-tuple-element.51.edges), channel_id=1, source_target_pairs={{0,1},{1,0},{2,3},{3,2},{4,5},{5,4},{6,7},{7,6},{8,9},{9,8},{10,11... | collective-permute-start | bytes 294920 | tf_op jit(solution)/shard_map/ppermute | solution.py:262
  84.0 11.0 %collective-permute-start.23 = (bf16[1,72,256]{2,1,0:T(8,128)(2,1)S(1)}, bf16[1,72,256]{2,1,0:T(8,128)(2,1)S(1)}, u32[]{:S(2)}, u32[]{:S(2)}) collective-permute-start(bf16[1,72,256]{2,1,0:T(8,128)(2,1)S(1)} %bitcast.209), channel_id=1, source_target_pairs={{0,24},{1,25},{2,26},{3,27},{4,28},{5,29},{6,30},{7,31},{8,16},{9,... | collective-permute-start | bytes 110600 | tf_op jit(solution)/shard_map/ppermute | solution.py:592
  84.1 10.9 %collective-permute-start.22 = (bf16[1,72,256]{2,1,0:T(8,128)(2,1)S(1)}, bf16[1,72,256]{2,1,0:T(8,128)(2,1)S(1)}, u32[]{:S(2)}, u32[]{:S(2)}) collective-permute-start(bf16[1,72,256]{2,1,0:T(8,128)(2,1)S(1)} %bitcast.210), channel_id=1, source_target_pairs={{0,16},{1,17},{2,18},{3,19},{4,20},{5,21},{6,22},{7,23},{8,24},{9,... | collective-permute-start | bytes 110600 | tf_op jit(solution)/shard_map/ppermute | solution.py:592
  84.3 10.7 %collective-permute-start.21 = (bf16[1,72,256]{2,1,0:T(8,128)(2,1)S(1)}, bf16[1,72,256]{2,1,0:T(8,128)(2,1)S(1)}, u32[]{:S(2)}, u32[]{:S(2)}) collective-permute-start(bf16[1,72,256]{2,1,0:T(8,128)(2,1)S(1)} %bitcast.211), channel_id=1, source_target_pairs={{0,8},{1,9},{2,10},{3,11},{4,12},{5,13},{6,14},{7,15},{8,0},{9,1},... | collective-permute-start | bytes 110600 | tf_op jit(solution)/shard_map/ppermute | solution.py:592
  90.5 12.4 %collective-permute-start.10 = (bf16[12,72,256]{2,1,0:T(8,128)(2,1)S(1)}, bf16[12,72,256]{2,1,0:T(8,128)(2,1)S(1)}, u32[]{:S(2)}, u32[]{:S(2)}) collective-permute-start(bf16[12,72,256]{2,1,0:T(8,128)(2,1)S(1)} %get-tuple-element.19), channel_id=1, source_target_pairs={{0,2},{1,3},{2,4},{3,5},{4,6},{5,7},{6,8},{7,9},{8,10},{9,11},{10,... | collective-permute-start | bytes 1327112 | tf_op jit(solution)/shard_map/ppermute | solution.py:278
  90.6 15.8 %collective-permute-start.11 = (bf16[12,72,256]{2,1,0:T(8,128)(2,1)S(1)}, bf16[12,72,256]{2,1,0:T(8,128)(2,1)S(1)}, u32[]{:S(2)}, u32[]{:S(2)}) collective-permute-start(bf16[12,72,256]{2,1,0:T(8,128)(2,1)S(1)} %get-tuple-element.20), channel_id=1, source_target_pairs={{0,30},{1,31},{2,0},{3,1},{4,2},{5,3},{6,4},{7,5},{8,6},{9,7},{10,... | collective-permute-start | bytes 1327112 | tf_op jit(solution)/shard_map/ppermute | solution.py:279
  95.1 16.1 %collective-permute-start.26 = (bf16[4,72,256]{2,1,0:T(8,128)(2,1)S(1)}, bf16[4,72,256]{2,1,0:T(8,128)(2,1)S(1)}, u32[]{:S(2)}, u32[]{:S(2)}) collective-permute-start(bf16[4,72,256]{2,1,0:T(8,128)(2,1)S(1)} %get-tuple-element.42), channel_id=1, source_target_pairs={{0,5},{1,4},{2,7},{3,6},{4,1},{5,0},{6,3},{7,2},{8,13},{9,12},{10,... | collective-permute-start | bytes 442376 | tf_op jit(solution)/shard_map/ppermute | solution.py:592
  95.2 16.0 %collective-permute-start.25 = (bf16[4,72,256]{2,1,0:T(8,128)(2,1)S(1)}, bf16[4,72,256]{2,1,0:T(8,128)(2,1)S(1)}, u32[]{:S(2)}, u32[]{:S(2)}) collective-permute-start(bf16[4,72,256]{2,1,0:T(8,128)(2,1)S(1)} %get-tuple-element.42), channel_id=1, source_target_pairs={{0,4},{1,5},{2,6},{3,7},{4,0},{5,1},{6,2},{7,3},{8,12},{9,13},{10,... | collective-permute-start | bytes 442376 | tf_op jit(solution)/shard_map/ppermute | solution.py:592
  97.3 14.0 %collective-permute-start.24 = (bf16[4,72,256]{2,1,0:T(8,128)(2,1)S(1)}, bf16[4,72,256]{2,1,0:T(8,128)(2,1)S(1)}, u32[]{:S(2)}, u32[]{:S(2)}) collective-permute-start(bf16[4,72,256]{2,1,0:T(8,128)(2,1)S(1)} %get-tuple-element.42), channel_id=1, source_target_pairs={{0,1},{1,0},{2,3},{3,2},{4,5},{5,4},{6,7},{7,6},{8,9},{9,8},{10,11... | collective-permute-start | bytes 442376 | tf_op jit(solution)/shard_map/ppermute | solution.py:592
  102.9 13.9 %collective-permute-start.12 = (bf16[12,72,256]{2,1,0:T(8,128)(2,1)S(1)}, bf16[12,72,256]{2,1,0:T(8,128)(2,1)S(1)}, u32[]{:S(2)}, u32[]{:S(2)}) collective-permute-start(bf16[12,72,256]{2,1,0:T(8,128)(2,1)S(1)} %get-tuple-element.23.edge), channel_id=1, source_target_pairs={{0,1},{1,0},{30,31},{31,30}} | collective-permute-start | bytes 1327112 | tf_op jit(solution)/shard_map/ppermute | solution.py:280
  106.4 13.2 %collective-permute-start.13 = (bf16[12,72,256]{2,1,0:T(8,128)(2,1)S(1)}, bf16[12,72,256]{2,1,0:T(8,128)(2,1)S(1)}, u32[]{:S(2)}, u32[]{:S(2)}) collective-permute-start(bf16[12,72,256]{2,1,0:T(8,128)(2,1)S(1)} %get-tuple-element.23.edge), channel_id=1, source_target_pairs={{0,31},{1,30},{30,1},{31,0}} | collective-permute-start | bytes 1327112 | tf_op jit(solution)/shard_map/ppermute | solution.py:281
  111.5 13.3 %collective-permute-start.27 = (bf16[16,72,256]{2,1,0:T(8,128)(2,1)S(1)}, bf16[16,72,256]{2,1,0:T(8,128)(2,1)S(1)}, u32[]{:S(2)}, u32[]{:S(2)}) collective-permute-start(bf16[16,72,256]{2,1,0:T(8,128)(2,1)S(1)} %get-tuple-element.32), channel_id=1, source_target_pairs={{0,2},{1,3},{2,0},{3,1},{4,6},{5,7},{6,4},{7,5},{8,10},{9,11},{10,... | collective-permute-start | bytes 1769480 | tf_op jit(solution)/shard_map/ppermute | solution.py:592
  (8 other events, 31.1 us)

commit v8 on v7

--- a/solution.py
+++ b/solution.py
@@ -296,25 +296,24 @@
     )(*inputs)
 
 
-def joint_strips(field, adjacency):
+def side_strips(field, adjacency, cols):
     face_count, tile_rows, width, channels = field.shape
-    cols = exchange_cols(field)
     strip = (face_count, 2 * width + 8, channels)
     tail = (face_count, 8, channels)
-    sides, top, bottom, edge = side_call(
+    return side_call(
         col_kernel,
         field,
         (adjacency, field, *cols),
         (cols[0].shape, strip, strip, strip),
         (tail, tail),
     )
-    up, down, row_same, row_cross = exchange_rows(top, bottom, edge)
-    return (field, sides, up, down, edge, row_same, row_cross)
 
 
 def pad_field(field, adjacency):
     face_count, tile_rows, width, channels = field.shape
-    strips = joint_strips(field, adjacency)
+    sides, top, bottom, edge = side_strips(field, adjacency, exchange_cols(field))
+    up, down, row_same, row_cross = exchange_rows(top, bottom, edge)
+    strips = (field, sides, up, down, edge, row_same, row_cross)
     padded = (face_count, tile_rows + 4, width + 4, channels)
     size = stack_places(tile_rows, width)[3]
     return pl.pallas_call(
@@ -467,9 +466,8 @@
                     out[face, y] = (partial[face, y] + term).astype(jnp.bfloat16)
 
 
-def return_field(field, adjacency, rotated):
+def return_field(field, adjacency, rotated, sides, up, down, edge, row_same, row_cross):
     face_count, tile_rows, width, channels = field.shape
-    _, sides, up, down, edge, row_same, row_cross = joint_strips(field, adjacency)
     padded = (face_count, tile_rows + 4, width + 4, channels)
     size = stack_places(tile_rows, width)[3]
     picks = pad_picks(tile_rows, width)
@@ -557,7 +555,7 @@
     return terms[0]
 
 
-def reduce_everywhere(matrix, vector):
+def reduce_everywhere(matrix, vector, field, adjacency, cols):
     count = lax.axis_size("frow") * lax.axis_size("fcol")
     index = lax.axis_index("frow") * lax.axis_size("fcol") + lax.axis_index("fcol")
     width = matrix.shape[-1]
@@ -565,15 +563,25 @@
     vector = jnp.concatenate([vector[None], pad], 0)
     part = matrix.reshape(-1, width)
     stages = reduce_stages()
-    for stage in stages:
+    for order, stage in enumerate(stages):
+        part, vector = part.astype(jnp.bfloat16), vector.astype(jnp.bfloat16)
+        if order == 0:
+            part, vector, *cols = lax.optimization_barrier((part, vector, *cols))
+            strips = side_strips(field, adjacency, cols)
+        if order == 1:
+            part, vector, *strips = lax.optimization_barrier((part, vector, *strips))
+            sides, top, bottom, edge = strips
+            up, down, row_same, row_cross = exchange_rows(top, bottom, edge)
+        if order == 2:
+            part, vector, up, down = lax.optimization_barrier((part, vector, up, down))
         offsets = stage_offsets(stage)
         place = stage_place(index, stage)
         part = part.reshape(len(offsets), -1, width).astype(jnp.bfloat16)
         vector = lax.optimization_barrier(vector.astype(jnp.bfloat16))
         rows = part.shape[1]
         sums, vectors = [], []
-        for order, offset in enumerate(offsets):
-            piece = lax.dynamic_slice_in_dim(part, place ^ order, 1, 0)[0]
+        for turn, offset in enumerate(offsets):
+            piece = lax.dynamic_slice_in_dim(part, place ^ turn, 1, 0)[0]
             if offset:
                 packed = jnp.concatenate([piece, vector], 0)
                 packed = lax.ppermute(packed, axes, [(i, i ^ offset) for i in range(count)])
@@ -585,7 +593,9 @@
         part = fold_sum(sums)
         vector = fold_sum(vectors)
     part = lax.optimization_barrier(part.astype(jnp.bfloat16))[None]
-    for stage in stages[::-1]:
+    for order, stage in enumerate(stages[::-1]):
+        if order == len(stages) - 2:
+            part, row_same, row_cross = lax.optimization_barrier((part, row_same, row_cross))
         offsets = stage_offsets(stage)
         place = stage_place(index, stage)
         pieces = [part] + [
@@ -600,7 +610,8 @@
             ],
             0,
         )
-    return (part.reshape(matrix.shape).astype(jnp.float32), vector[0])
+    rows = (sides, up, down, edge, row_same, row_cross)
+    return (part.reshape(matrix.shape).astype(jnp.float32), vector[0], rows)
 
 
 def local(face_input, kernel, convolution_bias, upstream, adjacency):
@@ -625,14 +636,16 @@
             )
     kernel_local = jnp.stack(tap_list, 0).reshape(kernel.shape)
     bias_local = jnp.sum(pre_grad.astype(jnp.float32), axis=(0, 1, 2))
-    kernel_total, bias_total = reduce_everywhere(kernel_local, bias_local)
+    kernel_total, bias_total, rows = reduce_everywhere(
+        kernel_local, bias_local, pre_grad, table, exchange_cols(pre_grad)
+    )
     scale = 1.0 / math.sqrt(
         face_count * tile_rows * lax.axis_size("frow") * tile_cols * lax.axis_size("fcol")
     )
     kernel_grad = kernel_total * scale
     bias_grad = bias_total * scale
     rotated = jnp.transpose(jnp.flip(kernel, (0, 1)), (0, 1, 3, 2))
-    input_gradient = return_field(pre_grad, table, rotated)
+    input_gradient = return_field(pre_grad, table, rotated, *rows)
     return (activation, input_gradient, kernel_grad, bias_grad)
 
 

time: 127 us -> 143 us (1.13)
  local copies, waits for them, and re-layouts: 7.37 us -> 18.2 us
  matrix products: 9.81 us -> 15.7 us
  other arithmetic: 13.7 us -> 12.1 us
    unnamed x28 -> x50, local copies, waits for them, and re-layouts: 4.59 us -> 14.1 us
    dot_general x9, matrix products: 3.8 us -> 9.66 us  [local(): lax.dot_general(window, pre_grad, (((0, 1, 2), (0, 1, 2)), ((), ())), pre...]
    ppermute x2, waiting for transfers between devices: 0.01 us -> 2.97 us  [exchange_cols(): beside = lax.ppermute(edges, axes, shifted_pairs(0, 1))]
    ppermute x2, waiting for transfers between devices: 3.54 us -> 1.28 us  [exchange_rows(): up = lax.ppermute(bottom, axes, shifted_pairs(1, 0))]
    ppermute x7, waiting for transfers between devices: 0.02 us -> 1.84 us  [reduce_everywhere(): lax.ppermute(part, axes, [(i, i ^ offset) for i in range(count)])]
    ppermute x2, waiting for transfers between devices: 3.88 us -> 2.36 us  [exchange_rows(): row_same = lax.ppermute(edge, axes, mirror_pairs(True, False, True))]
    convert_element_type x4, other arithmetic: 4.77 us -> 3.29 us  [reduce_everywhere(): part, vector = (part.astype(jnp.bfloat16), vector.astype(jnp.bfloat16))]
  transfers between devices with their start and end apart: 28 -> 28, of which waited for: 10 -> 13; matrix products, arithmetic and copies ran while one was open for 8% -> 15% of each run, Pallas kernels for 7% -> 7%
where the time goes in v8:
time: 143 us
  starting transfers between devices  49.1 us (34%)
  waiting for transfers between devices  28.9 us (20%)
  local copies, waits for them, and re-layouts  18.2 us (13%)
  Pallas kernels  17.7 us (12%)
  matrix products  15.7 us (11%)
  other arithmetic  12.1 us (8%)
    unnamed x50, local copies, waits for them, and re-layouts  14.1 us
    dot_general x9, matrix products, local(): lax.dot_general(window, pre_grad, (((0, 1, 2), (0, 1, 2)), ((), ())), pre...  9.66 us
    ppermute x7, starting transfers between devices, reduce_everywhere(): lax.ppermute(part, axes, [(i, i ^ offset) for i in range(count)])  8.11 us
    ppermute x2, waiting for transfers between devices, exchange_rows(): row_cross = lax.ppermute(edge, axes, mirror_pairs(True, True, True))  7.96 us
    ppermute x7, starting transfers between devices, reduce_everywhere(): packed = lax.ppermute(packed, axes, [(i, i ^ offset) for i in range(count)])  7.93 us
    ppermute x2, starting transfers between devices, exchange_rows(): down = lax.ppermute(top, axes, shifted_pairs(-1, 0))  7.93 us
    ppermute x7, waiting for transfers between devices, reduce_everywhere(): packed = lax.ppermute(packed, axes, [(i, i ^ offset) for i in range(count)])  6.52 us
    conv_general_dilated x2, matrix products, conv(): lax.conv_general_dilated(value, taps, (1, 1), 'VALID', rhs_dilation=(DILA...  6.06 us
  transfers between devices with their start and end apart: 28, of which 13 were waited for; matrix products, arithmetic and copies ran while one was open for 15% of the time, Pallas kernels for 7%

profile of v8, /device:TPU:0, one launch (start us, length us, event | category | flops | bytes accessed | tf_op | source)
XLA Modules:
  0.0 142.9 jit_solution(59905147418320574)
XLA Ops:
  1.9 3.0 %collective-permute-start = (bf16[12,16,256]{2,1,0:T(8,128)(2,1)S(1)}, bf16[12,16,256]{2,1,0:T(8,128)(2,1)S(1)}, u32[]{:S(2)}, u32[]{:S(2)}) collective-permute-start(bf16[12,16,256]{2,1,0:T(8,128)(2,1)S(1)} %get-tuple-element.89.edges), channel_id=1, source_target_pairs={{0,1},{1,0},{2,3},{3,2},{4,5},{5,4},{6,7},{7,6},{8,9},{9,8},{10,11... | collective-permute-start | bytes 294920 | tf_op jit(solution)/shard_map/ppermute | solution.py:262
  4.9 3.7 %collective-permute-start.1 = (bf16[12,8,256]{2,1,0:T(8,128)(2,1)S(1)}, bf16[12,8,256]{2,1,0:T(8,128)(2,1)S(1)}, u32[]{:S(2)}, u32[]{:S(2)}) collective-permute-start(bf16[12,8,256]{2,1,0:T(8,128)(2,1)S(1)} %get-tuple-element.88), channel_id=1, source_target_pairs={{0,30},{1,31},{2,28},{3,29},{4,26},{5,27},{6,24},{7,25},{8,22},{9,... | collective-permute-start | bytes 147464 | tf_op jit(solution)/shard_map/ppermute | solution.py:272
  9.8 1.6 %collective-permute-done.1.far_same = bf16[12,8,256]{2,1,0:T(8,128)(2,1)S(1)} collective-permute-done((bf16[12,8,256]{2,1,0:T(8,128)(2,1)S(1)}, bf16[12,8,256]{2,1,0:T(8,128)(2,1)S(1)}, u32[]{:S(2)}, u32[]{:S(2)}) %collective-permute-start.1) | collective-permute-done | bytes 49184 | tf_op jit(solution)/shard_map/ppermute | solution.py:272
  11.4 4.3 %collective-permute-done.2.far_cross = bf16[12,8,256]{2,1,0:T(8,128)(2,1)S(1)} collective-permute-done((bf16[12,8,256]{2,1,0:T(8,128)(2,1)S(1)}, bf16[12,8,256]{2,1,0:T(8,128)(2,1)S(1)}, u32[]{:S(2)}, u32[]{:S(2)}) %collective-permute-start.2) | collective-permute-done | bytes 49184 | tf_op jit(solution)/shard_map/ppermute | solution.py:273
  16.9 3.0 %shard_map.129 = (bf16[12,16,256]{2,1,0:T(8,128)(2,1)S(1)}, bf16[12,72,256]{2,1,0:T(8,128)(2,1)}, bf16[12,72,256]{2,1,0:T(8,128)(2,1)}, bf16[12,72,256]{2,1,0:T(8,128)(2,1)S(1)}) custom-call(s32[144]{0:T(256)S(1)} %reshape.46.adjacency, bf16[12,4,32,256]{3,2,1,0:T(8,128)(2,1)S(1)} %copy-done, bf16[12,16,256]{2,1,0:T(8,128)(2,1)S(1)} %get-tuple-element.89.edges, ...), custom_call_target="tpu_custom_call" | custom-call | flops 1000 | bytes 3000000 | tf_op jit(solution)/shard_map/pallas_call | solution.py:288
  20.9 3.5 %collective-permute-start.4 = (bf16[12,72,256]{2,1,0:T(8,128)(2,1)}, bf16[12,72,256]{2,1,0:T(8,128)(2,1)S(1)}, u32[]{:S(2)}, u32[]{:S(2)}) collective-permute-start(bf16[12,72,256]{2,1,0:T(8,128)(2,1)} %get-tuple-element.35), channel_id=1, source_target_pairs={{0,30},{1,31},{2,0},{3,1},{4,2},{5,3},{6,4},{7,5},{8,6},{9,7},{10,... | collective-permute-start | bytes 1327112 | tf_op jit(solution)/shard_map/ppermute | solution.py:279
  24.4 2.4 %collective-permute-start.5 = (bf16[12,72,256]{2,1,0:T(8,128)(2,1)S(1)}, bf16[12,72,256]{2,1,0:T(8,128)(2,1)S(1)}, u32[]{:S(2)}, u32[]{:S(2)}) collective-permute-start(bf16[12,72,256]{2,1,0:T(8,128)(2,1)S(1)} %get-tuple-element.36.refs_2_), channel_id=1, source_target_pairs={{0,1},{1,0},{30,31},{31,30}} | collective-permute-start | bytes 1327112 | tf_op jit(solution)/shard_map/ppermute | solution.py:280
  26.8 2.6 %collective-permute-start.6 = (bf16[12,72,256]{2,1,0:T(8,128)(2,1)S(1)}, bf16[12,72,256]{2,1,0:T(8,128)(2,1)S(1)}, u32[]{:S(2)}, u32[]{:S(2)}) collective-permute-start(bf16[12,72,256]{2,1,0:T(8,128)(2,1)S(1)} %get-tuple-element.36.refs_2_), channel_id=1, source_target_pairs={{0,31},{1,30},{30,1},{31,0}} | collective-permute-start | bytes 1327112 | tf_op jit(solution)/shard_map/ppermute | solution.py:281
  32.2 2.4 %collective-permute-done.5.refs_3_ = bf16[12,72,256]{2,1,0:T(8,128)(2,1)S(1)} collective-permute-done((bf16[12,72,256]{2,1,0:T(8,128)(2,1)S(1)}, bf16[12,72,256]{2,1,0:T(8,128)(2,1)S(1)}, u32[]{:S(2)}, u32[]{:S(2)}) %collective-permute-start.5) | collective-permute-done | bytes 442400 | tf_op jit(solution)/shard_map/ppermute | solution.py:280
  35.3 4.7 %collective-permute-done.6.refs_4_ = bf16[12,72,256]{2,1,0:T(8,128)(2,1)S(1)} collective-permute-done((bf16[12,72,256]{2,1,0:T(8,128)(2,1)S(1)}, bf16[12,72,256]{2,1,0:T(8,128)(2,1)S(1)}, u32[]{:S(2)}, u32[]{:S(2)}) %collective-permute-start.6) | collective-permute-done | bytes 442400 | tf_op jit(solution)/shard_map/ppermute | solution.py:281
  45.8 4.3 %shard_map.130 = bf16[12,8,36,256]{3,2,1,0:T(8,128)(2,1)S(1)} custom-call(s32[144]{0:T(256)S(1)} %reshape.46.adjacency, bf16[4,72,72]{2,1,0:T(8,128)(2,1)S(1)} %copy-done.12, bf16[320,384]{1,0:T(8,128)(2,1)S(1)} %copy-done.2, bf16[12,4,32,256]{3,2,1,0:T(8,128)(2,1)S(1)} %copy-done.1, bf16[12,16,256]{2,1,0:T(8,128)(2,1)S(1)} %get-tuple-element.33.sides, ...), custom_call_target="tpu_custom_call" | custom-call | flops 1000 | bytes 5000000 | tf_op jit(solution)/shard_map/pallas_call | solution.py:319
  50.1 3.0 %fusion.2 = f32[12,4,32,256]{3,0,2,1:T(8,128)S(1)} fusion(bf16[3,3,256,256]{3,2,1,0:T(8,128)(2,1)S(1)} %copy-done.17, bf16[12,8,36,256]{3,2,1,0:T(8,128)(2,1)S(1)} %shard_map.130), kind=kOutput, calls=%fused_computation.3 | convolution fusion | flops 1811939328 | bytes 4521984 | tf_op jit(solution)/shard_map/conv_general_dilated | solution.py:508
  55.9 5.4 %collective-permute-start.9 = (bf16[12,8,256]{2,1,0:T(8,128)(2,1)S(1)}, bf16[12,8,256]{2,1,0:T(8,128)(2,1)S(1)}, u32[]{:S(2)}, u32[]{:S(2)}) collective-permute-start(bf16[12,8,256]{2,1,0:T(8,128)(2,1)S(1)} %get-tuple-element.86), channel_id=1, source_target_pairs={{0,31},{1,30},{2,29},{3,28},{4,27},{5,26},{6,25},{7,24},{8,23},{9,... | collective-permute-start | bytes 147464 | tf_op jit(solution)/shard_map/ppermute | solution.py:273
  70.4 3.0 %collective-permute-done.7.beside = bf16[12,16,256]{2,1,0:T(8,128)(2,1)S(1)} collective-permute-done((bf16[12,16,256]{2,1,0:T(8,128)(2,1)S(1)}, bf16[12,16,256]{2,1,0:T(8,128)(2,1)S(1)}, u32[]{:S(2)}, u32[]{:S(2)}) %collective-permute-start.7) | collective-permute-done | bytes 98336 | tf_op jit(solution)/shard_map/ppermute | solution.py:262
  75.3 2.9 %shard_map.131 = (bf16[12,16,256]{2,1,0:T(8,128)(2,1)S(1)}, bf16[12,72,256]{2,1,0:T(8,128)(2,1)S(1)}, bf16[12,72,256]{2,1,0:T(8,128)(2,1)}, bf16[12,72,256]{2,1,0:T(8,128)(2,1)S(1)}) custom-call(s32[144]{0:T(256)S(1)} %reshape.46.adjacency, bf16[12,4,32,256]{3,2,1,0:T(8,128)(2,1)S(1)} %get-tuple-element.63.field, ...), custom_call_target="tpu_custom_call" | custom-call | flops 1000 | bytes 3000000 | tf_op jit(solution)/shard_map/pallas_call | solution.py:288
  81.3 2.0 %collective-permute-start.12 = (bf16[296,256]{1,0:T(8,128)(2,1)S(1)}, bf16[296,256]{1,0:T(8,128)(2,1)}, u32[]{:S(2)}, u32[]{:S(2)}) collective-permute-start(bf16[296,256]{1,0:T(8,128)(2,1)S(1)} %get-tuple-element.94), channel_id=1, source_target_pairs={{0,4},{1,5},{2,6},{3,7},{4,0},{5,1},{6,2},{7,3},{8,12},{9,13},{10,... | collective-permute-start | bytes 454664 | tf_op jit(solution)/shard_map/ppermute | solution.py:587
  83.3 1.5 %collective-permute-start.11 = (bf16[296,256]{1,0:T(8,128)(2,1)S(1)}, bf16[296,256]{1,0:T(8,128)(2,1)}, u32[]{:S(2)}, u32[]{:S(2)}) collective-permute-start(bf16[296,256]{1,0:T(8,128)(2,1)S(1)} %get-tuple-element.93), channel_id=1, source_target_pairs={{0,1},{1,0},{2,3},{3,2},{4,5},{5,4},{6,7},{7,6},{8,9},{9,8},{10,11... | collective-permute-start | bytes 454664 | tf_op jit(solution)/shard_map/ppermute | solution.py:587
  84.8 4.4 %collective-permute-start.15 = (bf16[12,72,256]{2,1,0:T(8,128)(2,1)S(1)}, bf16[12,72,256]{2,1,0:T(8,128)(2,1)S(1)}, u32[]{:S(2)}, u32[]{:S(2)}) collective-permute-start(bf16[12,72,256]{2,1,0:T(8,128)(2,1)S(1)} %get-tuple-element.51), channel_id=1, source_target_pairs={{0,30},{1,31},{2,0},{3,1},{4,2},{5,3},{6,4},{7,5},{8,6},{9,7},{10,... | collective-permute-start | bytes 1327112 | tf_op jit(solution)/shard_map/ppermute | solution.py:279
  89.3 6.5 %collective-permute-done.12 = bf16[296,256]{1,0:T(8,128)(2,1)} collective-permute-done((bf16[296,256]{1,0:T(8,128)(2,1)S(1)}, bf16[296,256]{1,0:T(8,128)(2,1)}, u32[]{:S(2)}, u32[]{:S(2)}) %collective-permute-start.12) | collective-permute-done | bytes 151584 | tf_op jit(solution)/shard_map/ppermute | solution.py:587
  97.9 4.3 %collective-permute-start.16 = (bf16[80,256]{1,0:T(8,128)(2,1)S(1)}, bf16[80,256]{1,0:T(8,128)(2,1)S(1)}, u32[]{:S(2)}, u32[]{:S(2)}) collective-permute-start(bf16[80,256]{1,0:T(8,128)(2,1)S(1)} %get-tuple-element.90), channel_id=1, source_target_pairs={{0,8},{1,9},{2,10},{3,11},{4,12},{5,13},{6,14},{7,15},{8,0},{9,1},... | collective-permute-start | bytes 122888 | tf_op jit(solution)/shard_map/ppermute | solution.py:587
  102.2 2.4 %copy.22 = bf16[3,3,256,256]{2,3,1,0:T(8,128)(2,1)} copy(bf16[3,3,256,256]{3,2,1,0:T(8,128)(2,1)} %param.11) | data formatting | bytes 2359296 | tf_op args[1]
  104.5 3.4 %collective-permute-start.22 = (bf16[12,72,256]{2,1,0:T(8,128)(2,1)S(1)}, bf16[12,72,256]{2,1,0:T(8,128)(2,1)S(1)}, u32[]{:S(2)}, u32[]{:S(2)}) collective-permute-start(bf16[12,72,256]{2,1,0:T(8,128)(2,1)S(1)} %get-tuple-element.56.edge), channel_id=1, source_target_pairs={{0,1},{1,0},{30,31},{31,30}} | collective-permute-start | bytes 1327112 | tf_op jit(solution)/shard_map/ppermute | solution.py:280
  107.9 2.9 %collective-permute-start.23 = (bf16[12,72,256]{2,1,0:T(8,128)(2,1)S(1)}, bf16[12,72,256]{2,1,0:T(8,128)(2,1)S(1)}, u32[]{:S(2)}, u32[]{:S(2)}) collective-permute-start(bf16[12,72,256]{2,1,0:T(8,128)(2,1)S(1)} %get-tuple-element.56.edge), channel_id=1, source_target_pairs={{0,31},{1,30},{30,1},{31,0}} | collective-permute-start | bytes 1327112 | tf_op jit(solution)/shard_map/ppermute | solution.py:281
  111.0 4.3 %collective-permute-start.19 = (bf16[1,72,256]{2,1,0:T(8,128)(2,1)S(1)}, bf16[1,72,256]{2,1,0:T(8,128)(2,1)S(1)}, u32[]{:S(2)}, u32[]{:S(2)}) collective-permute-start(bf16[1,72,256]{2,1,0:T(8,128)(2,1)S(1)} %bitcast.214), channel_id=1, source_target_pairs={{0,8},{1,9},{2,10},{3,11},{4,12},{5,13},{6,14},{7,15},{8,0},{9,1},... | collective-permute-start | bytes 110600 | tf_op jit(solution)/shard_map/ppermute | solution.py:602
  118.2 3.2 %collective-permute-done.23.far_cross = bf16[12,72,256]{2,1,0:T(8,128)(2,1)S(1)} collective-permute-done((bf16[12,72,256]{2,1,0:T(8,128)(2,1)S(1)}, bf16[12,72,256]{2,1,0:T(8,128)(2,1)S(1)}, u32[]{:S(2)}, u32[]{:S(2)}) %collective-permute-start.23) | collective-permute-done | bytes 442400 | tf_op jit(solution)/shard_map/ppermute | solution.py:281
  121.5 1.9 %collective-permute-start.25 = (bf16[4,72,256]{2,1,0:T(8,128)(2,1)S(1)}, bf16[4,72,256]{2,1,0:T(8,128)(2,1)S(1)}, u32[]{:S(2)}, u32[]{:S(2)}) collective-permute-start(bf16[4,72,256]{2,1,0:T(8,128)(2,1)S(1)} %pad_maximum_fusion.7), channel_id=1, source_target_pairs={{0,4},{1,5},{2,6},{3,7},{4,0},{5,1},{6,2},{7,3},{8,12},{9,13},{10,... | collective-permute-start | bytes 442376 | tf_op jit(solution)/shard_map/ppermute | solution.py:602
  123.4 1.6 %collective-permute-start.24 = (bf16[4,72,256]{2,1,0:T(8,128)(2,1)S(1)}, bf16[4,72,256]{2,1,0:T(8,128)(2,1)S(1)}, u32[]{:S(2)}, u32[]{:S(2)}) collective-permute-start(bf16[4,72,256]{2,1,0:T(8,128)(2,1)S(1)} %pad_maximum_fusion.7), channel_id=1, source_target_pairs={{0,1},{1,0},{2,3},{3,2},{4,5},{5,4},{6,7},{7,6},{8,9},{9,8},{10,11... | collective-permute-start | bytes 442376 | tf_op jit(solution)/shard_map/ppermute | solution.py:602
  124.9 2.0 %multiply_convert_fusion = bf16[12,4,32,256]{3,2,1,0:T(8,128)(2,1)} fusion(f32[256]{0:T(256)S(1)} %copy-done.22, f32[12,4,32,256]{3,0,2,1:T(8,128)S(1)} %copy-done.15), kind=kLoop, calls=%fused_computation.14 | loop fusion | flops 2359296 | bytes 2360320 | tf_op jit(solution)/shard_map/convert_element_type | solution.py:622
  126.9 2.9 %shard_map.132 = (bf16[12,8,36,256]{3,2,1,0:T(8,128)(2,1)S(1)}, f32[12,4,32,256]{3,2,1,0:T(8,128)S(1)}) custom-call(s32[144]{0:T(256)S(1)} %reshape.46.adjacency, bf16[320,384]{1,0:T(8,128)(2,1)S(1)} %copy-done.2, bf16[2,24,384]{2,1,0:T(8,128)(2,1)S(1)} %copy-done.13, bf16[3,3,256,256]{3,2,1,0:T(8,128)(2,1)S(1)} %reverse_bitcast_fusion.rotated, ...), custom_call_target="tpu_custom_call" | custom-call | flops 1000 | bytes 8000000 | tf_op jit(solution)/shard_map/pallas_call | solution.py:475
  131.6 3.1 %fusion = f32[12,4,32,256]{3,0,2,1:T(8,128)S(1)} fusion(bf16[3,3,256,256]{3,2,1,0:T(8,128)(2,1)S(1)} %copy-done.18, bf16[12,8,36,256]{3,2,1,0:T(8,128)(2,1)S(1)} %get-tuple-element.54), kind=kOutput, calls=%fused_computation.1 | convolution fusion | flops 1811939328 | bytes 4521984 | tf_op jit(solution)/shard_map/conv_general_dilated | solution.py:508
  136.2 4.6 %shard_map.133 = bf16[12,4,32,256]{3,2,1,0:T(8,128)(2,1)} custom-call(s32[144]{0:T(256)S(1)} %reshape.46.adjacency, bf16[4,192,72]{2,1,0:T(8,128)(2,1)S(1)} %copy-done.11, bf16[3,3,256,256]{3,2,1,0:T(8,128)(2,1)S(1)} %reverse_bitcast_fusion.rotated, f32[12,4,32,256]{3,2,1,0:T(8,128)S(1)} %copy_add_fusion.partial, ...), custom_call_target="tpu_custom_call" | custom-call | flops 1000 | bytes 5000000 | tf_op jit(solution)/shard_map/pallas_call | solution.py:493
  141.2 1.6 %convert_multiply_fusion = f32[32,72,256]{2,1,0:T(8,128)} fusion(bf16[16,72,256]{2,1,0:T(8,128)(2,1)S(1)} %get-tuple-element.65, bf16[16,72,256]{2,1,0:T(8,128)(2,1)S(1)} %get-tuple-element.64), kind=kLoop, calls=%fused_computation.5 | loop fusion | flops 1769472 | bytes 3538944 | tf_op jit(solution)/shard_map/mul | solution.py:645
  (129 shorter events, 39.5 us)
Async XLA Ops:
  0.6 40.2 %copy-start.2 = (bf16[320,384]{1,0:T(8,128)(2,1)S(1)}, bf16[320,384]{1,0:T(8,128)(2,1)}, u32[]{:S(2)}) copy-start(bf16[320,384]{1,0:T(8,128)(2,1)} %constant.71.clone.picks) | copy-start | bytes 737284
  1.9 13.8 %collective-permute-start = (bf16[12,16,256]{2,1,0:T(8,128)(2,1)S(1)}, bf16[12,16,256]{2,1,0:T(8,128)(2,1)S(1)}, u32[]{:S(2)}, u32[]{:S(2)}) collective-permute-start(bf16[12,16,256]{2,1,0:T(8,128)(2,1)S(1)} %get-tuple-element.89.edges), channel_id=1, source_target_pairs={{0,1},{1,0},{2,3},{3,2},{4,5},{5,4},{6,7},{7,6},{8,9},{9,8},{10,11... | collective-permute-start | bytes 294920 | tf_op jit(solution)/shard_map/ppermute | solution.py:262
  4.9 6.5 %collective-permute-start.1 = (bf16[12,8,256]{2,1,0:T(8,128)(2,1)S(1)}, bf16[12,8,256]{2,1,0:T(8,128)(2,1)S(1)}, u32[]{:S(2)}, u32[]{:S(2)}) collective-permute-start(bf16[12,8,256]{2,1,0:T(8,128)(2,1)S(1)} %get-tuple-element.88), channel_id=1, source_target_pairs={{0,30},{1,31},{2,28},{3,29},{4,26},{5,27},{6,24},{7,25},{8,22},{9,... | collective-permute-start | bytes 147464 | tf_op jit(solution)/shard_map/ppermute | solution.py:272
  8.6 7.1 %collective-permute-start.2 = (bf16[12,8,256]{2,1,0:T(8,128)(2,1)S(1)}, bf16[12,8,256]{2,1,0:T(8,128)(2,1)S(1)}, u32[]{:S(2)}, u32[]{:S(2)}) collective-permute-start(bf16[12,8,256]{2,1,0:T(8,128)(2,1)S(1)} %get-tuple-element.88), channel_id=1, source_target_pairs={{0,31},{1,30},{2,29},{3,28},{4,27},{5,26},{6,25},{7,24},{8,23},{9,... | collective-permute-start | bytes 147464 | tf_op jit(solution)/shard_map/ppermute | solution.py:273
  16.9 23.9 %copy-start.1 = (bf16[12,4,32,256]{3,2,1,0:T(8,128)(2,1)S(1)}, bf16[12,4,32,256]{3,2,1,0:T(8,128)(2,1)}, u32[]{:S(2)}) copy-start(bf16[12,4,32,256]{3,2,1,0:T(8,128)(2,1)} %field.3) | copy-start | bytes 2359300
  19.9 10.7 %collective-permute-start.3 = (bf16[12,72,256]{2,1,0:T(8,128)(2,1)}, bf16[12,72,256]{2,1,0:T(8,128)(2,1)S(1)}, u32[]{:S(2)}, u32[]{:S(2)}) collective-permute-start(bf16[12,72,256]{2,1,0:T(8,128)(2,1)} %get-tuple-element.34), channel_id=1, source_target_pairs={{0,2},{1,3},{2,4},{3,5},{4,6},{5,7},{6,8},{7,9},{8,10},{9,11},{10,... | collective-permute-start | bytes 1327112 | tf_op jit(solution)/shard_map/ppermute | solution.py:278
  20.9 10.6 %collective-permute-start.4 = (bf16[12,72,256]{2,1,0:T(8,128)(2,1)}, bf16[12,72,256]{2,1,0:T(8,128)(2,1)S(1)}, u32[]{:S(2)}, u32[]{:S(2)}) collective-permute-start(bf16[12,72,256]{2,1,0:T(8,128)(2,1)} %get-tuple-element.35), channel_id=1, source_target_pairs={{0,30},{1,31},{2,0},{3,1},{4,2},{5,3},{6,4},{7,5},{8,6},{9,7},{10,... | collective-permute-start | bytes 1327112 | tf_op jit(solution)/shard_map/ppermute | solution.py:279
  24.4 10.2 %collective-permute-start.5 = (bf16[12,72,256]{2,1,0:T(8,128)(2,1)S(1)}, bf16[12,72,256]{2,1,0:T(8,128)(2,1)S(1)}, u32[]{:S(2)}, u32[]{:S(2)}) collective-permute-start(bf16[12,72,256]{2,1,0:T(8,128)(2,1)S(1)} %get-tuple-element.36.refs_2_), channel_id=1, source_target_pairs={{0,1},{1,0},{30,31},{31,30}} | collective-permute-start | bytes 1327112 | tf_op jit(solution)/shard_map/ppermute | solution.py:280
  26.8 13.2 %collective-permute-start.6 = (bf16[12,72,256]{2,1,0:T(8,128)(2,1)S(1)}, bf16[12,72,256]{2,1,0:T(8,128)(2,1)S(1)}, u32[]{:S(2)}, u32[]{:S(2)}) collective-permute-start(bf16[12,72,256]{2,1,0:T(8,128)(2,1)S(1)} %get-tuple-element.36.refs_2_), channel_id=1, source_target_pairs={{0,31},{1,30},{30,1},{31,0}} | collective-permute-start | bytes 1327112 | tf_op jit(solution)/shard_map/ppermute | solution.py:281
  55.8 14.6 %collective-permute-start.8 = (bf16[12,8,256]{2,1,0:T(8,128)(2,1)S(1)}, bf16[12,8,256]{2,1,0:T(8,128)(2,1)S(1)}, u32[]{:S(2)}, u32[]{:S(2)}) collective-permute-start(bf16[12,8,256]{2,1,0:T(8,128)(2,1)S(1)} %get-tuple-element.86), channel_id=1, source_target_pairs={{0,30},{1,31},{2,28},{3,29},{4,26},{5,27},{6,24},{7,25},{8,22},{9,... | collective-permute-start | bytes 147464 | tf_op jit(solution)/shard_map/ppermute | solution.py:272
  55.9 14.5 %collective-permute-start.9 = (bf16[12,8,256]{2,1,0:T(8,128)(2,1)S(1)}, bf16[12,8,256]{2,1,0:T(8,128)(2,1)S(1)}, u32[]{:S(2)}, u32[]{:S(2)}) collective-permute-start(bf16[12,8,256]{2,1,0:T(8,128)(2,1)S(1)} %get-tuple-element.86), channel_id=1, source_target_pairs={{0,31},{1,30},{2,29},{3,28},{4,27},{5,26},{6,25},{7,24},{8,23},{9,... | collective-permute-start | bytes 147464 | tf_op jit(solution)/shard_map/ppermute | solution.py:273
  68.7 4.6 %collective-permute-start.7 = (bf16[12,16,256]{2,1,0:T(8,128)(2,1)S(1)}, bf16[12,16,256]{2,1,0:T(8,128)(2,1)S(1)}, u32[]{:S(2)}, u32[]{:S(2)}) collective-permute-start(bf16[12,16,256]{2,1,0:T(8,128)(2,1)S(1)} %get-tuple-element.39.edges), channel_id=1, source_target_pairs={{0,1},{1,0},{2,3},{3,2},{4,5},{5,4},{6,7},{7,6},{8,9},{9,8},{10,11... | collective-permute-start | bytes 294920 | tf_op jit(solution)/shard_map/ppermute | solution.py:262
  75.3 2.9 %collective-permute-start.10 = (bf16[1160,256]{1,0:T(8,128)(2,1)}, bf16[1160,256]{1,0:T(8,128)(2,1)S(1)}, u32[]{:S(2)}, u32[]{:S(2)}) collective-permute-start(bf16[1160,256]{1,0:T(8,128)(2,1)} %pad_maximum_fusion), channel_id=1, source_target_pairs={{0,2},{1,3},{2,0},{3,1},{4,6},{5,7},{6,4},{7,5},{8,10},{9,11},{10,... | collective-permute-start | bytes 1781768 | tf_op jit(solution)/shard_map/ppermute | solution.py:587
  81.3 8.0 %collective-permute-start.13 = (bf16[296,256]{1,0:T(8,128)(2,1)}, bf16[296,256]{1,0:T(8,128)(2,1)}, u32[]{:S(2)}, u32[]{:S(2)}) collective-permute-start(bf16[296,256]{1,0:T(8,128)(2,1)} %get-tuple-element.95), channel_id=1, source_target_pairs={{0,5},{1,4},{2,7},{3,6},{4,1},{5,0},{6,3},{7,2},{8,13},{9,12},{10,... | collective-permute-start | bytes 454664 | tf_op jit(solution)/shard_map/ppermute | solution.py:587
  81.3 14.4 %collective-permute-start.12 = (bf16[296,256]{1,0:T(8,128)(2,1)S(1)}, bf16[296,256]{1,0:T(8,128)(2,1)}, u32[]{:S(2)}, u32[]{:S(2)}) collective-permute-start(bf16[296,256]{1,0:T(8,128)(2,1)S(1)} %get-tuple-element.94), channel_id=1, source_target_pairs={{0,4},{1,5},{2,6},{3,7},{4,0},{5,1},{6,2},{7,3},{8,12},{9,13},{10,... | collective-permute-start | bytes 454664 | tf_op jit(solution)/shard_map/ppermute | solution.py:587
  83.3 12.5 %collective-permute-start.11 = (bf16[296,256]{1,0:T(8,128)(2,1)S(1)}, bf16[296,256]{1,0:T(8,128)(2,1)}, u32[]{:S(2)}, u32[]{:S(2)}) collective-permute-start(bf16[296,256]{1,0:T(8,128)(2,1)S(1)} %get-tuple-element.93), channel_id=1, source_target_pairs={{0,1},{1,0},{2,3},{3,2},{4,5},{5,4},{6,7},{7,6},{8,9},{9,8},{10,11... | collective-permute-start | bytes 454664 | tf_op jit(solution)/shard_map/ppermute | solution.py:587
  84.8 12.9 %collective-permute-start.14 = (bf16[12,72,256]{2,1,0:T(8,128)(2,1)}, bf16[12,72,256]{2,1,0:T(8,128)(2,1)S(1)}, u32[]{:S(2)}, u32[]{:S(2)}) collective-permute-start(bf16[12,72,256]{2,1,0:T(8,128)(2,1)} %get-tuple-element.50), channel_id=1, source_target_pairs={{0,2},{1,3},{2,4},{3,5},{4,6},{5,7},{6,8},{7,9},{8,10},{9,11},{10,... | collective-permute-start | bytes 1327112 | tf_op jit(solution)/shard_map/ppermute | solution.py:278
  84.8 12.9 %collective-permute-start.15 = (bf16[12,72,256]{2,1,0:T(8,128)(2,1)S(1)}, bf16[12,72,256]{2,1,0:T(8,128)(2,1)S(1)}, u32[]{:S(2)}, u32[]{:S(2)}) collective-permute-start(bf16[12,72,256]{2,1,0:T(8,128)(2,1)S(1)} %get-tuple-element.51), channel_id=1, source_target_pairs={{0,30},{1,31},{2,0},{3,1},{4,2},{5,3},{6,4},{7,5},{8,6},{9,7},{10,... | collective-permute-start | bytes 1327112 | tf_op jit(solution)/shard_map/ppermute | solution.py:279
  97.7 13.1 %collective-permute-start.18 = (bf16[80,256]{1,0:T(8,128)(2,1)S(1)}, bf16[80,256]{1,0:T(8,128)(2,1)S(1)}, u32[]{:S(2)}, u32[]{:S(2)}) collective-permute-start(bf16[80,256]{1,0:T(8,128)(2,1)S(1)} %get-tuple-element.92), channel_id=1, source_target_pairs={{0,24},{1,25},{2,26},{3,27},{4,28},{5,29},{6,30},{7,31},{8,16},{9,... | collective-permute-start | bytes 122888 | tf_op jit(solution)/shard_map/ppermute | solution.py:587
  97.8 13.0 %collective-permute-start.17 = (bf16[80,256]{1,0:T(8,128)(2,1)S(1)}, bf16[80,256]{1,0:T(8,128)(2,1)S(1)}, u32[]{:S(2)}, u32[]{:S(2)}) collective-permute-start(bf16[80,256]{1,0:T(8,128)(2,1)S(1)} %get-tuple-element.91), channel_id=1, source_target_pairs={{0,16},{1,17},{2,18},{3,19},{4,20},{5,21},{6,22},{7,23},{8,24},{9,... | collective-permute-start | bytes 122888 | tf_op jit(solution)/shard_map/ppermute | solution.py:587
  97.9 12.9 %collective-permute-start.16 = (bf16[80,256]{1,0:T(8,128)(2,1)S(1)}, bf16[80,256]{1,0:T(8,128)(2,1)S(1)}, u32[]{:S(2)}, u32[]{:S(2)}) collective-permute-start(bf16[80,256]{1,0:T(8,128)(2,1)S(1)} %get-tuple-element.90), channel_id=1, source_target_pairs={{0,8},{1,9},{2,10},{3,11},{4,12},{5,13},{6,14},{7,15},{8,0},{9,1},... | collective-permute-start | bytes 122888 | tf_op jit(solution)/shard_map/ppermute | solution.py:587
  104.5 13.7 %collective-permute-start.22 = (bf16[12,72,256]{2,1,0:T(8,128)(2,1)S(1)}, bf16[12,72,256]{2,1,0:T(8,128)(2,1)S(1)}, u32[]{:S(2)}, u32[]{:S(2)}) collective-permute-start(bf16[12,72,256]{2,1,0:T(8,128)(2,1)S(1)} %get-tuple-element.56.edge), channel_id=1, source_target_pairs={{0,1},{1,0},{30,31},{31,30}} | collective-permute-start | bytes 1327112 | tf_op jit(solution)/shard_map/ppermute | solution.py:280
  107.9 13.6 %collective-permute-start.23 = (bf16[12,72,256]{2,1,0:T(8,128)(2,1)S(1)}, bf16[12,72,256]{2,1,0:T(8,128)(2,1)S(1)}, u32[]{:S(2)}, u32[]{:S(2)}) collective-permute-start(bf16[12,72,256]{2,1,0:T(8,128)(2,1)S(1)} %get-tuple-element.56.edge), channel_id=1, source_target_pairs={{0,31},{1,30},{30,1},{31,0}} | collective-permute-start | bytes 1327112 | tf_op jit(solution)/shard_map/ppermute | solution.py:281
  110.9 14.1 %copy-start.15 = (f32[12,4,32,256]{3,0,2,1:T(8,128)S(1)}, f32[12,4,32,256]{3,0,2,1:T(8,128)}, u32[]{:S(2)}) copy-start(f32[12,4,32,256]{3,0,2,1:T(8,128)} %copy-done.14) | copy-start | bytes 4718596
  110.9 6.4 %collective-permute-start.21 = (bf16[1,72,256]{2,1,0:T(8,128)(2,1)S(1)}, bf16[1,72,256]{2,1,0:T(8,128)(2,1)S(1)}, u32[]{:S(2)}, u32[]{:S(2)}) collective-permute-start(bf16[1,72,256]{2,1,0:T(8,128)(2,1)S(1)} %bitcast.212), channel_id=1, source_target_pairs={{0,24},{1,25},{2,26},{3,27},{4,28},{5,29},{6,30},{7,31},{8,16},{9,... | collective-permute-start | bytes 110600 | tf_op jit(solution)/shard_map/ppermute | solution.py:602
  110.9 6.8 %collective-permute-start.20 = (bf16[1,72,256]{2,1,0:T(8,128)(2,1)S(1)}, bf16[1,72,256]{2,1,0:T(8,128)(2,1)S(1)}, u32[]{:S(2)}, u32[]{:S(2)}) collective-permute-start(bf16[1,72,256]{2,1,0:T(8,128)(2,1)S(1)} %bitcast.213), channel_id=1, source_target_pairs={{0,16},{1,17},{2,18},{3,19},{4,20},{5,21},{6,22},{7,23},{8,24},{9,... | collective-permute-start | bytes 110600 | tf_op jit(solution)/shard_map/ppermute | solution.py:602
  111.0 7.1 %collective-permute-start.19 = (bf16[1,72,256]{2,1,0:T(8,128)(2,1)S(1)}, bf16[1,72,256]{2,1,0:T(8,128)(2,1)S(1)}, u32[]{:S(2)}, u32[]{:S(2)}) collective-permute-start(bf16[1,72,256]{2,1,0:T(8,128)(2,1)S(1)} %bitcast.214), channel_id=1, source_target_pairs={{0,8},{1,9},{2,10},{3,11},{4,12},{5,13},{6,14},{7,15},{8,0},{9,1},... | collective-permute-start | bytes 110600 | tf_op jit(solution)/shard_map/ppermute | solution.py:602
  118.2 8.8 %copy-start.13 = (bf16[2,24,384]{2,1,0:T(8,128)(2,1)S(1)}, bf16[2,24,384]{2,1,0:T(8,128)(2,1)}, u32[]{:S(2)}) copy-start(bf16[2,24,384]{2,1,0:T(8,128)(2,1)} %constant.72.clone.col_picks) | copy-start | bytes 110596
  121.5 8.3 %collective-permute-start.26 = (bf16[4,72,256]{2,1,0:T(8,128)(2,1)S(1)}, bf16[4,72,256]{2,1,0:T(8,128)(2,1)S(1)}, u32[]{:S(2)}, u32[]{:S(2)}) collective-permute-start(bf16[4,72,256]{2,1,0:T(8,128)(2,1)S(1)} %pad_maximum_fusion.7), channel_id=1, source_target_pairs={{0,5},{1,4},{2,7},{3,6},{4,1},{5,0},{6,3},{7,2},{8,13},{9,12},{10,... | collective-permute-start | bytes 442376 | tf_op jit(solution)/shard_map/ppermute | solution.py:602
  121.5 8.7 %collective-permute-start.25 = (bf16[4,72,256]{2,1,0:T(8,128)(2,1)S(1)}, bf16[4,72,256]{2,1,0:T(8,128)(2,1)S(1)}, u32[]{:S(2)}, u32[]{:S(2)}) collective-permute-start(bf16[4,72,256]{2,1,0:T(8,128)(2,1)S(1)} %pad_maximum_fusion.7), channel_id=1, source_target_pairs={{0,4},{1,5},{2,6},{3,7},{4,0},{5,1},{6,2},{7,3},{8,12},{9,13},{10,... | collective-permute-start | bytes 442376 | tf_op jit(solution)/shard_map/ppermute | solution.py:602
  123.4 6.8 %collective-permute-start.24 = (bf16[4,72,256]{2,1,0:T(8,128)(2,1)S(1)}, bf16[4,72,256]{2,1,0:T(8,128)(2,1)S(1)}, u32[]{:S(2)}, u32[]{:S(2)}) collective-permute-start(bf16[4,72,256]{2,1,0:T(8,128)(2,1)S(1)} %pad_maximum_fusion.7), channel_id=1, source_target_pairs={{0,1},{1,0},{2,3},{3,2},{4,5},{5,4},{6,7},{7,6},{8,9},{9,8},{10,11... | collective-permute-start | bytes 442376 | tf_op jit(solution)/shard_map/ppermute | solution.py:602
  130.5 10.3 %collective-permute-start.27 = (bf16[16,72,256]{2,1,0:T(8,128)(2,1)S(1)}, bf16[16,72,256]{2,1,0:T(8,128)(2,1)S(1)}, u32[]{:S(2)}, u32[]{:S(2)}) collective-permute-start(bf16[16,72,256]{2,1,0:T(8,128)(2,1)S(1)} %get-tuple-element.70), channel_id=1, source_target_pairs={{0,2},{1,3},{2,0},{3,1},{4,6},{5,7},{6,4},{7,5},{8,10},{9,11},{10,... | collective-permute-start | bytes 1769480 | tf_op jit(solution)/shard_map/ppermute | solution.py:602
  (20 other events, 37.2 us)

commit v9 on v8

--- a/solution.py
+++ b/solution.py
@@ -235,10 +235,45 @@
             padded[face, q] = out[q * step : q * step + breadth]
 
 
+def copies(sources, targets, arrivals, first=0):
+    return [
+        pltpu.make_async_copy(source, target, arrivals.at[first + i])
+        for i, (source, target) in enumerate(zip(sources, targets))
+    ]
+
+
+def run_all(moves, begin):
+    for move in moves:
+        if begin:
+            move.start()
+        else:
+            move.wait()
+
+
+def on_row_edge():
+    row_place = lax.axis_index("frow")
+    return jnp.logical_or(row_place == 0, row_place == lax.axis_size("frow") - 1)
+
+
 def pad_kernel(adjacency, flips, picks, field, sides, *refs):
-    padded, stack = refs[-2:]
-    readers = joint_readers(*refs[:-2])
+    sources, padded, stack = refs[:5], refs[5], refs[6]
+    targets, arrivals = refs[7:12], refs[12]
+    near = copies(sources[:2], targets[:2], arrivals)
+    far = copies(sources[2:], targets[2:], arrivals, 2)
+    run_all(near, True)
+
+    @pl.when(on_row_edge())
+    def _():
+        run_all(far, True)
+
     stack[...] = jnp.zeros_like(stack)
+    run_all(near, False)
+
+    @pl.when(on_row_edge())
+    def _():
+        run_all(far, False)
+
+    readers = joint_readers(*targets)
 
     @pl.loop(0, field.shape[0])
     def _(face):
@@ -247,10 +282,10 @@
     write_padded(picks, stack, padded)
 
 
-def whole(count):
-    return [pl.BlockSpec(memory_space=pltpu.SMEM)] + [
-        pl.BlockSpec(memory_space=pltpu.VMEM) for _ in range(count)
-    ]
+def whole(count, left=0):
+    specs = [pl.BlockSpec(memory_space=pltpu.SMEM)]
+    specs += [pl.BlockSpec(memory_space=pltpu.VMEM) for _ in range(count)]
+    return specs + [pl.BlockSpec(memory_space=pltpu.HBM) for _ in range(left)]
 
 
 def exchange_cols(field):
@@ -319,9 +354,13 @@
     return pl.pallas_call(
         pad_kernel,
         out_shape=jax.ShapeDtypeStruct(padded, field.dtype),
-        in_specs=whole(len(strips) + 2),
+        in_specs=whole(4, 5),
         out_specs=pl.BlockSpec(memory_space=pltpu.VMEM),
-        scratch_shapes=[pltpu.VMEM((face_count, size, channels), field.dtype)],
+        scratch_shapes=[
+            pltpu.VMEM((face_count, size, channels), field.dtype),
+            *[pltpu.VMEM(up.shape, field.dtype) for _ in range(5)],
+            pltpu.SemaphoreType.DMA((5,)),
+        ],
         compiler_params=pltpu.CompilerParams(vmem_limit_bytes=vmem_bytes),
         cost_estimate=pl.CostEstimate(flops=1000, bytes_accessed=5000000, transcendentals=0),
     )(adjacency, row_flips(width), pad_picks(tile_rows, width), *strips)
@@ -361,9 +400,11 @@
 
 
 def return_kernel(
-    adjacency, picks, col_picks, rotated, field, sides, up, down, padded, extra, stack,
-    kept_picks, col_terms, col_sum,
+    adjacency, picks, col_picks, rotated, field, sides, above_strip, below_strip, padded, extra,
+    stack, kept_picks, col_terms, col_sum, up, down, arrivals,
 ):
+    moves = copies((above_strip, below_strip), (up, down), arrivals)
+    run_all(moves, True)
     face_count, tile_rows, width, channels = field.shape
     breadth = picks.shape[0] // (tile_rows + 4)
     half = 2 * tile_rows
@@ -387,6 +428,7 @@
     for face in range(face_count):
         stack[face, pl.ds(0, beside)] = field[face].reshape(beside, channels)
         stack[face, pl.ds(beside, 4 * tile_rows)] = sides[face]
+    run_all(moves, False)
     for near, place, at_edge in ((up, above, at_top), (down, below, at_bottom)):
 
         @pl.when(jnp.logical_not(at_edge))
@@ -432,12 +474,25 @@
 
 
 def seam_kernel(
-    adjacency, row_picks, rotated, partial, up, down, edge, far_same, far_cross, out, values
+    adjacency, row_picks, rotated, partial, up, down, edge, far_same, far_cross, out, values,
+    *refs,
 ):
+    targets, arrivals = refs[:5], refs[5]
+    moves = copies((up, down, edge, far_same, far_cross), targets, arrivals)
+
+    @pl.when(on_row_edge())
+    def _():
+        run_all(moves, True)
+
     face_count, tile_rows, width, channels = partial.shape
     row_place = lax.axis_index("frow")
     out[...] = partial[...].astype(jnp.bfloat16)
-    readers = joint_readers(up, down, edge, far_same, far_cross)
+
+    @pl.when(on_row_edge())
+    def _():
+        run_all(moves, False)
+
+    readers = joint_readers(*targets)
     for side in range(2):
 
         @pl.when(row_place == side * (lax.axis_size("frow") - 1))
@@ -478,13 +533,16 @@
             jax.ShapeDtypeStruct(padded, field.dtype),
             jax.ShapeDtypeStruct(field.shape, jnp.float32),
         ),
-        in_specs=whole(7),
+        in_specs=whole(5, 2),
         out_specs=[pl.BlockSpec(memory_space=pltpu.VMEM)] * 2,
         scratch_shapes=[
             pltpu.VMEM((face_count, size, channels), field.dtype),
             pltpu.VMEM(picks.shape, field.dtype),
             pltpu.VMEM((2, 3, cells, channels), field.dtype),
             pltpu.VMEM((cells, channels), jnp.float32),
+            pltpu.VMEM(up.shape, field.dtype),
+            pltpu.VMEM(up.shape, field.dtype),
+            pltpu.SemaphoreType.DMA((2,)),
         ],
         compiler_params=pltpu.CompilerParams(vmem_limit_bytes=vmem_bytes),
         cost_estimate=pl.CostEstimate(flops=1000, bytes_accessed=8000000, transcendentals=0),
@@ -493,9 +551,13 @@
     return pl.pallas_call(
         seam_kernel,
         out_shape=jax.ShapeDtypeStruct(field.shape, field.dtype),
-        in_specs=whole(8),
+        in_specs=whole(3, 5),
         out_specs=pl.BlockSpec(memory_space=pltpu.VMEM),
-        scratch_shapes=[pltpu.VMEM((face_count, 6 * width, channels), field.dtype)],
+        scratch_shapes=[
+            pltpu.VMEM((face_count, 6 * width, channels), field.dtype),
+            *[pltpu.VMEM(up.shape, field.dtype) for _ in range(5)],
+            pltpu.SemaphoreType.DMA((5,)),
+        ],
         compiler_params=pltpu.CompilerParams(vmem_limit_bytes=vmem_bytes),
         cost_estimate=pl.CostEstimate(flops=1000, bytes_accessed=5000000, transcendentals=0),
     )(
@@ -565,15 +627,11 @@
     stages = reduce_stages()
     for order, stage in enumerate(stages):
         part, vector = part.astype(jnp.bfloat16), vector.astype(jnp.bfloat16)
-        if order == 0:
-            part, vector, *cols = lax.optimization_barrier((part, vector, *cols))
+        if order == 2:
             strips = side_strips(field, adjacency, cols)
-        if order == 1:
             part, vector, *strips = lax.optimization_barrier((part, vector, *strips))
             sides, top, bottom, edge = strips
             up, down, row_same, row_cross = exchange_rows(top, bottom, edge)
-        if order == 2:
-            part, vector, up, down = lax.optimization_barrier((part, vector, up, down))
         offsets = stage_offsets(stage)
         place = stage_place(index, stage)
         part = part.reshape(len(offsets), -1, width).astype(jnp.bfloat16)
@@ -595,7 +653,7 @@
     part = lax.optimization_barrier(part.astype(jnp.bfloat16))[None]
     for order, stage in enumerate(stages[::-1]):
         if order == len(stages) - 2:
-            part, row_same, row_cross = lax.optimization_barrier((part, row_same, row_cross))
+            part, up, down = lax.optimization_barrier((part, up, down))
         offsets = stage_offsets(stage)
         place = stage_place(index, stage)
         pieces = [part] + [

time: 143 us -> 129 us (0.902)
  local copies, waits for them, and re-layouts: 18.2 us -> 7.27 us
  matrix products: 15.7 us -> 9.76 us
  starting transfers between devices: 49.1 us -> 44.6 us
  waiting for transfers between devices: 28.9 us -> 32 us
  Pallas kernels: 17.7 us -> 20.1 us
    unnamed x50 -> x36, local copies, waits for them, and re-layouts: 14.1 us -> 5.52 us
    dot_general x9, matrix products: 9.66 us -> 3.8 us  [local(): lax.dot_general(window, pre_grad, (((0, 1, 2), (0, 1, 2)), ((), ())), pre...]
    ppermute x2, waiting for transfers between devices: 1.63 us -> 6.38 us  [exchange_cols(): far_same = lax.ppermute(edge, axes, mirror_pairs(False, True, False))]
    ppermute x2, waiting for transfers between devices: 4.32 us -> 9.01 us  [exchange_cols(): far_cross = lax.ppermute(edge, axes, mirror_pairs(False, True, True))]
    ppermute x7, waiting for transfers between devices: 6.52 us -> 1.86 us  [reduce_everywhere(): packed = lax.ppermute(packed, axes, [(i, i ^ offset) for i in range(count)])]
    ppermute x2, starting transfers between devices: 5.6 us -> 1.12 us  [exchange_cols(): far_cross = lax.ppermute(edge, axes, mirror_pairs(False, True, True))]
    ppermute x2, waiting for transfers between devices: 2.97 us -> 0.01 us  [exchange_cols(): beside = lax.ppermute(edges, axes, shifted_pairs(0, 1))]
    ppermute x2, waiting for transfers between devices: 7.96 us -> 5.47 us  [exchange_rows(): row_cross = lax.ppermute(edge, axes, mirror_pairs(True, True, True))]
  transfers between devices with their start and end apart: 28 -> 28, of which waited for: 13 -> 9; matrix products, arithmetic and copies ran while one was open for 15% -> 9% of each run, Pallas kernels for 7% -> 9%
where the time goes in v9:
time: 129 us; the launch traced here: 128 us
  starting transfers between devices  44.6 us (35%)
  waiting for transfers between devices  32 us (25%)
  Pallas kernels  20.1 us (16%)
  other arithmetic  13.5 us (10%)
  matrix products  9.76 us (8%)
  local copies, waits for them, and re-layouts  7.27 us (6%)
    ppermute x2, waiting for transfers between devices, exchange_cols(): far_cross = lax.ppermute(edge, axes, mirror_pairs(False, True, True))  9.01 us
    ppermute x7, starting transfers between devices, reduce_everywhere(): lax.ppermute(part, axes, [(i, i ^ offset) for i in range(count)])  8.06 us
    ppermute x2, starting transfers between devices, exchange_rows(): down = lax.ppermute(top, axes, shifted_pairs(-1, 0))  7.92 us
    ppermute x7, starting transfers between devices, reduce_everywhere(): packed = lax.ppermute(packed, axes, [(i, i ^ offset) for i in range(count)])  7.88 us
    ppermute x2, waiting for transfers between devices, exchange_cols(): far_same = lax.ppermute(edge, axes, mirror_pairs(False, True, False))  6.38 us
    conv_general_dilated x2, matrix products, conv(): lax.conv_general_dilated(value, taps, (1, 1), 'VALID', rhs_dilation=(DILA...  5.95 us
    pallas_call x1, Pallas kernels, return_field(): pl.pallas_call(seam_kernel, out_shape=jax.ShapeDtypeStruct(field.shape, f...  5.86 us
    ppermute x2, starting transfers between devices, exchange_rows(): row_same = lax.ppermute(edge, axes, mirror_pairs(True, False, True))  5.83 us
  transfers between devices with their start and end apart: 28, of which 9 were waited for; matrix products, arithmetic and copies ran while one was open for 9% of the time, Pallas kernels for 9%

profile of v9, /device:TPU:0, one launch (start us, length us, event | category | flops | bytes accessed | tf_op | source)
XLA Modules:
  0.0 128.5 jit_solution(1243466188824344401)
XLA Ops:
  1.9 3.0 %collective-permute-start = (bf16[12,16,256]{2,1,0:T(8,128)(2,1)S(1)}, bf16[12,16,256]{2,1,0:T(8,128)(2,1)S(1)}, u32[]{:S(2)}, u32[]{:S(2)}) collective-permute-start(bf16[12,16,256]{2,1,0:T(8,128)(2,1)S(1)} %get-tuple-element.69.edges), channel_id=1, source_target_pairs={{0,1},{1,0},{2,3},{3,2},{4,5},{5,4},{6,7},{7,6},{8,9},{9,8},{10,11... | collective-permute-start | bytes 294920 | tf_op jit(solution)/shard_map/ppermute | solution.py:297
  4.9 3.7 %collective-permute-start.1 = (bf16[12,8,256]{2,1,0:T(8,128)(2,1)S(1)}, bf16[12,8,256]{2,1,0:T(8,128)(2,1)S(1)}, u32[]{:S(2)}, u32[]{:S(2)}) collective-permute-start(bf16[12,8,256]{2,1,0:T(8,128)(2,1)S(1)} %get-tuple-element.68), channel_id=1, source_target_pairs={{0,30},{1,31},{2,28},{3,29},{4,26},{5,27},{6,24},{7,25},{8,22},{9,... | collective-permute-start | bytes 147464 | tf_op jit(solution)/shard_map/ppermute | solution.py:307
  9.8 1.6 %collective-permute-done.1.far_same = bf16[12,8,256]{2,1,0:T(8,128)(2,1)S(1)} collective-permute-done((bf16[12,8,256]{2,1,0:T(8,128)(2,1)S(1)}, bf16[12,8,256]{2,1,0:T(8,128)(2,1)S(1)}, u32[]{:S(2)}, u32[]{:S(2)}) %collective-permute-start.1) | collective-permute-done | bytes 49184 | tf_op jit(solution)/shard_map/ppermute | solution.py:307
  11.4 4.3 %collective-permute-done.2.far_cross = bf16[12,8,256]{2,1,0:T(8,128)(2,1)S(1)} collective-permute-done((bf16[12,8,256]{2,1,0:T(8,128)(2,1)S(1)}, bf16[12,8,256]{2,1,0:T(8,128)(2,1)S(1)}, u32[]{:S(2)}, u32[]{:S(2)}) %collective-permute-start.2) | collective-permute-done | bytes 49184 | tf_op jit(solution)/shard_map/ppermute | solution.py:308
  16.9 3.1 %shard_map.129 = (bf16[12,16,256]{2,1,0:T(8,128)(2,1)S(1)}, bf16[12,72,256]{2,1,0:T(8,128)(2,1)}, bf16[12,72,256]{2,1,0:T(8,128)(2,1)}, bf16[12,72,256]{2,1,0:T(8,128)(2,1)S(1)}) custom-call(s32[144]{0:T(256)S(1)} %reshape.45.adjacency, bf16[12,4,32,256]{3,2,1,0:T(8,128)(2,1)S(1)} %copy-done, bf16[12,16,256]{2,1,0:T(8,128)(2,1)S(1)} %get-tuple-element.69.edges, ...), custom_call_target="tpu_custom_call" | custom-call | flops 1000 | bytes 3000000 | tf_op jit(solution)/shard_map/pallas_call | solution.py:323
  20.9 3.5 %collective-permute-start.4 = (bf16[12,72,256]{2,1,0:T(8,128)(2,1)}, bf16[12,72,256]{2,1,0:T(8,128)(2,1)S(1)}, u32[]{:S(2)}, u32[]{:S(2)}) collective-permute-start(bf16[12,72,256]{2,1,0:T(8,128)(2,1)} %get-tuple-element.25), channel_id=1, source_target_pairs={{0,30},{1,31},{2,0},{3,1},{4,2},{5,3},{6,4},{7,5},{8,6},{9,7},{10,... | collective-permute-start | bytes 1327112 | tf_op jit(solution)/shard_map/ppermute | solution.py:314
  24.4 2.4 %collective-permute-start.5 = (bf16[12,72,256]{2,1,0:T(8,128)(2,1)S(1)}, bf16[12,72,256]{2,1,0:T(8,128)(2,1)S(1)}, u32[]{:S(2)}, u32[]{:S(2)}) collective-permute-start(bf16[12,72,256]{2,1,0:T(8,128)(2,1)S(1)} %get-tuple-element.26.refs_2_), channel_id=1, source_target_pairs={{0,1},{1,0},{30,31},{31,30}} | collective-permute-start | bytes 1327112 | tf_op jit(solution)/shard_map/ppermute | solution.py:315
  26.8 2.6 %collective-permute-start.6 = (bf16[12,72,256]{2,1,0:T(8,128)(2,1)S(1)}, bf16[12,72,256]{2,1,0:T(8,128)(2,1)S(1)}, u32[]{:S(2)}, u32[]{:S(2)}) collective-permute-start(bf16[12,72,256]{2,1,0:T(8,128)(2,1)S(1)} %get-tuple-element.26.refs_2_), channel_id=1, source_target_pairs={{0,31},{1,30},{30,1},{31,0}} | collective-permute-start | bytes 1327112 | tf_op jit(solution)/shard_map/ppermute | solution.py:316
  30.7 3.9 %collective-permute-done.5.refs_3_ = bf16[12,72,256]{2,1,0:T(8,128)(2,1)S(1)} collective-permute-done((bf16[12,72,256]{2,1,0:T(8,128)(2,1)S(1)}, bf16[12,72,256]{2,1,0:T(8,128)(2,1)S(1)}, u32[]{:S(2)}, u32[]{:S(2)}) %collective-permute-start.5) | collective-permute-done | bytes 442400 | tf_op jit(solution)/shard_map/ppermute | solution.py:315
  34.6 5.5 %collective-permute-done.6.refs_4_ = bf16[12,72,256]{2,1,0:T(8,128)(2,1)S(1)} collective-permute-done((bf16[12,72,256]{2,1,0:T(8,128)(2,1)S(1)}, bf16[12,72,256]{2,1,0:T(8,128)(2,1)S(1)}, u32[]{:S(2)}, u32[]{:S(2)}) %collective-permute-start.6) | collective-permute-done | bytes 442400 | tf_op jit(solution)/shard_map/ppermute | solution.py:316
  40.1 5.5 %shard_map.130 = bf16[12,8,36,256]{3,2,1,0:T(8,128)(2,1)S(1)} custom-call(s32[144]{0:T(256)S(1)} %reshape.45.adjacency, bf16[4,72,72]{2,1,0:T(8,128)(2,1)S(1)} %copy-done.4, bf16[320,384]{1,0:T(8,128)(2,1)S(1)} %copy-done.2, bf16[12,4,32,256]{3,2,1,0:T(8,128)(2,1)S(1)} %copy-done.1, bf16[12,16,256]{2,1,0:T(8,128)(2,1)S(1)} %get-tuple-element.23.sides, ...), custom_call_target="tpu_custom_call" | custom-call | flops 1000 | bytes 5000000 | tf_op jit(solution)/shard_map/pallas_call | solution.py:354
  45.6 2.9 %fusion.2 = f32[12,4,32,256]{3,0,2,1:T(8,128)S(1)} fusion(bf16[3,3,256,256]{3,2,1,0:T(8,128)(2,1)S(1)} %copy-done.10, bf16[12,8,36,256]{3,2,1,0:T(8,128)(2,1)S(1)} %shard_map.130), kind=kOutput, calls=%fused_computation.3 | convolution fusion | flops 1811939328 | bytes 4521984 | tf_op jit(solution)/shard_map/conv_general_dilated | solution.py:570
  55.1 1.8 %collective-permute-done.7 = bf16[1160,256]{1,0:T(8,128)(2,1)S(1)} collective-permute-done((bf16[1160,256]{1,0:T(8,128)(2,1)S(1)}, bf16[1160,256]{1,0:T(8,128)(2,1)S(1)}, u32[]{:S(2)}, u32[]{:S(2)}) %collective-permute-start.7) | collective-permute-done | bytes 593952 | tf_op jit(solution)/shard_map/ppermute | solution.py:645
  59.1 2.9 %collective-permute-start.9 = (bf16[296,256]{1,0:T(8,128)(2,1)S(1)}, bf16[296,256]{1,0:T(8,128)(2,1)}, u32[]{:S(2)}, u32[]{:S(2)}) collective-permute-start(bf16[296,256]{1,0:T(8,128)(2,1)S(1)} %get-tuple-element.74), channel_id=1, source_target_pairs={{0,4},{1,5},{2,6},{3,7},{4,0},{5,1},{6,2},{7,3},{8,12},{9,13},{10,... | collective-permute-start | bytes 454664 | tf_op jit(solution)/shard_map/ppermute | solution.py:645
  62.7 1.6 %collective-permute-start.11 = (bf16[12,16,256]{2,1,0:T(8,128)(2,1)S(1)}, bf16[12,16,256]{2,1,0:T(8,128)(2,1)S(1)}, u32[]{:S(2)}, u32[]{:S(2)}) collective-permute-start(bf16[12,16,256]{2,1,0:T(8,128)(2,1)S(1)} %get-tuple-element.67.edges), channel_id=1, source_target_pairs={{0,1},{1,0},{2,3},{3,2},{4,5},{5,4},{6,7},{7,6},{8,9},{9,8},{10,11... | collective-permute-start | bytes 294920 | tf_op jit(solution)/shard_map/ppermute | solution.py:297
  64.2 4.8 %collective-permute-done.12.far_same = bf16[12,8,256]{2,1,0:T(8,128)(2,1)S(1)} collective-permute-done((bf16[12,8,256]{2,1,0:T(8,128)(2,1)S(1)}, bf16[12,8,256]{2,1,0:T(8,128)(2,1)S(1)}, u32[]{:S(2)}, u32[]{:S(2)}) %collective-permute-start.12) | collective-permute-done | bytes 49184 | tf_op jit(solution)/shard_map/ppermute | solution.py:307
  69.9 1.5 %copy.22 = bf16[3,3,256,256]{2,3,1,0:T(8,128)(2,1)} copy(bf16[3,3,256,256]{3,2,1,0:T(8,128)(2,1)S(1)} %copy-done.11) | data formatting | bytes 2359296 | tf_op args[1]
  71.4 4.7 %collective-permute-done.13.far_cross = bf16[12,8,256]{2,1,0:T(8,128)(2,1)S(1)} collective-permute-done((bf16[12,8,256]{2,1,0:T(8,128)(2,1)S(1)}, bf16[12,8,256]{2,1,0:T(8,128)(2,1)S(1)}, u32[]{:S(2)}, u32[]{:S(2)}) %collective-permute-start.13) | collective-permute-done | bytes 49184 | tf_op jit(solution)/shard_map/ppermute | solution.py:308
  76.1 2.2 %shard_map.131 = (bf16[12,16,256]{2,1,0:T(8,128)(2,1)S(1)}, bf16[12,72,256]{2,1,0:T(8,128)(2,1)S(1)}, bf16[12,72,256]{2,1,0:T(8,128)(2,1)S(1)}, bf16[12,72,256]{2,1,0:T(8,128)(2,1)S(1)}) custom-call(s32[144]{0:T(256)S(1)} %reshape.45.adjacency, bf16[12,4,32,256]{3,2,1,0:T(8,128)(2,1)S(1)} %get-tuple-element.43.field, ...), custom_call_target="tpu_custom_call" | custom-call | flops 1000 | bytes 3000000 | tf_op jit(solution)/shard_map/pallas_call | solution.py:323
  81.0 4.4 %collective-permute-start.14 = (bf16[80,256]{1,0:T(8,128)(2,1)S(1)}, bf16[80,256]{1,0:T(8,128)(2,1)S(1)}, u32[]{:S(2)}, u32[]{:S(2)}) collective-permute-start(bf16[80,256]{1,0:T(8,128)(2,1)S(1)} %get-tuple-element.70), channel_id=1, source_target_pairs={{0,8},{1,9},{2,10},{3,11},{4,12},{5,13},{6,14},{7,15},{8,0},{9,1},... | collective-permute-start | bytes 122888 | tf_op jit(solution)/shard_map/ppermute | solution.py:645
  85.5 4.4 %collective-permute-start.21 = (bf16[12,72,256]{2,1,0:T(8,128)(2,1)S(1)}, bf16[12,72,256]{2,1,0:T(8,128)(2,1)S(1)}, u32[]{:S(2)}, u32[]{:S(2)}) collective-permute-start(bf16[12,72,256]{2,1,0:T(8,128)(2,1)S(1)} %get-tuple-element.35), channel_id=1, source_target_pairs={{0,30},{1,31},{2,0},{3,1},{4,2},{5,3},{6,4},{7,5},{8,6},{9,7},{10,... | collective-permute-start | bytes 1327112 | tf_op jit(solution)/shard_map/ppermute | solution.py:314
  90.9 3.5 %collective-permute-start.17 = (bf16[1,72,256]{2,1,0:T(8,128)(2,1)S(1)}, bf16[1,72,256]{2,1,0:T(8,128)(2,1)S(1)}, u32[]{:S(2)}, u32[]{:S(2)}) collective-permute-start(bf16[1,72,256]{2,1,0:T(8,128)(2,1)S(1)} %bitcast.213), channel_id=1, source_target_pairs={{0,8},{1,9},{2,10},{3,11},{4,12},{5,13},{6,14},{7,15},{8,0},{9,1},... | collective-permute-start | bytes 110600 | tf_op jit(solution)/shard_map/ppermute | solution.py:660
  94.5 3.5 %multiply_convert_fusion = bf16[12,4,32,256]{3,2,1,0:T(8,128)(2,1)} fusion(f32[256]{0:T(256)} %param.12, f32[12,4,32,256]{3,0,2,1:T(8,128)} %copy-done.7), kind=kLoop, calls=%fused_computation.14 | loop fusion | flops 2359296 | bytes 2360320 | tf_op jit(solution)/shard_map/convert_element_type | solution.py:680
  98.0 3.4 %collective-permute-start.22 = (bf16[12,72,256]{2,1,0:T(8,128)(2,1)S(1)}, bf16[12,72,256]{2,1,0:T(8,128)(2,1)S(1)}, u32[]{:S(2)}, u32[]{:S(2)}) collective-permute-start(bf16[12,72,256]{2,1,0:T(8,128)(2,1)S(1)} %get-tuple-element.40.edge), channel_id=1, source_target_pairs={{0,1},{1,0},{30,31},{31,30}} | collective-permute-start | bytes 1327112 | tf_op jit(solution)/shard_map/ppermute | solution.py:315
  101.4 1.9 %collective-permute-start.23 = (bf16[12,72,256]{2,1,0:T(8,128)(2,1)S(1)}, bf16[12,72,256]{2,1,0:T(8,128)(2,1)S(1)}, u32[]{:S(2)}, u32[]{:S(2)}) collective-permute-start(bf16[12,72,256]{2,1,0:T(8,128)(2,1)S(1)} %get-tuple-element.40.edge), channel_id=1, source_target_pairs={{0,31},{1,30},{30,1},{31,0}} | collective-permute-start | bytes 1327112 | tf_op jit(solution)/shard_map/ppermute | solution.py:316
  103.5 2.0 %collective-permute-start.25 = (bf16[4,72,256]{2,1,0:T(8,128)(2,1)S(1)}, bf16[4,72,256]{2,1,0:T(8,128)(2,1)S(1)}, u32[]{:S(2)}, u32[]{:S(2)}) collective-permute-start(bf16[4,72,256]{2,1,0:T(8,128)(2,1)S(1)} %pad_maximum_fusion.7), channel_id=1, source_target_pairs={{0,4},{1,5},{2,6},{3,7},{4,0},{5,1},{6,2},{7,3},{8,12},{9,13},{10,... | collective-permute-start | bytes 442376 | tf_op jit(solution)/shard_map/ppermute | solution.py:660
  105.5 1.5 %collective-permute-start.24 = (bf16[4,72,256]{2,1,0:T(8,128)(2,1)S(1)}, bf16[4,72,256]{2,1,0:T(8,128)(2,1)S(1)}, u32[]{:S(2)}, u32[]{:S(2)}) collective-permute-start(bf16[4,72,256]{2,1,0:T(8,128)(2,1)S(1)} %pad_maximum_fusion.7), channel_id=1, source_target_pairs={{0,1},{1,0},{2,3},{3,2},{4,5},{5,4},{6,7},{7,6},{8,9},{9,8},{10,11... | collective-permute-start | bytes 442376 | tf_op jit(solution)/shard_map/ppermute | solution.py:660
  107.6 3.4 %shard_map.132 = (bf16[12,8,36,256]{3,2,1,0:T(8,128)(2,1)S(1)}, f32[12,4,32,256]{3,2,1,0:T(8,128)S(1)}) custom-call(s32[144]{0:T(256)S(1)} %reshape.45.adjacency, bf16[320,384]{1,0:T(8,128)(2,1)S(1)} %copy-done.2, bf16[2,24,384]{2,1,0:T(8,128)(2,1)S(1)} %copy-done.5, bf16[3,3,256,256]{3,2,1,0:T(8,128)(2,1)S(1)} %reverse_bitcast_fusion.rotated, ...), custom_call_target="tpu_custom_call" | custom-call | flops 1000 | bytes 8000000 | tf_op jit(solution)/shard_map/pallas_call | solution.py:530
  111.0 4.1 %collective-permute-done.25 = bf16[4,72,256]{2,1,0:T(8,128)(2,1)S(1)} collective-permute-done((bf16[4,72,256]{2,1,0:T(8,128)(2,1)S(1)}, bf16[4,72,256]{2,1,0:T(8,128)(2,1)S(1)}, u32[]{:S(2)}, u32[]{:S(2)}) %collective-permute-start.25) | collective-permute-done | bytes 147488 | tf_op jit(solution)/shard_map/ppermute | solution.py:660
  116.4 3.1 %fusion = f32[12,4,32,256]{3,0,2,1:T(8,128)S(1)} fusion(bf16[3,3,256,256]{3,2,1,0:T(8,128)(2,1)S(1)} %copy-done.12, bf16[12,8,36,256]{3,2,1,0:T(8,128)(2,1)S(1)} %get-tuple-element.38), kind=kOutput, calls=%fused_computation.1 | convolution fusion | flops 1811939328 | bytes 4521984 | tf_op jit(solution)/shard_map/conv_general_dilated | solution.py:570
  120.5 5.9 %shard_map.133 = bf16[12,4,32,256]{3,2,1,0:T(8,128)(2,1)} custom-call(s32[144]{0:T(256)S(1)} %reshape.45.adjacency, bf16[4,192,72]{2,1,0:T(8,128)(2,1)S(1)} %copy-done.3, bf16[3,3,256,256]{3,2,1,0:T(8,128)(2,1)S(1)} %reverse_bitcast_fusion.rotated, f32[12,4,32,256]{3,2,1,0:T(8,128)S(1)} %copy_add_fusion.partial, ...), custom_call_target="tpu_custom_call" | custom-call | flops 1000 | bytes 5000000 | tf_op jit(solution)/shard_map/pallas_call | solution.py:551
  126.8 1.6 %convert_multiply_fusion = f32[32,72,256]{2,1,0:T(8,128)} fusion(bf16[16,72,256]{2,1,0:T(8,128)(2,1)S(1)} %get-tuple-element.45, bf16[16,72,256]{2,1,0:T(8,128)(2,1)S(1)} %get-tuple-element.44), kind=kLoop, calls=%fused_computation.5 | loop fusion | flops 1769472 | bytes 3538944 | tf_op jit(solution)/shard_map/mul | solution.py:703
  (114 shorter events, 23.0 us)
Async XLA Ops:
  0.6 39.4 %copy-start.4 = (bf16[4,72,72]{2,1,0:T(8,128)(2,1)S(1)}, bf16[4,72,72]{2,1,0:T(8,128)(2,1)}, u32[]{:S(2)}) copy-start(bf16[4,72,72]{2,1,0:T(8,128)(2,1)} %constant.70.clone.flips) | copy-start | bytes 124420
  0.6 39.4 %copy-start.2 = (bf16[320,384]{1,0:T(8,128)(2,1)S(1)}, bf16[320,384]{1,0:T(8,128)(2,1)}, u32[]{:S(2)}) copy-start(bf16[320,384]{1,0:T(8,128)(2,1)} %constant.71.clone.picks) | copy-start | bytes 737284
  1.9 13.8 %collective-permute-start = (bf16[12,16,256]{2,1,0:T(8,128)(2,1)S(1)}, bf16[12,16,256]{2,1,0:T(8,128)(2,1)S(1)}, u32[]{:S(2)}, u32[]{:S(2)}) collective-permute-start(bf16[12,16,256]{2,1,0:T(8,128)(2,1)S(1)} %get-tuple-element.69.edges), channel_id=1, source_target_pairs={{0,1},{1,0},{2,3},{3,2},{4,5},{5,4},{6,7},{7,6},{8,9},{9,8},{10,11... | collective-permute-start | bytes 294920 | tf_op jit(solution)/shard_map/ppermute | solution.py:297
  4.9 6.5 %collective-permute-start.1 = (bf16[12,8,256]{2,1,0:T(8,128)(2,1)S(1)}, bf16[12,8,256]{2,1,0:T(8,128)(2,1)S(1)}, u32[]{:S(2)}, u32[]{:S(2)}) collective-permute-start(bf16[12,8,256]{2,1,0:T(8,128)(2,1)S(1)} %get-tuple-element.68), channel_id=1, source_target_pairs={{0,30},{1,31},{2,28},{3,29},{4,26},{5,27},{6,24},{7,25},{8,22},{9,... | collective-permute-start | bytes 147464 | tf_op jit(solution)/shard_map/ppermute | solution.py:307
  8.6 7.1 %collective-permute-start.2 = (bf16[12,8,256]{2,1,0:T(8,128)(2,1)S(1)}, bf16[12,8,256]{2,1,0:T(8,128)(2,1)S(1)}, u32[]{:S(2)}, u32[]{:S(2)}) collective-permute-start(bf16[12,8,256]{2,1,0:T(8,128)(2,1)S(1)} %get-tuple-element.68), channel_id=1, source_target_pairs={{0,31},{1,30},{2,29},{3,28},{4,27},{5,26},{6,25},{7,24},{8,23},{9,... | collective-permute-start | bytes 147464 | tf_op jit(solution)/shard_map/ppermute | solution.py:308
  16.9 23.2 %copy-start.1 = (bf16[12,4,32,256]{3,2,1,0:T(8,128)(2,1)S(1)}, bf16[12,4,32,256]{3,2,1,0:T(8,128)(2,1)}, u32[]{:S(2)}) copy-start(bf16[12,4,32,256]{3,2,1,0:T(8,128)(2,1)} %field.3) | copy-start | bytes 2359300
  20.0 10.7 %collective-permute-start.3 = (bf16[12,72,256]{2,1,0:T(8,128)(2,1)}, bf16[12,72,256]{2,1,0:T(8,128)(2,1)S(1)}, u32[]{:S(2)}, u32[]{:S(2)}) collective-permute-start(bf16[12,72,256]{2,1,0:T(8,128)(2,1)} %get-tuple-element.24), channel_id=1, source_target_pairs={{0,2},{1,3},{2,4},{3,5},{4,6},{5,7},{6,8},{7,9},{8,10},{9,11},{10,... | collective-permute-start | bytes 1327112 | tf_op jit(solution)/shard_map/ppermute | solution.py:313
  20.9 9.8 %collective-permute-start.4 = (bf16[12,72,256]{2,1,0:T(8,128)(2,1)}, bf16[12,72,256]{2,1,0:T(8,128)(2,1)S(1)}, u32[]{:S(2)}, u32[]{:S(2)}) collective-permute-start(bf16[12,72,256]{2,1,0:T(8,128)(2,1)} %get-tuple-element.25), channel_id=1, source_target_pairs={{0,30},{1,31},{2,0},{3,1},{4,2},{5,3},{6,4},{7,5},{8,6},{9,7},{10,... | collective-permute-start | bytes 1327112 | tf_op jit(solution)/shard_map/ppermute | solution.py:314
  24.4 10.2 %collective-permute-start.5 = (bf16[12,72,256]{2,1,0:T(8,128)(2,1)S(1)}, bf16[12,72,256]{2,1,0:T(8,128)(2,1)S(1)}, u32[]{:S(2)}, u32[]{:S(2)}) collective-permute-start(bf16[12,72,256]{2,1,0:T(8,128)(2,1)S(1)} %get-tuple-element.26.refs_2_), channel_id=1, source_target_pairs={{0,1},{1,0},{30,31},{31,30}} | collective-permute-start | bytes 1327112 | tf_op jit(solution)/shard_map/ppermute | solution.py:315
  26.8 13.2 %collective-permute-start.6 = (bf16[12,72,256]{2,1,0:T(8,128)(2,1)S(1)}, bf16[12,72,256]{2,1,0:T(8,128)(2,1)S(1)}, u32[]{:S(2)}, u32[]{:S(2)}) collective-permute-start(bf16[12,72,256]{2,1,0:T(8,128)(2,1)S(1)} %get-tuple-element.26.refs_2_), channel_id=1, source_target_pairs={{0,31},{1,30},{30,1},{31,0}} | collective-permute-start | bytes 1327112 | tf_op jit(solution)/shard_map/ppermute | solution.py:316
  54.9 2.0 %collective-permute-start.7 = (bf16[1160,256]{1,0:T(8,128)(2,1)S(1)}, bf16[1160,256]{1,0:T(8,128)(2,1)S(1)}, u32[]{:S(2)}, u32[]{:S(2)}) collective-permute-start(bf16[1160,256]{1,0:T(8,128)(2,1)S(1)} %pad_maximum_fusion), channel_id=1, source_target_pairs={{0,2},{1,3},{2,0},{3,1},{4,6},{5,7},{6,4},{7,5},{8,10},{9,11},{10,... | collective-permute-start | bytes 1781768 | tf_op jit(solution)/shard_map/ppermute | solution.py:645
  59.1 19.3 %collective-permute-start.10 = (bf16[296,256]{1,0:T(8,128)(2,1)}, bf16[296,256]{1,0:T(8,128)(2,1)}, u32[]{:S(2)}, u32[]{:S(2)}) collective-permute-start(bf16[296,256]{1,0:T(8,128)(2,1)} %get-tuple-element.75), channel_id=1, source_target_pairs={{0,5},{1,4},{2,7},{3,6},{4,1},{5,0},{6,3},{7,2},{8,13},{9,12},{10,... | collective-permute-start | bytes 454664 | tf_op jit(solution)/shard_map/ppermute | solution.py:645
  59.1 19.3 %collective-permute-start.9 = (bf16[296,256]{1,0:T(8,128)(2,1)S(1)}, bf16[296,256]{1,0:T(8,128)(2,1)}, u32[]{:S(2)}, u32[]{:S(2)}) collective-permute-start(bf16[296,256]{1,0:T(8,128)(2,1)S(1)} %get-tuple-element.74), channel_id=1, source_target_pairs={{0,4},{1,5},{2,6},{3,7},{4,0},{5,1},{6,2},{7,3},{8,12},{9,13},{10,... | collective-permute-start | bytes 454664 | tf_op jit(solution)/shard_map/ppermute | solution.py:645
  62.0 16.3 %collective-permute-start.8 = (bf16[296,256]{1,0:T(8,128)(2,1)S(1)}, bf16[296,256]{1,0:T(8,128)(2,1)}, u32[]{:S(2)}, u32[]{:S(2)}) collective-permute-start(bf16[296,256]{1,0:T(8,128)(2,1)S(1)} %get-tuple-element.73), channel_id=1, source_target_pairs={{0,1},{1,0},{2,3},{3,2},{4,5},{5,4},{6,7},{7,6},{8,9},{9,8},{10,11... | collective-permute-start | bytes 454664 | tf_op jit(solution)/shard_map/ppermute | solution.py:645
  62.6 6.4 %collective-permute-start.12 = (bf16[12,8,256]{2,1,0:T(8,128)(2,1)S(1)}, bf16[12,8,256]{2,1,0:T(8,128)(2,1)S(1)}, u32[]{:S(2)}, u32[]{:S(2)}) collective-permute-start(bf16[12,8,256]{2,1,0:T(8,128)(2,1)S(1)} %get-tuple-element.66), channel_id=1, source_target_pairs={{0,30},{1,31},{2,28},{3,29},{4,26},{5,27},{6,24},{7,25},{8,22},{9,... | collective-permute-start | bytes 147464 | tf_op jit(solution)/shard_map/ppermute | solution.py:307
  62.7 13.4 %collective-permute-start.11 = (bf16[12,16,256]{2,1,0:T(8,128)(2,1)S(1)}, bf16[12,16,256]{2,1,0:T(8,128)(2,1)S(1)}, u32[]{:S(2)}, u32[]{:S(2)}) collective-permute-start(bf16[12,16,256]{2,1,0:T(8,128)(2,1)S(1)} %get-tuple-element.67.edges), channel_id=1, source_target_pairs={{0,1},{1,0},{2,3},{3,2},{4,5},{5,4},{6,7},{7,6},{8,9},{9,8},{10,11... | collective-permute-start | bytes 294920 | tf_op jit(solution)/shard_map/ppermute | solution.py:297
  69.0 7.1 %collective-permute-start.13 = (bf16[12,8,256]{2,1,0:T(8,128)(2,1)S(1)}, bf16[12,8,256]{2,1,0:T(8,128)(2,1)S(1)}, u32[]{:S(2)}, u32[]{:S(2)}) collective-permute-start(bf16[12,8,256]{2,1,0:T(8,128)(2,1)S(1)} %get-tuple-element.66), channel_id=1, source_target_pairs={{0,31},{1,30},{2,29},{3,28},{4,27},{5,26},{6,25},{7,24},{8,23},{9,... | collective-permute-start | bytes 147464 | tf_op jit(solution)/shard_map/ppermute | solution.py:308
  81.0 9.0 %collective-permute-start.16 = (bf16[80,256]{1,0:T(8,128)(2,1)}, bf16[80,256]{1,0:T(8,128)(2,1)S(1)}, u32[]{:S(2)}, u32[]{:S(2)}) collective-permute-start(bf16[80,256]{1,0:T(8,128)(2,1)} %get-tuple-element.72), channel_id=1, source_target_pairs={{0,24},{1,25},{2,26},{3,27},{4,28},{5,29},{6,30},{7,31},{8,16},{9,... | collective-permute-start | bytes 122888 | tf_op jit(solution)/shard_map/ppermute | solution.py:645
  81.0 9.0 %collective-permute-start.15 = (bf16[80,256]{1,0:T(8,128)(2,1)S(1)}, bf16[80,256]{1,0:T(8,128)(2,1)S(1)}, u32[]{:S(2)}, u32[]{:S(2)}) collective-permute-start(bf16[80,256]{1,0:T(8,128)(2,1)S(1)} %get-tuple-element.71), channel_id=1, source_target_pairs={{0,16},{1,17},{2,18},{3,19},{4,20},{5,21},{6,22},{7,23},{8,24},{9,... | collective-permute-start | bytes 122888 | tf_op jit(solution)/shard_map/ppermute | solution.py:645
  81.0 9.0 %collective-permute-start.14 = (bf16[80,256]{1,0:T(8,128)(2,1)S(1)}, bf16[80,256]{1,0:T(8,128)(2,1)S(1)}, u32[]{:S(2)}, u32[]{:S(2)}) collective-permute-start(bf16[80,256]{1,0:T(8,128)(2,1)S(1)} %get-tuple-element.70), channel_id=1, source_target_pairs={{0,8},{1,9},{2,10},{3,11},{4,12},{5,13},{6,14},{7,15},{8,0},{9,1},... | collective-permute-start | bytes 122888 | tf_op jit(solution)/shard_map/ppermute | solution.py:645
  85.4 18.0 %collective-permute-start.20 = (bf16[12,72,256]{2,1,0:T(8,128)(2,1)}, bf16[12,72,256]{2,1,0:T(8,128)(2,1)S(1)}, u32[]{:S(2)}, u32[]{:S(2)}) collective-permute-start(bf16[12,72,256]{2,1,0:T(8,128)(2,1)} %copy-done.6), channel_id=1, source_target_pairs={{0,2},{1,3},{2,4},{3,5},{4,6},{5,7},{6,8},{7,9},{8,10},{9,11},{10,... | collective-permute-start | bytes 1327112 | tf_op jit(solution)/shard_map/ppermute | solution.py:313
  85.5 17.9 %collective-permute-start.21 = (bf16[12,72,256]{2,1,0:T(8,128)(2,1)S(1)}, bf16[12,72,256]{2,1,0:T(8,128)(2,1)S(1)}, u32[]{:S(2)}, u32[]{:S(2)}) collective-permute-start(bf16[12,72,256]{2,1,0:T(8,128)(2,1)S(1)} %get-tuple-element.35), channel_id=1, source_target_pairs={{0,30},{1,31},{2,0},{3,1},{4,2},{5,3},{6,4},{7,5},{8,6},{9,7},{10,... | collective-permute-start | bytes 1327112 | tf_op jit(solution)/shard_map/ppermute | solution.py:314
  90.0 17.6 %copy-start.5 = (bf16[2,24,384]{2,1,0:T(8,128)(2,1)S(1)}, bf16[2,24,384]{2,1,0:T(8,128)(2,1)}, u32[]{:S(2)}) copy-start(bf16[2,24,384]{2,1,0:T(8,128)(2,1)} %constant.72.clone.col_picks) | copy-start | bytes 110596
  90.0 8.0 %collective-permute-start.19 = (bf16[1,72,256]{2,1,0:T(8,128)(2,1)S(1)}, bf16[1,72,256]{2,1,0:T(8,128)(2,1)S(1)}, u32[]{:S(2)}, u32[]{:S(2)}) collective-permute-start(bf16[1,72,256]{2,1,0:T(8,128)(2,1)S(1)} %bitcast.211), channel_id=1, source_target_pairs={{0,24},{1,25},{2,26},{3,27},{4,28},{5,29},{6,30},{7,31},{8,16},{9,... | collective-permute-start | bytes 110600 | tf_op jit(solution)/shard_map/ppermute | solution.py:660
  90.1 11.3 %collective-permute-start.18 = (bf16[1,72,256]{2,1,0:T(8,128)(2,1)S(1)}, bf16[1,72,256]{2,1,0:T(8,128)(2,1)S(1)}, u32[]{:S(2)}, u32[]{:S(2)}) collective-permute-start(bf16[1,72,256]{2,1,0:T(8,128)(2,1)S(1)} %bitcast.212), channel_id=1, source_target_pairs={{0,16},{1,17},{2,18},{3,19},{4,20},{5,21},{6,22},{7,23},{8,24},{9,... | collective-permute-start | bytes 110600 | tf_op jit(solution)/shard_map/ppermute | solution.py:660
  90.9 12.4 %collective-permute-start.17 = (bf16[1,72,256]{2,1,0:T(8,128)(2,1)S(1)}, bf16[1,72,256]{2,1,0:T(8,128)(2,1)S(1)}, u32[]{:S(2)}, u32[]{:S(2)}) collective-permute-start(bf16[1,72,256]{2,1,0:T(8,128)(2,1)S(1)} %bitcast.213), channel_id=1, source_target_pairs={{0,8},{1,9},{2,10},{3,11},{4,12},{5,13},{6,14},{7,15},{8,0},{9,1},... | collective-permute-start | bytes 110600 | tf_op jit(solution)/shard_map/ppermute | solution.py:660
  98.0 22.5 %collective-permute-start.22 = (bf16[12,72,256]{2,1,0:T(8,128)(2,1)S(1)}, bf16[12,72,256]{2,1,0:T(8,128)(2,1)S(1)}, u32[]{:S(2)}, u32[]{:S(2)}) collective-permute-start(bf16[12,72,256]{2,1,0:T(8,128)(2,1)S(1)} %get-tuple-element.40.edge), channel_id=1, source_target_pairs={{0,1},{1,0},{30,31},{31,30}} | collective-permute-start | bytes 1327112 | tf_op jit(solution)/shard_map/ppermute | solution.py:315
  101.4 19.1 %collective-permute-start.23 = (bf16[12,72,256]{2,1,0:T(8,128)(2,1)S(1)}, bf16[12,72,256]{2,1,0:T(8,128)(2,1)S(1)}, u32[]{:S(2)}, u32[]{:S(2)}) collective-permute-start(bf16[12,72,256]{2,1,0:T(8,128)(2,1)S(1)} %get-tuple-element.40.edge), channel_id=1, source_target_pairs={{0,31},{1,30},{30,1},{31,0}} | collective-permute-start | bytes 1327112 | tf_op jit(solution)/shard_map/ppermute | solution.py:316
  103.5 7.5 %collective-permute-start.26 = (bf16[4,72,256]{2,1,0:T(8,128)(2,1)S(1)}, bf16[4,72,256]{2,1,0:T(8,128)(2,1)S(1)}, u32[]{:S(2)}, u32[]{:S(2)}) collective-permute-start(bf16[4,72,256]{2,1,0:T(8,128)(2,1)S(1)} %pad_maximum_fusion.7), channel_id=1, source_target_pairs={{0,5},{1,4},{2,7},{3,6},{4,1},{5,0},{6,3},{7,2},{8,13},{9,12},{10,... | collective-permute-start | bytes 442376 | tf_op jit(solution)/shard_map/ppermute | solution.py:660
  103.5 11.5 %collective-permute-start.25 = (bf16[4,72,256]{2,1,0:T(8,128)(2,1)S(1)}, bf16[4,72,256]{2,1,0:T(8,128)(2,1)S(1)}, u32[]{:S(2)}, u32[]{:S(2)}) collective-permute-start(bf16[4,72,256]{2,1,0:T(8,128)(2,1)S(1)} %pad_maximum_fusion.7), channel_id=1, source_target_pairs={{0,4},{1,5},{2,6},{3,7},{4,0},{5,1},{6,2},{7,3},{8,12},{9,13},{10,... | collective-permute-start | bytes 442376 | tf_op jit(solution)/shard_map/ppermute | solution.py:660
  105.5 9.5 %collective-permute-start.24 = (bf16[4,72,256]{2,1,0:T(8,128)(2,1)S(1)}, bf16[4,72,256]{2,1,0:T(8,128)(2,1)S(1)}, u32[]{:S(2)}, u32[]{:S(2)}) collective-permute-start(bf16[4,72,256]{2,1,0:T(8,128)(2,1)S(1)} %pad_maximum_fusion.7), channel_id=1, source_target_pairs={{0,1},{1,0},{2,3},{3,2},{4,5},{5,4},{6,7},{7,6},{8,9},{9,8},{10,11... | collective-permute-start | bytes 442376 | tf_op jit(solution)/shard_map/ppermute | solution.py:660
  115.3 11.0 %collective-permute-start.27 = (bf16[16,72,256]{2,1,0:T(8,128)(2,1)S(1)}, bf16[16,72,256]{2,1,0:T(8,128)(2,1)S(1)}, u32[]{:S(2)}, u32[]{:S(2)}) collective-permute-start(bf16[16,72,256]{2,1,0:T(8,128)(2,1)S(1)} %get-tuple-element.50), channel_id=1, source_target_pairs={{0,2},{1,3},{2,0},{3,1},{4,6},{5,7},{6,4},{7,5},{8,10},{9,11},{10,... | collective-permute-start | bytes 1769480 | tf_op jit(solution)/shard_map/ppermute | solution.py:660
  (12 other events, 57.5 us)

commit v10 on v9

--- a/solution.py
+++ b/solution.py
@@ -124,7 +124,7 @@
 
 
 def side_kernel(
-    adjacency, edges, beside, far_same, far_cross, side_out, upper_out, lower_out, seam
+    adjacency, edges, beside, far, side_out, upper_out, lower_out, seam
 ):
     face_count, both_sides, channels = edges.shape
     tile_rows = both_sides // 4
@@ -154,11 +154,11 @@
 
             @pl.when(kind == 2)
             def _():
-                seam[face] = pick(col_flip(2, tile_rows), far_cross[source])
+                seam[face] = pick(col_flip(2, tile_rows), far[source][half:])
 
             @pl.when(kind == 3)
             def _():
-                seam[face] = pick(col_flip(3, tile_rows), far_same[source])
+                seam[face] = pick(col_flip(3, tile_rows), far[source][:half])
 
     upper_pick = tail_pick(0, tile_rows)
     lower_pick = tail_pick(tile_rows - 2, tile_rows)
@@ -177,12 +177,15 @@
 
 
 def col_kernel(
-    adjacency, field, edges, beside, far_same, far_cross, side_out, top_out, bottom_out, edge_out,
-    upper, lower, seam,
+    adjacency, edges, beside, far, source, side_out, top_out, bottom_out, edge_out, upper, lower,
+    seam, field, arrivals,
 ):
+    moves = copies([source], [field], arrivals)
+    run_all(moves, True)
     face_count, tile_rows, width, channels = field.shape
     at_top = lax.axis_index("frow") == 0
-    side_kernel(adjacency, edges, beside, far_same, far_cross, side_out, upper, lower, seam)
+    side_kernel(adjacency, edges, beside, far, side_out, upper, lower, seam)
+    run_all(moves, False)
     for face in range(face_count):
         for d in range(2):
             rows = pl.ds(d * width, width)
@@ -303,10 +306,14 @@
             ],
             1,
         )
-    edge = jnp.where(lax.axis_index("fcol") == 0, left, right)
-    far_same = lax.ppermute(edge, axes, mirror_pairs(False, True, False))
-    far_cross = lax.ppermute(edge, axes, mirror_pairs(False, True, True))
-    return (edges, beside, far_same, far_cross)
+    half = 2 * tile_rows
+    packed = jnp.where(
+        lax.axis_index("fcol") == 0,
+        jnp.concatenate([left, beside[:, half:]], 1),
+        jnp.concatenate([right, beside[:, :half]], 1),
+    )
+    far = lax.ppermute(packed, axes, mirror_pairs(False, True, False))
+    return (edges, beside, far)
 
 
 def exchange_rows(top, bottom, edge):
@@ -317,31 +324,28 @@
     return (up, down, row_same, row_cross)
 
 
-def side_call(body, field, inputs, outputs, scratch):
-    face_count, tile_rows, _, channels = field.shape
-    scratch = [*scratch, (face_count, 2 * tile_rows, channels)]
-    return pl.pallas_call(
-        body,
-        out_shape=[jax.ShapeDtypeStruct(shape, field.dtype) for shape in outputs],
-        in_specs=whole(len(inputs) - 1),
-        out_specs=[pl.BlockSpec(memory_space=pltpu.VMEM) for _ in outputs],
-        scratch_shapes=[pltpu.VMEM(shape, field.dtype) for shape in scratch],
-        compiler_params=pltpu.CompilerParams(vmem_limit_bytes=vmem_bytes),
-        cost_estimate=pl.CostEstimate(flops=1000, bytes_accessed=3000000, transcendentals=0),
-    )(*inputs)
-
-
 def side_strips(field, adjacency, cols):
     face_count, tile_rows, width, channels = field.shape
     strip = (face_count, 2 * width + 8, channels)
-    tail = (face_count, 8, channels)
-    return side_call(
+    tail = pltpu.VMEM((face_count, 8, channels), field.dtype)
+    return pl.pallas_call(
         col_kernel,
-        field,
-        (adjacency, field, *cols),
-        (cols[0].shape, strip, strip, strip),
-        (tail, tail),
-    )
+        out_shape=[
+            jax.ShapeDtypeStruct(shape, field.dtype)
+            for shape in (cols[0].shape, strip, strip, strip)
+        ],
+        in_specs=whole(3) + [pl.BlockSpec(memory_space=pl.ANY)],
+        out_specs=[pl.BlockSpec(memory_space=pltpu.VMEM)] * 4,
+        scratch_shapes=[
+            tail,
+            tail,
+            pltpu.VMEM((face_count, 2 * tile_rows, channels), field.dtype),
+            pltpu.VMEM(field.shape, field.dtype),
+            pltpu.SemaphoreType.DMA((1,)),
+        ],
+        compiler_params=pltpu.CompilerParams(vmem_limit_bytes=vmem_bytes),
+        cost_estimate=pl.CostEstimate(flops=1000, bytes_accessed=3000000, transcendentals=0),
+    )(adjacency, *cols, field)
 
 
 def pad_field(field, adjacency):
@@ -627,9 +631,9 @@
     stages = reduce_stages()
     for order, stage in enumerate(stages):
         part, vector = part.astype(jnp.bfloat16), vector.astype(jnp.bfloat16)
-        if order == 2:
+        if order == 0:
             strips = side_strips(field, adjacency, cols)
-            part, vector, *strips = lax.optimization_barrier((part, vector, *strips))
+        if order == 1:
             sides, top, bottom, edge = strips
             up, down, row_same, row_cross = exchange_rows(top, bottom, edge)
         offsets = stage_offsets(stage)
@@ -653,7 +657,7 @@
     part = lax.optimization_barrier(part.astype(jnp.bfloat16))[None]
     for order, stage in enumerate(stages[::-1]):
         if order == len(stages) - 2:
-            part, up, down = lax.optimization_barrier((part, up, down))
+            pass
         offsets = stage_offsets(stage)
         place = stage_place(index, stage)
         pieces = [part] + [
@@ -679,6 +683,7 @@
     preactivation = conv(padded_input, kernel) + convolution_bias
     activation = gelu_value(preactivation).astype(jnp.bfloat16)
     pre_grad = (upstream.astype(jnp.float32) * gelu_slope(preactivation)).astype(jnp.bfloat16)
+    activation, pre_grad = lax.optimization_barrier((activation, pre_grad))
     tap_list = []
     for a in range(3):
         for b in range(3):

time: 129 us -> 124 us (0.961)
  waiting for transfers between devices: 32 us -> 27.3 us
  starting transfers between devices: 44.6 us -> 47 us
  other arithmetic: 13.5 us -> 11.3 us
    ppermute x4 -> x2, waiting for transfers between devices: 15.4 us -> 3.08 us  [exchange_cols(): far = lax.ppermute(packed, axes, mirror_pairs(False, True, False))]
    ppermute x7, waiting for transfers between devices: 1.86 us -> 11.2 us  [reduce_everywhere(): packed = lax.ppermute(packed, axes, [(i, i ^ offset) for i in range(count)])]
    ppermute x2, starting transfers between devices: 4.48 us -> 8.88 us  [exchange_rows(): row_cross = lax.ppermute(edge, axes, mirror_pairs(True, True, True))]
    ppermute x7, waiting for transfers between devices: 4.1 us -> 0.02 us  [reduce_everywhere(): lax.ppermute(part, axes, [(i, i ^ offset) for i in range(count)])]
    ppermute x2, waiting for transfers between devices: 3.88 us -> 0.01 us  [exchange_rows(): row_same = lax.ppermute(edge, axes, mirror_pairs(True, False, True))]
    ppermute x2, waiting for transfers between devices: 0.01 us -> 2.8 us  [exchange_cols(): beside = lax.ppermute(edges, axes, shifted_pairs(0, 1))]
    ppermute x2, waiting for transfers between devices: 1.28 us -> 3.68 us  [exchange_rows(): up = lax.ppermute(bottom, axes, shifted_pairs(1, 0))]
    another operation x2 -> x3, other arithmetic: 0.1 us -> 1.89 us  [reduce_everywhere(): stacked = jnp.stack(pieces, 0)]
  transfers between devices with their start and end apart: 28 -> 26, of which waited for: 9 -> 10; matrix products, arithmetic and copies ran while one was open for 9% -> 11% of each run, Pallas kernels for 9% -> 9%
where the time goes in v10:
time: 124 us
  starting transfers between devices  47 us (38%)
  waiting for transfers between devices  27.3 us (22%)
  Pallas kernels  19.8 us (16%)
  other arithmetic  11.3 us (9%)
  matrix products  9.87 us (8%)
  local copies, waits for them, and re-layouts  7.34 us (6%)
    ppermute x7, waiting for transfers between devices, reduce_everywhere(): packed = lax.ppermute(packed, axes, [(i, i ^ offset) for i in range(count)])  11.2 us
    ppermute x2, starting transfers between devices, exchange_rows(): row_cross = lax.ppermute(edge, axes, mirror_pairs(True, True, True))  8.88 us
    ppermute x2, starting transfers between devices, exchange_rows(): down = lax.ppermute(top, axes, shifted_pairs(-1, 0))  8.86 us
    ppermute x7, starting transfers between devices, reduce_everywhere(): lax.ppermute(part, axes, [(i, i ^ offset) for i in range(count)])  8 us
    ppermute x7, starting transfers between devices, reduce_everywhere(): packed = lax.ppermute(packed, axes, [(i, i ^ offset) for i in range(count)])  8 us
    ppermute x2, waiting for transfers between devices, exchange_rows(): row_cross = lax.ppermute(edge, axes, mirror_pairs(True, True, True))  6.44 us
    ppermute x2, starting transfers between devices, exchange_rows(): row_same = lax.ppermute(edge, axes, mirror_pairs(True, False, True))  6.14 us
    conv_general_dilated x2, matrix products, conv(): lax.conv_general_dilated(value, taps, (1, 1), 'VALID', rhs_dilation=(DILA...  6.08 us
  transfers between devices with their start and end apart: 26, of which 10 were waited for; matrix products, arithmetic and copies ran while one was open for 11% of the time, Pallas kernels for 9%

profile of v10, /device:TPU:0, one launch (start us, length us, event | category | flops | bytes accessed | tf_op | source)
XLA Modules:
  0.0 123.7 jit_solution(16432027075264671765)
XLA Ops:
  2.0 3.0 %collective-permute-start = (bf16[12,16,256]{2,1,0:T(8,128)(2,1)S(1)}, bf16[12,16,256]{2,1,0:T(8,128)(2,1)S(1)}, u32[]{:S(2)}, u32[]{:S(2)}) collective-permute-start(bf16[12,16,256]{2,1,0:T(8,128)(2,1)S(1)} %constant_dynamic-update-slice_fusion.edges), channel_id=1, source_target_pairs={{0,1},{1,0},{2,3},{3,2},{4,5},{5,4},{6,7},{7,6},{8,9},{9,8},{10,11... | collective-permute-start | bytes 294920 | tf_op jit(solution)/shard_map/ppermute | solution.py:300
  5.0 2.8 %collective-permute-done.beside = bf16[12,16,256]{2,1,0:T(8,128)(2,1)S(1)} collective-permute-done((bf16[12,16,256]{2,1,0:T(8,128)(2,1)S(1)}, bf16[12,16,256]{2,1,0:T(8,128)(2,1)S(1)}, u32[]{:S(2)}, u32[]{:S(2)}) %collective-permute-start) | collective-permute-done | bytes 98336 | tf_op jit(solution)/shard_map/ppermute | solution.py:300
  7.8 3.2 %collective-permute-start.1 = (bf16[12,16,256]{2,1,0:T(8,128)(2,1)S(1)}, bf16[12,16,256]{2,1,0:T(8,128)(2,1)S(1)}, u32[]{:S(2)}, u32[]{:S(2)}) collective-permute-start(bf16[12,16,256]{2,1,0:T(8,128)(2,1)S(1)} %maximum_select_fusion), channel_id=1, source_target_pairs={{0,30},{1,31},{2,28},{3,29},{4,26},{5,27},{6,24},{7,25},{8,22},{9,... | collective-permute-start | bytes 294920 | tf_op jit(solution)/shard_map/ppermute | solution.py:315
  12.0 3.1 %collective-permute-done.1.far = bf16[12,16,256]{2,1,0:T(8,128)(2,1)S(1)} collective-permute-done((bf16[12,16,256]{2,1,0:T(8,128)(2,1)S(1)}, bf16[12,16,256]{2,1,0:T(8,128)(2,1)S(1)}, u32[]{:S(2)}, u32[]{:S(2)}) %collective-permute-start.1) | collective-permute-done | bytes 98336 | tf_op jit(solution)/shard_map/ppermute | solution.py:315
  15.0 3.0 %shard_map.129 = (bf16[12,16,256]{2,1,0:T(8,128)(2,1)S(1)}, bf16[12,72,256]{2,1,0:T(8,128)(2,1)}, bf16[12,72,256]{2,1,0:T(8,128)(2,1)}, bf16[12,72,256]{2,1,0:T(8,128)(2,1)S(1)}) custom-call(s32[144]{0:T(256)S(1)} %reshape.45.adjacency, bf16[12,16,256]{2,1,0:T(8,128)(2,1)S(1)} %constant_dynamic-update-slice_fusion.edges, ...), custom_call_target="tpu_custom_call" | custom-call | flops 1000 | bytes 3000000 | tf_op jit(solution)/shard_map/pallas_call | solution.py:331
  18.0 4.1 %collective-permute-start.4 = (bf16[12,72,256]{2,1,0:T(8,128)(2,1)S(1)}, bf16[12,72,256]{2,1,0:T(8,128)(2,1)S(1)}, u32[]{:S(2)}, u32[]{:S(2)}) collective-permute-start(bf16[12,72,256]{2,1,0:T(8,128)(2,1)S(1)} %get-tuple-element.19.refs_2_), channel_id=1, source_target_pairs={{0,1},{1,0},{30,31},{31,30}} | collective-permute-start | bytes 1327112 | tf_op jit(solution)/shard_map/ppermute | solution.py:322
  22.1 3.7 %collective-permute-start.5 = (bf16[12,72,256]{2,1,0:T(8,128)(2,1)S(1)}, bf16[12,72,256]{2,1,0:T(8,128)(2,1)S(1)}, u32[]{:S(2)}, u32[]{:S(2)}) collective-permute-start(bf16[12,72,256]{2,1,0:T(8,128)(2,1)S(1)} %get-tuple-element.19.refs_2_), channel_id=1, source_target_pairs={{0,31},{1,30},{30,1},{31,0}} | collective-permute-start | bytes 1327112 | tf_op jit(solution)/shard_map/ppermute | solution.py:323
  25.9 4.4 %collective-permute-start.3 = (bf16[12,72,256]{2,1,0:T(8,128)(2,1)}, bf16[12,72,256]{2,1,0:T(8,128)(2,1)S(1)}, u32[]{:S(2)}, u32[]{:S(2)}) collective-permute-start(bf16[12,72,256]{2,1,0:T(8,128)(2,1)} %get-tuple-element.18), channel_id=1, source_target_pairs={{0,30},{1,31},{2,0},{3,1},{4,2},{5,3},{6,4},{7,5},{8,6},{9,7},{10,... | collective-permute-start | bytes 1327112 | tf_op jit(solution)/shard_map/ppermute | solution.py:321
  30.4 6.4 %collective-permute-done.5.refs_4_ = bf16[12,72,256]{2,1,0:T(8,128)(2,1)S(1)} collective-permute-done((bf16[12,72,256]{2,1,0:T(8,128)(2,1)S(1)}, bf16[12,72,256]{2,1,0:T(8,128)(2,1)S(1)}, u32[]{:S(2)}, u32[]{:S(2)}) %collective-permute-start.5) | collective-permute-done | bytes 442400 | tf_op jit(solution)/shard_map/ppermute | solution.py:323
  36.8 3.3 %collective-permute-done.2.refs_0_ = bf16[12,72,256]{2,1,0:T(8,128)(2,1)S(1)} collective-permute-done((bf16[12,72,256]{2,1,0:T(8,128)(2,1)}, bf16[12,72,256]{2,1,0:T(8,128)(2,1)S(1)}, u32[]{:S(2)}, u32[]{:S(2)}) %collective-permute-start.2) | collective-permute-done | bytes 442400 | tf_op jit(solution)/shard_map/ppermute | solution.py:320
  40.1 5.5 %shard_map.130 = bf16[12,8,36,256]{3,2,1,0:T(8,128)(2,1)S(1)} custom-call(s32[144]{0:T(256)S(1)} %reshape.45.adjacency, bf16[4,72,72]{2,1,0:T(8,128)(2,1)S(1)} %copy-done.3, bf16[320,384]{1,0:T(8,128)(2,1)S(1)} %copy-done.1, bf16[12,4,32,256]{3,2,1,0:T(8,128)(2,1)S(1)} %copy-done, bf16[12,16,256]{2,1,0:T(8,128)(2,1)S(1)} %get-tuple-element.16.sides, ...), custom_call_target="tpu_custom_call" | custom-call | flops 1000 | bytes 5000000 | tf_op jit(solution)/shard_map/pallas_call | solution.py:358
  45.6 3.0 %fusion.2 = f32[12,4,32,256]{3,0,2,1:T(8,128)S(1)} fusion(bf16[3,3,256,256]{3,2,1,0:T(8,128)(2,1)S(1)} %copy-done.5, bf16[12,8,36,256]{3,2,1,0:T(8,128)(2,1)S(1)} %shard_map.130), kind=kOutput, calls=%fused_computation.3 | convolution fusion | flops 1811939328 | bytes 4521984 | tf_op jit(solution)/shard_map/conv_general_dilated | solution.py:574
  48.7 2.5 %fusion.9 = (bf16[12,4,32,256]{3,2,1,0:T(8,128)(2,1)S(1)}, bf16[12,4,32,256]{3,2,1,0:T(8,128)(2,1)}) fusion(bf16[12,4,32,256]{3,2,1,0:T(8,128)(2,1)S(1)} %copy-done.7, f32[256]{0:T(256)S(1)} %copy-done.9, f32[12,4,32,256]{3,0,2,1:T(8,128)S(1)} %fusion.2), kind=kLoop, calls=%fused_computation.11 | loop fusion | flops 5898240 | bytes 3933184 | tf_op jit(solution)/shard_map/convert_element_type | solution.py:685
  57.0 1.5 %collective-permute-done.12 = bf16[1160,256]{1,0:T(8,128)(2,1)} collective-permute-done((bf16[1160,256]{1,0:T(8,128)(2,1)}, bf16[1160,256]{1,0:T(8,128)(2,1)}, u32[]{:S(2)}, u32[]{:S(2)}) %collective-permute-start.12) | collective-permute-done | bytes 593952 | tf_op jit(solution)/shard_map/ppermute | solution.py:649
  61.2 2.9 %collective-permute-start.15 = (bf16[296,256]{1,0:T(8,128)(2,1)S(1)}, bf16[296,256]{1,0:T(8,128)(2,1)S(1)}, u32[]{:S(2)}, u32[]{:S(2)}) collective-permute-start(bf16[296,256]{1,0:T(8,128)(2,1)S(1)} %get-tuple-element.63), channel_id=1, source_target_pairs={{0,5},{1,4},{2,7},{3,6},{4,1},{5,0},{6,3},{7,2},{8,13},{9,12},{10,... | collective-permute-start | bytes 454664 | tf_op jit(solution)/shard_map/ppermute | solution.py:649
  64.1 3.3 %collective-permute-done.13 = bf16[296,256]{1,0:T(8,128)(2,1)S(1)} collective-permute-done((bf16[296,256]{1,0:T(8,128)(2,1)S(1)}, bf16[296,256]{1,0:T(8,128)(2,1)S(1)}, u32[]{:S(2)}, u32[]{:S(2)}) %collective-permute-start.13) | collective-permute-done | bytes 151584 | tf_op jit(solution)/shard_map/ppermute | solution.py:649
  67.4 2.7 %collective-permute-done.14 = bf16[296,256]{1,0:T(8,128)(2,1)S(1)} collective-permute-done((bf16[296,256]{1,0:T(8,128)(2,1)S(1)}, bf16[296,256]{1,0:T(8,128)(2,1)S(1)}, u32[]{:S(2)}, u32[]{:S(2)}) %collective-permute-start.14) | collective-permute-done | bytes 151584 | tf_op jit(solution)/shard_map/ppermute | solution.py:649
  70.3 2.3 %collective-permute-start.17 = (bf16[80,256]{1,0:T(8,128)(2,1)S(1)}, bf16[80,256]{1,0:T(8,128)(2,1)S(1)}, u32[]{:S(2)}, u32[]{:S(2)}) collective-permute-start(bf16[80,256]{1,0:T(8,128)(2,1)S(1)} %get-tuple-element.59), channel_id=1, source_target_pairs={{0,16},{1,17},{2,18},{3,19},{4,20},{5,21},{6,22},{7,23},{8,24},{9,... | collective-permute-start | bytes 122888 | tf_op jit(solution)/shard_map/ppermute | solution.py:649
  72.7 2.0 %collective-permute-start.18 = (bf16[80,256]{1,0:T(8,128)(2,1)S(1)}, bf16[80,256]{1,0:T(8,128)(2,1)S(1)}, u32[]{:S(2)}, u32[]{:S(2)}) collective-permute-start(bf16[80,256]{1,0:T(8,128)(2,1)S(1)} %get-tuple-element.60), channel_id=1, source_target_pairs={{0,24},{1,25},{2,26},{3,27},{4,28},{5,29},{6,30},{7,31},{8,16},{9,... | collective-permute-start | bytes 122888 | tf_op jit(solution)/shard_map/ppermute | solution.py:649
  75.4 3.2 %collective-permute-done.18 = bf16[80,256]{1,0:T(8,128)(2,1)S(1)} collective-permute-done((bf16[80,256]{1,0:T(8,128)(2,1)S(1)}, bf16[80,256]{1,0:T(8,128)(2,1)S(1)}, u32[]{:S(2)}, u32[]{:S(2)}) %collective-permute-start.18) | collective-permute-done | bytes 40992 | tf_op jit(solution)/shard_map/ppermute | solution.py:649
  78.7 2.6 %collective-permute-start.20 = (bf16[1,72,256]{2,1,0:T(8,128)(2,1)S(1)}, bf16[1,72,256]{2,1,0:T(8,128)(2,1)S(1)}, u32[]{:S(2)}, u32[]{:S(2)}) collective-permute-start(bf16[1,72,256]{2,1,0:T(8,128)(2,1)S(1)} %bitcast.209), channel_id=1, source_target_pairs={{0,16},{1,17},{2,18},{3,19},{4,20},{5,21},{6,22},{7,23},{8,24},{9,... | collective-permute-start | bytes 110600 | tf_op jit(solution)/shard_map/ppermute | solution.py:664
  81.3 1.8 %collective-permute-start.21 = (bf16[1,72,256]{2,1,0:T(8,128)(2,1)S(1)}, bf16[1,72,256]{2,1,0:T(8,128)(2,1)S(1)}, u32[]{:S(2)}, u32[]{:S(2)}) collective-permute-start(bf16[1,72,256]{2,1,0:T(8,128)(2,1)S(1)} %bitcast.210), channel_id=1, source_target_pairs={{0,24},{1,25},{2,26},{3,27},{4,28},{5,29},{6,30},{7,31},{8,16},{9,... | collective-permute-start | bytes 110600 | tf_op jit(solution)/shard_map/ppermute | solution.py:664
  83.1 2.0 %shard_map.131 = (bf16[12,16,256]{2,1,0:T(8,128)(2,1)S(1)}, bf16[12,72,256]{2,1,0:T(8,128)(2,1)S(1)}, bf16[12,72,256]{2,1,0:T(8,128)(2,1)S(1)}, bf16[12,72,256]{2,1,0:T(8,128)(2,1)S(1)}) custom-call(s32[144]{0:T(256)S(1)} %reshape.45.adjacency, bf16[12,16,256]{2,1,0:T(8,128)(2,1)S(1)} %constant_dynamic-update-slice_fusion.2.edges, ...), custom_call_target="tpu_custom_call" | custom-call | flops 1000 | bytes 3000000 | tf_op jit(solution)/shard_map/pallas_call | solution.py:331
  85.2 4.4 %collective-permute-start.9 = (bf16[12,72,256]{2,1,0:T(8,128)(2,1)S(1)}, bf16[12,72,256]{2,1,0:T(8,128)(2,1)S(1)}, u32[]{:S(2)}, u32[]{:S(2)}) collective-permute-start(bf16[12,72,256]{2,1,0:T(8,128)(2,1)S(1)} %get-tuple-element.24), channel_id=1, source_target_pairs={{0,30},{1,31},{2,0},{3,1},{4,2},{5,3},{6,4},{7,5},{8,6},{9,7},{10,... | collective-permute-start | bytes 1327112 | tf_op jit(solution)/shard_map/ppermute | solution.py:321
  90.9 3.0 %collective-permute-start.24 = (bf16[4,72,256]{2,1,0:T(8,128)(2,1)}, bf16[4,72,256]{2,1,0:T(8,128)(2,1)}, u32[]{:S(2)}, u32[]{:S(2)}) collective-permute-start(bf16[4,72,256]{2,1,0:T(8,128)(2,1)} %get-tuple-element.46), channel_id=1, source_target_pairs={{0,5},{1,4},{2,7},{3,6},{4,1},{5,0},{6,3},{7,2},{8,13},{9,12},{10,... | collective-permute-start | bytes 442376 | tf_op jit(solution)/shard_map/ppermute | solution.py:664
  93.9 2.4 %copy.22 = bf16[3,3,256,256]{2,3,1,0:T(8,128)(2,1)} copy(bf16[3,3,256,256]{3,2,1,0:T(8,128)(2,1)} %param.11) | data formatting | bytes 2359296 | tf_op args[1]
  98.0 2.0 %collective-permute-start.10 = (bf16[12,72,256]{2,1,0:T(8,128)(2,1)S(1)}, bf16[12,72,256]{2,1,0:T(8,128)(2,1)S(1)}, u32[]{:S(2)}, u32[]{:S(2)}) collective-permute-start(bf16[12,72,256]{2,1,0:T(8,128)(2,1)S(1)} %get-tuple-element.27.edge), channel_id=1, source_target_pairs={{0,1},{1,0},{30,31},{31,30}} | collective-permute-start | bytes 1327112 | tf_op jit(solution)/shard_map/ppermute | solution.py:322
  100.1 5.2 %collective-permute-start.11 = (bf16[12,72,256]{2,1,0:T(8,128)(2,1)S(1)}, bf16[12,72,256]{2,1,0:T(8,128)(2,1)S(1)}, u32[]{:S(2)}, u32[]{:S(2)}) collective-permute-start(bf16[12,72,256]{2,1,0:T(8,128)(2,1)S(1)} %get-tuple-element.27.edge), channel_id=1, source_target_pairs={{0,31},{1,30},{30,1},{31,0}} | collective-permute-start | bytes 1327112 | tf_op jit(solution)/shard_map/ppermute | solution.py:323
  105.3 3.4 %shard_map.132 = (bf16[12,8,36,256]{3,2,1,0:T(8,128)(2,1)S(1)}, f32[12,4,32,256]{3,2,1,0:T(8,128)S(1)}) custom-call(s32[144]{0:T(256)S(1)} %reshape.45.adjacency, bf16[320,384]{1,0:T(8,128)(2,1)S(1)} %copy-done.1, bf16[2,24,384]{2,1,0:T(8,128)(2,1)S(1)} %copy-done.4, bf16[3,3,256,256]{3,2,1,0:T(8,128)(2,1)S(1)} %reverse_bitcast_fusion.rotated, ...), custom_call_target="tpu_custom_call" | custom-call | flops 1000 | bytes 8000000 | tf_op jit(solution)/shard_map/pallas_call | solution.py:534
  111.1 3.1 %fusion = f32[12,4,32,256]{3,0,2,1:T(8,128)S(1)} fusion(bf16[3,3,256,256]{3,2,1,0:T(8,128)(2,1)S(1)} %copy-done.6, bf16[12,8,36,256]{3,2,1,0:T(8,128)(2,1)S(1)} %get-tuple-element.25), kind=kOutput, calls=%fused_computation.1 | convolution fusion | flops 1811939328 | bytes 4521984 | tf_op jit(solution)/shard_map/conv_general_dilated | solution.py:574
  115.2 5.9 %shard_map.133 = bf16[12,4,32,256]{3,2,1,0:T(8,128)(2,1)} custom-call(s32[144]{0:T(256)S(1)} %reshape.45.adjacency, bf16[4,192,72]{2,1,0:T(8,128)(2,1)S(1)} %copy-done.2, bf16[3,3,256,256]{3,2,1,0:T(8,128)(2,1)S(1)} %reverse_bitcast_fusion.rotated, f32[12,4,32,256]{3,2,1,0:T(8,128)S(1)} %copy_add_fusion.partial, ...), custom_call_target="tpu_custom_call" | custom-call | flops 1000 | bytes 5000000 | tf_op jit(solution)/shard_map/pallas_call | solution.py:555
  122.1 1.6 %convert_multiply_fusion = f32[32,72,256]{2,1,0:T(8,128)} fusion(bf16[16,72,256]{2,1,0:T(8,128)(2,1)S(1)} %get-tuple-element.31, bf16[16,72,256]{2,1,0:T(8,128)(2,1)S(1)} %get-tuple-element.30), kind=kLoop, calls=%fused_computation.5 | loop fusion | flops 1769472 | bytes 3538944 | tf_op jit(solution)/shard_map/mul | solution.py:708
  (102 shorter events, 19.0 us)
Async XLA Ops:
  0.6 39.5 %copy-start.3 = (bf16[4,72,72]{2,1,0:T(8,128)(2,1)S(1)}, bf16[4,72,72]{2,1,0:T(8,128)(2,1)}, u32[]{:S(2)}) copy-start(bf16[4,72,72]{2,1,0:T(8,128)(2,1)} %constant.70.clone.flips) | copy-start | bytes 124420
  0.6 39.5 %copy-start.1 = (bf16[320,384]{1,0:T(8,128)(2,1)S(1)}, bf16[320,384]{1,0:T(8,128)(2,1)}, u32[]{:S(2)}) copy-start(bf16[320,384]{1,0:T(8,128)(2,1)} %constant.71.clone.picks) | copy-start | bytes 737284
  0.7 14.4 %copy-start = (bf16[12,4,32,256]{3,2,1,0:T(8,128)(2,1)S(1)}, bf16[12,4,32,256]{3,2,1,0:T(8,128)(2,1)}, u32[]{:S(2)}) copy-start(bf16[12,4,32,256]{3,2,1,0:T(8,128)(2,1)} %field.1) | copy-start | bytes 2359300
  2.0 5.8 %collective-permute-start = (bf16[12,16,256]{2,1,0:T(8,128)(2,1)S(1)}, bf16[12,16,256]{2,1,0:T(8,128)(2,1)S(1)}, u32[]{:S(2)}, u32[]{:S(2)}) collective-permute-start(bf16[12,16,256]{2,1,0:T(8,128)(2,1)S(1)} %constant_dynamic-update-slice_fusion.edges), channel_id=1, source_target_pairs={{0,1},{1,0},{2,3},{3,2},{4,5},{5,4},{6,7},{7,6},{8,9},{9,8},{10,11... | collective-permute-start | bytes 294920 | tf_op jit(solution)/shard_map/ppermute | solution.py:300
  7.8 7.2 %collective-permute-start.1 = (bf16[12,16,256]{2,1,0:T(8,128)(2,1)S(1)}, bf16[12,16,256]{2,1,0:T(8,128)(2,1)S(1)}, u32[]{:S(2)}, u32[]{:S(2)}) collective-permute-start(bf16[12,16,256]{2,1,0:T(8,128)(2,1)S(1)} %maximum_select_fusion), channel_id=1, source_target_pairs={{0,30},{1,31},{2,28},{3,29},{4,26},{5,27},{6,24},{7,25},{8,22},{9,... | collective-permute-start | bytes 294920 | tf_op jit(solution)/shard_map/ppermute | solution.py:315
  18.0 12.4 %collective-permute-start.4 = (bf16[12,72,256]{2,1,0:T(8,128)(2,1)S(1)}, bf16[12,72,256]{2,1,0:T(8,128)(2,1)S(1)}, u32[]{:S(2)}, u32[]{:S(2)}) collective-permute-start(bf16[12,72,256]{2,1,0:T(8,128)(2,1)S(1)} %get-tuple-element.19.refs_2_), channel_id=1, source_target_pairs={{0,1},{1,0},{30,31},{31,30}} | collective-permute-start | bytes 1327112 | tf_op jit(solution)/shard_map/ppermute | solution.py:322
  22.1 14.7 %collective-permute-start.5 = (bf16[12,72,256]{2,1,0:T(8,128)(2,1)S(1)}, bf16[12,72,256]{2,1,0:T(8,128)(2,1)S(1)}, u32[]{:S(2)}, u32[]{:S(2)}) collective-permute-start(bf16[12,72,256]{2,1,0:T(8,128)(2,1)S(1)} %get-tuple-element.19.refs_2_), channel_id=1, source_target_pairs={{0,31},{1,30},{30,1},{31,0}} | collective-permute-start | bytes 1327112 | tf_op jit(solution)/shard_map/ppermute | solution.py:323
  25.9 14.2 %collective-permute-start.2 = (bf16[12,72,256]{2,1,0:T(8,128)(2,1)}, bf16[12,72,256]{2,1,0:T(8,128)(2,1)S(1)}, u32[]{:S(2)}, u32[]{:S(2)}) collective-permute-start(bf16[12,72,256]{2,1,0:T(8,128)(2,1)} %get-tuple-element.17), channel_id=1, source_target_pairs={{0,2},{1,3},{2,4},{3,5},{4,6},{5,7},{6,8},{7,9},{8,10},{9,11},{10,... | collective-permute-start | bytes 1327112 | tf_op jit(solution)/shard_map/ppermute | solution.py:320
  25.9 14.2 %collective-permute-start.3 = (bf16[12,72,256]{2,1,0:T(8,128)(2,1)}, bf16[12,72,256]{2,1,0:T(8,128)(2,1)S(1)}, u32[]{:S(2)}, u32[]{:S(2)}) collective-permute-start(bf16[12,72,256]{2,1,0:T(8,128)(2,1)} %get-tuple-element.18), channel_id=1, source_target_pairs={{0,30},{1,31},{2,0},{3,1},{4,2},{5,3},{6,4},{7,5},{8,6},{9,7},{10,... | collective-permute-start | bytes 1327112 | tf_op jit(solution)/shard_map/ppermute | solution.py:321
  40.1 5.5 %copy-start.5 = (bf16[3,3,256,256]{3,2,1,0:T(8,128)(2,1)S(1)}, bf16[3,3,256,256]{3,2,1,0:T(8,128)(2,1)}, u32[]{:S(2)}) copy-start(bf16[3,3,256,256]{3,2,1,0:T(8,128)(2,1)} %param.11) | copy-start | bytes 3538948
  56.2 2.4 %collective-permute-start.12 = (bf16[1160,256]{1,0:T(8,128)(2,1)}, bf16[1160,256]{1,0:T(8,128)(2,1)}, u32[]{:S(2)}, u32[]{:S(2)}) collective-permute-start(bf16[1160,256]{1,0:T(8,128)(2,1)} %pad_maximum_fusion), channel_id=1, source_target_pairs={{0,2},{1,3},{2,0},{3,1},{4,6},{5,7},{6,4},{7,5},{8,10},{9,11},{10,... | collective-permute-start | bytes 1781768 | tf_op jit(solution)/shard_map/ppermute | solution.py:649
  56.4 7.7 %collective-permute-start.6 = (bf16[12,16,256]{2,1,0:T(8,128)(2,1)S(1)}, bf16[12,16,256]{2,1,0:T(8,128)(2,1)S(1)}, u32[]{:S(2)}, u32[]{:S(2)}) collective-permute-start(bf16[12,16,256]{2,1,0:T(8,128)(2,1)S(1)} %constant_dynamic-update-slice_fusion.2.edges), channel_id=1, source_target_pairs={{0,1},{1,0},{2,3},{3,2},{4,5},{5,4},{6,7},{7,6},{8,9},{9,8},{10,11... | collective-permute-start | bytes 294920 | tf_op jit(solution)/shard_map/ppermute | solution.py:300
  60.5 6.8 %collective-permute-start.13 = (bf16[296,256]{1,0:T(8,128)(2,1)S(1)}, bf16[296,256]{1,0:T(8,128)(2,1)S(1)}, u32[]{:S(2)}, u32[]{:S(2)}) collective-permute-start(bf16[296,256]{1,0:T(8,128)(2,1)S(1)} %get-tuple-element.61), channel_id=1, source_target_pairs={{0,1},{1,0},{2,3},{3,2},{4,5},{5,4},{6,7},{7,6},{8,9},{9,8},{10,11... | collective-permute-start | bytes 454664 | tf_op jit(solution)/shard_map/ppermute | solution.py:649
  61.2 8.9 %collective-permute-start.14 = (bf16[296,256]{1,0:T(8,128)(2,1)S(1)}, bf16[296,256]{1,0:T(8,128)(2,1)S(1)}, u32[]{:S(2)}, u32[]{:S(2)}) collective-permute-start(bf16[296,256]{1,0:T(8,128)(2,1)S(1)} %get-tuple-element.62), channel_id=1, source_target_pairs={{0,4},{1,5},{2,6},{3,7},{4,0},{5,1},{6,2},{7,3},{8,12},{9,13},{10,... | collective-permute-start | bytes 454664 | tf_op jit(solution)/shard_map/ppermute | solution.py:649
  61.2 8.9 %collective-permute-start.15 = (bf16[296,256]{1,0:T(8,128)(2,1)S(1)}, bf16[296,256]{1,0:T(8,128)(2,1)S(1)}, u32[]{:S(2)}, u32[]{:S(2)}) collective-permute-start(bf16[296,256]{1,0:T(8,128)(2,1)S(1)} %get-tuple-element.63), channel_id=1, source_target_pairs={{0,5},{1,4},{2,7},{3,6},{4,1},{5,0},{6,3},{7,2},{8,13},{9,12},{10,... | collective-permute-start | bytes 454664 | tf_op jit(solution)/shard_map/ppermute | solution.py:649
  70.3 4.6 %collective-permute-start.16 = (bf16[80,256]{1,0:T(8,128)(2,1)S(1)}, bf16[80,256]{1,0:T(8,128)(2,1)S(1)}, u32[]{:S(2)}, u32[]{:S(2)}) collective-permute-start(bf16[80,256]{1,0:T(8,128)(2,1)S(1)} %get-tuple-element.58), channel_id=1, source_target_pairs={{0,8},{1,9},{2,10},{3,11},{4,12},{5,13},{6,14},{7,15},{8,0},{9,1},... | collective-permute-start | bytes 122888 | tf_op jit(solution)/shard_map/ppermute | solution.py:649
  70.3 5.0 %collective-permute-start.17 = (bf16[80,256]{1,0:T(8,128)(2,1)S(1)}, bf16[80,256]{1,0:T(8,128)(2,1)S(1)}, u32[]{:S(2)}, u32[]{:S(2)}) collective-permute-start(bf16[80,256]{1,0:T(8,128)(2,1)S(1)} %get-tuple-element.59), channel_id=1, source_target_pairs={{0,16},{1,17},{2,18},{3,19},{4,20},{5,21},{6,22},{7,23},{8,24},{9,... | collective-permute-start | bytes 122888 | tf_op jit(solution)/shard_map/ppermute | solution.py:649
  72.7 5.9 %collective-permute-start.18 = (bf16[80,256]{1,0:T(8,128)(2,1)S(1)}, bf16[80,256]{1,0:T(8,128)(2,1)S(1)}, u32[]{:S(2)}, u32[]{:S(2)}) collective-permute-start(bf16[80,256]{1,0:T(8,128)(2,1)S(1)} %get-tuple-element.60), channel_id=1, source_target_pairs={{0,24},{1,25},{2,26},{3,27},{4,28},{5,29},{6,30},{7,31},{8,16},{9,... | collective-permute-start | bytes 122888 | tf_op jit(solution)/shard_map/ppermute | solution.py:649
  74.8 8.3 %collective-permute-start.7 = (bf16[12,16,256]{2,1,0:T(8,128)(2,1)S(1)}, bf16[12,16,256]{2,1,0:T(8,128)(2,1)S(1)}, u32[]{:S(2)}, u32[]{:S(2)}) collective-permute-start(bf16[12,16,256]{2,1,0:T(8,128)(2,1)S(1)} %maximum_select_fusion.1), channel_id=1, source_target_pairs={{0,30},{1,31},{2,28},{3,29},{4,26},{5,27},{6,24},{7,25},{8,22},{9,... | collective-permute-start | bytes 294920 | tf_op jit(solution)/shard_map/ppermute | solution.py:315
  78.6 11.0 %collective-permute-start.19 = (bf16[1,72,256]{2,1,0:T(8,128)(2,1)S(1)}, bf16[1,72,256]{2,1,0:T(8,128)(2,1)S(1)}, u32[]{:S(2)}, u32[]{:S(2)}) collective-permute-start(bf16[1,72,256]{2,1,0:T(8,128)(2,1)S(1)} %bitcast.208), channel_id=1, source_target_pairs={{0,8},{1,9},{2,10},{3,11},{4,12},{5,13},{6,14},{7,15},{8,0},{9,1},... | collective-permute-start | bytes 110600 | tf_op jit(solution)/shard_map/ppermute | solution.py:664
  78.7 10.9 %collective-permute-start.20 = (bf16[1,72,256]{2,1,0:T(8,128)(2,1)S(1)}, bf16[1,72,256]{2,1,0:T(8,128)(2,1)S(1)}, u32[]{:S(2)}, u32[]{:S(2)}) collective-permute-start(bf16[1,72,256]{2,1,0:T(8,128)(2,1)S(1)} %bitcast.209), channel_id=1, source_target_pairs={{0,16},{1,17},{2,18},{3,19},{4,20},{5,21},{6,22},{7,23},{8,24},{9,... | collective-permute-start | bytes 110600 | tf_op jit(solution)/shard_map/ppermute | solution.py:664
  81.3 8.4 %collective-permute-start.21 = (bf16[1,72,256]{2,1,0:T(8,128)(2,1)S(1)}, bf16[1,72,256]{2,1,0:T(8,128)(2,1)S(1)}, u32[]{:S(2)}, u32[]{:S(2)}) collective-permute-start(bf16[1,72,256]{2,1,0:T(8,128)(2,1)S(1)} %bitcast.210), channel_id=1, source_target_pairs={{0,24},{1,25},{2,26},{3,27},{4,28},{5,29},{6,30},{7,31},{8,16},{9,... | collective-permute-start | bytes 110600 | tf_op jit(solution)/shard_map/ppermute | solution.py:664
  85.1 12.9 %collective-permute-start.8 = (bf16[12,72,256]{2,1,0:T(8,128)(2,1)S(1)}, bf16[12,72,256]{2,1,0:T(8,128)(2,1)S(1)}, u32[]{:S(2)}, u32[]{:S(2)}) collective-permute-start(bf16[12,72,256]{2,1,0:T(8,128)(2,1)S(1)} %get-tuple-element.23), channel_id=1, source_target_pairs={{0,2},{1,3},{2,4},{3,5},{4,6},{5,7},{6,8},{7,9},{8,10},{9,11},{10,... | collective-permute-start | bytes 1327112 | tf_op jit(solution)/shard_map/ppermute | solution.py:320
  85.2 14.9 %collective-permute-start.9 = (bf16[12,72,256]{2,1,0:T(8,128)(2,1)S(1)}, bf16[12,72,256]{2,1,0:T(8,128)(2,1)S(1)}, u32[]{:S(2)}, u32[]{:S(2)}) collective-permute-start(bf16[12,72,256]{2,1,0:T(8,128)(2,1)S(1)} %get-tuple-element.24), channel_id=1, source_target_pairs={{0,30},{1,31},{2,0},{3,1},{4,2},{5,3},{6,4},{7,5},{8,6},{9,7},{10,... | collective-permute-start | bytes 1327112 | tf_op jit(solution)/shard_map/ppermute | solution.py:321
  90.4 18.2 %collective-permute-start.22 = (bf16[4,72,256]{2,1,0:T(8,128)(2,1)}, bf16[4,72,256]{2,1,0:T(8,128)(2,1)}, u32[]{:S(2)}, u32[]{:S(2)}) collective-permute-start(bf16[4,72,256]{2,1,0:T(8,128)(2,1)} %get-tuple-element.46), channel_id=1, source_target_pairs={{0,1},{1,0},{2,3},{3,2},{4,5},{5,4},{6,7},{7,6},{8,9},{9,8},{10,11... | collective-permute-start | bytes 442376 | tf_op jit(solution)/shard_map/ppermute | solution.py:664
  90.9 17.7 %collective-permute-start.23 = (bf16[4,72,256]{2,1,0:T(8,128)(2,1)}, bf16[4,72,256]{2,1,0:T(8,128)(2,1)}, u32[]{:S(2)}, u32[]{:S(2)}) collective-permute-start(bf16[4,72,256]{2,1,0:T(8,128)(2,1)} %get-tuple-element.46), channel_id=1, source_target_pairs={{0,4},{1,5},{2,6},{3,7},{4,0},{5,1},{6,2},{7,3},{8,12},{9,13},{10,... | collective-permute-start | bytes 442376 | tf_op jit(solution)/shard_map/ppermute | solution.py:664
  90.9 17.8 %collective-permute-start.24 = (bf16[4,72,256]{2,1,0:T(8,128)(2,1)}, bf16[4,72,256]{2,1,0:T(8,128)(2,1)}, u32[]{:S(2)}, u32[]{:S(2)}) collective-permute-start(bf16[4,72,256]{2,1,0:T(8,128)(2,1)} %get-tuple-element.46), channel_id=1, source_target_pairs={{0,5},{1,4},{2,7},{3,6},{4,1},{5,0},{6,3},{7,2},{8,13},{9,12},{10,... | collective-permute-start | bytes 442376 | tf_op jit(solution)/shard_map/ppermute | solution.py:664
  96.3 9.0 %copy-start.4 = (bf16[2,24,384]{2,1,0:T(8,128)(2,1)S(1)}, bf16[2,24,384]{2,1,0:T(8,128)(2,1)}, u32[]{:S(2)}) copy-start(bf16[2,24,384]{2,1,0:T(8,128)(2,1)} %constant.72.clone.col_picks) | copy-start | bytes 110596
  98.0 17.1 %collective-permute-start.10 = (bf16[12,72,256]{2,1,0:T(8,128)(2,1)S(1)}, bf16[12,72,256]{2,1,0:T(8,128)(2,1)S(1)}, u32[]{:S(2)}, u32[]{:S(2)}) collective-permute-start(bf16[12,72,256]{2,1,0:T(8,128)(2,1)S(1)} %get-tuple-element.27.edge), channel_id=1, source_target_pairs={{0,1},{1,0},{30,31},{31,30}} | collective-permute-start | bytes 1327112 | tf_op jit(solution)/shard_map/ppermute | solution.py:322
  100.1 15.1 %collective-permute-start.11 = (bf16[12,72,256]{2,1,0:T(8,128)(2,1)S(1)}, bf16[12,72,256]{2,1,0:T(8,128)(2,1)S(1)}, u32[]{:S(2)}, u32[]{:S(2)}) collective-permute-start(bf16[12,72,256]{2,1,0:T(8,128)(2,1)S(1)} %get-tuple-element.27.edge), channel_id=1, source_target_pairs={{0,31},{1,30},{30,1},{31,0}} | collective-permute-start | bytes 1327112 | tf_op jit(solution)/shard_map/ppermute | solution.py:323
  105.3 3.4 %copy-start.8 = (bf16[1,4,72,256]{3,2,1,0:T(8,128)(2,1)S(1)}, bf16[1,4,72,256]{3,2,1,0:T(8,128)(2,1)}, u32[]{:S(2)}) copy-start(bf16[1,4,72,256]{3,2,1,0:T(8,128)(2,1)} %get-tuple-element.45) | copy-start | bytes 442372
  110.0 11.7 %collective-permute-start.25 = (bf16[16,72,256]{2,1,0:T(8,128)(2,1)S(1)}, bf16[16,72,256]{2,1,0:T(8,128)(2,1)S(1)}, u32[]{:S(2)}, u32[]{:S(2)}) collective-permute-start(bf16[16,72,256]{2,1,0:T(8,128)(2,1)S(1)} %get-tuple-element.36), channel_id=1, source_target_pairs={{0,2},{1,3},{2,0},{3,1},{4,6},{5,7},{6,4},{7,5},{8,10},{9,11},{10,... | collective-permute-start | bytes 1769480 | tf_op jit(solution)/shard_map/ppermute | solution.py:664
  (4 other events, 8.4 us)
